TPU v7x, 32 devices: a whole 2x2x4 slice. The times are simulated.
32 devices in a mesh: dp: 4 (over x, core), context: 4 (over z), tensor: 2 (over y).
Axes of the slice: x: 2, y: 2, z: 4, core: 2. Of those that a mesh axis runs over, the one named last changes fastest.
Arguments:
- tokens: bfloat16 [8, 1024, 768], P('dp', 'context'), may hold values from -6 to 6
- lengths: int32 [8], P('dp'), may hold values from 256 to 1024, as said below
- ln1_gain: bfloat16 [768], replicated, may hold values from 0.099609375 to 1.8984375
- ln1_bias: bfloat16 [768], replicated, may hold values from -2 to 2
- w_query: bfloat16 [768, 768], P('dp', 'tensor'), may hold values from -0.21875 to 0.21875
- b_query: bfloat16 [768], P('tensor'), may hold values from -3 to 3
- w_key: bfloat16 [768, 768], P('dp', 'tensor'), may hold values from -0.21875 to 0.21875
- w_value: bfloat16 [768, 768], P('dp', 'tensor'), may hold values from -0.21875 to 0.21875
- b_value: bfloat16 [768], P('tensor'), may hold values from -0.29882812 to 0.29882812
- w_out: bfloat16 [768, 768], P('tensor', 'dp'), may hold values from -1.75 to 1.75
- b_out: bfloat16 [768], replicated, may hold values from -2 to 2
- ln2_gain: bfloat16 [768], replicated, may hold values from 0.099609375 to 1.8984375
- ln2_bias: bfloat16 [768], replicated, may hold values from -2 to 2
- w_up: bfloat16 [768, 3072], P('dp', 'tensor'), may hold values from -0.21875 to 0.21875
- b_up: bfloat16 [3072], P('tensor'), may hold values from -3 to 3
- w_down: bfloat16 [3072, 768], P('tensor', 'dp'), may hold values from -0.109375 to 0.109375
- b_down: bfloat16 [768], replicated, may hold values from -2 to 2
- cotangent: bfloat16 [8, 1024, 768], P('dp', 'context'), may hold values from -6 to 6
Outputs:
- output: bfloat16 [8, 1024, 768], P('dp', 'context')
- input_grad: bfloat16 [8, 1024, 768], P('dp', 'context')
- grad_ln1_gain: float32 [768], replicated
- grad_ln1_bias: float32 [768], replicated
- grad_w_query: float32 [768, 768], P('dp', 'tensor')
- grad_b_query: float32 [768], P('tensor')
- grad_w_key: float32 [768, 768], P('dp', 'tensor')
- grad_w_value: float32 [768, 768], P('dp', 'tensor')
- grad_b_value: float32 [768], P('tensor')
- grad_w_out: float32 [768, 768], P('tensor', 'dp')
- grad_b_out: float32 [768], replicated
- grad_ln2_gain: float32 [768], replicated
- grad_ln2_bias: float32 [768], replicated
- grad_w_up: float32 [768, 3072], P('dp', 'tensor')
- grad_b_up: float32 [3072], P('tensor')
- grad_w_down: float32 [3072, 768], P('tensor', 'dp')
- grad_b_down: float32 [768], replicated
Inputs may be any that keep to these rules, and one draw needn't show every extreme that they name: Sequence n holds lengths[n] real patch rows at its start, the rest is padding; at least one sequence has 1024 real rows.
All inputs are finite; a program needn't handle non-finite values.
Results may differ from a plain program's by a relative error of at most 0.035.
Values may be sent and summed in bfloat16 or wider, within the bound.
No kernel may reach another device: no remote copies, remote signals or barrier semaphores. Data moves between devices by JAX's collectives and lax.ppermute only.
A program may use at most 192 MiB of HBM per device.

v0:
```python
import jax
import jax.numpy as jnp
from jax import lax
from jax.sharding import PartitionSpec as P

HEAD_DIM = 64


epsilon = 1e-06
masked_value = -1e30


def norm_rows(values, gain_vec, bias_vec):
    average = jnp.mean(values, axis=-1, keepdims=True)
    centred = values - average
    spread = jnp.mean(centred * centred, axis=-1, keepdims=True)
    return centred * lax.rsqrt(spread + epsilon) * gain_vec + bias_vec


def gelu_tanh(values):
    return jax.nn.gelu(values, approximate=True)


def dense(left, right):
    return jnp.dot(left, right, preferred_element_type=jnp.float32)


def dense_tn(left, right):
    return lax.dot_general(
        left, right, (((0,), (0,)), ((), ())), preferred_element_type=jnp.float32
    )


def dense_nt(left, right):
    return lax.dot_general(
        left, right, (((1,), (1,)), ((), ())), preferred_element_type=jnp.float32
    )


def per_device(
    tokens,
    lengths,
    ln1_gain,
    ln1_bias,
    w_query,
    b_query,
    w_key,
    w_value,
    b_value,
    w_out,
    b_out,
    ln2_gain,
    ln2_bias,
    w_up,
    b_up,
    w_down,
    b_down,
    cotangent,
):
    seq_count, shard_rows, width = tokens.shape
    full_len = shard_rows * lax.axis_size("context")
    local_width = w_query.shape[1]
    local_heads = local_width // HEAD_DIM
    scale = HEAD_DIM ** (-0.5)
    row_count = seq_count * shard_rows
    query_weight, key_weight, value_weight, up_weight, out_weight, down_weight = (
        lax.all_gather(w_query, "dp", axis=0, tiled=True),
        lax.all_gather(w_key, "dp", axis=0, tiled=True),
        lax.all_gather(w_value, "dp", axis=0, tiled=True),
        lax.all_gather(w_up, "dp", axis=0, tiled=True),
        lax.all_gather(w_out, "dp", axis=1, tiled=True),
        lax.all_gather(w_down, "dp", axis=1, tiled=True),
    )
    gain_one = ln1_gain.astype(jnp.float32)
    bias_one = ln1_bias.astype(jnp.float32)
    query_bias = b_query.astype(jnp.float32)
    value_bias = b_value.astype(jnp.float32)
    out_bias = b_out.astype(jnp.float32)
    gain_two = ln2_gain.astype(jnp.float32)
    bias_two = ln2_bias.astype(jnp.float32)
    up_bias = b_up.astype(jnp.float32)
    down_bias = b_down.astype(jnp.float32)
    places = lax.axis_index("context") * shard_rows + jnp.arange(shard_rows, dtype=jnp.int32)
    keep = (places[None, :] < lengths[:, None]).astype(jnp.float32).reshape(row_count, 1)
    key_places = jnp.arange(full_len, dtype=jnp.int32)
    rows_in = tokens.reshape(row_count, width).astype(jnp.float32)
    normed_one, pull_one = jax.vjp(norm_rows, rows_in, gain_one, bias_one)
    normed_low = normed_one.astype(jnp.bfloat16)
    queries = (dense(normed_low, query_weight) + query_bias).astype(jnp.bfloat16)
    keys_own = dense(normed_low, key_weight).astype(jnp.bfloat16)
    values_own = (dense(normed_low, value_weight) + value_bias).astype(jnp.bfloat16)
    keys_whole, values_whole = (
        lax.all_gather(
            keys_own.reshape(seq_count, shard_rows, local_width), "context", axis=1, tiled=True
        ),
        lax.all_gather(
            values_own.reshape(seq_count, shard_rows, local_width), "context", axis=1, tiled=True
        ),
    )
    query_heads = queries.reshape(seq_count, shard_rows, local_heads, HEAD_DIM)
    head_outs = []
    log_sums = []
    for member in range(seq_count):
        key_heads = keys_whole[member].reshape(full_len, local_heads, HEAD_DIM)
        value_heads = values_whole[member].reshape(full_len, local_heads, HEAD_DIM)
        raw_scores = (
            jnp.einsum(
                "qhd,khd->hqk", query_heads[member], key_heads, preferred_element_type=jnp.float32
            )
            * scale
        )
        live = (key_places < lengths[member])[None, None, :]
        masked = jnp.where(live, raw_scores, masked_value)
        largest = jnp.max(masked, axis=-1, keepdims=True)
        log_total = largest + jnp.log(jnp.sum(jnp.exp(masked - largest), axis=-1, keepdims=True))
        probs_low = jnp.exp(masked - log_total).astype(jnp.bfloat16)
        mixed_heads = jnp.einsum(
            "hqk,khd->qhd", probs_low, value_heads, preferred_element_type=jnp.float32
        )
        head_outs.append(mixed_heads.reshape(shard_rows, local_width))
        log_sums.append(log_total)
    context_low = jnp.concatenate(head_outs, axis=0).astype(jnp.bfloat16)
    attention = (
        lax.psum(dense(context_low, out_weight).astype(jnp.bfloat16), "tensor").astype(jnp.float32)
        + out_bias
    )
    middle = rows_in + keep * attention
    normed_two, pull_two = jax.vjp(norm_rows, middle, gain_two, bias_two)
    normed_two_low = normed_two.astype(jnp.bfloat16)
    hidden_pre = dense(normed_two_low, up_weight) + up_bias
    hidden, pull_gelu = jax.vjp(gelu_tanh, hidden_pre)
    hidden_low = hidden.astype(jnp.bfloat16)
    feed = (
        lax.psum(dense(hidden_low, down_weight).astype(jnp.bfloat16), "tensor").astype(jnp.float32)
        + down_bias
    )
    output = (middle + keep * feed).astype(jnp.bfloat16).reshape(tokens.shape)
    grad_top = cotangent.reshape(row_count, width).astype(jnp.float32)
    d_feed = (keep * grad_top).astype(jnp.bfloat16)
    grad_down_bias = jnp.sum(d_feed.astype(jnp.float32), axis=0)
    grad_down = dense_tn(hidden_low, d_feed)
    d_hidden = dense_nt(d_feed, down_weight)
    d_pre = pull_gelu(d_hidden)[0].astype(jnp.bfloat16)
    grad_up_bias = jnp.sum(d_pre.astype(jnp.float32), axis=0)
    grad_up = dense_tn(normed_two_low, d_pre)
    d_normed_two = lax.psum(dense_nt(d_pre, up_weight).astype(jnp.bfloat16), "tensor").astype(
        jnp.float32
    )
    d_middle, grad_gain_two, grad_bias_two = pull_two(d_normed_two)
    d_middle = d_middle + grad_top
    d_attention = (keep * d_middle).astype(jnp.bfloat16)
    grad_out_bias = jnp.sum(d_attention.astype(jnp.float32), axis=0)
    grad_out = dense_tn(context_low, d_attention)
    d_context = dense_nt(d_attention, out_weight).astype(jnp.bfloat16)
    back_keys, back_values = (keys_whole, values_whole)
    d_context_heads = d_context.reshape(seq_count, shard_rows, local_heads, HEAD_DIM)
    query_grads = []
    own_grads = []
    inner_rows = []
    for member in range(seq_count):
        key_heads = back_keys[member].reshape(full_len, local_heads, HEAD_DIM)
        value_heads = back_values[member].reshape(full_len, local_heads, HEAD_DIM)
        raw_scores = (
            jnp.einsum(
                "qhd,khd->hqk", query_heads[member], key_heads, preferred_element_type=jnp.float32
            )
            * scale
        )
        live = (key_places < lengths[member])[None, None, :]
        probs = jnp.where(live, jnp.exp(raw_scores - log_sums[member]), 0.0)
        d_probs = jnp.einsum(
            "qhd,khd->hqk", d_context_heads[member], value_heads, preferred_element_type=jnp.float32
        )
        inner = jnp.sum(probs * d_probs, axis=-1, keepdims=True)
        d_scores = (probs * (d_probs - inner)).astype(jnp.bfloat16)
        d_query = (
            jnp.einsum("hqk,khd->qhd", d_scores, key_heads, preferred_element_type=jnp.float32)
            * scale
        )
        query_grads.append(d_query.reshape(shard_rows, local_width))
        inner_rows.append(inner[:, :, 0])
        d_keys = (
            jnp.einsum(
                "hqk,qhd->khd", d_scores, query_heads[member], preferred_element_type=jnp.float32
            )
            * scale
        )
        d_values = jnp.einsum(
            "hqk,qhd->khd",
            probs.astype(jnp.bfloat16),
            d_context_heads[member],
            preferred_element_type=jnp.float32,
        )
        key_term = jnp.concatenate(
            [d_keys.reshape(full_len, local_width), d_values.reshape(full_len, local_width)], axis=1
        )
        own_grads.append(
            lax.psum_scatter(
                key_term.astype(jnp.bfloat16), "context", scatter_dimension=0, tiled=True
            ).astype(jnp.float32)
        )
    d_query_low = jnp.concatenate(query_grads, axis=0).astype(jnp.bfloat16)
    key_value_grads = jnp.concatenate(own_grads, axis=0)
    d_keys_low = key_value_grads[:, :local_width].astype(jnp.bfloat16)
    d_values_low = key_value_grads[:, local_width:].astype(jnp.bfloat16)
    grad_query = dense_tn(normed_low, d_query_low)
    grad_query_bias = jnp.sum(d_query_low.astype(jnp.float32), axis=0)
    grad_key = dense_tn(normed_low, d_keys_low)
    grad_value = dense_tn(normed_low, d_values_low)
    grad_value_bias = jnp.sum(d_values_low.astype(jnp.float32), axis=0)
    d_normed_one = lax.psum(
        (
            dense_nt(d_query_low, query_weight)
            + dense_nt(d_keys_low, key_weight)
            + dense_nt(d_values_low, value_weight)
        ).astype(jnp.bfloat16),
        "tensor",
    ).astype(jnp.float32)
    d_rows, grad_gain_one, grad_bias_one = pull_one(d_normed_one)
    input_grad = (d_rows + d_middle).astype(jnp.bfloat16).reshape(tokens.shape)
    data_sums = (
        lax.psum_scatter(
            grad_query.astype(jnp.bfloat16), "dp", scatter_dimension=0, tiled=True
        ).astype(jnp.float32),
        lax.psum_scatter(
            grad_key.astype(jnp.bfloat16), "dp", scatter_dimension=0, tiled=True
        ).astype(jnp.float32),
        lax.psum_scatter(
            grad_value.astype(jnp.bfloat16), "dp", scatter_dimension=0, tiled=True
        ).astype(jnp.float32),
        lax.psum_scatter(
            grad_up.astype(jnp.bfloat16), "dp", scatter_dimension=0, tiled=True
        ).astype(jnp.float32),
        lax.psum_scatter(
            grad_out.astype(jnp.bfloat16), "dp", scatter_dimension=1, tiled=True
        ).astype(jnp.float32),
        lax.psum_scatter(
            grad_down.astype(jnp.bfloat16), "dp", scatter_dimension=1, tiled=True
        ).astype(jnp.float32),
    )
    owned_sums = (
        lax.psum(data_sums[0].astype(jnp.bfloat16), "context").astype(jnp.float32),
        lax.psum(data_sums[1].astype(jnp.bfloat16), "context").astype(jnp.float32),
        lax.psum(data_sums[2].astype(jnp.bfloat16), "context").astype(jnp.float32),
        lax.psum(data_sums[3].astype(jnp.bfloat16), "context").astype(jnp.float32),
        lax.psum(data_sums[4].astype(jnp.bfloat16), "context").astype(jnp.float32),
        lax.psum(data_sums[5].astype(jnp.bfloat16), "context").astype(jnp.float32),
    )
    small_sums = lax.psum(
        (
            grad_gain_one,
            grad_bias_one,
            grad_query_bias,
            grad_value_bias,
            grad_out_bias,
            grad_gain_two,
            grad_bias_two,
            grad_up_bias,
            grad_down_bias,
        ),
        ("dp", "context"),
    )
    return (
        output,
        input_grad,
        small_sums[0],
        small_sums[1],
        owned_sums[0],
        small_sums[2],
        owned_sums[1],
        owned_sums[2],
        small_sums[3],
        owned_sums[4],
        small_sums[4],
        small_sums[5],
        small_sums[6],
        owned_sums[3],
        small_sums[7],
        owned_sums[5],
        small_sums[8],
    )


def solution(mesh):
    return jax.shard_map(
        per_device,
        mesh=mesh,
        in_specs=(
            P("dp", "context", None),
            P("dp"),
            P(),
            P(),
            P("dp", "tensor"),
            P("tensor"),
            P("dp", "tensor"),
            P("dp", "tensor"),
            P("tensor"),
            P("tensor", "dp"),
            P(),
            P(),
            P(),
            P("dp", "tensor"),
            P("tensor"),
            P("tensor", "dp"),
            P(),
            P("dp", "context", None),
        ),
        out_specs=(
            P("dp", "context", None),
            P("dp", "context", None),
            P(),
            P(),
            P("dp", "tensor"),
            P("tensor"),
            P("dp", "tensor"),
            P("dp", "tensor"),
            P("tensor"),
            P("tensor", "dp"),
            P(),
            P(),
            P(),
            P("dp", "tensor"),
            P("tensor"),
            P("tensor", "dp"),
            P(),
        ),
        check_vma=False,
    )
```

profile of v0, /device:TPU:0, one launch (start us, length us, event | category | flops | bytes accessed | tf_op | source)
XLA Modules:
  0.0 626.5 jit_solution(15701705273460138657)
XLA Ops:
  10.2 1.5 fusion.37
  13.1 9.3 %all_gather.24 = bf16[768,384]{1,0:T(8,128)(2,1)S(1)} all-gather(bf16[192,384]{1,0:T(8,128)(2,1)} %param.25), channel_id=1, replica_groups=mesh['dp'=4,'context'=4,'tensor'=2] {'dp'}, dimensions={0}, use_global_device_ids=true | all-gather | bytes 737280 | tf_op jit(solution)/shard_map/all_gather | solution.py:69
  22.8 1.3 fusion.44
  24.2 7.6 %all_gather.27 = bf16[768,384]{1,0:T(8,128)(2,1)S(1)} all-gather(bf16[192,384]{1,0:T(8,128)(2,1)S(1)} %copy-done.28), channel_id=1, replica_groups=mesh['dp'=4,'context'=4,'tensor'=2] {'dp'}, dimensions={0}, use_global_device_ids=true | all-gather | bytes 737280 | tf_op jit(solution)/shard_map/all_gather | solution.py:68
  35.8 7.6 %all_gather.26 = bf16[768,384]{1,0:T(8,128)(2,1)S(1)} all-gather(bf16[192,384]{1,0:T(8,128)(2,1)S(1)} %copy-done.29), channel_id=1, replica_groups=mesh['dp'=4,'context'=4,'tensor'=2] {'dp'}, dimensions={0}, use_global_device_ids=true | all-gather | bytes 737280 | tf_op jit(solution)/shard_map/all_gather | solution.py:67
  43.5 8.6 %all_gather.29 = bf16[384,768]{0,1:T(8,128)(2,1)} all-gather(bf16[384,192]{0,1:T(8,128)(2,1)S(1)} %copy-done.30), channel_id=1, replica_groups=mesh['dp'=4,'context'=4,'tensor'=2] {'dp'}, dimensions={1}, use_global_device_ids=true | all-gather | bytes 737280 | tf_op jit(solution)/shard_map/all_gather | solution.py:71
  52.7 9.6 %all-gather.5.cloned.1.call-done = bf16[2,1024,384]{2,1,0:T(8,128)(2,1)} async-done(((bf16[2,256,384]{2,1,0:T(8,128)(2,1)}), bf16[2,1024,384]{2,1,0:T(8,128)(2,1)}) %all-gather.5.cloned.1.call-update) | async-done | bytes 1572880 | tf_op jit(solution)/shard_map/all_gather | solution.py:96
  62.3 1.5 fusion.76
  65.0 35.4 %all-gather.7.cloned.1.call-done = bf16[2,1024,384]{2,1,0:T(8,128)(2,1)} async-done(((bf16[2,256,384]{2,1,0:T(8,128)(2,1)}), bf16[2,1024,384]{2,1,0:T(8,128)(2,1)}) %all-gather.7.cloned.1.call-update) | async-done | bytes 1572880 | tf_op jit(solution)/shard_map/all_gather | solution.py:93
  100.4 2.4 fusion.75
  103.1 1.7 copy.38
  107.2 1.6 exponential_reduce_fusion
  110.0 1.6 exponential_reduce_fusion.1
  111.6 1.5 fusion.48
  113.4 1.5 fusion.49
  115.5 1.5 convolution_convert_fusion.4
  122.1 28.3 %all-reduce.8.cloned.1.call-done = bf16[512,768]{1,0:T(8,128)(2,1)} async-done(((bf16[512,768]{1,0:T(8,128)(2,1)}), bf16[512,768]{1,0:T(8,128)(2,1)}) %all-reduce.8.cloned.1.call-update) | async-done | bytes 786448 | tf_op jit(solution)/shard_map/psum | solution.py:124
  150.4 2.5 fusion.74
  154.9 5.0 fusion.80
  159.9 7.5 %all-gather.9.cloned.1.call-done = bf16[768,1536]{1,0:T(8,128)(2,1)} async-done(((bf16[192,1536]{1,0:T(8,128)(2,1)}), bf16[768,1536]{1,0:T(8,128)(2,1)}) %all-gather.9.cloned.1.call-update) | async-done | bytes 2359312 | tf_op jit(solution)/shard_map/all_gather | solution.py:70
  167.4 7.7 %convert_reduce_fusion = (f32[1536]{0:T(1024)}, bf16[512,1536]{1,0:T(8,128)(2,1)S(1)}, f32[512,1536]{1,0:T(8,128)}) fusion(f32[512,1536]{1,0:T(8,128)} %fusion.80, f32[1536]{0:T(1024)} %convert_element_type.233, bf16[768,1536]{1,0:T(8,128)(2,1)} %all-gather.9.cloned.1.call-done, f32[512,768]{1,0:T(8,128)S(1)} %get-tuple-element.48, ...), kind=kOutput, calls=%fused_computation.28 | convolution fusion | flops 1228012032 | bytes 11819008 | tf_op jit(solution)/shard_map/dot_general | solution.py:25
  176.3 2.3 convolution_convert_fusion.2
  178.7 34.4 %all-reduce.10.cloned.1.call-done = bf16[512,768]{1,0:T(8,128)(2,1)} async-done(((bf16[512,768]{1,0:T(8,128)(2,1)}), bf16[512,768]{1,0:T(8,128)(2,1)}) %all-reduce.10.cloned.1.call-update) | async-done | bytes 786448 | tf_op jit(solution)/shard_map/psum | solution.py:146
  213.1 2.5 fusion.27
  216.4 2.0 fusion.73
  221.1 1.4 fusion.38
  222.5 2.1 multiply_reduce_fusion.1
  224.6 1.8 multiply_convert_fusion.1
  226.4 1.7 copy-done.3
  230.4 4.7 multiply_reduce_fusion
  235.3 1.7 multiply_convert_fusion
  237.7 1.3 fusion.41
  239.1 1.3 pad_maximum_fusion.1
  240.6 2.6 convolution_convert_fusion.5
  243.2 3.4 fusion.46
  247.8 1.4 convolution_convert_fusion.8
  249.3 4.5 convolution_convert_fusion.1
  253.8 5.1 convolution_convert_fusion
  259.0 6.5 %reduce-scatter.9.cloned.1.call-done = bf16[256,768]{0,1:T(8,128)(2,1)} async-done(((bf16[1024,768]{0,1:T(8,128)(2,1)}), bf16[256,768]{0,1:T(8,128)(2,1)}) %reduce-scatter.9.cloned.1.call-update) | async-done | bytes 393232 | tf_op jit(solution)/shard_map/reduce_scatter | solution.py:198
  265.5 1.8 constant_dynamic-update-slice_fusion.1
  267.3 34.7 %reduce-scatter.11.cloned.1.call-done = bf16[256,768]{0,1:T(8,128)(2,1)} async-done(((bf16[1024,768]{0,1:T(8,128)(2,1)}), bf16[256,768]{0,1:T(8,128)(2,1)}) %reduce-scatter.11.cloned.1.call-update) | async-done | bytes 393232 | tf_op jit(solution)/shard_map/reduce_scatter | solution.py:198
  302.0 1.8 constant_dynamic-update-slice_fusion
  303.8 2.7 convolution_convert_fusion.6
  306.5 2.6 convolution_convert_fusion.7
  309.5 5.7 convolution_convert_fusion.3
  317.1 1.5 add_convert_fusion.1
  318.7 6.9 %reduce-scatter.19.cloned.1.call-done = bf16[384,192]{0,1:T(8,128)(2,1)} async-done(((bf16[384,768]{0,1:T(8,128)(2,1)}), bf16[384,192]{0,1:T(8,128)(2,1)}) %reduce-scatter.19.cloned.1.call-update) | async-done | bytes 147472 | tf_op jit(solution)/shard_map/reduce_scatter | solution.py:234
  325.5 25.2 %reduce-scatter.13.cloned.1.call-done = bf16[192,384]{1,0:T(8,128)(2,1)} async-done(((bf16[768,384]{1,0:T(8,128)(2,1)}), bf16[192,384]{1,0:T(8,128)(2,1)}) %reduce-scatter.13.cloned.1.call-update) | async-done | bytes 147472 | tf_op jit(solution)/shard_map/reduce_scatter | solution.py:222
  350.7 35.7 %reduce-scatter.21.cloned.1.call-done = bf16[192,1536]{1,0:T(8,128)(2,1)} async-done(((bf16[768,1536]{1,0:T(8,128)(2,1)}), bf16[192,1536]{1,0:T(8,128)(2,1)}) %reduce-scatter.21.cloned.1.call-update) | async-done | bytes 589840 | tf_op jit(solution)/shard_map/reduce_scatter | solution.py:231
  386.4 35.7 %reduce-scatter.23.cloned.1.call-done = bf16[1536,192]{0,1:T(8,128)(2,1)} async-done(((bf16[1536,768]{0,1:T(8,128)(2,1)}), bf16[1536,192]{0,1:T(8,128)(2,1)}) %reduce-scatter.23.cloned.1.call-update) | async-done | bytes 589840 | tf_op jit(solution)/shard_map/reduce_scatter | solution.py:237
  422.1 24.6 %reduce-scatter.17.cloned.1.call-done = bf16[192,384]{1,0:T(8,128)(2,1)} async-done(((bf16[768,384]{1,0:T(8,128)(2,1)}), bf16[192,384]{1,0:T(8,128)(2,1)}) %reduce-scatter.17.cloned.1.call-update) | async-done | bytes 147472 | tf_op jit(solution)/shard_map/reduce_scatter | solution.py:228
  446.7 24.5 %reduce-scatter.15.cloned.1.call-done = bf16[192,384]{1,0:T(8,128)(2,1)} async-done(((bf16[768,384]{1,0:T(8,128)(2,1)}), bf16[192,384]{1,0:T(8,128)(2,1)}) %reduce-scatter.15.cloned.1.call-update) | async-done | bytes 147472 | tf_op jit(solution)/shard_map/reduce_scatter | solution.py:225
  471.8 1.5 convert_reduce_fusion.4
  475.2 51.2 %all-reduce.14.cloned.1.call-done = (bf16[512,768]{1,0:T(8,128)(2,1)}, bf16[512,768]{1,0:T(8,128)(2,1)}) async-done(((bf16[512,768]{1,0:T(8,128)(2,1)}, bf16[512,768]{1,0:T(8,128)(2,1)}), (bf16[512,768]{1,0:T(8,128)(2,1)}, bf16[512,768]{1,0:T(8,128)(2,1)})) %all-reduce.14.cloned.1.call-update) | async-done | bytes 1572880 | tf_op jit(solution)/shard_map/psum | solution.py:134
  526.4 1.7 convert_reduce_fusion.1
  528.7 2.1 fusion.28
  530.8 65.3 %all-reduce = (f32[768]{0:T(1024)}, f32[768]{0:T(1024)}, f32[384]{0:T(512)}, f32[384]{0:T(512)}, f32[768]{0:T(1024)}, /*index=5*/f32[768]{0:T(1024)}, f32[768]{0:T(1024)}, f32[1536]{0:T(1024)}, f32[768]{0:T(1024)}) all-reduce(f32[768]{0:T(1024)S(1)} %get-tuple-element.19, ...), channel_id=1, replica_groups=mesh['dp'=4,'context'=4,'tensor'=2] {'dp','context'}, use_global_device_ids=true, to_apply=%region_21.22 | all-reduce | flops 6912 | bytes 55296 | tf_op jit(solution)/shard_map/psum | solution.py:249
  596.2 3.4 add_convert_fusion
  599.5 9.6 %all-reduce.12.cloned.1.call-done = (bf16[192,384]{1,0:T(8,128)(2,1)}, bf16[192,384]{1,0:T(8,128)(2,1)}, bf16[192,384]{1,0:T(8,128)(2,1)}, bf16[384,192]{0,1:T(8...) async-done(((bf16[192,384]{1,0:T(8,128)(2,1)}, bf16[192,384]{1,0:T(8,128)(2,1)}, bf16[192,384]{1,0:T(8,128)(2,1)}, bf16[384,192]{0,1:T(8,128)(2,1)}, ...) | async-done | bytes 1769488 | tf_op jit(solution)/shard_map/psum | solution.py:242
  609.2 1.7 convert_element_type.255
  610.9 1.6 convert_element_type.258
  612.5 1.6 convert_element_type.260
  614.1 1.6 convert_element_type.263
  615.8 2.2 convert_element_type.266
  (221 shorter events, 37.1 us)
Async XLA Ops:
  8.0 14.4 %copy-start.2 = (bf16[2,256,768]{2,1,0:T(8,128)(2,1)S(1)}, bf16[2,256,768]{2,1,0:T(8,128)(2,1)}, u32[]{:S(2)}) copy-start(bf16[2,256,768]{2,1,0:T(8,128)(2,1)} %param.18) | copy-start | bytes 2359300
  8.0 54.3 %all-gather.5.cloned.1.call-start = ((), (), s32[]{:S(2)}) async-start(), calls=%async_computation.8 | async-start | bytes 1966080 | tf_op jit(solution)/shard_map/all_gather | solution.py:96
  11.7 12.5 %copy-start.42 = (f32[1,2,2,128]{3,1,2,0:T(2,128)}, f32[1,2,2,128]{3,1,2,0:T(2,128)S(1)}, u32[]{:S(2)}) copy-start(f32[1,2,2,128]{3,1,2,0:T(2,128)S(1)} %copy.41) | copy-start | bytes 6148
  11.7 12.5 %copy-start.34 = (f32[512]{0:T(512)}, f32[512]{0:T(512)S(1)}, u32[]{:S(2)}) copy-start(f32[512]{0:T(512)S(1)} %rsqrt.20) | copy-start | bytes 6148
  13.1 11.1 %copy-start.28 = (bf16[192,384]{1,0:T(8,128)(2,1)S(1)}, bf16[192,384]{1,0:T(8,128)(2,1)}, u32[]{:S(2)}) copy-start(bf16[192,384]{1,0:T(8,128)(2,1)} %param.24) | copy-start | bytes 442372
  22.4 9.5 %copy-start.15 = (bf16[768,384]{1,0:T(8,128)(2,1)}, bf16[768,384]{1,0:T(8,128)(2,1)S(1)}, u32[]{:S(2)}) copy-start(bf16[768,384]{1,0:T(8,128)(2,1)S(1)} %all_gather.24) | copy-start | bytes 1769476
  22.8 29.3 %copy-start.21 = (bf16[512,768]{1,0:T(8,128)(2,1)}, bf16[512,768]{1,0:T(8,128)(2,1)S(1)}, u32[]{:S(2)}) copy-start(bf16[512,768]{1,0:T(8,128)(2,1)S(1)} %fusion.35) | copy-start | bytes 2359300
  22.8 10.5 %copy-start.57 = (bf16[384]{0:T(512)(128)(2,1)S(1)}, bf16[384]{0:T(512)(128)(2,1)}, u32[]{:S(2)}) copy-start(bf16[384]{0:T(512)(128)(2,1)} %param.23) | copy-start | bytes 2308
  22.8 10.5 %copy-start.50 = (s32[2]{0:T(128)S(1)}, s32[2]{0:T(128)}, u32[]{:S(2)}) copy-start(s32[2]{0:T(128)} %param.19) | copy-start | bytes 28
  22.8 13.0 %copy-start.29 = (bf16[192,384]{1,0:T(8,128)(2,1)S(1)}, bf16[192,384]{1,0:T(8,128)(2,1)}, u32[]{:S(2)}) copy-start(bf16[192,384]{1,0:T(8,128)(2,1)} %param.22) | copy-start | bytes 442372
  24.1 19.3 %copy-start.30 = (bf16[384,192]{0,1:T(8,128)(2,1)S(1)}, bf16[384,192]{0,1:T(8,128)(2,1)}, u32[]{:S(2)}) copy-start(bf16[384,192]{0,1:T(8,128)(2,1)} %param.27) | copy-start | bytes 442372
  24.2 76.2 %all-gather.7.cloned.1.call-start = ((), (), s32[]{:S(2)}) async-start(), calls=%async_computation.9 | async-start | bytes 1966080 | tf_op jit(solution)/shard_map/all_gather | solution.py:93
  31.9 20.7 %copy-start.17 = (bf16[768,384]{1,0:T(8,128)(2,1)}, bf16[768,384]{1,0:T(8,128)(2,1)S(1)}, u32[]{:S(2)}) copy-start(bf16[768,384]{1,0:T(8,128)(2,1)S(1)} %all_gather.27) | copy-start | bytes 1769476
  33.2 117.1 %all-reduce.8.cloned.1.call-start = ((), (), s32[]{:S(2)}) async-start(), calls=%async_computation.10 | async-start | bytes 1572864 | tf_op jit(solution)/shard_map/psum | solution.py:124
  35.8 71.3 %copy-start.44 = (pred[1024]{0:T(1024)(128)(4,1)}, pred[1024]{0:T(1024)(128)(4,1)S(1)}, u32[]{:S(2)}) copy-start(pred[1024]{0:T(1024)(128)(4,1)S(1)} %iota_compare_fusion) | copy-start | bytes 3076
  43.5 9.2 %copy-start.19 = (bf16[768,384]{1,0:T(8,128)(2,1)}, bf16[768,384]{1,0:T(8,128)(2,1)S(1)}, u32[]{:S(2)}) copy-start(bf16[768,384]{1,0:T(8,128)(2,1)S(1)} %all_gather.26) | copy-start | bytes 1769476
  103.1 5.7 copy-start.8
  104.8 2.3 copy-start.9
  107.1 4.4 copy-start
  109.9 3.2 copy-start.1
  113.1 1.8 copy-start.59
  113.4 2.2 copy-start.26
  114.8 3.6 copy-start.51
  114.8 4.8 copy-start.53
  114.9 5.4 copy-start.54
  114.9 6.0 copy-start.55
  114.9 6.6 %copy-start.52 = (bf16[1536]{0:T(1024)(128)(2,1)S(1)}, bf16[1536]{0:T(1024)(128)(2,1)}, u32[]{:S(2)}) copy-start(bf16[1536]{0:T(1024)(128)(2,1)} %param.32) | copy-start | bytes 9220
  114.9 35.5 %copy-start.7 = (bf16[2,256,768]{2,1,0:T(8,128)(2,1)S(1)}, bf16[2,256,768]{2,1,0:T(8,128)(2,1)}, u32[]{:S(2)}) copy-start(bf16[2,256,768]{2,1,0:T(8,128)(2,1)} %param.35) | copy-start | bytes 2359300
  117.0 37.9 %all-gather.11.cloned.1.call-start = ((), (), s32[]{:S(2)}) async-start(), calls=%async_computation.12 | async-start | bytes 2949120 | tf_op jit(solution)/shard_map/all_gather | solution.py:72
  117.6 49.8 %all-gather.9.cloned.1.call-start = ((), (), s32[]{:S(2)}) async-start(), calls=%async_computation.11 | async-start | bytes 2949120 | tf_op jit(solution)/shard_map/all_gather | solution.py:70
  118.2 94.9 %all-reduce.10.cloned.1.call-start = ((), (), s32[]{:S(2)}) async-start(), calls=%async_computation.13 | async-start | bytes 1572864 | tf_op jit(solution)/shard_map/psum | solution.py:146
  167.4 8.9 %copy-start.58 = (bf16[768,1536]{1,0:T(8,128)(2,1)S(1)}, bf16[768,1536]{1,0:T(8,128)(2,1)}, u32[]{:S(2)}) copy-start(bf16[768,1536]{1,0:T(8,128)(2,1)} %all-gather.9.cloned.1.call-done) | copy-start | bytes 7077892
  178.6 86.9 %reduce-scatter.9.cloned.1.call-start = ((), (), s32[]{:S(2)}) async-start(), calls=%async_computation.14 | async-start | bytes 1966080 | tf_op jit(solution)/shard_map/reduce_scatter | solution.py:198
  213.1 7.9 %slice-start.2 = ((s8[6291456]{0:T(1024)(128)(4,1)}), s8[4194304]{0:T(1024)(128)(4,1)S(1)}, s32[]{:S(2)}) async-start(s8[6291456]{0:T(1024)(128)(4,1)} %bitcast.127), calls=%async_computation.26 | async-start | bytes 8388608
  215.7 2.7 copy-start.36
  216.4 4.7 slice-start.3
  218.3 2.0 copy-start.6
  218.3 2.0 copy-start.40
  218.4 2.7 copy-start.32
  218.4 2.7 copy-start.48
  226.3 1.7 copy-start.3
  230.1 71.9 %reduce-scatter.11.cloned.1.call-start = ((), (), s32[]{:S(2)}) async-start(), calls=%async_computation.15 | async-start | bytes 1966080 | tf_op jit(solution)/shard_map/reduce_scatter | solution.py:198
  230.3 4.7 slice-start
  230.4 4.9 slice-start.1
  230.4 4.9 copy-start.46
  237.1 2.0 copy-start.4
  240.5 85.1 %reduce-scatter.19.cloned.1.call-start = ((), (), s32[]{:S(2)}) async-start(), calls=%async_computation.19 | async-start | bytes 737280 | tf_op jit(solution)/shard_map/reduce_scatter | solution.py:234
  243.2 107.6 %reduce-scatter.13.cloned.1.call-start = ((), (), s32[]{:S(2)}) async-start(), calls=%async_computation.16 | async-start | bytes 737280 | tf_op jit(solution)/shard_map/reduce_scatter | solution.py:222
  243.2 3.4 copy-start.5
  243.2 3.4 copy-start.10
  249.2 137.2 %reduce-scatter.21.cloned.1.call-start = ((), (), s32[]{:S(2)}) async-start(), calls=%async_computation.20 | async-start | bytes 2949120 | tf_op jit(solution)/shard_map/reduce_scatter | solution.py:231
  253.8 168.3 %reduce-scatter.23.cloned.1.call-start = ((), (), s32[]{:S(2)}) async-start(), calls=%async_computation.21 | async-start | bytes 2949120 | tf_op jit(solution)/shard_map/reduce_scatter | solution.py:237
  259.0 187.7 %reduce-scatter.17.cloned.1.call-start = ((), (), s32[]{:S(2)}) async-start(), calls=%async_computation.18 | async-start | bytes 737280 | tf_op jit(solution)/shard_map/reduce_scatter | solution.py:228
  306.5 164.7 %reduce-scatter.15.cloned.1.call-start = ((), (), s32[]{:S(2)}) async-start(), calls=%async_computation.17 | async-start | bytes 737280 | tf_op jit(solution)/shard_map/reduce_scatter | solution.py:225
  309.2 217.2 %all-reduce.14.cloned.1.call-start = ((), (), s32[]{:S(2)}) async-start(), calls=%async_computation.23 | async-start | bytes 3145728 | tf_op jit(solution)/shard_map/psum | solution.py:134
  309.5 5.7 copy-start.20
  315.2 1.9 copy-start.16
  318.6 152.6 %copy-start.56 = (bf16[768]{0:T(1024)(128)(2,1)S(1)}, bf16[768]{0:T(1024)(128)(2,1)}, u32[]{:S(2)}) copy-start(bf16[768]{0:T(1024)(128)(2,1)} %param.34) | copy-start | bytes 4612
  318.6 290.5 %all-reduce.12.cloned.1.call-start = ((), (), s32[]{:S(2)}) async-start(), calls=%async_computation.22 | async-start | bytes 3538944 | tf_op jit(solution)/shard_map/psum | solution.py:242
  471.2 57.6 %copy-start.35 = (f32[512]{0:T(512)S(1)}, f32[512]{0:T(512)}, u32[]{:S(2)}) copy-start(f32[512]{0:T(512)} %copy-done.34) | copy-start | bytes 6148
  471.8 124.4 %copy-start.37 = (f32[1,2,2,128]{3,1,2,0:T(2,128)S(1)}, f32[1,2,2,128]{3,1,2,0:T(2,128)}, u32[]{:S(2)}) copy-start(f32[1,2,2,128]{3,1,2,0:T(2,128)} %copy.39) | copy-start | bytes 6148
  474.0 56.8 %copy-start.43 = (f32[768]{0:T(1024)S(1)}, f32[768]{0:T(1024)}, u32[]{:S(2)}) copy-start(f32[768]{0:T(1024)} %convert_reduce_fusion.4) | copy-start | bytes 9220
  474.0 56.8 %copy-start.49 = (f32[384]{0:T(512)S(1)}, f32[384]{0:T(512)}, u32[]{:S(2)}) copy-start(f32[384]{0:T(512)} %convert_reduce_fusion.7) | copy-start | bytes 4612
  609.2 8.8 %copy-start.25 = (bf16[1536,192]{0,1:T(8,128)(2,1)S(1)}, bf16[1536,192]{0,1:T(8,128)(2,1)}, u32[]{:S(2)}) copy-start(bf16[1536,192]{0,1:T(8,128)(2,1)} %get-tuple-element.38) | copy-start | bytes 1769476
  (20 other events, 27.1 us)
Sparse Core Ops, SparseCore 0:
  24.3 37.9 all-gather.4
  64.4 35.9 all-gather.6
  117.1 33.1 all-reduce.7
  178.8 34.3 all-reduce.9
  230.2 35.2 reduce-scatter.8
  267.7 34.2 reduce-scatter.10
  304.5 21.0 reduce-scatter.18
  328.6 22.0 reduce-scatter.12
  353.3 33.0 reduce-scatter.20
  388.9 33.0 reduce-scatter.22
  424.6 22.0 reduce-scatter.16
  449.0 22.0 reduce-scatter.14
  474.7 51.6 all-reduce.13
  529.3 79.7 all-reduce.11
Sparse Core Ops, SparseCore 1:
  119.1 22.7 all-gather.10
  143.4 23.9 all-gather.8
where the time goes:
time: 630 us; the launch traced here: 627 us
  waiting for transfers between devices  371 us (59%)
  blocking collectives  98.5 us (16%)
  matrix products  67.9 us (11%)
  other arithmetic  51 us (8%)
  local copies, waits for them, and re-layouts  20.3 us (3%)
  between operations  16.6 us (3%)
    psum x1, blocking collectives, per_device(): lax.psum((grad_gain_one, grad_bias_one, grad_query_bias, grad_value_bias,...  65.3 us
    psum x1, waiting for transfers between devices, per_device(): lax.psum(dense(hidden_low, down_weight).astype(jnp.bfloat16), 'tensor')  51.2 us
    reduce_scatter x2, waiting for transfers between devices, per_device(): lax.psum_scatter(key_term.astype(jnp.bfloat16), 'context', scatter_dimens...  41.2 us
    reduce_scatter x1, waiting for transfers between devices, per_device(): lax.psum_scatter(grad_down.astype(jnp.bfloat16), 'dp', scatter_dimension=...  35.7 us
    reduce_scatter x1, waiting for transfers between devices, per_device(): lax.psum_scatter(grad_up.astype(jnp.bfloat16), 'dp', scatter_dimension=0,...  35.7 us
    all_gather x1, waiting for transfers between devices, per_device(): lax.all_gather(keys_own.reshape(seq_count, shard_rows, local_width), 'con...  35.4 us
    psum x1, waiting for transfers between devices, per_device(): lax.psum(dense_nt(d_pre, up_weight).astype(jnp.bfloat16), 'tensor')  34.4 us
    psum x1, waiting for transfers between devices, per_device(): lax.psum(dense(context_low, out_weight).astype(jnp.bfloat16), 'tensor')  28.3 us
  transfers between devices with their start and end apart: 16, of which 15 were waited for; matrix products, arithmetic and copies ran while one was open for 12% of the time, Pallas kernels for 0%

commit v1 on v0

--- a/solution.py
+++ b/solution.py
@@ -1,6 +1,10 @@
+import functools
+
 import jax
 import jax.numpy as jnp
 from jax import lax
+from jax.experimental import pallas as pl
+from jax.experimental.pallas import tpu as pltpu
 from jax.sharding import PartitionSpec as P
 
 HEAD_DIM = 64
@@ -37,7 +41,7 @@
     )
 
 
-def per_device(
+def per_device_general(
     tokens,
     lengths,
     ln1_gain,
@@ -281,9 +285,814 @@
     )
 
 
+def live_bias(info, count):
+    places = lax.broadcasted_iota(jnp.int32, (count, 2 * HEAD_DIM), 0)
+    return jnp.concatenate(
+        [jnp.where(info[k] + places < info[8], 0.0, masked_value) for k in range(8)], axis=0
+    ).astype(jnp.bfloat16)
+
+
+def split_pair(array, extra):
+    lane = lax.broadcasted_iota(jnp.int32, array.shape, 1)
+    zero = jnp.zeros((), jnp.bfloat16)
+    left = jnp.where(lane < HEAD_DIM, array, jnp.where(lane == HEAD_DIM, extra, zero))
+    right = jnp.where(lane >= HEAD_DIM, array, jnp.where(lane == 0, extra, zero))
+    return left, right
+
+
+LOG_SCALE = HEAD_DIM ** (-0.5) * 1.4426950408889634
+
+
+def attend_kernel(info, query_ref, own_ref, other_ref, out_ref, log_ref, *, steps):
+    pair = 2 * HEAD_DIM
+    rows = query_ref.shape[0]
+    count = rows // 4
+    step = rows // steps
+    keys = jnp.concatenate([own_ref[:, :pair], other_ref[:, :pair]], axis=0)
+    values = jnp.concatenate([own_ref[:, pair:], other_ref[:, pair:]], axis=0)
+    values_t = values.T
+    key_heads = split_pair(keys, live_bias(info, count))
+    query_heads = split_pair(query_ref[...], jnp.ones((), jnp.bfloat16))
+    for s in range(steps):
+        mixed = []
+        for head in range(2):
+            query = query_heads[head][s * step : (s + 1) * step]
+            scores = dense_nt(key_heads[head], query)
+            largest = jnp.max(scores, axis=0, keepdims=True)
+            weights = jnp.exp2((scores - largest) * LOG_SCALE)
+            total = jnp.sum(weights, axis=0, keepdims=True)
+            part = dense(
+                values_t[head * HEAD_DIM : (head + 1) * HEAD_DIM], weights.astype(jnp.bfloat16)
+            )
+            mixed.append(part / total)
+            log_ref[0, head : head + 1, s * step : (s + 1) * step] = (
+                largest * LOG_SCALE + jnp.log2(total)
+            )
+        out_ref[s * step : (s + 1) * step, :] = jnp.concatenate(mixed, axis=0).T.astype(jnp.bfloat16)
+
+
+def attend(info, queries, pair_own, pair_other, steps=2):
+    rows, width = queries.shape
+    pair = 2 * HEAD_DIM
+    groups = width // pair
+    work = 4 * rows * 2 * rows * width
+    return pl.pallas_call(
+        functools.partial(attend_kernel, steps=steps),
+        out_shape=(
+            jax.ShapeDtypeStruct((rows, width), jnp.bfloat16),
+            jax.ShapeDtypeStruct((groups, 2, rows), jnp.float32),
+        ),
+        grid_spec=pltpu.PrefetchScalarGridSpec(
+            num_scalar_prefetch=1,
+            grid=(groups,),
+            in_specs=[
+                pl.BlockSpec((rows, pair), lambda g, info: (0, g)),
+                pl.BlockSpec((rows, 2 * pair), lambda g, info: (0, g)),
+                pl.BlockSpec((rows, 2 * pair), lambda g, info: (0, g)),
+            ],
+            out_specs=(
+                pl.BlockSpec((rows, pair), lambda g, info: (0, g)),
+                pl.BlockSpec((1, 2, rows), lambda g, info: (g, 0, 0)),
+            ),
+        ),
+        compiler_params=pltpu.CompilerParams(vmem_limit_bytes=48 << 20),
+        cost_estimate=pl.CostEstimate(
+            flops=4 * work, bytes_accessed=12 * rows * width, transcendentals=work // (2 * HEAD_DIM)
+        ),
+    )(info, queries, pair_own, pair_other)
+
+
+def attend_back_kernel(
+    info,
+    query_ref,
+    own_ref,
+    other_ref,
+    out_ref,
+    grad_ref,
+    log_ref,
+    d_query_ref,
+    d_own_ref,
+    d_other_ref,
+    *,
+    steps,
+):
+    pair = 2 * HEAD_DIM
+    rows = query_ref.shape[0]
+    step = rows // steps
+    scale = HEAD_DIM ** (-0.5)
+    keys = jnp.concatenate([own_ref[:, :pair], other_ref[:, :pair]], axis=0)
+    values = jnp.concatenate([own_ref[:, pair:], other_ref[:, pair:]], axis=0)
+    keys_t = keys.T
+    key_heads = split_pair(keys, live_bias(info, rows // 4))
+    value_heads = split_pair(values, jnp.zeros((), jnp.bfloat16))
+    query_heads = split_pair(query_ref[...], jnp.ones((), jnp.bfloat16))
+    inner_t = (grad_ref[...].astype(jnp.float32) * out_ref[...].astype(jnp.float32)).T
+    d_keys = [0.0, 0.0]
+    d_values = [0.0, 0.0]
+    for s in range(steps):
+        part = slice(s * step, (s + 1) * step)
+        query = query_ref[part, :]
+        grad = grad_ref[part, :]
+        d_query = []
+        for head in range(2):
+            dims = slice(head * HEAD_DIM, (head + 1) * HEAD_DIM)
+            inner = jnp.sum(inner_t[dims, part], axis=0, keepdims=True)
+            scores = dense_nt(key_heads[head], query_heads[head][part])
+            probs = jnp.exp2(scores * LOG_SCALE - log_ref[0, head : head + 1, part])
+            d_probs = dense_nt(value_heads[head], grad)
+            d_scores = (probs * (d_probs - inner)).astype(jnp.bfloat16)
+            d_query.append(dense(keys_t[dims], d_scores))
+            d_keys[head] += dense(d_scores, query)
+            d_values[head] += dense(probs.astype(jnp.bfloat16), grad)
+        d_query_ref[part, :] = (jnp.concatenate(d_query, axis=0).T * scale).astype(jnp.bfloat16)
+    left = lax.broadcasted_iota(jnp.int32, d_keys[0].shape, 1) < HEAD_DIM
+    d_key = (jnp.where(left, d_keys[0], d_keys[1]) * scale).astype(jnp.bfloat16)
+    d_value = jnp.where(left, d_values[0], d_values[1]).astype(jnp.bfloat16)
+    d_own_ref[:, :pair] = d_key[:rows]
+    d_own_ref[:, pair:] = d_value[:rows]
+    d_other_ref[:, :pair] = d_key[rows:]
+    d_other_ref[:, pair:] = d_value[rows:]
+
+
+def attend_back(info, queries, pair_own, pair_other, mixed, d_mixed, logs, steps=2):
+    rows, width = queries.shape
+    pair = 2 * HEAD_DIM
+    groups = width // pair
+    work = 4 * rows * 2 * rows * width
+    narrow = pl.BlockSpec((rows, pair), lambda g, info: (0, g))
+    wide = pl.BlockSpec((rows, 2 * pair), lambda g, info: (0, g))
+    return pl.pallas_call(
+        functools.partial(attend_back_kernel, steps=steps),
+        out_shape=(
+            jax.ShapeDtypeStruct((rows, width), jnp.bfloat16),
+            jax.ShapeDtypeStruct((rows, 2 * width), jnp.bfloat16),
+            jax.ShapeDtypeStruct((rows, 2 * width), jnp.bfloat16),
+        ),
+        grid_spec=pltpu.PrefetchScalarGridSpec(
+            num_scalar_prefetch=1,
+            grid=(groups,),
+            in_specs=[
+                narrow,
+                wide,
+                wide,
+                narrow,
+                narrow,
+                pl.BlockSpec((1, 2, rows), lambda g, info: (g, 0, 0)),
+            ],
+            out_specs=(narrow, wide, wide),
+        ),
+        compiler_params=pltpu.CompilerParams(vmem_limit_bytes=48 << 20),
+        cost_estimate=pl.CostEstimate(
+            flops=10 * work, bytes_accessed=24 * rows * width, transcendentals=work // (2 * HEAD_DIM)
+        ),
+    )(info, queries, pair_own, pair_other, mixed, d_mixed, logs)
+
+
+def held(info, quarters, count, width):
+    places = lax.broadcasted_iota(jnp.int32, (count, width), 0)
+    return jnp.concatenate([info[k] + places < info[8] for k in range(quarters)], axis=0)
+
+
+def row_stats(values):
+    centred = values - jnp.mean(values, axis=-1, keepdims=True)
+    spread = jnp.mean(centred * centred, axis=-1, keepdims=True)
+    root = lax.rsqrt(spread + epsilon)
+    return centred * root, root
+
+
+def row_pull(normed, root, grad):
+    return root * (
+        grad
+        - jnp.mean(grad, axis=-1, keepdims=True)
+        - normed * jnp.mean(grad * normed, axis=-1, keepdims=True)
+    )
+
+
+def settle(parts, out_ref):
+    rows = parts[0].shape[0]
+    mine = lax.axis_index("dp")
+    for step, part in enumerate(parts):
+        start = pl.multiple_of((mine ^ step) * rows, rows)
+        out_ref[pl.ds(start, rows), :] = part[...]
+
+
+def enter_kernel(
+    first_ref, second_ref, gain_ref, bias_ref, q_bias_ref, v_bias_ref, a, b, c, d,
+    rows_ref, normed_ref, query_ref, pair_ref, proj_ref,
+):
+    pair = 2 * HEAD_DIM
+    settle((a, b, c, d), proj_ref)
+    rows = jnp.concatenate([first_ref[0], second_ref[0], first_ref[1], second_ref[1]], axis=0)
+    rows_ref[...] = rows
+    normed, _ = row_stats(rows.astype(jnp.float32))
+    normed = normed * gain_ref[...].astype(jnp.float32) + bias_ref[...].astype(jnp.float32)
+    normed = normed.astype(jnp.bfloat16)
+    normed_ref[...] = normed
+    local = query_ref.shape[1]
+    mixed = dense(normed, proj_ref[...])
+    query_ref[...] = (mixed[:, :local] + q_bias_ref[...].astype(jnp.float32)).astype(jnp.bfloat16)
+    for g in range(local // pair):
+        cols = slice(g * pair, (g + 1) * pair)
+        key = mixed[:, local + g * pair : local + (g + 1) * pair]
+        value = mixed[:, 2 * local + g * pair : 2 * local + (g + 1) * pair]
+        value = value + v_bias_ref[:, cols].astype(jnp.float32)
+        pair_ref[:, 2 * g * pair : (2 * g + 1) * pair] = key.astype(jnp.bfloat16)
+        pair_ref[:, (2 * g + 1) * pair : (2 * g + 2) * pair] = value.astype(jnp.bfloat16)
+
+
+def enter(first, second, gain, bias, q_bias, v_bias, blocks):
+    half, width = first.shape[1:]
+    rows = 4 * half
+    local = q_bias.shape[1]
+    low = lambda *shape: jax.ShapeDtypeStruct(shape, jnp.bfloat16)
+    return pl.pallas_call(
+        enter_kernel,
+        out_shape=(
+            low(rows, width),
+            low(rows, width),
+            low(rows, local),
+            low(rows, 2 * local),
+            low(width, 3 * local),
+        ),
+        compiler_params=pltpu.CompilerParams(vmem_limit_bytes=48 << 20),
+        cost_estimate=pl.CostEstimate(
+            flops=6 * rows * width * local, bytes_accessed=10 << 20, transcendentals=rows
+        ),
+    )(first, second, gain, bias, q_bias, v_bias, *blocks)
+
+
+ROOT_TWO_OVER_PI = 0.7978845608028654
+CUBE = 0.044715
+
+
+def middle_kernel(
+    info, rows_ref, own_ref, peer_ref, top0_ref, top1_ref, gain_ref, bias_ref, out_bias_ref,
+    oa, ob, oc, od, ua, ub, uc, ud, da, db, dc, dd, up_bias_ref,
+    mid_ref, normed_ref, feed_ref, hidden_ref, d_pre_ref, d_own_ref, d_peer_ref,
+    f_own_ref, f_peer_ref, out_ref, g_up_ref, g_down_ref,
+    outs, ups, downs, acc_d, acc_f,
+):
+    step = pl.program_id(0)
+    rows, width = rows_ref.shape
+    half = rows // 2
+    local = own_ref.shape[1]
+
+    @pl.when(step == 0)
+    def _():
+        settle((oa, ob, oc, od), outs)
+        out_ref[...] = outs[:, :local]
+        peer = jnp.concatenate([peer_ref[half:, :], peer_ref[:half, :]], axis=0)
+        attention = (
+            dense_nt(own_ref[...], outs[:, :local])
+            + dense_nt(peer, outs[:, local:])
+            + out_bias_ref[...].astype(jnp.float32)
+        )
+        real = held(info, 4, rows // 4, width)
+        mid = rows_ref[...].astype(jnp.float32) + jnp.where(real, attention, 0.0)
+        mid_ref[...] = mid
+        normed, _ = row_stats(mid)
+        normed = normed * gain_ref[...].astype(jnp.float32) + bias_ref[...].astype(jnp.float32)
+        normed_ref[...] = normed.astype(jnp.bfloat16)
+        top = jnp.concatenate([top0_ref[0], top1_ref[0], top0_ref[1], top1_ref[1]], axis=0)
+        feed = jnp.where(real, top.astype(jnp.float32), 0.0)
+        feed_ref[...] = feed.astype(jnp.bfloat16)
+        g_down_ref[...] = jnp.sum(feed, axis=0, keepdims=True)
+        acc_d[...] = jnp.zeros_like(acc_d)
+        acc_f[...] = jnp.zeros_like(acc_f)
+
+    settle((ua, ub, uc, ud), ups)
+    settle((da, db, dc, dd), downs)
+    pre = dense(normed_ref[...], ups[...]) + up_bias_ref[...].astype(jnp.float32)
+    d_hidden = dense(feed_ref[...], downs[...])
+    square = pre * pre
+    bend = jnp.tanh(ROOT_TWO_OVER_PI * pre * (1.0 + CUBE * square))
+    half_up = 0.5 + 0.5 * bend
+    hidden = (pre * half_up).astype(jnp.bfloat16)
+    slope = half_up + (pre * half_up) * (1.0 - bend) * (
+        ROOT_TWO_OVER_PI + 3.0 * CUBE * ROOT_TWO_OVER_PI * square
+    )
+    d_pre = (d_hidden * slope).astype(jnp.bfloat16)
+    hidden_ref[...] = hidden
+    d_pre_ref[...] = d_pre
+    g_up_ref[...] = jnp.sum(d_pre.astype(jnp.float32), axis=0, keepdims=True)
+    acc_d[...] += dense_nt(d_pre, ups[...])
+    acc_f[...] += dense_nt(hidden, downs[...])
+
+    @pl.when(step == pl.num_programs(0) - 1)
+    def _():
+        low = acc_d[...].astype(jnp.bfloat16)
+        d_own_ref[...] = low[:half]
+        d_peer_ref[...] = low[half:]
+        low = acc_f[...].astype(jnp.bfloat16)
+        f_own_ref[...] = low[:half]
+        f_peer_ref[...] = low[half:]
+
+
+def middle_part(info, rows_low, own, peer, top, gain, bias, out_bias, packs, up_bias):
+    rows, width = rows_low.shape
+    local = own.shape[1]
+    shard = packs[0].shape[0]
+    hidden = up_bias.shape[1]
+    tile = 384
+    low = lambda *shape: jax.ShapeDtypeStruct(shape, jnp.bfloat16)
+    full = lambda *shape: jax.ShapeDtypeStruct(shape, jnp.float32)
+    fixed = lambda array: pl.BlockSpec(array.shape, lambda i, info: (0,) * array.ndim)
+    columns = lambda height: pl.BlockSpec((height, tile), lambda i, info: (0, i))
+    outs = pl.BlockSpec((shard, width), lambda i, info: (0, 0))
+    first_up, first_down = width // tile, (width + hidden) // tile
+    ups = pl.BlockSpec((shard, tile), lambda i, info: (0, first_up + i))
+    downs = pl.BlockSpec((shard, tile), lambda i, info: (0, first_down + i))
+    whole = (rows_low, own, peer, *top, gain, bias, out_bias)
+    shapes = (
+        full(rows, width),
+        low(rows, width),
+        low(rows, width),
+        low(rows, hidden),
+        low(rows, hidden),
+        low(rows // 2, width),
+        low(rows // 2, width),
+        low(rows // 2, width),
+        low(rows // 2, width),
+        low(width, local),
+        full(1, hidden),
+        full(1, width),
+    )
+    tiled = (3, 4, 10)
+    return pl.pallas_call(
+        middle_kernel,
+        out_shape=shapes,
+        grid_spec=pltpu.PrefetchScalarGridSpec(
+            num_scalar_prefetch=1,
+            grid=(hidden // tile,),
+            in_specs=[fixed(a) for a in whole] + [outs] * 4 + [ups] * 4 + [downs] * 4 + [columns(1)],
+            out_specs=tuple(
+                columns(s.shape[0]) if k in tiled else fixed(s) for k, s in enumerate(shapes)
+            ),
+            scratch_shapes=[
+                pltpu.VMEM((width, 2 * local), jnp.bfloat16),
+                pltpu.VMEM((width, tile), jnp.bfloat16),
+                pltpu.VMEM((width, tile), jnp.bfloat16),
+                pltpu.VMEM((rows, width), jnp.float32),
+                pltpu.VMEM((rows, width), jnp.float32),
+            ],
+        ),
+        compiler_params=pltpu.CompilerParams(vmem_limit_bytes=52 << 20),
+        cost_estimate=pl.CostEstimate(
+            flops=8 * rows * width * hidden, bytes_accessed=20 << 20, transcendentals=rows * hidden
+        ),
+    )(info, *whole, *packs, *packs, *packs, up_bias)
+
+
+def turn_kernel(
+    info, mid_ref, d_own_ref, d_peer_ref, got_own_ref, got_peer_ref, top0_ref, top1_ref,
+    gain_ref, out_ref, d_mid_ref, d_att_ref, d_mix_ref, sums_ref,
+):
+    rows, width = mid_ref.shape
+    half = rows // 2
+    f32 = lambda ref: ref[...].astype(jnp.float32)
+    grad = jnp.concatenate(
+        [f32(d_own_ref) + f32(got_own_ref), f32(d_peer_ref) + f32(got_peer_ref)], axis=0
+    )
+    normed, root = row_stats(mid_ref[...])
+    top = jnp.concatenate([top0_ref[0], top1_ref[0], top0_ref[1], top1_ref[1]], axis=0)
+    d_mid = top.astype(jnp.float32) + row_pull(
+        normed, root, grad * gain_ref[...].astype(jnp.float32)
+    )
+    d_mid_ref[...] = d_mid[:half]
+    d_att = jnp.where(held(info, 4, rows // 4, width), d_mid, 0.0).astype(jnp.bfloat16)
+    d_att_ref[...] = d_att
+    d_mix_ref[...] = dense(d_att, out_ref[...]).astype(jnp.bfloat16)
+    sums_ref[0:1, :] = jnp.sum(grad * normed, axis=0, keepdims=True)
+    sums_ref[1:2, :] = jnp.sum(grad, axis=0, keepdims=True)
+    sums_ref[2:3, :] = jnp.sum(d_att.astype(jnp.float32), axis=0, keepdims=True)
+
+
+def turn(info, mid, d_own, d_peer, got_own, got_peer, top, gain, out_t):
+    rows, width = mid.shape
+    local = out_t.shape[1]
+    args = (mid, d_own, d_peer, got_own, got_peer, *top, gain, out_t)
+    return pl.pallas_call(
+        turn_kernel,
+        out_shape=(
+            jax.ShapeDtypeStruct((rows // 2, width), jnp.float32),
+            jax.ShapeDtypeStruct((rows, width), jnp.bfloat16),
+            jax.ShapeDtypeStruct((rows, local), jnp.bfloat16),
+            jax.ShapeDtypeStruct((3, width), jnp.float32),
+        ),
+        in_specs=[pl.BlockSpec(memory_space=pltpu.SMEM)]
+        + [pl.BlockSpec(memory_space=pltpu.VMEM)] * len(args),
+        compiler_params=pltpu.CompilerParams(vmem_limit_bytes=48 << 20),
+        cost_estimate=pl.CostEstimate(
+            flops=2 * rows * width * local, bytes_accessed=8 << 20, transcendentals=rows
+        ),
+    )(info, *args)
+
+
+def leave_kernel(
+    rows_ref, d_query_ref, d_pair_ref, got_ref, proj_ref, d_proj_ref, own_ref, peer_ref, sums_ref,
+    bias_ref,
+):
+    pair = 2 * HEAD_DIM
+    rows, local = d_query_ref.shape
+    half = rows // 2
+    d_proj_ref[:, :local] = d_query_ref[...]
+    for g in range(local // pair):
+        for k in range(2):
+            cols = slice((2 * g + k) * pair, (2 * g + k + 1) * pair)
+            total = d_pair_ref[:, cols].astype(jnp.float32) + got_ref[:, cols].astype(jnp.float32)
+            start = (k + 1) * local + g * pair
+            d_proj_ref[:, start : start + pair] = total.astype(jnp.bfloat16)
+    d_proj = d_proj_ref[...]
+    bias_ref[...] = jnp.sum(d_proj.astype(jnp.float32), axis=0, keepdims=True)
+    grad = dense_nt(d_proj, proj_ref[...])
+    low = grad.astype(jnp.bfloat16)
+    own_ref[...] = low[:half]
+    peer_ref[...] = low[half:]
+    normed, _ = row_stats(rows_ref[...].astype(jnp.float32))
+    sums_ref[0:1, :] = jnp.sum(grad * normed, axis=0, keepdims=True)
+    sums_ref[1:2, :] = jnp.sum(grad, axis=0, keepdims=True)
+
+
+def leave(rows_low, d_query, d_pair, got, proj):
+    rows, width = rows_low.shape
+    local = d_query.shape[1]
+    low = lambda *shape: jax.ShapeDtypeStruct(shape, jnp.bfloat16)
+    return pl.pallas_call(
+        leave_kernel,
+        out_shape=(
+            low(rows, 3 * local),
+            low(rows // 2, width),
+            low(rows // 2, width),
+            jax.ShapeDtypeStruct((2, width), jnp.float32),
+            jax.ShapeDtypeStruct((1, 3 * local), jnp.float32),
+        ),
+        compiler_params=pltpu.CompilerParams(vmem_limit_bytes=48 << 20),
+        cost_estimate=pl.CostEstimate(
+            flops=6 * rows * width * local, bytes_accessed=8 << 20, transcendentals=rows
+        ),
+    )(rows_low, d_query, d_pair, got, proj)
+
+
+def finish_kernel(rows_ref, own_ref, got_ref, gain_ref, d_mid_ref, first_ref, second_ref):
+    half = rows_ref.shape[0]
+    normed, root = row_stats(rows_ref[...].astype(jnp.float32))
+    grad = own_ref[...].astype(jnp.float32) + got_ref[...].astype(jnp.float32)
+    d_rows = row_pull(normed, root, grad * gain_ref[...].astype(jnp.float32)) + d_mid_ref[...]
+    low = d_rows.astype(jnp.bfloat16)
+    first_ref[...] = low[: half // 2]
+    second_ref[...] = low[half // 2 :]
+
+
+def finish(rows_low, own, got, gain, d_mid):
+    half, width = own.shape
+    top_half = pl.BlockSpec((half, width), lambda i: (0, 0))
+    fixed = lambda a: pl.BlockSpec(a.shape, lambda i: (0,) * a.ndim)
+    piece = jax.ShapeDtypeStruct((half // 2, width), jnp.bfloat16)
+    return pl.pallas_call(
+        finish_kernel,
+        out_shape=(piece, piece),
+        grid=(1,),
+        in_specs=[top_half, fixed(own), fixed(got), fixed(gain), fixed(d_mid)],
+        out_specs=(fixed(piece), fixed(piece)),
+        compiler_params=pltpu.CompilerParams(vmem_limit_bytes=32 << 20),
+        cost_estimate=pl.CostEstimate(
+            flops=20 * half * width, bytes_accessed=4 << 20, transcendentals=half
+        ),
+    )(rows_low, own, got, gain, d_mid)
+
+
+def weight_grad_kernel(*refs, pairs, extra):
+    count = 2 * pairs + extra
+    lefts, rights = refs[0 : 2 * pairs : 2], refs[1 : 2 * pairs : 2]
+    own_ref, far_ref, send_ref = refs[count : count + 3]
+    turned = refs[count + 3 :]
+    rows = own_ref.shape[0]
+    mine = lax.axis_index("dp")
+    targets = (own_ref, send_ref.at[:rows], far_ref, send_ref.at[rows : 2 * rows])
+    start = 0
+    for left, right, scratch in zip(lefts, rights, turned):
+        scratch[...] = left[...].T
+        width = right.shape[1]
+        for step, target in enumerate(targets):
+            place = pl.multiple_of((mine ^ step) * rows, rows)
+            grad = dense(scratch[pl.ds(place, rows), :], right[...])
+            target[:, start : start + width] = grad.astype(jnp.bfloat16)
+        start += width
+    if extra:
+        high, low = split_bits(refs[2 * pairs][...])
+        send_ref[2 * rows :, :] = jnp.concatenate([high, low], axis=0)
+
+
+def split_bits(values):
+    high = values.astype(jnp.bfloat16)
+    return high, (values - high.astype(jnp.float32)).astype(jnp.bfloat16)
+
+
+def weight_grad(operands, vectors=None):
+    depth, width = operands[0].shape
+    columns = sum(right.shape[1] for right in operands[1::2])
+    rows = width // 4
+    pairs = len(operands) // 2
+    extra = () if vectors is None else (vectors,)
+    more = 0 if vectors is None else 2 * vectors.shape[0]
+    low = lambda *shape: jax.ShapeDtypeStruct(shape, jnp.bfloat16)
+    return pl.pallas_call(
+        functools.partial(weight_grad_kernel, pairs=pairs, extra=len(extra)),
+        out_shape=(low(rows, columns), low(rows, columns), low(2 * rows + more, columns)),
+        scratch_shapes=[pltpu.VMEM((width, depth), jnp.bfloat16)] * pairs,
+        compiler_params=pltpu.CompilerParams(vmem_limit_bytes=48 << 20),
+        cost_estimate=pl.CostEstimate(
+            flops=2 * depth * width * columns, bytes_accessed=6 << 20, transcendentals=0
+        ),
+    )(*operands, *extra)
+
+
+def add_terms(left, right):
+    f32 = lambda value: value.astype(jnp.float32)
+    half = left.shape[0] // 2
+    total = f32(left[:half]) + f32(left[half:]) + (f32(right[:half]) + f32(right[half:]))
+    return jnp.concatenate(split_bits(total), axis=0)
+
+
+def merge_kernel(own_ref, far_ref, vectors_ref, got_ref, sum_ref, send_ref):
+    rows = own_ref.shape[0]
+    sum_ref[:rows, :] = own_ref[...] + got_ref[:rows, :]
+    send_ref[:rows, :] = far_ref[...] + got_ref[rows : 2 * rows, :]
+    terms = jnp.concatenate(split_bits(vectors_ref[...]), axis=0)
+    terms = add_terms(terms, got_ref[2 * rows :, :])
+    sum_ref[rows:, :] = terms
+    send_ref[rows:, :] = terms
+
+
+def merge(own, far, vectors, got):
+    packet = jax.ShapeDtypeStruct((got.shape[0] - own.shape[0], own.shape[1]), jnp.bfloat16)
+    return pl.pallas_call(
+        merge_kernel,
+        out_shape=(packet, packet),
+        cost_estimate=pl.CostEstimate(flops=1 << 20, bytes_accessed=4 << 20, transcendentals=0),
+    )(own, far, vectors, got)
+
+
+def add_kernel(left_ref, right_ref, out_ref, *, rows):
+    out_ref[:rows, :] = left_ref[:rows, :] + right_ref[:rows, :]
+    out_ref[rows:, :] = add_terms(left_ref[rows:, :], right_ref[rows:, :])
+
+
+def add_packets(left, right, rows):
+    return pl.pallas_call(
+        functools.partial(add_kernel, rows=rows),
+        out_shape=jax.ShapeDtypeStruct(left.shape, left.dtype),
+        cost_estimate=pl.CostEstimate(flops=1 << 20, bytes_accessed=2 << 20, transcendentals=0),
+    )(left, right)
+
+
+def exchange(value, bit):
+    size = lax.axis_size("dp")
+    return lax.ppermute(value, "dp", [(i, i ^ bit) for i in range(size)])
+
+
+def swap_tensor(value):
+    return lax.ppermute(value, "tensor", [(0, 1), (1, 0)])
+
+
+def together(*values):
+    return lax.optimization_barrier(values)
+
+
+def route(value, step, inward):
+    pairs = []
+    for far in range(2):
+        for near in range(2):
+            for plane in range(4):
+                home = (2 * far + near) * 4 + plane
+                away = (2 * far + plane // 2) * 4 + 2 * near + (step ^ (plane % 2))
+                pairs.append((away, home) if inward else (home, away))
+    return lax.ppermute(value, ("dp", "context"), pairs)
+
+
+def pick_in(array, odd, upper):
+    picked = []
+    for step in range(2):
+        one = jnp.where(odd, array[1 - step], array[step])
+        picked.append(jnp.where(upper, one[::-1], one))
+    return picked
+
+
+def join_out(near, far, odd, upper):
+    arranged = [jnp.where(odd, jnp.stack(v[::-1]), jnp.stack(v)) for v in (near, far)]
+    own, peer = arranged
+    return jnp.where(upper, jnp.stack([peer, own], axis=1), jnp.stack([own, peer], axis=1))
+
+
+def gathered(shard, far_shard):
+    return (shard, exchange(shard, 1), far_shard, exchange(far_shard, 1))
+
+
+def inward(value):
+    return lax.ppermute(value, "context", [(0, 1), (3, 2)])
+
+
+def across(value):
+    return lax.ppermute(value, "context", [(1, 2), (2, 1)])
+
+
+def outward(value):
+    return lax.ppermute(value, "context", [(1, 0), (2, 3)])
+
+
+def per_device_planes(
+    tokens,
+    lengths,
+    ln1_gain,
+    ln1_bias,
+    w_query,
+    b_query,
+    w_key,
+    w_value,
+    b_value,
+    w_out,
+    b_out,
+    ln2_gain,
+    ln2_bias,
+    w_up,
+    b_up,
+    w_down,
+    b_down,
+    cotangent,
+):
+    block, width = tokens.shape[1:]
+    half = block // 2
+    local_width = w_query.shape[1]
+    member = lax.axis_index("dp")
+    near = member % 2
+    plane = lax.axis_index("context")
+    side = lax.axis_index("tensor")
+    odd = plane % 2 == 1
+    upper = side == 1
+    inner = (plane == 1) | (plane == 2)
+    row = lambda vector: vector.reshape(1, -1)
+
+    by_half = (2, 2, half, width)
+    picked = pick_in(tokens.reshape(by_half), odd, upper)
+    *picked, w_query, w_key, w_value, w_out = together(*picked, w_query, w_key, w_value, w_out)
+    rows_parts = [route(picked[step], step, True) for step in range(2)]
+    proj_own = jnp.concatenate([w_query, w_key, w_value], axis=1)
+    proj_far = exchange(proj_own, 2)
+    proj_blocks = gathered(proj_own, proj_far)
+    out_own = w_out.T
+    out_own = jnp.concatenate([out_own, swap_tensor(out_own)], axis=1)
+    proj_far, out_own, w_up, w_down = together(proj_far, out_own, w_up, w_down)
+    pack_own = jnp.concatenate([out_own, w_up, w_down.T], axis=1)
+    pack_far = exchange(pack_own, 2)
+
+    lengths_near = jnp.where(plane // 2 == near, lengths, exchange(lengths, 1))
+    length = jnp.where(odd, lengths_near[1], lengths_near[0])
+    index = jnp.arange(9, dtype=jnp.int32)
+    quarter = index % 4
+    core = jnp.where(index < 4, near, 1 - near)
+    piece = jnp.where(quarter < 2, side, 1 - side)
+    starts = (2 * core + (quarter % 2 ^ plane % 2)) * block + piece * half
+    info = jnp.where(index < 8, starts, length)
+
+    rows_low, normed_low, queries, pair_own, proj = enter(
+        *rows_parts, row(ln1_gain), row(ln1_bias), row(b_query), row(b_value), proj_blocks
+    )
+    pair_other = exchange(pair_own, 1)
+    pair_other, cotangent = together(pair_other, cotangent)
+    top_picked = pick_in(cotangent.reshape(by_half), odd, upper)
+    top_parts = [route(top_picked[step], step, True) for step in range(2)]
+    mixed, logs = attend(info, queries, pair_own, pair_other, 1)
+    mixed_peer = swap_tensor(mixed)
+    mixed, pack_own, pack_far = together(mixed, pack_own, pack_far)
+    packs = gathered(pack_own, pack_far)
+
+    (
+        middle,
+        normed_two,
+        d_feed,
+        hidden,
+        d_pre,
+        d_own,
+        d_peer,
+        feed_own,
+        feed_peer,
+        out_t,
+        grad_up_bias,
+        grad_down_bias,
+    ) = middle_part(
+        info,
+        rows_low,
+        mixed,
+        mixed_peer,
+        top_parts,
+        row(ln2_gain),
+        row(ln2_bias),
+        row(b_out),
+        packs,
+        row(b_up),
+    )
+    got_own = swap_tensor(d_peer)
+    got_peer = swap_tensor(d_own)
+
+    own, far, send = weight_grad((d_feed, hidden))
+    got = exchange(send, 1)
+    shard = got.shape[0] // 2
+    down_own, down_far = own + got[:shard], far + got[shard:]
+    down_sum = down_own + exchange(down_far, 2)
+    own, far, send = weight_grad((normed_two, d_pre))
+    got = exchange(send, 1)
+    up_own, up_far = own + got[:shard], far + got[shard:]
+    up_far, down_sum = together(up_far, down_sum)
+    up_sum = up_own + exchange(up_far, 2)
+
+    got_own, got_peer, feed_peer = together(got_own, got_peer, feed_peer)
+    feed_got = swap_tensor(feed_peer)
+    d_middle, d_attention, d_mixed, sums_two = turn(
+        info, middle, d_own, d_peer, got_own, got_peer, top_parts, row(ln2_gain), out_t
+    )
+    d_mixed, down_sum = together(d_mixed, down_sum)
+    down_got = inward(down_sum)
+    d_queries, d_pair, d_pair_other = attend_back(
+        info, queries, pair_own, pair_other, mixed, d_mixed, logs, 1
+    )
+    d_pair_other, down_got, up_sum, feed_got = together(d_pair_other, down_got, up_sum, feed_got)
+    down_sum = down_sum + down_got
+    down_got = across(down_sum)
+    up_got = inward(up_sum)
+    d_proj, one_own, one_peer, sums_one, proj_bias = leave(
+        rows_low, d_queries, d_pair, exchange(d_pair_other, 1), proj
+    )
+    sums_one = sums_one + swap_tensor(sums_one)
+    one_got = swap_tensor(one_peer)
+    vectors = jnp.concatenate(
+        [
+            grad_up_bias,
+            jnp.concatenate([grad_down_bias, sums_two[2:]], axis=1),
+            sums_two[:2].reshape(1, -1),
+            sums_one.reshape(1, -1),
+            jnp.pad(proj_bias, ((0, 0), (0, local_width))),
+            jnp.zeros((3, 4 * local_width), jnp.float32),
+        ],
+        axis=0,
+    )
+    own, far, send = weight_grad((normed_low, d_proj, d_attention, mixed), vectors)
+    packet, packet_far = merge(own, far, vectors, exchange(send, 1))
+    packet = add_packets(packet, exchange(packet_far, 2), shard)
+
+    first_row = info[:2, None, None] + lax.broadcasted_iota(jnp.int32, (2, half, 1), 1)
+    feed = feed_own.astype(jnp.float32) + feed_got.astype(jnp.float32) + b_down.astype(jnp.float32)
+    keep = (first_row < length).astype(jnp.float32)
+    output_rows = middle[:block].reshape(2, half, width) + keep * feed.reshape(2, half, width)
+    output_rows = output_rows.astype(jnp.bfloat16)
+    out_near = [route(output_rows[step], step, False) for step in range(2)]
+    output = join_out(out_near, [swap_tensor(v) for v in out_near], odd, upper)
+
+    input_rows = finish(rows_low, one_own, one_got, row(ln1_gain), d_middle)
+    in_near = [route(input_rows[step], step, False) for step in range(2)]
+    input_grad = join_out(in_near, [swap_tensor(v) for v in in_near], odd, upper)
+
+    down_sum = down_sum + down_got
+    down_sum = jnp.where(inner, down_sum, outward(down_sum))
+    up_sum = up_sum + up_got
+    up_sum = up_sum + across(up_sum)
+    up_sum = jnp.where(inner, up_sum, outward(up_sum))
+    packet = add_packets(packet, inward(packet), shard)
+    packet = add_packets(packet, across(packet), shard)
+    packet = jnp.where(inner, packet, outward(packet)).astype(jnp.float32)
+
+    count = vectors.shape[0]
+    vectors = packet[shard : shard + count] + packet[shard + count :]
+    grads = packet[:shard]
+    return (
+        output.reshape(tokens.shape),
+        input_grad.reshape(tokens.shape),
+        vectors[3, :width],
+        vectors[3, width:],
+        grads[:, :local_width],
+        vectors[4, :local_width],
+        grads[:, local_width : 2 * local_width],
+        grads[:, 2 * local_width : 3 * local_width],
+        vectors[4, 2 * local_width : 3 * local_width],
+        grads[:, 3 * local_width :].T,
+        vectors[1, width:],
+        vectors[2, :width],
+        vectors[2, width:],
+        up_sum.astype(jnp.float32),
+        vectors[0],
+        down_sum.astype(jnp.float32).T,
+        vectors[1, :width],
+    )
+
+
+def pick(mesh):
+    sizes = mesh.shape
+    planes = sizes["dp"] == 4 and sizes["context"] == 4 and sizes["tensor"] == 2
+    return per_device_planes if planes else per_device_general
+
+
 def solution(mesh):
     return jax.shard_map(
-        per_device,
+        pick(mesh),
         mesh=mesh,
         in_specs=(
             P("dp", "context", None),

time: 630 us -> 272 us (0.43)
  waiting for transfers between devices: 371 us -> 107 us
  blocking collectives: 98.5 us -> 0 us
  matrix products: 67.9 us -> 0 us
  starting transfers between devices: 1.3 us -> 67.4 us
  Pallas kernels: 0 us -> 55.4 us
  other arithmetic: 51 us -> 17.8 us
  between operations: 16.6 us -> 2.83 us
    reduce_scatter x8 -> x0, waiting for transfers between devices: 194 us -> none  [the longest x2 41.2 us: per_device(): lax.psum_scatter(key_term.astype(jnp.bfloat16), 'context', scatter_dimens...]
    psum x4 -> x0, waiting for transfers between devices: 124 us -> none  [the longest x1 51.2 us: per_device(): lax.psum(dense(hidden_low, down_weight).astype(jnp.bfloat16), 'tensor')]
    ppermute x0 -> x43, waiting for transfers between devices: none -> 107 us  [the longest x3 32.4 us: outward(): return lax.ppermute(value, 'context', [(1, 0), (2, 3)])]
    dot_general x30 -> x0, matrix products: 67.9 us -> none  [the longest x6 18.9 us: dense_tn(): lax.dot_general(left, right, (((0,), (0,)), ((), ())), preferred_element_...]
    ppermute x0 -> x43, starting transfers between devices: none -> 67.4 us  [the longest x15 22.8 us: exchange(): return lax.ppermute(value, 'dp', [(i, i ^ bit) for i in range(size)])]
    psum x1 -> x0, blocking collectives: 65.3 us -> none  [per_device(): lax.psum((grad_gain_one, grad_bias_one, grad_query_bias, grad_value_bias,...]
    pallas_call x0 -> x14, Pallas kernels: none -> 55.4 us  [the longest x1 15.1 us: middle_part(): pl.pallas_call(middle_kernel, out_shape=shapes, grid_spec=pltpu.PrefetchS...]
    all_gather x4 -> x0, waiting for transfers between devices: 52.5 us -> none  [the longest x1 35.4 us: per_device(): lax.all_gather(keys_own.reshape(seq_count, shard_rows, local_width), 'con...]
  transfers between devices with their start and end apart: 16 -> 43, of which waited for: 15 -> 18; matrix products, arithmetic and copies ran while one was open for 12% -> 7% of each run, Pallas kernels for 0% -> 12%
where the time goes in v1:
time: 272 us; the launch traced here: 271 us
  waiting for transfers between devices  107 us (39%)
  starting transfers between devices  67.4 us (25%)
  Pallas kernels  55.4 us (20%)
  local copies, waits for them, and re-layouts  20.6 us (8%)
  other arithmetic  17.8 us (7%)
  between operations  2.83 us (1%)
    ppermute x3, waiting for transfers between devices, outward(): return lax.ppermute(value, 'context', [(1, 0), (2, 3)])  32.4 us
    ppermute x11, waiting for transfers between devices, swap_tensor(): return lax.ppermute(value, 'tensor', [(0, 1), (1, 0)])  24.5 us
    ppermute x15, waiting for transfers between devices, exchange(): return lax.ppermute(value, 'dp', [(i, i ^ bit) for i in range(size)])  24.2 us
    ppermute x15, starting transfers between devices, exchange(): return lax.ppermute(value, 'dp', [(i, i ^ bit) for i in range(size)])  22.8 us
    ppermute x8, waiting for transfers between devices, route(): return lax.ppermute(value, ('dp', 'context'), pairs)  20.7 us
    ppermute x3, starting transfers between devices, inward(): return lax.ppermute(value, 'context', [(0, 1), (3, 2)])  16.1 us
    unnamed x107, local copies, waits for them, and re-layouts  15.8 us
    pallas_call x1, Pallas kernels, middle_part(): pl.pallas_call(middle_kernel, out_shape=shapes, grid_spec=pltpu.PrefetchS...  15.1 us
  transfers between devices with their start and end apart: 43, of which 18 were waited for; matrix products, arithmetic and copies ran while one was open for 7% of the time, Pallas kernels for 12%

profile of v1, /device:TPU:0, one launch (start us, length us, event | category | flops | bytes accessed | tf_op | source)
XLA Modules:
  0.0 271.0 jit_solution(4194663735459325209)
XLA Ops:
  0.7 1.2 broadcast_select_fusion.2
  2.9 3.0 %collective-permute-start.4 = (bf16[192,1152]{1,0:T(8,128)(2,1)S(1)}, bf16[192,1152]{1,0:T(8,128)(2,1)S(1)}, u32[]{:S(2)}, u32[]{:S(2)}) collective-permute-start(bf16[192,1152]{1,0:T(8,128)(2,1)S(1)} %constant_dynamic-update-slice_fusion.a), channel_id=1, source_target_pairs={{0,16},{8,24},{16,0},{24,8},{1,17},{9,25},{17,1},{25,9},{2,18},{10... | collective-permute-start | bytes 1327112 | tf_op jit(solution)/shard_map/ppermute | solution.py:851
  5.9 1.5 collective-permute-start.7
  8.1 1.6 collective-permute-start.2
  9.8 1.5 collective-permute-done.7
  11.3 4.8 %collective-permute-done.4.c = bf16[192,1152]{1,0:T(8,128)(2,1)S(1)} collective-permute-done((bf16[192,1152]{1,0:T(8,128)(2,1)S(1)}, bf16[192,1152]{1,0:T(8,128)(2,1)S(1)}, u32[]{:S(2)}, u32[]{:S(2)}) %collective-permute-start.4) | collective-permute-done | bytes 442400 | tf_op jit(solution)/shard_map/ppermute | solution.py:851
  16.1 1.3 pad_maximum_fusion.oa.ua.da
  17.4 1.7 collective-permute-start.8
  19.3 2.1 shard_map.305
  23.1 7.1 %collective-permute-start.6 = (bf16[512,768]{1,0:T(8,128)(2,1)S(1)}, bf16[512,768]{1,0:T(8,128)(2,1)S(1)}, u32[]{:S(2)}, u32[]{:S(2)}) collective-permute-start(bf16[512,768]{1,0:T(8,128)(2,1)S(1)} %get-tuple-element.93.own_ref), channel_id=1, source_target_pairs={{0,8},{8,0},{16,24},{24,16},{1,9},{9,1},{17,25},{25,17},{2,10},{10... | collective-permute-start | bytes 2359304 | tf_op jit(solution)/shard_map/ppermute | solution.py:851
  30.2 1.9 collective-permute-done
  34.1 7.0 %shard_map.306 = (bf16[512,384]{1,0:T(8,128)(2,1)S(1)}, f32[3,2,512]{2,1,0:T(2,128)S(1)}) custom-call(s32[9]{0:T(128)S(1)} %compare_select_fusion.4.info, bf16[512,384]{1,0:T(8,128)(2,1)S(1)} %get-tuple-element.92.query_ref, bf16[512,768]{1,0:T(8,128)(2,1)S(1)} %get-tuple-element.93.own_ref, bf16[512,768]{1,0:T(8,128)(2,1)S(1)} %collective-permute-done.6.other_ref), custom_call_target="tpu_custom_call" | custom-call | flops 3221225472 | bytes 2359296 | tf_op jit(solution)/shard_map/pallas_call | solution.py:339
  41.1 11.3 %collective-permute-done.8.oc.uc.dc = bf16[192,3840]{1,0:T(8,128)(2,1)} collective-permute-done((bf16[192,3840]{1,0:T(8,128)(2,1)}, bf16[192,3840]{1,0:T(8,128)(2,1)}, u32[]{:S(2)}, u32[]{:S(2)}) %collective-permute-start.8) | collective-permute-done | bytes 1474592 | tf_op jit(solution)/shard_map/ppermute | solution.py:851
  54.1 1.9 collective-permute-start.11
  56.0 1.5 collective-permute-start.9
  57.6 7.8 %collective-permute-done.11.top1_ref = bf16[2,128,768]{2,1,0:T(8,128)(2,1)S(1)} collective-permute-done((bf16[2,128,768]{2,1,0:T(8,128)(2,1)S(1)}, bf16[2,128,768]{2,1,0:T(8,128)(2,1)S(1)}, u32[]{:S(2)}, u32[]{:S(2)}) %collective-permute-start.11) | collective-permute-done | bytes 393248 | tf_op jit(solution)/shard_map/ppermute | solution.py:870
  67.3 15.1 %shard_map.307 = (f32[512,768]{1,0:T(8,128)}, bf16[512,768]{1,0:T(8,128)(2,1)}, bf16[512,768]{1,0:T(8,128)(2,1)}, bf16[512,1536]{1,0:T(8,128)(2,1)}, bf16[512,15...) custom-call(s32[9]{0:T(128)S(1)} %compare_select_fusion.4.info, ...), custom_call_target="tpu_custom_call" | custom-call | flops 4831838208 | bytes 20971520 | tf_op jit(solution)/shard_map/pallas_call | solution.py:621
  82.5 1.4 copy-done.11
  83.9 1.1 copy-done.19
  85.0 1.6 shard_map.310
  86.6 6.7 %collective-permute-start.17 = (bf16[384,1536]{1,0:T(8,128)(2,1)S(1)}, bf16[384,1536]{1,0:T(8,128)(2,1)S(1)}, u32[]{:S(2)}, u32[]{:S(2)}) collective-permute-start(bf16[384,1536]{1,0:T(8,128)(2,1)S(1)} %get-tuple-element.120), channel_id=1, source_target_pairs={{0,8},{8,0},{16,24},{24,16},{1,9},{9,1},{17,25},{25,17},{2,10},{10... | collective-permute-start | bytes 3538952 | tf_op jit(solution)/shard_map/ppermute | solution.py:851
  93.3 1.6 shard_map.309
  95.1 1.6 collective-permute-start.14
  97.2 1.6 collective-permute-start.18
  98.8 8.2 %collective-permute-done.14.got_own_ref = bf16[256,768]{1,0:T(8,128)(2,1)S(1)} collective-permute-done((bf16[256,768]{1,0:T(8,128)(2,1)S(1)}, bf16[256,768]{1,0:T(8,128)(2,1)S(1)}, u32[]{:S(2)}, u32[]{:S(2)}) %collective-permute-start.14) | collective-permute-done | bytes 393248 | tf_op jit(solution)/shard_map/ppermute | solution.py:855
  107.0 8.0 %collective-permute-done.15.got_peer_ref = bf16[256,768]{1,0:T(8,128)(2,1)S(1)} collective-permute-done((bf16[256,768]{1,0:T(8,128)(2,1)S(1)}, bf16[256,768]{1,0:T(8,128)(2,1)S(1)}, u32[]{:S(2)}, u32[]{:S(2)}) %collective-permute-start.15) | collective-permute-done | bytes 393248 | tf_op jit(solution)/shard_map/ppermute | solution.py:855
  115.0 1.5 collective-permute-start.21
  116.5 3.2 %shard_map.308 = (f32[256,768]{1,0:T(8,128)S(1)}, bf16[512,768]{1,0:T(8,128)(2,1)S(1)}, bf16[512,384]{1,0:T(8,128)(2,1)S(1)}, f32[3,768]{1,0:T(4,128)S(1)}) custom-call(s32[9]{0:T(128)S(1)} %compare_select_fusion.4.info, f32[512,768]{1,0:T(8,128)} %get-tuple-element.104.mid_ref, bf16[256,768]{1,0:T(8,128)(2,1)S(1)} %get-tuple-element.106.d_own_ref, ...), custom_call_target="tpu_custom_call" | custom-call | flops 301989888 | bytes 8388608 | tf_op jit(solution)/shard_map/pallas_call | solution.py:674
  120.7 1.5 collective-permute-start.20
  122.1 7.0 %collective-permute-start.19 = (bf16[192,1536]{1,0:T(8,128)(2,1)S(1)}, bf16[192,1536]{1,0:T(8,128)(2,1)S(1)}, u32[]{:S(2)}, u32[]{:S(2)}) collective-permute-start(bf16[192,1536]{1,0:T(8,128)(2,1)S(1)} %fusion.1), channel_id=1, source_target_pairs={{0,2},{6,4},{1,3},{7,5},{8,10},{14,12},{9,11},{15,13},{16,18},{22,... | collective-permute-start | bytes 1769480 | tf_op jit(solution)/shard_map/ppermute | solution.py:892
  129.2 9.6 %shard_map.311 = (bf16[512,384]{1,0:T(8,128)(2,1)S(1)}, bf16[512,768]{1,0:T(8,128)(2,1)S(1)}, bf16[512,768]{1,0:T(8,128)(2,1)S(1)}) custom-call(s32[9]{0:T(128)S(1)} %compare_select_fusion.4.info, bf16[512,384]{1,0:T(8,128)(2,1)S(1)} %get-tuple-element.92.query_ref, bf16[512,768]{1,0:T(8,128)(2,1)S(1)} %get-tuple-element.93.own_ref, ...), custom_call_target="tpu_custom_call" | custom-call | flops 8053063680 | bytes 4718592 | tf_op jit(solution)/shard_map/pallas_call | solution.py:424
  140.8 2.3 collective-permute-done.26.got_ref
  143.0 3.3 %shard_map.312 = (bf16[512,1152]{1,0:T(8,128)(2,1)S(1)}, bf16[256,768]{1,0:T(8,128)(2,1)S(1)}, bf16[256,768]{1,0:T(8,128)(2,1)S(1)}, f32[2,768]{1,0:T(2,128)S(1)}, f32[1,1152]{1,0:T(1,128)S(1)}) custom-call(bf16[512,768]{1,0:T(8,128)(2,1)S(1)} %copy-done.1, bf16[512,384]{1,0:T(8,128)(2,1)S(1)} %get-tuple-element.131.d_query_ref, ...), custom_call_target="tpu_custom_call" | custom-call | flops 905969664 | bytes 8388608 | tf_op jit(solution)/shard_map/pallas_call | solution.py:720
  147.9 3.1 %collective-permute-done.32 = f32[2,768]{1,0:T(2,128)S(1)} collective-permute-done((f32[2,768]{1,0:T(2,128)S(1)}, f32[2,768]{1,0:T(2,128)S(1)}, u32[]{:S(2)}, u32[]{:S(2)}) %collective-permute-start.32) | collective-permute-done | bytes 6176 | tf_op jit(solution)/shard_map/ppermute | solution.py:855
  151.1 1.3 copy-done.13
  152.4 1.1 copy-done.17
  153.5 1.1 copy-done.21
  154.6 1.8 shard_map.314
  158.1 5.2 %collective-permute-start.38 = (bf16[192,1536]{1,0:T(8,128)(2,1)}, bf16[192,1536]{1,0:T(8,128)(2,1)}, u32[]{:S(2)}, u32[]{:S(2)}) collective-permute-start(bf16[192,1536]{1,0:T(8,128)(2,1)} %fusion), channel_id=1, source_target_pairs={{0,2},{6,4},{1,3},{7,5},{8,10},{14,12},{9,11},{15,13},{16,18},{22,... | collective-permute-start | bytes 1769480 | tf_op jit(solution)/shard_map/ppermute | solution.py:892
  164.4 2.9 %shard_map.315 = (bf16[208,1536]{1,0:T(8,128)(2,1)}, bf16[208,1536]{1,0:T(8,128)(2,1)}) custom-call(bf16[192,1536]{1,0:T(8,128)(2,1)} %copy-done.7, bf16[192,1536]{1,0:T(8,128)(2,1)} %copy-done.8, f32[8,1536]{1,0:T(8,128)} %copy-done.9, bf16[400,1536]{1,0:T(8,128)(2,1)} %copy-done.27), custom_call_target="tpu_custom_call" | custom-call | flops 1048576 | bytes 4194304 | tf_op jit(solution)/shard_map/pallas_call | solution.py:829
  167.9 1.2 slice.112
  170.0 1.5 collective-permute-start.41
  171.8 4.3 %collective-permute-done.38 = bf16[192,1536]{1,0:T(8,128)(2,1)} collective-permute-done((bf16[192,1536]{1,0:T(8,128)(2,1)}, bf16[192,1536]{1,0:T(8,128)(2,1)}, u32[]{:S(2)}, u32[]{:S(2)}) %collective-permute-start.38) | collective-permute-done | bytes 589856 | tf_op jit(solution)/shard_map/ppermute | solution.py:892
  176.1 2.2 add.112
  178.3 1.5 collective-permute-start.39
  180.2 3.8 %collective-permute-done.34.right_ref = bf16[208,1536]{1,0:T(8,128)(2,1)} collective-permute-done((bf16[208,1536]{1,0:T(8,128)(2,1)}, bf16[208,1536]{1,0:T(8,128)(2,1)}, u32[]{:S(2)}, u32[]{:S(2)}) %collective-permute-start.34) | collective-permute-done | bytes 639008 | tf_op jit(solution)/shard_map/ppermute | solution.py:851
  184.1 2.2 shard_map.316.left_ref
  186.3 3.9 %collective-permute-start.35 = (bf16[208,1536]{1,0:T(8,128)(2,1)}, bf16[208,1536]{1,0:T(8,128)(2,1)}, u32[]{:S(2)}, u32[]{:S(2)}) collective-permute-start(bf16[208,1536]{1,0:T(8,128)(2,1)} %shard_map.316.left_ref), channel_id=1, source_target_pairs={{0,2},{6,4},{1,3},{7,5},{8,10},{14,12},{9,11},{15,13},{16,18},{22,... | collective-permute-start | bytes 1916936 | tf_op jit(solution)/shard_map/ppermute | solution.py:892
  190.3 2.2 add.115
  192.5 1.3 collective-permute-start.42
  193.8 12.9 %collective-permute-done.22 = bf16[128,768]{1,0:T(8,128)(2,1)S(1)} collective-permute-done((bf16[128,768]{1,0:T(8,128)(2,1)S(1)}, bf16[128,768]{1,0:T(8,128)(2,1)S(1)}, u32[]{:S(2)}, u32[]{:S(2)}) %collective-permute-start.22) | collective-permute-done | bytes 196640 | tf_op jit(solution)/shard_map/ppermute | solution.py:870
  207.4 1.6 collective-permute-start.23
  209.6 2.5 collective-permute-start.28
  212.9 1.4 add.113
  214.8 2.2 shard_map.317.left_ref
  217.0 1.3 collective-permute-start.40
  218.3 1.6 collective-permute-start.29
  221.1 2.2 convert_bitcast_fusion
  224.0 3.0 %collective-permute-done.31 = bf16[128,768]{1,0:T(8,128)(2,1)S(1)} collective-permute-done((bf16[128,768]{1,0:T(8,128)(2,1)S(1)}, bf16[128,768]{1,0:T(8,128)(2,1)S(1)}, u32[]{:S(2)}, u32[]{:S(2)}) %collective-permute-start.31) | collective-permute-done | bytes 196640 | tf_op jit(solution)/shard_map/ppermute | solution.py:855
  227.0 1.2 maximum_select_fusion.2
  230.0 2.2 shard_map.318
  232.2 1.3 collective-permute-start.37
  235.4 1.1 select_convert_fusion.1
  236.5 31.5 %collective-permute-done.37 = bf16[208,1536]{1,0:T(8,128)(2,1)S(1)} collective-permute-done((bf16[208,1536]{1,0:T(8,128)(2,1)}, bf16[208,1536]{1,0:T(8,128)(2,1)S(1)}, u32[]{:S(2)}, u32[]{:S(2)}) %collective-permute-start.37) | collective-permute-done | bytes 639008 | tf_op jit(solution)/shard_map/ppermute | solution.py:900
  (196 shorter events, 29.1 us)
Async XLA Ops:
  2.0 14.1 %copy-start.32 = (bf16[1536,192]{0,1:T(8,128)(2,1)S(1)}, bf16[1536,192]{0,1:T(8,128)(2,1)}, u32[]{:S(2)}) copy-start(bf16[1536,192]{0,1:T(8,128)(2,1)} %param.33) | copy-start | bytes 1769476
  2.0 14.1 %copy-start.33 = (bf16[192,1536]{1,0:T(8,128)(2,1)S(1)}, bf16[192,1536]{1,0:T(8,128)(2,1)}, u32[]{:S(2)}) copy-start(bf16[192,1536]{1,0:T(8,128)(2,1)} %param.31) | copy-start | bytes 1769476
  2.9 13.2 %collective-permute-start.4 = (bf16[192,1152]{1,0:T(8,128)(2,1)S(1)}, bf16[192,1152]{1,0:T(8,128)(2,1)S(1)}, u32[]{:S(2)}, u32[]{:S(2)}) collective-permute-start(bf16[192,1152]{1,0:T(8,128)(2,1)S(1)} %constant_dynamic-update-slice_fusion.a), channel_id=1, source_target_pairs={{0,16},{8,24},{16,0},{24,8},{1,17},{9,25},{17,1},{25,9},{2,18},{10... | collective-permute-start | bytes 1327112 | tf_op jit(solution)/shard_map/ppermute | solution.py:851
  5.9 5.3 %collective-permute-start.7 = (bf16[192,384]{1,0:T(8,128)(2,1)S(1)}, bf16[192,384]{1,0:T(8,128)(2,1)S(1)}, u32[]{:S(2)}, u32[]{:S(2)}) collective-permute-start(bf16[192,384]{1,0:T(8,128)(2,1)S(1)} %bitcast.54), channel_id=1, source_target_pairs={{0,1},{1,0},{2,3},{3,2},{4,5},{5,4},{6,7},{7,6},{8,9},{9,8},{10,11... | collective-permute-start | bytes 442376 | tf_op jit(solution)/shard_map/ppermute | solution.py:855
  7.4 11.8 %collective-permute-start.3 = (bf16[192,1152]{1,0:T(8,128)(2,1)S(1)}, bf16[192,1152]{1,0:T(8,128)(2,1)S(1)}, u32[]{:S(2)}, u32[]{:S(2)}) collective-permute-start(bf16[192,1152]{1,0:T(8,128)(2,1)S(1)} %constant_dynamic-update-slice_fusion.a), channel_id=1, source_target_pairs={{0,8},{8,0},{16,24},{24,16},{1,9},{9,1},{17,25},{25,17},{2,10},{10... | collective-permute-start | bytes 1327112 | tf_op jit(solution)/shard_map/ppermute | solution.py:851
  7.4 11.8 %collective-permute-start.1 = (bf16[2,128,768]{2,1,0:T(8,128)(2,1)S(1)}, bf16[2,128,768]{2,1,0:T(8,128)(2,1)S(1)}, u32[]{:S(2)}, u32[]{:S(2)}) collective-permute-start(bf16[2,128,768]{2,1,0:T(8,128)(2,1)S(1)} %reverse_select_fusion.3), channel_id=1, source_target_pairs={{0,0},{2,2},{8,4},{10,6},{4,8},{6,10},{12,12},{14,14},{16,16},{18,... | collective-permute-start | bytes 1179656 | tf_op jit(solution)/shard_map/ppermute | solution.py:870
  8.1 11.1 %collective-permute-start.2 = (bf16[2,128,768]{2,1,0:T(8,128)(2,1)S(1)}, bf16[2,128,768]{2,1,0:T(8,128)(2,1)S(1)}, u32[]{:S(2)}, u32[]{:S(2)}) collective-permute-start(bf16[2,128,768]{2,1,0:T(8,128)(2,1)S(1)} %reverse_select_fusion.2), channel_id=1, source_target_pairs={{2,0},{0,2},{10,4},{8,6},{6,8},{4,10},{14,12},{12,14},{18,16},{16,... | collective-permute-start | bytes 1179656 | tf_op jit(solution)/shard_map/ppermute | solution.py:870
  16.1 3.2 %collective-permute-start.5 = (bf16[192,1152]{1,0:T(8,128)(2,1)S(1)}, bf16[192,1152]{1,0:T(8,128)(2,1)S(1)}, u32[]{:S(2)}, u32[]{:S(2)}) collective-permute-start(bf16[192,1152]{1,0:T(8,128)(2,1)S(1)} %collective-permute-done.4.c), channel_id=1, source_target_pairs={{0,8},{8,0},{16,24},{24,16},{1,9},{9,1},{17,25},{25,17},{2,10},{10... | collective-permute-start | bytes 1327112 | tf_op jit(solution)/shard_map/ppermute | solution.py:851
  17.4 35.0 %collective-permute-start.8 = (bf16[192,3840]{1,0:T(8,128)(2,1)}, bf16[192,3840]{1,0:T(8,128)(2,1)}, u32[]{:S(2)}, u32[]{:S(2)}) collective-permute-start(bf16[192,3840]{1,0:T(8,128)(2,1)} %pad_maximum_fusion.oa.ua.da), channel_id=1, source_target_pairs={{0,16},{8,24},{16,0},{24,8},{1,17},{9,25},{17,1},{25,9},{2,18},{10... | collective-permute-start | bytes 4423688 | tf_op jit(solution)/shard_map/ppermute | solution.py:851
  19.2 11.0 %copy-start.50 = (s32[2]{0:T(128)S(1)}, s32[2]{0:T(128)}, u32[]{:S(2)}) copy-start(s32[2]{0:T(128)} %param.19) | copy-start | bytes 28
  23.1 11.0 %collective-permute-start.6 = (bf16[512,768]{1,0:T(8,128)(2,1)S(1)}, bf16[512,768]{1,0:T(8,128)(2,1)S(1)}, u32[]{:S(2)}, u32[]{:S(2)}) collective-permute-start(bf16[512,768]{1,0:T(8,128)(2,1)S(1)} %get-tuple-element.93.own_ref), channel_id=1, source_target_pairs={{0,8},{8,0},{16,24},{24,16},{1,9},{9,1},{17,25},{25,17},{2,10},{10... | collective-permute-start | bytes 2359304 | tf_op jit(solution)/shard_map/ppermute | solution.py:851
  30.2 1.9 collective-permute-start
  34.1 7.0 %copy-start.14 = (bf16[512,768]{1,0:T(8,128)(2,1)}, bf16[512,768]{1,0:T(8,128)(2,1)S(1)}, u32[]{:S(2)}) copy-start(bf16[512,768]{1,0:T(8,128)(2,1)S(1)} %collective-permute-done.6.other_ref) | copy-start | bytes 2359300
  34.1 18.9 %copy-start.28 = (bf16[2,256,768]{2,1,0:T(8,128)(2,1)S(1)}, bf16[2,256,768]{2,1,0:T(8,128)(2,1)}, u32[]{:S(2)}) copy-start(bf16[2,256,768]{2,1,0:T(8,128)(2,1)} %param.35) | copy-start | bytes 2359300
  52.4 5.1 %copy-start.45 = (bf16[768]{0:T(1024)(128)(2,1)S(1)}, bf16[768]{0:T(1024)(128)(2,1)}, u32[]{:S(2)}) copy-start(bf16[768]{0:T(1024)(128)(2,1)} %param.29) | copy-start | bytes 4612
  52.4 5.1 %copy-start.41 = (bf16[1536]{0:T(1024)(128)(2,1)S(1)}, bf16[1536]{0:T(1024)(128)(2,1)}, u32[]{:S(2)}) copy-start(bf16[1536]{0:T(1024)(128)(2,1)} %param.32) | copy-start | bytes 9220
  52.4 5.1 %copy-start.46 = (bf16[768]{0:T(1024)(128)(2,1)S(1)}, bf16[768]{0:T(1024)(128)(2,1)}, u32[]{:S(2)}) copy-start(bf16[768]{0:T(1024)(128)(2,1)} %param.30) | copy-start | bytes 4612
  52.4 5.1 %copy-start.47 = (bf16[768]{0:T(1024)(128)(2,1)S(1)}, bf16[768]{0:T(1024)(128)(2,1)}, u32[]{:S(2)}) copy-start(bf16[768]{0:T(1024)(128)(2,1)} %param.28) | copy-start | bytes 4612
  52.4 13.1 %collective-permute-start.12 = (bf16[192,3840]{1,0:T(8,128)(2,1)}, bf16[192,3840]{1,0:T(8,128)(2,1)S(1)}, u32[]{:S(2)}, u32[]{:S(2)}) collective-permute-start(bf16[192,3840]{1,0:T(8,128)(2,1)} %pad_maximum_fusion.oa.ua.da), channel_id=1, source_target_pairs={{0,8},{8,0},{16,24},{24,16},{1,9},{9,1},{17,25},{25,17},{2,10},{10... | collective-permute-start | bytes 4423688 | tf_op jit(solution)/shard_map/ppermute | solution.py:851
  52.5 13.0 %collective-permute-start.13 = (bf16[192,3840]{1,0:T(8,128)(2,1)}, bf16[192,3840]{1,0:T(8,128)(2,1)S(1)}, u32[]{:S(2)}, u32[]{:S(2)}) collective-permute-start(bf16[192,3840]{1,0:T(8,128)(2,1)} %collective-permute-done.8.oc.uc.dc), channel_id=1, source_target_pairs={{0,8},{8,0},{16,24},{24,16},{1,9},{9,1},{17,25},{25,17},{2,10},{10... | collective-permute-start | bytes 4423688 | tf_op jit(solution)/shard_map/ppermute | solution.py:851
  53.1 4.4 %collective-permute-start.10 = (bf16[2,128,768]{2,1,0:T(8,128)(2,1)S(1)}, bf16[2,128,768]{2,1,0:T(8,128)(2,1)S(1)}, u32[]{:S(2)}, u32[]{:S(2)}) collective-permute-start(bf16[2,128,768]{2,1,0:T(8,128)(2,1)S(1)} %reverse_select_fusion.1), channel_id=1, source_target_pairs={{0,0},{2,2},{8,4},{10,6},{4,8},{6,10},{12,12},{14,14},{16,16},{18,... | collective-permute-start | bytes 1179656 | tf_op jit(solution)/shard_map/ppermute | solution.py:870
  54.1 11.3 %collective-permute-start.11 = (bf16[2,128,768]{2,1,0:T(8,128)(2,1)S(1)}, bf16[2,128,768]{2,1,0:T(8,128)(2,1)S(1)}, u32[]{:S(2)}, u32[]{:S(2)}) collective-permute-start(bf16[2,128,768]{2,1,0:T(8,128)(2,1)S(1)} %reverse_select_fusion), channel_id=1, source_target_pairs={{2,0},{0,2},{10,4},{8,6},{6,8},{4,10},{14,12},{12,14},{18,16},{16,... | collective-permute-start | bytes 1179656 | tf_op jit(solution)/shard_map/ppermute | solution.py:870
  56.0 9.5 %collective-permute-start.9 = (bf16[512,384]{1,0:T(8,128)(2,1)S(1)}, bf16[512,384]{1,0:T(8,128)(2,1)S(1)}, u32[]{:S(2)}, u32[]{:S(2)}) collective-permute-start(bf16[512,384]{1,0:T(8,128)(2,1)S(1)} %get-tuple-element.100.own_ref.out_ref.refs_3_), channel_id=1, source_target_pairs={{0,1},{1,0},{2,3},{3,2},{4,5},{5,4},{6,7},{7,6},{8,9},{9,8},{10,11... | collective-permute-start | bytes 1179656 | tf_op jit(solution)/shard_map/ppermute | solution.py:855
  57.6 7.9 %copy-start.2 = (bf16[2,128,768]{2,1,0:T(8,128)(2,1)}, bf16[2,128,768]{2,1,0:T(8,128)(2,1)S(1)}, u32[]{:S(2)}) copy-start(bf16[2,128,768]{2,1,0:T(8,128)(2,1)S(1)} %collective-permute-done.10.top0_ref) | copy-start | bytes 1179652
  85.0 8.3 %copy-start.10 = (bf16[512,1536]{1,0:T(8,128)(2,1)S(1)}, bf16[512,1536]{1,0:T(8,128)(2,1)}, u32[]{:S(2)}) copy-start(bf16[512,1536]{1,0:T(8,128)(2,1)} %get-tuple-element.114.refs_1_) | copy-start | bytes 4718596
  85.0 8.3 %copy-start.18 = (bf16[512,768]{1,0:T(8,128)(2,1)S(1)}, bf16[512,768]{1,0:T(8,128)(2,1)}, u32[]{:S(2)}) copy-start(bf16[512,768]{1,0:T(8,128)(2,1)} %get-tuple-element.113.refs_0_) | copy-start | bytes 2359300
  86.6 10.5 %collective-permute-start.17 = (bf16[384,1536]{1,0:T(8,128)(2,1)S(1)}, bf16[384,1536]{1,0:T(8,128)(2,1)S(1)}, u32[]{:S(2)}, u32[]{:S(2)}) collective-permute-start(bf16[384,1536]{1,0:T(8,128)(2,1)S(1)} %get-tuple-element.120), channel_id=1, source_target_pairs={{0,8},{8,0},{16,24},{24,16},{1,9},{9,1},{17,25},{25,17},{2,10},{10... | collective-permute-start | bytes 3538952 | tf_op jit(solution)/shard_map/ppermute | solution.py:851
  94.9 21.6 %copy-start.3 = (bf16[2,128,768]{2,1,0:T(8,128)(2,1)S(1)}, bf16[2,128,768]{2,1,0:T(8,128)(2,1)}, u32[]{:S(2)}) copy-start(bf16[2,128,768]{2,1,0:T(8,128)(2,1)} %copy-done.2) | copy-start | bytes 1179652
  94.9 21.6 %copy-start.5 = (bf16[2,128,768]{2,1,0:T(8,128)(2,1)S(1)}, bf16[2,128,768]{2,1,0:T(8,128)(2,1)}, u32[]{:S(2)}) copy-start(bf16[2,128,768]{2,1,0:T(8,128)(2,1)} %copy-done.4) | copy-start | bytes 1179652
  95.0 21.6 %copy-start.6 = (bf16[768,384]{1,0:T(8,128)(2,1)S(1)}, bf16[768,384]{1,0:T(8,128)(2,1)}, u32[]{:S(2)}) copy-start(bf16[768,384]{1,0:T(8,128)(2,1)} %get-tuple-element.111.out_ref) | copy-start | bytes 1769476
  95.0 24.8 %collective-permute-start.16 = (bf16[384,1536]{1,0:T(8,128)(2,1)S(1)}, bf16[384,1536]{1,0:T(8,128)(2,1)S(1)}, u32[]{:S(2)}, u32[]{:S(2)}) collective-permute-start(bf16[384,1536]{1,0:T(8,128)(2,1)S(1)} %get-tuple-element.116), channel_id=1, source_target_pairs={{0,8},{8,0},{16,24},{24,16},{1,9},{9,1},{17,25},{25,17},{2,10},{10... | collective-permute-start | bytes 3538952 | tf_op jit(solution)/shard_map/ppermute | solution.py:851
  95.1 12.0 %collective-permute-start.14 = (bf16[256,768]{1,0:T(8,128)(2,1)S(1)}, bf16[256,768]{1,0:T(8,128)(2,1)S(1)}, u32[]{:S(2)}, u32[]{:S(2)}) collective-permute-start(bf16[256,768]{1,0:T(8,128)(2,1)S(1)} %get-tuple-element.107.d_peer_ref), channel_id=1, source_target_pairs={{0,1},{1,0},{2,3},{3,2},{4,5},{5,4},{6,7},{7,6},{8,9},{9,8},{10,11... | collective-permute-start | bytes 1179656 | tf_op jit(solution)/shard_map/ppermute | solution.py:855
  96.6 18.4 %collective-permute-start.15 = (bf16[256,768]{1,0:T(8,128)(2,1)S(1)}, bf16[256,768]{1,0:T(8,128)(2,1)S(1)}, u32[]{:S(2)}, u32[]{:S(2)}) collective-permute-start(bf16[256,768]{1,0:T(8,128)(2,1)S(1)} %get-tuple-element.106.d_own_ref), channel_id=1, source_target_pairs={{0,1},{1,0},{2,3},{3,2},{4,5},{5,4},{6,7},{7,6},{8,9},{9,8},{10,11... | collective-permute-start | bytes 1179656 | tf_op jit(solution)/shard_map/ppermute | solution.py:855
  97.2 22.7 %collective-permute-start.18 = (bf16[192,1536]{1,0:T(8,128)(2,1)S(1)}, bf16[192,1536]{1,0:T(8,128)(2,1)S(1)}, u32[]{:S(2)}, u32[]{:S(2)}) collective-permute-start(bf16[192,1536]{1,0:T(8,128)(2,1)S(1)} %slice_add_fusion.1), channel_id=1, source_target_pairs={{0,16},{8,24},{16,0},{24,8},{1,17},{9,25},{17,1},{25,9},{2,18},{10... | collective-permute-start | bytes 1769480 | tf_op jit(solution)/shard_map/ppermute | solution.py:851
  115.0 24.8 %collective-permute-start.21 = (bf16[256,768]{1,0:T(8,128)(2,1)S(1)}, bf16[256,768]{1,0:T(8,128)(2,1)S(1)}, u32[]{:S(2)}, u32[]{:S(2)}) collective-permute-start(bf16[256,768]{1,0:T(8,128)(2,1)S(1)} %get-tuple-element.129), channel_id=1, source_target_pairs={{0,1},{1,0},{2,3},{3,2},{4,5},{5,4},{6,7},{7,6},{8,9},{9,8},{10,11... | collective-permute-start | bytes 1179656 | tf_op jit(solution)/shard_map/ppermute | solution.py:855
  119.9 9.3 %copy-start.15 = (bf16[512,768]{1,0:T(8,128)(2,1)S(1)}, bf16[512,768]{1,0:T(8,128)(2,1)}, u32[]{:S(2)}) copy-start(bf16[512,768]{1,0:T(8,128)(2,1)} %copy-done.14) | copy-start | bytes 2359300
  120.7 18.2 %copy-start.25 = (bf16[192,1536]{1,0:T(8,128)(2,1)}, bf16[192,1536]{1,0:T(8,128)(2,1)S(1)}, u32[]{:S(2)}) copy-start(bf16[192,1536]{1,0:T(8,128)(2,1)S(1)} %fusion.1) | copy-start | bytes 1769476
  120.7 18.2 %collective-permute-start.20 = (bf16[192,1536]{1,0:T(8,128)(2,1)S(1)}, bf16[192,1536]{1,0:T(8,128)(2,1)S(1)}, u32[]{:S(2)}, u32[]{:S(2)}) collective-permute-start(bf16[192,1536]{1,0:T(8,128)(2,1)S(1)} %slice_add_fusion.3), channel_id=1, source_target_pairs={{0,16},{8,24},{16,0},{24,8},{1,17},{9,25},{17,1},{25,9},{2,18},{10... | collective-permute-start | bytes 1769480 | tf_op jit(solution)/shard_map/ppermute | solution.py:851
  122.1 18.6 %collective-permute-start.19 = (bf16[192,1536]{1,0:T(8,128)(2,1)S(1)}, bf16[192,1536]{1,0:T(8,128)(2,1)S(1)}, u32[]{:S(2)}, u32[]{:S(2)}) collective-permute-start(bf16[192,1536]{1,0:T(8,128)(2,1)S(1)} %fusion.1), channel_id=1, source_target_pairs={{0,2},{6,4},{1,3},{7,5},{8,10},{14,12},{9,11},{15,13},{16,18},{22,... | collective-permute-start | bytes 1769480 | tf_op jit(solution)/shard_map/ppermute | solution.py:892
  139.8 6.5 %copy-start.34 = (bf16[256,768]{1,0:T(8,128)(2,1)}, bf16[256,768]{1,0:T(8,128)(2,1)S(1)}, u32[]{:S(2)}) copy-start(bf16[256,768]{1,0:T(8,128)(2,1)S(1)} %collective-permute-done.21) | copy-start | bytes 1179652
  140.7 5.6 %copy-start.30 = (bf16[192,1536]{1,0:T(8,128)(2,1)}, bf16[192,1536]{1,0:T(8,128)(2,1)S(1)}, u32[]{:S(2)}) copy-start(bf16[192,1536]{1,0:T(8,128)(2,1)S(1)} %collective-permute-done.19) | copy-start | bytes 1769476
  140.7 2.3 collective-permute-start.26
  147.3 3.6 %collective-permute-start.32 = (f32[2,768]{1,0:T(2,128)S(1)}, f32[2,768]{1,0:T(2,128)S(1)}, u32[]{:S(2)}, u32[]{:S(2)}) collective-permute-start(f32[2,768]{1,0:T(2,128)S(1)} %get-tuple-element.146), channel_id=1, source_target_pairs={{0,1},{1,0},{2,3},{3,2},{4,5},{5,4},{6,7},{7,6},{8,9},{9,8},{10,11... | collective-permute-start | bytes 18440 | tf_op jit(solution)/shard_map/ppermute | solution.py:855
  151.1 5.4 %copy-start.9 = (f32[8,1536]{1,0:T(8,128)}, f32[8,1536]{1,0:T(8,128)S(1)}, u32[]{:S(2)}) copy-start(f32[8,1536]{1,0:T(8,128)S(1)} %concatenate.75.refs_4_.vectors_ref) | copy-start | bytes 147460
  158.1 5.2 %collective-permute-start.33 = (bf16[400,1536]{1,0:T(8,128)(2,1)S(1)}, bf16[400,1536]{1,0:T(8,128)(2,1)S(1)}, u32[]{:S(2)}, u32[]{:S(2)}) collective-permute-start(bf16[400,1536]{1,0:T(8,128)(2,1)S(1)} %get-tuple-element.150), channel_id=1, source_target_pairs={{0,8},{8,0},{16,24},{24,16},{1,9},{9,1},{17,25},{25,17},{2,10},{10... | collective-permute-start | bytes 3686408 | tf_op jit(solution)/shard_map/ppermute | solution.py:851
  158.1 17.9 %collective-permute-start.38 = (bf16[192,1536]{1,0:T(8,128)(2,1)}, bf16[192,1536]{1,0:T(8,128)(2,1)}, u32[]{:S(2)}, u32[]{:S(2)}) collective-permute-start(bf16[192,1536]{1,0:T(8,128)(2,1)} %fusion), channel_id=1, source_target_pairs={{0,2},{6,4},{1,3},{7,5},{8,10},{14,12},{9,11},{15,13},{16,18},{22,... | collective-permute-start | bytes 1769480 | tf_op jit(solution)/shard_map/ppermute | solution.py:892
  167.3 16.8 %collective-permute-start.34 = (bf16[208,1536]{1,0:T(8,128)(2,1)}, bf16[208,1536]{1,0:T(8,128)(2,1)}, u32[]{:S(2)}, u32[]{:S(2)}) collective-permute-start(bf16[208,1536]{1,0:T(8,128)(2,1)} %get-tuple-element.152), channel_id=1, source_target_pairs={{0,16},{8,24},{16,0},{24,8},{1,17},{9,25},{17,1},{25,9},{2,18},{10... | collective-permute-start | bytes 1916936 | tf_op jit(solution)/shard_map/ppermute | solution.py:851
  170.0 20.2 %collective-permute-start.41 = (bf16[192,1536]{1,0:T(8,128)(2,1)}, bf16[192,1536]{1,0:T(8,128)(2,1)}, u32[]{:S(2)}, u32[]{:S(2)}) collective-permute-start(bf16[192,1536]{1,0:T(8,128)(2,1)} %add.114), channel_id=1, source_target_pairs={{2,4},{4,2},{3,5},{5,3},{10,12},{12,10},{11,13},{13,11},{18,20},{2... | collective-permute-start | bytes 1769480 | tf_op jit(solution)/shard_map/ppermute | solution.py:896
  178.3 33.9 %collective-permute-start.39 = (bf16[192,1536]{1,0:T(8,128)(2,1)}, bf16[192,1536]{1,0:T(8,128)(2,1)}, u32[]{:S(2)}, u32[]{:S(2)}) collective-permute-start(bf16[192,1536]{1,0:T(8,128)(2,1)} %add.112), channel_id=1, source_target_pairs={{2,4},{4,2},{3,5},{5,3},{10,12},{12,10},{11,13},{13,11},{18,20},{2... | collective-permute-start | bytes 1769480 | tf_op jit(solution)/shard_map/ppermute | solution.py:896
  179.7 27.6 %collective-permute-start.27 = (bf16[256,768]{1,0:T(8,128)(2,1)S(1)}, bf16[256,768]{1,0:T(8,128)(2,1)S(1)}, u32[]{:S(2)}, u32[]{:S(2)}) collective-permute-start(bf16[256,768]{1,0:T(8,128)(2,1)S(1)} %get-tuple-element.136), channel_id=1, source_target_pairs={{0,1},{1,0},{2,3},{3,2},{4,5},{5,4},{6,7},{7,6},{8,9},{9,8},{10,11... | collective-permute-start | bytes 1179656 | tf_op jit(solution)/shard_map/ppermute | solution.py:855
  186.3 28.0 %collective-permute-start.35 = (bf16[208,1536]{1,0:T(8,128)(2,1)}, bf16[208,1536]{1,0:T(8,128)(2,1)}, u32[]{:S(2)}, u32[]{:S(2)}) collective-permute-start(bf16[208,1536]{1,0:T(8,128)(2,1)} %shard_map.316.left_ref), channel_id=1, source_target_pairs={{0,2},{6,4},{1,3},{7,5},{8,10},{14,12},{9,11},{15,13},{16,18},{22,... | collective-permute-start | bytes 1916936 | tf_op jit(solution)/shard_map/ppermute | solution.py:892
  190.2 16.5 %collective-permute-start.22 = (bf16[128,768]{1,0:T(8,128)(2,1)S(1)}, bf16[128,768]{1,0:T(8,128)(2,1)S(1)}, u32[]{:S(2)}, u32[]{:S(2)}) collective-permute-start(bf16[128,768]{1,0:T(8,128)(2,1)S(1)} %get-tuple-element.171), channel_id=1, source_target_pairs={{0,2},{2,0},{4,10},{6,8},{8,6},{10,4},{12,14},{14,12},{16,18},{18,... | collective-permute-start | bytes 589832 | tf_op jit(solution)/shard_map/ppermute | solution.py:870
  192.5 27.9 %collective-permute-start.42 = (bf16[192,1536]{1,0:T(8,128)(2,1)}, bf16[192,1536]{1,0:T(8,128)(2,1)}, u32[]{:S(2)}, u32[]{:S(2)}) collective-permute-start(bf16[192,1536]{1,0:T(8,128)(2,1)} %add.115), channel_id=1, source_target_pairs={{2,0},{4,6},{3,1},{5,7},{10,8},{12,14},{11,9},{13,15},{18,16},{20,... | collective-permute-start | bytes 1769480 | tf_op jit(solution)/shard_map/ppermute | solution.py:900
  206.7 2.9 %collective-permute-start.24 = (bf16[128,768]{1,0:T(8,128)(2,1)S(1)}, bf16[128,768]{1,0:T(8,128)(2,1)S(1)}, u32[]{:S(2)}, u32[]{:S(2)}) collective-permute-start(bf16[128,768]{1,0:T(8,128)(2,1)S(1)} %get-tuple-element.172), channel_id=1, source_target_pairs={{0,0},{2,2},{4,8},{6,10},{8,4},{10,6},{12,12},{14,14},{16,16},{18,... | collective-permute-start | bytes 589832 | tf_op jit(solution)/shard_map/ppermute | solution.py:870
  207.4 9.7 %collective-permute-start.23 = (bf16[128,768]{1,0:T(8,128)(2,1)S(1)}, bf16[128,768]{1,0:T(8,128)(2,1)S(1)}, u32[]{:S(2)}, u32[]{:S(2)}) collective-permute-start(bf16[128,768]{1,0:T(8,128)(2,1)S(1)} %collective-permute-done.22), channel_id=1, source_target_pairs={{0,1},{1,0},{2,3},{3,2},{4,5},{5,4},{6,7},{7,6},{8,9},{9,8},{10,11... | collective-permute-start | bytes 589832 | tf_op jit(solution)/shard_map/ppermute | solution.py:855
  209.6 8.7 %collective-permute-start.28 = (bf16[128,768]{1,0:T(8,128)(2,1)S(1)}, bf16[128,768]{1,0:T(8,128)(2,1)S(1)}, u32[]{:S(2)}, u32[]{:S(2)}) collective-permute-start(bf16[128,768]{1,0:T(8,128)(2,1)S(1)} %get-tuple-element.138), channel_id=1, source_target_pairs={{0,2},{2,0},{4,10},{6,8},{8,6},{10,4},{12,14},{14,12},{16,18},{18,... | collective-permute-start | bytes 589832 | tf_op jit(solution)/shard_map/ppermute | solution.py:870
  212.1 7.8 %collective-permute-start.30 = (bf16[128,768]{1,0:T(8,128)(2,1)S(1)}, bf16[128,768]{1,0:T(8,128)(2,1)S(1)}, u32[]{:S(2)}, u32[]{:S(2)}) collective-permute-start(bf16[128,768]{1,0:T(8,128)(2,1)S(1)} %get-tuple-element.139), channel_id=1, source_target_pairs={{0,0},{2,2},{4,8},{6,10},{8,4},{10,6},{12,12},{14,14},{16,16},{18,... | collective-permute-start | bytes 589832 | tf_op jit(solution)/shard_map/ppermute | solution.py:870
  214.3 9.1 %collective-permute-start.25 = (bf16[128,768]{1,0:T(8,128)(2,1)S(1)}, bf16[128,768]{1,0:T(8,128)(2,1)}, u32[]{:S(2)}, u32[]{:S(2)}) collective-permute-start(bf16[128,768]{1,0:T(8,128)(2,1)S(1)} %collective-permute-done.24), channel_id=1, source_target_pairs={{0,1},{1,0},{2,3},{3,2},{4,5},{5,4},{6,7},{7,6},{8,9},{9,8},{10,11... | collective-permute-start | bytes 589832 | tf_op jit(solution)/shard_map/ppermute | solution.py:855
  217.0 18.4 %collective-permute-start.40 = (bf16[192,1536]{1,0:T(8,128)(2,1)S(1)}, bf16[192,1536]{1,0:T(8,128)(2,1)S(1)}, u32[]{:S(2)}, u32[]{:S(2)}) collective-permute-start(bf16[192,1536]{1,0:T(8,128)(2,1)S(1)} %add.113), channel_id=1, source_target_pairs={{2,0},{4,6},{3,1},{5,7},{10,8},{12,14},{11,9},{13,15},{18,16},{20,... | collective-permute-start | bytes 1769480 | tf_op jit(solution)/shard_map/ppermute | solution.py:900
  218.3 5.7 %collective-permute-start.29 = (bf16[128,768]{1,0:T(8,128)(2,1)S(1)}, bf16[128,768]{1,0:T(8,128)(2,1)S(1)}, u32[]{:S(2)}, u32[]{:S(2)}) collective-permute-start(bf16[128,768]{1,0:T(8,128)(2,1)S(1)} %collective-permute-done.28), channel_id=1, source_target_pairs={{0,1},{1,0},{2,3},{3,2},{4,5},{5,4},{6,7},{7,6},{8,9},{9,8},{10,11... | collective-permute-start | bytes 589832 | tf_op jit(solution)/shard_map/ppermute | solution.py:855
  219.9 7.1 %collective-permute-start.31 = (bf16[128,768]{1,0:T(8,128)(2,1)S(1)}, bf16[128,768]{1,0:T(8,128)(2,1)S(1)}, u32[]{:S(2)}, u32[]{:S(2)}) collective-permute-start(bf16[128,768]{1,0:T(8,128)(2,1)S(1)} %collective-permute-done.30), channel_id=1, source_target_pairs={{0,1},{1,0},{2,3},{3,2},{4,5},{5,4},{6,7},{7,6},{8,9},{9,8},{10,11... | collective-permute-start | bytes 589832 | tf_op jit(solution)/shard_map/ppermute | solution.py:855
  220.4 8.8 %collective-permute-start.36 = (bf16[208,1536]{1,0:T(8,128)(2,1)}, bf16[208,1536]{1,0:T(8,128)(2,1)S(1)}, u32[]{:S(2)}, u32[]{:S(2)}) collective-permute-start(bf16[208,1536]{1,0:T(8,128)(2,1)} %shard_map.317.left_ref), channel_id=1, source_target_pairs={{2,4},{4,2},{3,5},{5,3},{10,12},{12,10},{11,13},{13,11},{18,20},{2... | collective-permute-start | bytes 1916936 | tf_op jit(solution)/shard_map/ppermute | solution.py:896
  232.2 35.8 %collective-permute-start.37 = (bf16[208,1536]{1,0:T(8,128)(2,1)}, bf16[208,1536]{1,0:T(8,128)(2,1)S(1)}, u32[]{:S(2)}, u32[]{:S(2)}) collective-permute-start(bf16[208,1536]{1,0:T(8,128)(2,1)} %shard_map.318), channel_id=1, source_target_pairs={{2,0},{4,6},{3,1},{5,7},{10,8},{12,14},{11,9},{13,15},{18,16},{20,... | collective-permute-start | bytes 1916936 | tf_op jit(solution)/shard_map/ppermute | solution.py:900
  234.5 33.5 %copy-start.24 = (bf16[208,1536]{1,0:T(8,128)(2,1)S(1)}, bf16[208,1536]{1,0:T(8,128)(2,1)}, u32[]{:S(2)}) copy-start(bf16[208,1536]{1,0:T(8,128)(2,1)} %shard_map.318) | copy-start | bytes 1916932
  (30 other events, 51.3 us)

commit v2 on v1

--- a/solution.py
+++ b/solution.py
@@ -303,41 +303,33 @@
 LOG_SCALE = HEAD_DIM ** (-0.5) * 1.4426950408889634
 
 
-def attend_kernel(info, query_ref, own_ref, other_ref, out_ref, log_ref, *, steps):
+def attend_kernel(info, query_ref, own_ref, other_ref, out_ref, log_ref):
     pair = 2 * HEAD_DIM
-    rows = query_ref.shape[0]
-    count = rows // 4
-    step = rows // steps
+    count = query_ref.shape[0] // 4
     keys = jnp.concatenate([own_ref[:, :pair], other_ref[:, :pair]], axis=0)
     values = jnp.concatenate([own_ref[:, pair:], other_ref[:, pair:]], axis=0)
     values_t = values.T
     key_heads = split_pair(keys, live_bias(info, count))
     query_heads = split_pair(query_ref[...], jnp.ones((), jnp.bfloat16))
-    for s in range(steps):
-        mixed = []
-        for head in range(2):
-            query = query_heads[head][s * step : (s + 1) * step]
-            scores = dense_nt(key_heads[head], query)
-            largest = jnp.max(scores, axis=0, keepdims=True)
-            weights = jnp.exp2((scores - largest) * LOG_SCALE)
-            total = jnp.sum(weights, axis=0, keepdims=True)
-            part = dense(
-                values_t[head * HEAD_DIM : (head + 1) * HEAD_DIM], weights.astype(jnp.bfloat16)
-            )
-            mixed.append(part / total)
-            log_ref[0, head : head + 1, s * step : (s + 1) * step] = (
-                largest * LOG_SCALE + jnp.log2(total)
-            )
-        out_ref[s * step : (s + 1) * step, :] = jnp.concatenate(mixed, axis=0).T.astype(jnp.bfloat16)
-
-
-def attend(info, queries, pair_own, pair_other, steps=2):
+    mixed = []
+    for head in range(2):
+        scores = dense_nt(key_heads[head], query_heads[head])
+        largest = jnp.max(scores, axis=0, keepdims=True)
+        weights = jnp.exp2((scores - largest) * LOG_SCALE)
+        total = jnp.sum(weights, axis=0, keepdims=True)
+        dims = slice(head * HEAD_DIM, (head + 1) * HEAD_DIM)
+        mixed.append(dense(values_t[dims], weights.astype(jnp.bfloat16)) / total)
+        log_ref[0, head : head + 1, :] = largest * LOG_SCALE + jnp.log2(total)
+    out_ref[...] = jnp.concatenate(mixed, axis=0).T.astype(jnp.bfloat16)
+
+
+def attend(info, queries, pair_own, pair_other):
     rows, width = queries.shape
     pair = 2 * HEAD_DIM
     groups = width // pair
     work = 4 * rows * 2 * rows * width
     return pl.pallas_call(
-        functools.partial(attend_kernel, steps=steps),
+        attend_kernel,
         out_shape=(
             jax.ShapeDtypeStruct((rows, width), jnp.bfloat16),
             jax.ShapeDtypeStruct((groups, 2, rows), jnp.float32),
@@ -368,89 +360,113 @@
     own_ref,
     other_ref,
     out_ref,
-    grad_ref,
+    d_own_ref,
+    d_peer_ref,
+    proj_ref,
     log_ref,
     d_query_ref,
-    d_own_ref,
+    d_pair_ref,
     d_other_ref,
-    *,
-    steps,
 ):
     pair = 2 * HEAD_DIM
     rows = query_ref.shape[0]
-    step = rows // steps
     scale = HEAD_DIM ** (-0.5)
     keys = jnp.concatenate([own_ref[:, :pair], other_ref[:, :pair]], axis=0)
     values = jnp.concatenate([own_ref[:, pair:], other_ref[:, pair:]], axis=0)
     keys_t = keys.T
     key_heads = split_pair(keys, live_bias(info, rows // 4))
     value_heads = split_pair(values, jnp.zeros((), jnp.bfloat16))
-    query_heads = split_pair(query_ref[...], jnp.ones((), jnp.bfloat16))
-    inner_t = (grad_ref[...].astype(jnp.float32) * out_ref[...].astype(jnp.float32)).T
-    d_keys = [0.0, 0.0]
-    d_values = [0.0, 0.0]
-    for s in range(steps):
-        part = slice(s * step, (s + 1) * step)
-        query = query_ref[part, :]
-        grad = grad_ref[part, :]
-        d_query = []
-        for head in range(2):
-            dims = slice(head * HEAD_DIM, (head + 1) * HEAD_DIM)
-            inner = jnp.sum(inner_t[dims, part], axis=0, keepdims=True)
-            scores = dense_nt(key_heads[head], query_heads[head][part])
-            probs = jnp.exp2(scores * LOG_SCALE - log_ref[0, head : head + 1, part])
-            d_probs = dense_nt(value_heads[head], grad)
-            d_scores = (probs * (d_probs - inner)).astype(jnp.bfloat16)
-            d_query.append(dense(keys_t[dims], d_scores))
-            d_keys[head] += dense(d_scores, query)
-            d_values[head] += dense(probs.astype(jnp.bfloat16), grad)
-        d_query_ref[part, :] = (jnp.concatenate(d_query, axis=0).T * scale).astype(jnp.bfloat16)
+    query = query_ref[...]
+    query_heads = split_pair(query, jnp.ones((), jnp.bfloat16))
+    d_att = jnp.concatenate([d_own_ref[...], d_peer_ref[...]], axis=0)
+    grad = dense(d_att, proj_ref[...]).astype(jnp.bfloat16)
+    inner_t = (grad.astype(jnp.float32) * out_ref[...].astype(jnp.float32)).T
+    d_query, d_keys, d_values = [], [], []
+    for head in range(2):
+        dims = slice(head * HEAD_DIM, (head + 1) * HEAD_DIM)
+        inner = jnp.sum(inner_t[dims], axis=0, keepdims=True)
+        scores = dense_nt(key_heads[head], query_heads[head])
+        probs = jnp.exp2(scores * LOG_SCALE - log_ref[0, head : head + 1, :])
+        d_probs = dense_nt(value_heads[head], grad)
+        d_scores = (probs * (d_probs - inner)).astype(jnp.bfloat16)
+        d_query.append(dense(keys_t[dims], d_scores))
+        d_keys.append(dense(d_scores, query))
+        d_values.append(dense(probs.astype(jnp.bfloat16), grad))
+    d_query_ref[...] = (jnp.concatenate(d_query, axis=0).T * scale).astype(jnp.bfloat16)
     left = lax.broadcasted_iota(jnp.int32, d_keys[0].shape, 1) < HEAD_DIM
     d_key = (jnp.where(left, d_keys[0], d_keys[1]) * scale).astype(jnp.bfloat16)
     d_value = jnp.where(left, d_values[0], d_values[1]).astype(jnp.bfloat16)
-    d_own_ref[:, :pair] = d_key[:rows]
-    d_own_ref[:, pair:] = d_value[:rows]
+    d_pair_ref[:, :pair] = d_key[:rows]
+    d_pair_ref[:, pair:] = d_value[:rows]
     d_other_ref[:, :pair] = d_key[rows:]
     d_other_ref[:, pair:] = d_value[rows:]
 
 
-def attend_back(info, queries, pair_own, pair_other, mixed, d_mixed, logs, steps=2):
-    rows, width = queries.shape
+def attend_back(info, queries, pair_own, pair_other, mixed, d_own, d_peer, out_t, logs):
+    rows, local = queries.shape
+    width = out_t.shape[0]
     pair = 2 * HEAD_DIM
-    groups = width // pair
-    work = 4 * rows * 2 * rows * width
+    work = 4 * rows * 2 * rows * local
     narrow = pl.BlockSpec((rows, pair), lambda g, info: (0, g))
     wide = pl.BlockSpec((rows, 2 * pair), lambda g, info: (0, g))
+    halves = pl.BlockSpec((rows // 2, width), lambda g, info: (0, 0))
     return pl.pallas_call(
-        functools.partial(attend_back_kernel, steps=steps),
-        out_shape=(
-            jax.ShapeDtypeStruct((rows, width), jnp.bfloat16),
-            jax.ShapeDtypeStruct((rows, 2 * width), jnp.bfloat16),
-            jax.ShapeDtypeStruct((rows, 2 * width), jnp.bfloat16),
+        attend_back_kernel,
+        out_shape=tuple(
+            jax.ShapeDtypeStruct((rows, columns), jnp.bfloat16)
+            for columns in (local, 2 * local, 2 * local)
         ),
         grid_spec=pltpu.PrefetchScalarGridSpec(
             num_scalar_prefetch=1,
-            grid=(groups,),
+            grid=(local // pair,),
             in_specs=[
                 narrow,
                 wide,
                 wide,
                 narrow,
-                narrow,
+                halves,
+                halves,
+                pl.BlockSpec((width, pair), lambda g, info: (0, g)),
                 pl.BlockSpec((1, 2, rows), lambda g, info: (g, 0, 0)),
             ],
             out_specs=(narrow, wide, wide),
         ),
         compiler_params=pltpu.CompilerParams(vmem_limit_bytes=48 << 20),
         cost_estimate=pl.CostEstimate(
-            flops=10 * work, bytes_accessed=24 * rows * width, transcendentals=work // (2 * HEAD_DIM)
-        ),
-    )(info, queries, pair_own, pair_other, mixed, d_mixed, logs)
+            flops=10 * work, bytes_accessed=24 * rows * local, transcendentals=work // (2 * HEAD_DIM)
+        ),
+    )(info, queries, pair_own, pair_other, mixed, d_own, d_peer, out_t, logs)
 
 
 def held(info, quarters, count, width):
     places = lax.broadcasted_iota(jnp.int32, (count, width), 0)
     return jnp.concatenate([info[k] + places < info[8] for k in range(quarters)], axis=0)
+
+
+def fixed(array):
+    return pl.BlockSpec(array.shape, lambda i: (0,) * len(array.shape))
+
+
+def call_once(kernel, args, shapes, flops, scratch=()):
+    moved = sum(a.size * a.dtype.itemsize for a in (*args, *shapes))
+    return pl.pallas_call(
+        kernel,
+        out_shape=tuple(shapes),
+        grid=(1,),
+        in_specs=[fixed(a) for a in args],
+        out_specs=tuple(fixed(s) for s in shapes),
+        scratch_shapes=list(scratch),
+        compiler_params=pltpu.CompilerParams(vmem_limit_bytes=48 << 20),
+        cost_estimate=pl.CostEstimate(flops=flops, bytes_accessed=moved, transcendentals=0),
+    )(*args)
+
+
+def low(*shape):
+    return jax.ShapeDtypeStruct(shape, jnp.bfloat16)
+
+
+def full(*shape):
+    return jax.ShapeDtypeStruct(shape, jnp.float32)
 
 
 def row_stats(values):
@@ -477,12 +493,12 @@
 
 
 def enter_kernel(
-    first_ref, second_ref, gain_ref, bias_ref, q_bias_ref, v_bias_ref, a, b, c, d,
+    own0, own1, peer0, peer1, gain_ref, bias_ref, q_bias_ref, v_bias_ref, a, b, c, d,
     rows_ref, normed_ref, query_ref, pair_ref, proj_ref,
 ):
     pair = 2 * HEAD_DIM
     settle((a, b, c, d), proj_ref)
-    rows = jnp.concatenate([first_ref[0], second_ref[0], first_ref[1], second_ref[1]], axis=0)
+    rows = jnp.concatenate([own0[...], own1[...], peer0[...], peer1[...]], axis=0)
     rows_ref[...] = rows
     normed, _ = row_stats(rows.astype(jnp.float32))
     normed = normed * gain_ref[...].astype(jnp.float32) + bias_ref[...].astype(jnp.float32)
@@ -500,25 +516,19 @@
         pair_ref[:, (2 * g + 1) * pair : (2 * g + 2) * pair] = value.astype(jnp.bfloat16)
 
 
-def enter(first, second, gain, bias, q_bias, v_bias, blocks):
-    half, width = first.shape[1:]
+def enter(pieces, gain, bias, q_bias, v_bias, blocks):
+    half, width = pieces[0].shape
     rows = 4 * half
     local = q_bias.shape[1]
-    low = lambda *shape: jax.ShapeDtypeStruct(shape, jnp.bfloat16)
-    return pl.pallas_call(
-        enter_kernel,
-        out_shape=(
-            low(rows, width),
-            low(rows, width),
-            low(rows, local),
-            low(rows, 2 * local),
-            low(width, 3 * local),
-        ),
-        compiler_params=pltpu.CompilerParams(vmem_limit_bytes=48 << 20),
-        cost_estimate=pl.CostEstimate(
-            flops=6 * rows * width * local, bytes_accessed=10 << 20, transcendentals=rows
-        ),
-    )(first, second, gain, bias, q_bias, v_bias, *blocks)
+    shapes = (
+        low(rows, width),
+        low(rows, width),
+        low(rows, local),
+        low(rows, 2 * local),
+        low(width, 3 * local),
+    )
+    args = (*pieces, gain, bias, q_bias, v_bias, *blocks)
+    return call_once(enter_kernel, args, shapes, 6 * rows * width * local)
 
 
 ROOT_TWO_OVER_PI = 0.7978845608028654
@@ -526,7 +536,7 @@
 
 
 def middle_kernel(
-    info, rows_ref, own_ref, peer_ref, top0_ref, top1_ref, gain_ref, bias_ref, out_bias_ref,
+    info, rows_ref, own_ref, peer_ref, top0, top1, top2, top3, gain_ref, bias_ref, out_bias_ref,
     oa, ob, oc, od, ua, ub, uc, ud, da, db, dc, dd, up_bias_ref,
     mid_ref, normed_ref, feed_ref, hidden_ref, d_pre_ref, d_own_ref, d_peer_ref,
     f_own_ref, f_peer_ref, out_ref, g_up_ref, g_down_ref,
@@ -553,7 +563,7 @@
         normed, _ = row_stats(mid)
         normed = normed * gain_ref[...].astype(jnp.float32) + bias_ref[...].astype(jnp.float32)
         normed_ref[...] = normed.astype(jnp.bfloat16)
-        top = jnp.concatenate([top0_ref[0], top1_ref[0], top0_ref[1], top1_ref[1]], axis=0)
+        top = jnp.concatenate([top0[...], top1[...], top2[...], top3[...]], axis=0)
         feed = jnp.where(real, top.astype(jnp.float32), 0.0)
         feed_ref[...] = feed.astype(jnp.bfloat16)
         g_down_ref[...] = jnp.sum(feed, axis=0, keepdims=True)
@@ -588,20 +598,15 @@
         f_peer_ref[...] = low[half:]
 
 
-def middle_part(info, rows_low, own, peer, top, gain, bias, out_bias, packs, up_bias):
+def middle_part(info, rows_low, own, peer, top, gain, bias, out_bias, packs, downs, up_bias):
     rows, width = rows_low.shape
     local = own.shape[1]
-    shard = packs[0].shape[0]
+    shard = downs[0].shape[0]
     hidden = up_bias.shape[1]
     tile = 384
-    low = lambda *shape: jax.ShapeDtypeStruct(shape, jnp.bfloat16)
-    full = lambda *shape: jax.ShapeDtypeStruct(shape, jnp.float32)
-    fixed = lambda array: pl.BlockSpec(array.shape, lambda i, info: (0,) * array.ndim)
+    fixed = lambda array: pl.BlockSpec(array.shape, lambda i, info: (0,) * len(array.shape))
     columns = lambda height: pl.BlockSpec((height, tile), lambda i, info: (0, i))
-    outs = pl.BlockSpec((shard, width), lambda i, info: (0, 0))
-    first_up, first_down = width // tile, (width + hidden) // tile
-    ups = pl.BlockSpec((shard, tile), lambda i, info: (0, first_up + i))
-    downs = pl.BlockSpec((shard, tile), lambda i, info: (0, first_down + i))
+    outs = pl.BlockSpec((shard, width), lambda i, info: (0, hidden // width))
     whole = (rows_low, own, peer, *top, gain, bias, out_bias)
     shapes = (
         full(rows, width),
@@ -624,7 +629,7 @@
         grid_spec=pltpu.PrefetchScalarGridSpec(
             num_scalar_prefetch=1,
             grid=(hidden // tile,),
-            in_specs=[fixed(a) for a in whole] + [outs] * 4 + [ups] * 4 + [downs] * 4 + [columns(1)],
+            in_specs=[fixed(a) for a in whole] + [outs] * 4 + [columns(shard)] * 8 + [columns(1)],
             out_specs=tuple(
                 columns(s.shape[0]) if k in tiled else fixed(s) for k, s in enumerate(shapes)
             ),
@@ -640,68 +645,65 @@
         cost_estimate=pl.CostEstimate(
             flops=8 * rows * width * hidden, bytes_accessed=20 << 20, transcendentals=rows * hidden
         ),
-    )(info, *whole, *packs, *packs, *packs, up_bias)
+    )(info, *whole, *packs, *packs, *downs, up_bias)
 
 
 def turn_kernel(
-    info, mid_ref, d_own_ref, d_peer_ref, got_own_ref, got_peer_ref, top0_ref, top1_ref,
-    gain_ref, out_ref, d_mid_ref, d_att_ref, d_mix_ref, sums_ref,
+    info, mid_ref, d_own_ref, got_ref, top0, top1, gain_ref, d_mid_ref, d_att_ref, sums_ref
 ):
-    rows, width = mid_ref.shape
-    half = rows // 2
-    f32 = lambda ref: ref[...].astype(jnp.float32)
-    grad = jnp.concatenate(
-        [f32(d_own_ref) + f32(got_own_ref), f32(d_peer_ref) + f32(got_peer_ref)], axis=0
-    )
+    half, width = d_own_ref.shape
+    grad = d_own_ref[...].astype(jnp.float32) + got_ref[...].astype(jnp.float32)
     normed, root = row_stats(mid_ref[...])
-    top = jnp.concatenate([top0_ref[0], top1_ref[0], top0_ref[1], top1_ref[1]], axis=0)
-    d_mid = top.astype(jnp.float32) + row_pull(
-        normed, root, grad * gain_ref[...].astype(jnp.float32)
-    )
-    d_mid_ref[...] = d_mid[:half]
-    d_att = jnp.where(held(info, 4, rows // 4, width), d_mid, 0.0).astype(jnp.bfloat16)
+    top = jnp.concatenate([top0[...], top1[...]], axis=0).astype(jnp.float32)
+    d_mid = top + row_pull(normed, root, grad * gain_ref[...].astype(jnp.float32))
+    d_mid_ref[...] = d_mid
+    d_att = jnp.where(held(info, 2, half // 2, width), d_mid, 0.0).astype(jnp.bfloat16)
     d_att_ref[...] = d_att
-    d_mix_ref[...] = dense(d_att, out_ref[...]).astype(jnp.bfloat16)
     sums_ref[0:1, :] = jnp.sum(grad * normed, axis=0, keepdims=True)
     sums_ref[1:2, :] = jnp.sum(grad, axis=0, keepdims=True)
     sums_ref[2:3, :] = jnp.sum(d_att.astype(jnp.float32), axis=0, keepdims=True)
 
 
-def turn(info, mid, d_own, d_peer, got_own, got_peer, top, gain, out_t):
-    rows, width = mid.shape
-    local = out_t.shape[1]
-    args = (mid, d_own, d_peer, got_own, got_peer, *top, gain, out_t)
+def turn(info, mid, d_own, got, top, gain):
+    half, width = d_own.shape
+    fixed = lambda a: pl.BlockSpec(a.shape, lambda i, info: (0,) * len(a.shape))
+    first = pl.BlockSpec((half, width), lambda i, info: (0, 0))
+    shapes = (
+        jax.ShapeDtypeStruct((half, width), jnp.float32),
+        jax.ShapeDtypeStruct((half, width), jnp.bfloat16),
+        jax.ShapeDtypeStruct((3, width), jnp.float32),
+    )
     return pl.pallas_call(
         turn_kernel,
-        out_shape=(
-            jax.ShapeDtypeStruct((rows // 2, width), jnp.float32),
-            jax.ShapeDtypeStruct((rows, width), jnp.bfloat16),
-            jax.ShapeDtypeStruct((rows, local), jnp.bfloat16),
-            jax.ShapeDtypeStruct((3, width), jnp.float32),
-        ),
-        in_specs=[pl.BlockSpec(memory_space=pltpu.SMEM)]
-        + [pl.BlockSpec(memory_space=pltpu.VMEM)] * len(args),
-        compiler_params=pltpu.CompilerParams(vmem_limit_bytes=48 << 20),
+        out_shape=shapes,
+        grid_spec=pltpu.PrefetchScalarGridSpec(
+            num_scalar_prefetch=1,
+            grid=(1,),
+            in_specs=[first, fixed(d_own), fixed(got), fixed(top[0]), fixed(top[1]), fixed(gain)],
+            out_specs=tuple(fixed(s) for s in shapes),
+        ),
+        compiler_params=pltpu.CompilerParams(vmem_limit_bytes=32 << 20),
         cost_estimate=pl.CostEstimate(
-            flops=2 * rows * width * local, bytes_accessed=8 << 20, transcendentals=rows
-        ),
-    )(info, *args)
+            flops=40 * half * width, bytes_accessed=4 << 20, transcendentals=half
+        ),
+    )(info, mid, d_own, got, *top, gain)
 
 
 def leave_kernel(
-    rows_ref, d_query_ref, d_pair_ref, got_ref, proj_ref, d_proj_ref, own_ref, peer_ref, sums_ref,
-    bias_ref,
+    rows_ref, proj_ref, d_query_ref, d_pair_ref, got_ref,
+    d_proj_ref, own_ref, peer_ref, sums_ref, bias_ref,
 ):
     pair = 2 * HEAD_DIM
     rows, local = d_query_ref.shape
     half = rows // 2
     d_proj_ref[:, :local] = d_query_ref[...]
+    total = (d_pair_ref[...].astype(jnp.float32) + got_ref[...].astype(jnp.float32)).astype(
+        jnp.bfloat16
+    )
     for g in range(local // pair):
         for k in range(2):
-            cols = slice((2 * g + k) * pair, (2 * g + k + 1) * pair)
-            total = d_pair_ref[:, cols].astype(jnp.float32) + got_ref[:, cols].astype(jnp.float32)
             start = (k + 1) * local + g * pair
-            d_proj_ref[:, start : start + pair] = total.astype(jnp.bfloat16)
+            d_proj_ref[:, start : start + pair] = total[:, (2 * g + k) * pair : (2 * g + k + 1) * pair]
     d_proj = d_proj_ref[...]
     bias_ref[...] = jnp.sum(d_proj.astype(jnp.float32), axis=0, keepdims=True)
     grad = dense_nt(d_proj, proj_ref[...])
@@ -713,24 +715,18 @@
     sums_ref[1:2, :] = jnp.sum(grad, axis=0, keepdims=True)
 
 
-def leave(rows_low, d_query, d_pair, got, proj):
+def leave(rows_low, proj, d_query, d_pair, got):
     rows, width = rows_low.shape
-    local = d_query.shape[1]
-    low = lambda *shape: jax.ShapeDtypeStruct(shape, jnp.bfloat16)
-    return pl.pallas_call(
-        leave_kernel,
-        out_shape=(
-            low(rows, 3 * local),
-            low(rows // 2, width),
-            low(rows // 2, width),
-            jax.ShapeDtypeStruct((2, width), jnp.float32),
-            jax.ShapeDtypeStruct((1, 3 * local), jnp.float32),
-        ),
-        compiler_params=pltpu.CompilerParams(vmem_limit_bytes=48 << 20),
-        cost_estimate=pl.CostEstimate(
-            flops=6 * rows * width * local, bytes_accessed=8 << 20, transcendentals=rows
-        ),
-    )(rows_low, d_query, d_pair, got, proj)
+    columns = proj.shape[1]
+    shapes = (
+        low(rows, columns),
+        low(rows // 2, width),
+        low(rows // 2, width),
+        full(2, width),
+        full(1, columns),
+    )
+    args = (rows_low, proj, d_query, d_pair, got)
+    return call_once(leave_kernel, args, shapes, 2 * rows * width * columns)
 
 
 def finish_kernel(rows_ref, own_ref, got_ref, gain_ref, d_mid_ref, first_ref, second_ref):
@@ -761,26 +757,24 @@
     )(rows_low, own, got, gain, d_mid)
 
 
-def weight_grad_kernel(*refs, pairs, extra):
-    count = 2 * pairs + extra
-    lefts, rights = refs[0 : 2 * pairs : 2], refs[1 : 2 * pairs : 2]
-    own_ref, far_ref, send_ref = refs[count : count + 3]
-    turned = refs[count + 3 :]
+def weight_grad_kernel(*refs, counts):
+    lefts, used = [], 0
+    for count in counts:
+        lefts.append((refs[used : used + count], refs[used + count]))
+        used += count + 1
+    own_ref, far_ref, send_ref = refs[used : used + 3]
     rows = own_ref.shape[0]
     mine = lax.axis_index("dp")
-    targets = (own_ref, send_ref.at[:rows], far_ref, send_ref.at[rows : 2 * rows])
+    targets = (own_ref, send_ref.at[:rows], far_ref, send_ref.at[rows:])
     start = 0
-    for left, right, scratch in zip(lefts, rights, turned):
-        scratch[...] = left[...].T
+    for (pieces, right), turned in zip(lefts, refs[used + 3 :]):
+        turned[...] = jnp.concatenate([piece[...] for piece in pieces], axis=0).T
         width = right.shape[1]
         for step, target in enumerate(targets):
             place = pl.multiple_of((mine ^ step) * rows, rows)
-            grad = dense(scratch[pl.ds(place, rows), :], right[...])
+            grad = dense(turned[pl.ds(place, rows), :], right[...])
             target[:, start : start + width] = grad.astype(jnp.bfloat16)
         start += width
-    if extra:
-        high, low = split_bits(refs[2 * pairs][...])
-        send_ref[2 * rows :, :] = jnp.concatenate([high, low], axis=0)
 
 
 def split_bits(values):
@@ -788,23 +782,17 @@
     return high, (values - high.astype(jnp.float32)).astype(jnp.bfloat16)
 
 
-def weight_grad(operands, vectors=None):
-    depth, width = operands[0].shape
-    columns = sum(right.shape[1] for right in operands[1::2])
+def weight_grad(*products):
+    depth, width = products[0][-1].shape[0], products[0][0].shape[1]
+    columns = sum(product[-1].shape[1] for product in products)
     rows = width // 4
-    pairs = len(operands) // 2
-    extra = () if vectors is None else (vectors,)
-    more = 0 if vectors is None else 2 * vectors.shape[0]
-    low = lambda *shape: jax.ShapeDtypeStruct(shape, jnp.bfloat16)
-    return pl.pallas_call(
-        functools.partial(weight_grad_kernel, pairs=pairs, extra=len(extra)),
-        out_shape=(low(rows, columns), low(rows, columns), low(2 * rows + more, columns)),
-        scratch_shapes=[pltpu.VMEM((width, depth), jnp.bfloat16)] * pairs,
-        compiler_params=pltpu.CompilerParams(vmem_limit_bytes=48 << 20),
-        cost_estimate=pl.CostEstimate(
-            flops=2 * depth * width * columns, bytes_accessed=6 << 20, transcendentals=0
-        ),
-    )(*operands, *extra)
+    shapes = (low(rows, columns), low(rows, columns), low(2 * rows, columns))
+    turned = [pltpu.VMEM((width, depth), jnp.bfloat16)] * len(products)
+    kernel = functools.partial(
+        weight_grad_kernel, counts=tuple(len(product) - 1 for product in products)
+    )
+    args = [array for product in products for array in product]
+    return call_once(kernel, args, shapes, 2 * depth * width * columns, turned)
 
 
 def add_terms(left, right):
@@ -814,23 +802,20 @@
     return jnp.concatenate(split_bits(total), axis=0)
 
 
-def merge_kernel(own_ref, far_ref, vectors_ref, got_ref, sum_ref, send_ref):
+def merge_kernel(own_ref, far_ref, got_ref, mine_ref, theirs_ref, sum_ref, send_ref):
     rows = own_ref.shape[0]
     sum_ref[:rows, :] = own_ref[...] + got_ref[:rows, :]
-    send_ref[:rows, :] = far_ref[...] + got_ref[rows : 2 * rows, :]
-    terms = jnp.concatenate(split_bits(vectors_ref[...]), axis=0)
-    terms = add_terms(terms, got_ref[2 * rows :, :])
+    send_ref[:rows, :] = far_ref[...] + got_ref[rows:, :]
+    terms = jnp.concatenate(split_bits(mine_ref[...] + theirs_ref[...]), axis=0)
     sum_ref[rows:, :] = terms
     send_ref[rows:, :] = terms
 
 
-def merge(own, far, vectors, got):
-    packet = jax.ShapeDtypeStruct((got.shape[0] - own.shape[0], own.shape[1]), jnp.bfloat16)
-    return pl.pallas_call(
-        merge_kernel,
-        out_shape=(packet, packet),
-        cost_estimate=pl.CostEstimate(flops=1 << 20, bytes_accessed=4 << 20, transcendentals=0),
-    )(own, far, vectors, got)
+def merge(own, far, got, mine, theirs):
+    rows, columns = own.shape
+    packet = low(rows + 2 * mine.shape[0], columns)
+    args = (own, far, got, mine, theirs)
+    return call_once(merge_kernel, args, (packet, packet), own.size)
 
 
 def add_kernel(left_ref, right_ref, out_ref, *, rows):
@@ -839,11 +824,8 @@
 
 
 def add_packets(left, right, rows):
-    return pl.pallas_call(
-        functools.partial(add_kernel, rows=rows),
-        out_shape=jax.ShapeDtypeStruct(left.shape, left.dtype),
-        cost_estimate=pl.CostEstimate(flops=1 << 20, bytes_accessed=2 << 20, transcendentals=0),
-    )(left, right)
+    kernel = functools.partial(add_kernel, rows=rows)
+    return call_once(kernel, (left, right), (low(*left.shape),), left.size)[0]
 
 
 def exchange(value, bit):
@@ -871,11 +853,8 @@
 
 
 def pick_in(array, odd, upper):
-    picked = []
-    for step in range(2):
-        one = jnp.where(odd, array[1 - step], array[step])
-        picked.append(jnp.where(upper, one[::-1], one))
-    return picked
+    mine = jnp.where(upper, array[:, 1], array[:, 0])
+    return [jnp.where(odd, mine[1 - step], mine[step]) for step in range(2)]
 
 
 def join_out(near, far, odd, upper):
@@ -886,6 +865,10 @@
 
 def gathered(shard, far_shard):
     return (shard, exchange(shard, 1), far_shard, exchange(far_shard, 1))
+
+
+def edges(value):
+    return lax.ppermute(value, "context", [(0, 1), (1, 0), (2, 3), (3, 2)])
 
 
 def inward(value):
@@ -933,19 +916,35 @@
     row = lambda vector: vector.reshape(1, -1)
 
     by_half = (2, 2, half, width)
+    groups = local_width // (2 * HEAD_DIM)
     picked = pick_in(tokens.reshape(by_half), odd, upper)
-    *picked, w_query, w_key, w_value, w_out = together(*picked, w_query, w_key, w_value, w_out)
+    *picked, w_query, w_key, w_value = together(*picked, w_query, w_key, w_value)
     rows_parts = [route(picked[step], step, True) for step in range(2)]
     proj_own = jnp.concatenate([w_query, w_key, w_value], axis=1)
     proj_far = exchange(proj_own, 2)
-    proj_blocks = gathered(proj_own, proj_far)
+    proj_near = exchange(proj_own, 1)
     out_own = w_out.T
-    out_own = jnp.concatenate([out_own, swap_tensor(out_own)], axis=1)
-    proj_far, out_own, w_up, w_down = together(proj_far, out_own, w_up, w_down)
-    pack_own = jnp.concatenate([out_own, w_up, w_down.T], axis=1)
+    out_peer = swap_tensor(out_own)
+    lengths_other = exchange(lengths, 1)
+    *rows_parts, proj_far, proj_near, out_peer, lengths_other, w_down, cotangent = together(
+        *rows_parts, proj_far, proj_near, out_peer, lengths_other, w_down, cotangent
+    )
+
+    rows_parts += [swap_tensor(v) for v in rows_parts]
+    proj_last = exchange(proj_far, 1)
+    down_own = w_down.T
+    down_far = exchange(down_own, 2)
+    top_picked = pick_in(cotangent.reshape(by_half), odd, upper)
+    top_parts = [route(top_picked[step], step, True) for step in range(2)]
+    *rows_parts, proj_last, down_far, w_up, top_0, top_1 = together(
+        *rows_parts, proj_last, down_far, w_up, *top_parts
+    )
+
+    pack_own = jnp.concatenate([w_up, out_own, out_peer], axis=1)
     pack_far = exchange(pack_own, 2)
-
-    lengths_near = jnp.where(plane // 2 == near, lengths, exchange(lengths, 1))
+    top_parts = [top_0, top_1, swap_tensor(top_0), swap_tensor(top_1)]
+    proj_blocks = (proj_own, proj_near, proj_far, proj_last)
+    lengths_near = jnp.where(plane // 2 == near, lengths, lengths_other)
     length = jnp.where(odd, lengths_near[1], lengths_near[0])
     index = jnp.arange(9, dtype=jnp.int32)
     quarter = index % 4
@@ -955,17 +954,21 @@
     info = jnp.where(index < 8, starts, length)
 
     rows_low, normed_low, queries, pair_own, proj = enter(
-        *rows_parts, row(ln1_gain), row(ln1_bias), row(b_query), row(b_value), proj_blocks
+        rows_parts, row(ln1_gain), row(ln1_bias), row(b_query), row(b_value), proj_blocks
     )
     pair_other = exchange(pair_own, 1)
-    pair_other, cotangent = together(pair_other, cotangent)
-    top_picked = pick_in(cotangent.reshape(by_half), odd, upper)
-    top_parts = [route(top_picked[step], step, True) for step in range(2)]
-    mixed, logs = attend(info, queries, pair_own, pair_other, 1)
+    mixed, logs = attend(info, queries, pair_own, pair_other)
+
+    mixed, down_own, down_far, pack_own, *top_parts = together(
+        mixed, down_own, down_far, pack_own, *top_parts
+    )
     mixed_peer = swap_tensor(mixed)
-    mixed, pack_own, pack_far = together(mixed, pack_own, pack_far)
-    packs = gathered(pack_own, pack_far)
-
+    down_blocks = gathered(down_own, down_far)
+    pack_near = exchange(pack_own, 1)
+    mixed_peer, pack_near, pack_far, *down_blocks = together(
+        mixed_peer, pack_near, pack_far, *down_blocks
+    )
+    pack_blocks = (pack_own, pack_near, pack_far, exchange(pack_far, 1))
     (
         middle,
         normed_two,
@@ -988,56 +991,37 @@
         row(ln2_gain),
         row(ln2_bias),
         row(b_out),
-        packs,
+        pack_blocks,
+        down_blocks,
         row(b_up),
     )
-    got_own = swap_tensor(d_peer)
-    got_peer = swap_tensor(d_own)
-
-    own, far, send = weight_grad((d_feed, hidden))
-    got = exchange(send, 1)
-    shard = got.shape[0] // 2
-    down_own, down_far = own + got[:shard], far + got[shard:]
-    down_sum = down_own + exchange(down_far, 2)
-    own, far, send = weight_grad((normed_two, d_pre))
-    got = exchange(send, 1)
-    up_own, up_far = own + got[:shard], far + got[shard:]
-    up_far, down_sum = together(up_far, down_sum)
-    up_sum = up_own + exchange(up_far, 2)
-
-    got_own, got_peer, feed_peer = together(got_own, got_peer, feed_peer)
+
+    got = swap_tensor(d_peer)
+    down_own, down_far, down_send = weight_grad((d_feed, hidden))
+    up_own, up_far, up_send = weight_grad((normed_two, d_pre))
+    got, down_send, up_send, feed_peer = together(got, down_send, up_send, feed_peer)
+
+    down_got = exchange(down_send, 1)
+    d_middle, d_att, sums_two = turn(info, middle, d_own, got, top_parts[:2], row(ln2_gain))
+    d_att, down_got, up_send = together(d_att, down_got, up_send)
+
+    shard = down_own.shape[0]
+    columns = hidden.shape[1]
+    d_att_peer = swap_tensor(d_att)
+    got_1 = exchange(down_far + down_got[shard:], 2)
+    down_own = down_own + down_got[:shard]
+    up_got = exchange(up_send, 1)
+    d_att_peer, got_1, up_got, feed_peer = together(d_att_peer, got_1, up_got, feed_peer)
+
+    sum_1 = down_own + got_1
+    got_1 = inward(sum_1)
+    got_2 = exchange(up_far + up_got[shard:], 2)
+    up_own = up_own + up_got[:shard]
     feed_got = swap_tensor(feed_peer)
-    d_middle, d_attention, d_mixed, sums_two = turn(
-        info, middle, d_own, d_peer, got_own, got_peer, top_parts, row(ln2_gain), out_t
-    )
-    d_mixed, down_sum = together(d_mixed, down_sum)
-    down_got = inward(down_sum)
-    d_queries, d_pair, d_pair_other = attend_back(
-        info, queries, pair_own, pair_other, mixed, d_mixed, logs, 1
-    )
-    d_pair_other, down_got, up_sum, feed_got = together(d_pair_other, down_got, up_sum, feed_got)
-    down_sum = down_sum + down_got
-    down_got = across(down_sum)
-    up_got = inward(up_sum)
-    d_proj, one_own, one_peer, sums_one, proj_bias = leave(
-        rows_low, d_queries, d_pair, exchange(d_pair_other, 1), proj
-    )
-    sums_one = sums_one + swap_tensor(sums_one)
-    one_got = swap_tensor(one_peer)
-    vectors = jnp.concatenate(
-        [
-            grad_up_bias,
-            jnp.concatenate([grad_down_bias, sums_two[2:]], axis=1),
-            sums_two[:2].reshape(1, -1),
-            sums_one.reshape(1, -1),
-            jnp.pad(proj_bias, ((0, 0), (0, local_width))),
-            jnp.zeros((3, 4 * local_width), jnp.float32),
-        ],
-        axis=0,
-    )
-    own, far, send = weight_grad((normed_low, d_proj, d_attention, mixed), vectors)
-    packet, packet_far = merge(own, far, vectors, exchange(send, 1))
-    packet = add_packets(packet, exchange(packet_far, 2), shard)
+    d_queries, d_pair, d_send = attend_back(
+        info, queries, pair_own, pair_other, mixed, d_att, d_att_peer, out_t, logs
+    )
+    d_send, got_1, got_2, feed_got = together(d_send, got_1, got_2, feed_got)
 
     first_row = info[:2, None, None] + lax.broadcasted_iota(jnp.int32, (2, half, 1), 1)
     feed = feed_own.astype(jnp.float32) + feed_got.astype(jnp.float32) + b_down.astype(jnp.float32)
@@ -1045,42 +1029,84 @@
     output_rows = middle[:block].reshape(2, half, width) + keep * feed.reshape(2, half, width)
     output_rows = output_rows.astype(jnp.bfloat16)
     out_near = [route(output_rows[step], step, False) for step in range(2)]
-    output = join_out(out_near, [swap_tensor(v) for v in out_near], odd, upper)
+    sum_1 = sum_1 + got_1
+    sum_2 = up_own + got_2
+    d_proj, one_own, one_peer, sums_one, proj_bias = leave(
+        rows_low, proj, d_queries, d_pair, exchange(d_send, 1)
+    )
+    sides = jnp.concatenate([sums_one, sums_two], axis=0)
+    one_peer, sides, sum_1, sum_2, *out_near = together(one_peer, sides, sum_1, sum_2, *out_near)
+
+    one_got = swap_tensor(one_peer)
+    got_1 = across(sum_1)
+    got_2 = inward(sum_2)
+    own, far, send = weight_grad((normed_low, d_proj), (d_att, d_att_peer, mixed))
+    send, one_got, got_1, got_2 = together(send, one_got, got_1, got_2)
 
     input_rows = finish(rows_low, one_own, one_got, row(ln1_gain), d_middle)
+    send_got = exchange(send, 1)
+    sides_got = swap_tensor(sides)
+    *input_rows, send_got, sides_got = together(*input_rows, send_got, sides_got)
+
+    flat = jnp.concatenate(
+        [proj_bias[0], (sides + sides_got).reshape(-1), grad_up_bias[0], grad_down_bias[0]]
+    )
+    vectors = jnp.pad(flat, (0, 8 * columns - flat.shape[0])).reshape(8, columns)
+    packet, packet_far = merge(own, far, send_got, vectors, exchange(vectors, 1))
+    packet_got = exchange(packet_far, 2)
     in_near = [route(input_rows[step], step, False) for step in range(2)]
-    input_grad = join_out(in_near, [swap_tensor(v) for v in in_near], odd, upper)
-
-    down_sum = down_sum + down_got
-    down_sum = jnp.where(inner, down_sum, outward(down_sum))
-    up_sum = up_sum + up_got
-    up_sum = up_sum + across(up_sum)
-    up_sum = jnp.where(inner, up_sum, outward(up_sum))
-    packet = add_packets(packet, inward(packet), shard)
-    packet = add_packets(packet, across(packet), shard)
-    packet = jnp.where(inner, packet, outward(packet)).astype(jnp.float32)
+    out_far = [swap_tensor(v) for v in out_near]
+    sum_1 = sum_1 + got_1
+    sum_2 = sum_2 + got_2
+    packet_got, sum_1, sum_2, *pieces = together(packet_got, sum_1, sum_2, *in_near, *out_far)
+
+    in_near, out_far = pieces[:2], pieces[2:]
+    packet = add_packets(packet, packet_got, shard)
+    padded = jnp.concatenate([sum_1, packet[shard:]], axis=0)
+    got_3 = edges(jnp.where(inner, padded, packet))
+    got_2 = across(sum_2)
+    in_far = [swap_tensor(v) for v in in_near]
+    got_2, got_3, *in_far = together(got_2, got_3, *in_far)
+
+    sum_2 = sum_2 + got_2
+    sum_1 = jnp.where(inner, sum_1, got_3[:shard])
+    packet = add_packets(packet, got_3, shard)
+    packet_got = across(packet)
+    got_2 = outward(sum_2)
+    input_grad = join_out(in_near, in_far, odd, upper)
+    grad_down = sum_1.astype(jnp.float32).T
+    packet_got, got_2 = together(packet_got, got_2)
+
+    packet = add_packets(packet, packet_got, shard)
+    packet_got = outward(packet)
+    grad_up = jnp.where(inner, sum_2, got_2).astype(jnp.float32)
+    output = join_out(out_near, out_far, odd, upper)
+    packet = jnp.where(inner, packet, packet_got).astype(jnp.float32)
 
     count = vectors.shape[0]
-    vectors = packet[shard : shard + count] + packet[shard + count :]
+    flat = (packet[shard : shard + count] + packet[shard + count :]).reshape(-1)
+    wide = 3 * local_width
+    ends = [wide + k * width for k in range(6)] + [wide + 5 * width + columns]
+    part = lambda k, size: flat[ends[k] : ends[k] + size]
     grads = packet[:shard]
     return (
         output.reshape(tokens.shape),
         input_grad.reshape(tokens.shape),
-        vectors[3, :width],
-        vectors[3, width:],
+        part(0, width),
+        part(1, width),
         grads[:, :local_width],
-        vectors[4, :local_width],
+        flat[:local_width],
         grads[:, local_width : 2 * local_width],
-        grads[:, 2 * local_width : 3 * local_width],
-        vectors[4, 2 * local_width : 3 * local_width],
-        grads[:, 3 * local_width :].T,
-        vectors[1, width:],
-        vectors[2, :width],
-        vectors[2, width:],
-        up_sum.astype(jnp.float32),
-        vectors[0],
-        down_sum.astype(jnp.float32).T,
-        vectors[1, :width],
+        grads[:, 2 * local_width : wide],
+        flat[2 * local_width : wide],
+        grads[:, wide:].T,
+        part(4, width),
+        part(2, width),
+        part(3, width),
+        grad_up,
+        part(5, columns),
+        grad_down,
+        part(6, width),
     )
 
 

time: 272 us -> 252 us (0.926)
  waiting for transfers between devices: 107 us -> 94.8 us
  Pallas kernels: 55.4 us -> 46.4 us
    ppermute x8, waiting for transfers between devices: 20.7 us -> 3.9 us  [route(): return lax.ppermute(value, ('dp', 'context'), pairs)]
    ppermute x11 -> x15, waiting for transfers between devices: 24.5 us -> 33.6 us  [swap_tensor(): return lax.ppermute(value, 'tensor', [(0, 1), (1, 0)])]
    pallas_call x12, Pallas kernels: 39.7 us -> 30.8 us  [the longest x9 11.7 us: call_once(): pl.pallas_call(kernel, out_shape=tuple(shapes), grid=(1,), in_specs=[fixe...]
    ppermute x11 -> x15, starting transfers between devices: 11.9 us -> 19 us  [swap_tensor(): return lax.ppermute(value, 'tensor', [(0, 1), (1, 0)])]
    ppermute x15 -> x19, starting transfers between devices: 22.8 us -> 17.7 us  [exchange(): return lax.ppermute(value, 'dp', [(i, i ^ bit) for i in range(size)])]
    ppermute x3 -> x2, starting transfers between devices: 16.1 us -> 11.9 us  [inward(): return lax.ppermute(value, 'context', [(0, 1), (3, 2)])]
    ppermute x3 -> x2, waiting for transfers between devices: 5.2 us -> 1.16 us  [inward(): return lax.ppermute(value, 'context', [(0, 1), (3, 2)])]
    add x9 -> x10, other arithmetic: 7.95 us -> 3.93 us  [the longest x2 1.52 us: per_device_planes(): sum_2 = sum_2 + got_2]
  transfers between devices with their start and end apart: 43 -> 50, of which waited for: 18 -> 23; matrix products, arithmetic and copies ran while one was open for 7% -> 5% of each run, Pallas kernels for 12% -> 12%
where the time goes in v2:
time: 252 us; the launch traced here: 251 us
  waiting for transfers between devices  94.8 us (38%)
  starting transfers between devices  69.4 us (28%)
  Pallas kernels  46.4 us (18%)
  local copies, waits for them, and re-layouts  21.2 us (8%)
  other arithmetic  15.9 us (6%)
  between operations  3.04 us (1%)
    ppermute x15, waiting for transfers between devices, swap_tensor(): return lax.ppermute(value, 'tensor', [(0, 1), (1, 0)])  33.6 us
    ppermute x2, waiting for transfers between devices, outward(): return lax.ppermute(value, 'context', [(1, 0), (2, 3)])  29.1 us
    ppermute x19, waiting for transfers between devices, exchange(): return lax.ppermute(value, 'dp', [(i, i ^ bit) for i in range(size)])  24.2 us
    ppermute x15, starting transfers between devices, swap_tensor(): return lax.ppermute(value, 'tensor', [(0, 1), (1, 0)])  19 us
    ppermute x19, starting transfers between devices, exchange(): return lax.ppermute(value, 'dp', [(i, i ^ bit) for i in range(size)])  17.7 us
    unnamed x126, local copies, waits for them, and re-layouts  17.6 us
    pallas_call x1, Pallas kernels, middle_part(): pl.pallas_call(middle_kernel, out_shape=shapes, grid_spec=pltpu.PrefetchS...  15 us
    ppermute x8, starting transfers between devices, route(): return lax.ppermute(value, ('dp', 'context'), pairs)  12.8 us
  transfers between devices with their start and end apart: 50, of which 23 were waited for; matrix products, arithmetic and copies ran while one was open for 5% of the time, Pallas kernels for 12%

profile of v2, /device:TPU:0, one launch (start us, length us, event | category | flops | bytes accessed | tf_op | source)
XLA Modules:
  0.0 250.7 jit_solution(6267357361414797971)
XLA Ops:
  0.7 1.3 slice_select_fusion.1
  2.2 3.0 %collective-permute-start.2 = (bf16[192,1152]{1,0:T(8,128)(2,1)S(1)}, bf16[192,1152]{1,0:T(8,128)(2,1)S(1)}, u32[]{:S(2)}, u32[]{:S(2)}) collective-permute-start(bf16[192,1152]{1,0:T(8,128)(2,1)S(1)} %constant_dynamic-update-slice_fusion.a), channel_id=1, source_target_pairs={{0,16},{8,24},{16,0},{24,8},{1,17},{9,25},{17,1},{25,9},{2,18},{10... | collective-permute-start | bytes 1327112 | tf_op jit(solution)/shard_map/ppermute | solution.py:833
  5.9 1.6 collective-permute-start.1
  7.5 3.8 %collective-permute-start.5 = (s32[2]{0:T(128)S(1)}, s32[2]{0:T(128)S(1)}, u32[]{:S(2)}, u32[]{:S(2)}) collective-permute-start(s32[2]{0:T(128)S(1)} %copy-done.54), channel_id=1, source_target_pairs={{0,8},{8,0},{16,24},{24,16},{1,9},{9,1},{17,25},{25,17},{2,10},{10... | collective-permute-start | bytes 32 | tf_op jit(solution)/shard_map/ppermute | solution.py:833
  12.2 1.5 collective-permute-start.4
  13.7 4.5 %collective-permute-done.4 = bf16[192,384]{1,0:T(8,128)(2,1)S(1)} collective-permute-done((bf16[192,384]{1,0:T(8,128)(2,1)S(1)}, bf16[192,384]{1,0:T(8,128)(2,1)S(1)}, u32[]{:S(2)}, u32[]{:S(2)}) %collective-permute-start.4) | collective-permute-done | bytes 147488 | tf_op jit(solution)/shard_map/ppermute | solution.py:837
  20.3 1.2 collective-permute-start.11
  21.5 1.7 collective-permute-start.6
  23.6 2.4 collective-permute-done.11.top1
  27.9 3.0 %collective-permute-done.7.peer1 = bf16[128,768]{1,0:T(8,128)(2,1)S(1)} collective-permute-done((bf16[128,768]{1,0:T(8,128)(2,1)S(1)}, bf16[128,768]{1,0:T(8,128)(2,1)S(1)}, u32[]{:S(2)}, u32[]{:S(2)}) %collective-permute-start.7) | collective-permute-done | bytes 196640 | tf_op jit(solution)/shard_map/ppermute | solution.py:837
  31.6 2.5 collective-permute-done.9.dc
  35.9 2.0 shard_map.305
  40.5 3.5 %collective-permute-start.12 = (bf16[512,768]{1,0:T(8,128)(2,1)S(1)}, bf16[512,768]{1,0:T(8,128)(2,1)S(1)}, u32[]{:S(2)}, u32[]{:S(2)}) collective-permute-start(bf16[512,768]{1,0:T(8,128)(2,1)S(1)} %get-tuple-element.160.own_ref), channel_id=1, source_target_pairs={{0,8},{8,0},{16,24},{24,16},{1,9},{9,1},{17,25},{25,17},{2,10},{10... | collective-permute-start | bytes 2359304 | tf_op jit(solution)/shard_map/ppermute | solution.py:833
  45.9 1.6 collective-permute-start.13
  48.0 1.2 pad_maximum_fusion.oa.ua
  49.2 1.6 collective-permute-start.17
  50.9 7.2 %shard_map.306 = (bf16[512,384]{1,0:T(8,128)(2,1)S(1)}, f32[3,2,512]{2,1,0:T(2,128)S(1)}) custom-call(s32[9]{0:T(128)S(1)} %compare_select_fusion.4.info, bf16[512,384]{1,0:T(8,128)(2,1)S(1)} %copy-done.23, bf16[512,768]{1,0:T(8,128)(2,1)S(1)} %get-tuple-element.160.own_ref, bf16[512,768]{1,0:T(8,128)(2,1)S(1)} %collective-permute-done.12.other_ref), custom_call_target="tpu_custom_call" | custom-call | flops 3221225472 | bytes 2359296 | tf_op jit(solution)/shard_map/pallas_call | solution.py:331
  58.8 1.5 collective-permute-start.15
  60.3 10.0 %collective-permute-done.17.oc.uc = bf16[192,2304]{1,0:T(8,128)(2,1)S(1)} collective-permute-done((bf16[192,2304]{1,0:T(8,128)(2,1)S(1)}, bf16[192,2304]{1,0:T(8,128)(2,1)S(1)}, u32[]{:S(2)}, u32[]{:S(2)}) %collective-permute-start.17) | collective-permute-done | bytes 884768 | tf_op jit(solution)/shard_map/ppermute | solution.py:833
  70.6 2.3 collective-permute-done.20.od.ud
  73.8 15.0 %shard_map.307 = (f32[512,768]{1,0:T(8,128)}, bf16[512,768]{1,0:T(8,128)(2,1)}, bf16[512,768]{1,0:T(8,128)(2,1)}, bf16[512,1536]{1,0:T(8,128)(2,1)}, bf16[512,15...) custom-call(s32[9]{0:T(128)S(1)} %compare_select_fusion.4.info, ...), custom_call_target="tpu_custom_call" | custom-call | flops 4831838208 | bytes 20971520 | tf_op jit(solution)/shard_map/pallas_call | solution.py:626
  88.8 1.6 collective-permute-start.21
  90.5 1.4 copy-done.26
  93.0 1.6 shard_map.309
  94.6 1.6 shard_map.308
  96.2 3.8 %collective-permute-done.21.got_ref = bf16[256,768]{1,0:T(8,128)(2,1)S(1)} collective-permute-done((bf16[256,768]{1,0:T(8,128)(2,1)S(1)}, bf16[256,768]{1,0:T(8,128)(2,1)S(1)}, u32[]{:S(2)}, u32[]{:S(2)}) %collective-permute-start.21) | collective-permute-done | bytes 393248 | tf_op jit(solution)/shard_map/ppermute | solution.py:837
  100.1 1.3 shard_map.310
  101.4 1.5 collective-permute-done.22
  103.1 1.6 collective-permute-start.24
  104.7 1.5 collective-permute-start.23
  106.4 9.4 %collective-permute-done.23.d_peer_ref.refs_3_ = bf16[256,768]{1,0:T(8,128)(2,1)S(1)} collective-permute-done((bf16[256,768]{1,0:T(8,128)(2,1)S(1)}, bf16[256,768]{1,0:T(8,128)(2,1)S(1)}, u32[]{:S(2)}, u32[]{:S(2)}) %collective-permute-start.23) | collective-permute-done | bytes 393248 | tf_op jit(solution)/shard_map/ppermute | solution.py:837
  115.8 3.0 %collective-permute-done.24 = bf16[192,1536]{1,0:T(8,128)(2,1)S(1)} collective-permute-done((bf16[192,1536]{1,0:T(8,128)(2,1)S(1)}, bf16[192,1536]{1,0:T(8,128)(2,1)S(1)}, u32[]{:S(2)}, u32[]{:S(2)}) %collective-permute-start.24) | collective-permute-done | bytes 589856 | tf_op jit(solution)/shard_map/ppermute | solution.py:833
  118.9 1.6 collective-permute-start.27
  120.6 1.3 collective-permute-start.26
  121.9 1.6 collective-permute-start.28
  123.5 10.6 %shard_map.311 = (bf16[512,384]{1,0:T(8,128)(2,1)S(1)}, bf16[512,768]{1,0:T(8,128)(2,1)S(1)}, bf16[512,768]{1,0:T(8,128)(2,1)S(1)}) custom-call(s32[9]{0:T(128)S(1)} %compare_select_fusion.4.info, bf16[512,384]{1,0:T(8,128)(2,1)S(1)} %copy-done.24, bf16[512,768]{1,0:T(8,128)(2,1)S(1)} %copy-done.10, bf16[512,768]{1,0:T(8,128)(2,1)S(1)} %copy-done.12, ...), custom_call_target="tpu_custom_call" | custom-call | flops 8053063680 | bytes 4718592 | tf_op jit(solution)/shard_map/pallas_call | solution.py:413
  135.2 2.5 collective-permute-start.31
  138.0 1.4 copy-done.2
  139.4 3.3 %shard_map.312 = (bf16[512,1152]{1,0:T(8,128)(2,1)S(1)}, bf16[256,768]{1,0:T(8,128)(2,1)S(1)}, bf16[256,768]{1,0:T(8,128)(2,1)S(1)}, f32[2,768]{1,0:T(2,128)S(1)}, f32[1,1152]{1,0:T(1,128)S(1)}) custom-call(bf16[512,768]{1,0:T(8,128)(2,1)S(1)} %copy-done.2, bf16[768,1152]{1,0:T(8,128)(2,1)} %get-tuple-element.157.proj_ref, ...), custom_call_target="tpu_custom_call" | custom-call | flops 905969664 | bytes 6498816 | tf_op jit(solution)/shard_map/pallas_call | solution.py:452
  143.5 1.5 collective-permute-start.33
  144.9 10.6 %collective-permute-start.34 = (bf16[192,1536]{1,0:T(8,128)(2,1)S(1)}, bf16[192,1536]{1,0:T(8,128)(2,1)S(1)}, u32[]{:S(2)}, u32[]{:S(2)}) collective-permute-start(bf16[192,1536]{1,0:T(8,128)(2,1)S(1)} %add_add_fusion.1), channel_id=1, source_target_pairs={{0,2},{6,4},{1,3},{7,5},{8,10},{14,12},{9,11},{15,13},{16,18},{22,... | collective-permute-start | bytes 1769480 | tf_op jit(solution)/shard_map/ppermute | solution.py:875
  155.5 1.5 collective-permute-start.32
  157.0 2.8 %shard_map.313 = (bf16[192,1536]{1,0:T(8,128)(2,1)S(1)}, bf16[192,1536]{1,0:T(8,128)(2,1)S(1)}, bf16[384,1536]{1,0:T(8,128)(2,1)}) custom-call(bf16[512,768]{1,0:T(8,128)(2,1)S(1)} %copy-done.21, bf16[512,1152]{1,0:T(8,128)(2,1)S(1)} %get-tuple-element.213.refs_1_, bf16[256,768]{1,0:T(8,128)(2,1)S(1)} %get-tuple-element.196.d_own_ref.refs_2_, ...), custom_call_target="tpu_custom_call" | custom-call | flops 1207959552 | bytes 5505024 | tf_op jit(solution)/shard_map/pallas_call | solution.py:452
  160.7 4.9 %collective-permute-done.32.got_ref = bf16[256,768]{1,0:T(8,128)(2,1)S(1)} collective-permute-done((bf16[256,768]{1,0:T(8,128)(2,1)S(1)}, bf16[256,768]{1,0:T(8,128)(2,1)S(1)}, u32[]{:S(2)}, u32[]{:S(2)}) %collective-permute-start.32) | collective-permute-done | bytes 393248 | tf_op jit(solution)/shard_map/ppermute | solution.py:837
  168.3 1.5 collective-permute-start.36
  179.0 1.5 collective-permute-start.42
  180.5 3.0 %collective-permute-start.39 = (bf16[128,768]{1,0:T(8,128)(2,1)}, bf16[128,768]{1,0:T(8,128)(2,1)}, u32[]{:S(2)}, u32[]{:S(2)}) collective-permute-start(bf16[128,768]{1,0:T(8,128)(2,1)} %copy-done.19), channel_id=1, source_target_pairs={{0,0},{2,2},{4,8},{6,10},{8,4},{10,6},{12,12},{14,14},{16,16},{18,... | collective-permute-start | bytes 589832 | tf_op jit(solution)/shard_map/ppermute | solution.py:852
  183.5 2.5 collective-permute-start.40
  186.0 1.4 add.113
  187.4 1.2 add.112
  188.6 1.2 collective-permute-done.42
  189.8 1.5 collective-permute-done.40
  191.3 3.1 %collective-permute-done.38.right_ref = bf16[208,1536]{1,0:T(8,128)(2,1)S(1)} collective-permute-done((bf16[208,1536]{1,0:T(8,128)(2,1)S(1)}, bf16[208,1536]{1,0:T(8,128)(2,1)S(1)}, u32[]{:S(2)}, u32[]{:S(2)}) %collective-permute-start.38) | collective-permute-done | bytes 639008 | tf_op jit(solution)/shard_map/ppermute | solution.py:833
  194.6 2.5 %collective-permute-start.44 = (bf16[208,1536]{1,0:T(8,128)(2,1)S(1)}, bf16[208,1536]{1,0:T(8,128)(2,1)S(1)}, u32[]{:S(2)}, u32[]{:S(2)}) collective-permute-start(bf16[208,1536]{1,0:T(8,128)(2,1)S(1)} %maximum_select_fusion.2), channel_id=1, source_target_pairs={{0,2},{2,0},{4,6},{6,4},{1,3},{3,1},{5,7},{7,5},{8,10},{10,8},{12,... | collective-permute-start | bytes 1916936 | tf_op jit(solution)/shard_map/ppermute | solution.py:871
  198.5 1.5 collective-permute-start.46
  200.0 1.3 maximum_select_fusion.6
  201.3 1.3 maximum_select_fusion.3
  203.6 2.4 collective-permute-done.45
  206.0 3.0 %collective-permute-done.46 = bf16[128,768]{1,0:T(8,128)(2,1)S(1)} collective-permute-done((bf16[128,768]{1,0:T(8,128)(2,1)}, bf16[128,768]{1,0:T(8,128)(2,1)S(1)}, u32[]{:S(2)}, u32[]{:S(2)}) %collective-permute-start.46) | collective-permute-done | bytes 196640 | tf_op jit(solution)/shard_map/ppermute | solution.py:837
  209.1 2.8 %collective-permute-done.44.right_ref = bf16[208,1536]{1,0:T(8,128)(2,1)S(1)} collective-permute-done((bf16[208,1536]{1,0:T(8,128)(2,1)S(1)}, bf16[208,1536]{1,0:T(8,128)(2,1)S(1)}, u32[]{:S(2)}, u32[]{:S(2)}) %collective-permute-start.44) | collective-permute-done | bytes 639008 | tf_op jit(solution)/shard_map/ppermute | solution.py:871
  211.9 1.3 collective-permute-start.48
  215.2 13.4 %collective-permute-done.48 = bf16[192,1536]{1,0:T(8,128)(2,1)S(1)} collective-permute-done((bf16[192,1536]{1,0:T(8,128)(2,1)S(1)}, bf16[192,1536]{1,0:T(8,128)(2,1)S(1)}, u32[]{:S(2)}, u32[]{:S(2)}) %collective-permute-start.48) | collective-permute-done | bytes 589856 | tf_op jit(solution)/shard_map/ppermute | solution.py:883
  228.8 1.3 collective-permute-start.49
  232.1 15.7 %collective-permute-done.49 = bf16[208,1536]{1,0:T(8,128)(2,1)S(1)} collective-permute-done((bf16[208,1536]{1,0:T(8,128)(2,1)S(1)}, bf16[208,1536]{1,0:T(8,128)(2,1)S(1)}, u32[]{:S(2)}, u32[]{:S(2)}) %collective-permute-start.49) | collective-permute-done | bytes 639008 | tf_op jit(solution)/shard_map/ppermute | solution.py:883
  (232 shorter events, 39.6 us)
Async XLA Ops:
  0.7 18.2 %copy-start.34 = (bf16[2,256,768]{2,1,0:T(8,128)(2,1)S(1)}, bf16[2,256,768]{2,1,0:T(8,128)(2,1)}, u32[]{:S(2)}) copy-start(bf16[2,256,768]{2,1,0:T(8,128)(2,1)} %param.35) | copy-start | bytes 2359300
  2.1 21.4 %copy-start.47 = (bf16[768]{0:T(1024)(128)(2,1)S(1)}, bf16[768]{0:T(1024)(128)(2,1)}, u32[]{:S(2)}) copy-start(bf16[768]{0:T(1024)(128)(2,1)} %param.20) | copy-start | bytes 4612
  2.1 21.4 %copy-start.48 = (bf16[768]{0:T(1024)(128)(2,1)S(1)}, bf16[768]{0:T(1024)(128)(2,1)}, u32[]{:S(2)}) copy-start(bf16[768]{0:T(1024)(128)(2,1)} %param.21) | copy-start | bytes 4612
  2.1 21.4 %copy-start.52 = (bf16[384]{0:T(512)(128)(2,1)S(1)}, bf16[384]{0:T(512)(128)(2,1)}, u32[]{:S(2)}) copy-start(bf16[384]{0:T(512)(128)(2,1)} %param.23) | copy-start | bytes 2308
  2.1 21.4 %copy-start.53 = (bf16[384]{0:T(512)(128)(2,1)S(1)}, bf16[384]{0:T(512)(128)(2,1)}, u32[]{:S(2)}) copy-start(bf16[384]{0:T(512)(128)(2,1)} %param.26) | copy-start | bytes 2308
  2.2 16.0 %collective-permute-start.2 = (bf16[192,1152]{1,0:T(8,128)(2,1)S(1)}, bf16[192,1152]{1,0:T(8,128)(2,1)S(1)}, u32[]{:S(2)}, u32[]{:S(2)}) collective-permute-start(bf16[192,1152]{1,0:T(8,128)(2,1)S(1)} %constant_dynamic-update-slice_fusion.a), channel_id=1, source_target_pairs={{0,16},{8,24},{16,0},{24,8},{1,17},{9,25},{17,1},{25,9},{2,18},{10... | collective-permute-start | bytes 1327112 | tf_op jit(solution)/shard_map/ppermute | solution.py:833
  5.2 13.0 %collective-permute-start.3 = (bf16[192,1152]{1,0:T(8,128)(2,1)S(1)}, bf16[192,1152]{1,0:T(8,128)(2,1)S(1)}, u32[]{:S(2)}, u32[]{:S(2)}) collective-permute-start(bf16[192,1152]{1,0:T(8,128)(2,1)S(1)} %constant_dynamic-update-slice_fusion.a), channel_id=1, source_target_pairs={{0,8},{8,0},{16,24},{24,16},{1,9},{9,1},{17,25},{25,17},{2,10},{10... | collective-permute-start | bytes 1327112 | tf_op jit(solution)/shard_map/ppermute | solution.py:833
  5.2 13.0 %collective-permute-start = (bf16[128,768]{1,0:T(8,128)(2,1)S(1)}, bf16[128,768]{1,0:T(8,128)(2,1)S(1)}, u32[]{:S(2)}, u32[]{:S(2)}) collective-permute-start(bf16[128,768]{1,0:T(8,128)(2,1)S(1)} %get-tuple-element.139), channel_id=1, source_target_pairs={{0,0},{2,2},{8,4},{10,6},{4,8},{6,10},{12,12},{14,14},{16,16},{18,... | collective-permute-start | bytes 589832 | tf_op jit(solution)/shard_map/ppermute | solution.py:852
  5.9 12.4 %collective-permute-start.1 = (bf16[128,768]{1,0:T(8,128)(2,1)S(1)}, bf16[128,768]{1,0:T(8,128)(2,1)S(1)}, u32[]{:S(2)}, u32[]{:S(2)}) collective-permute-start(bf16[128,768]{1,0:T(8,128)(2,1)S(1)} %get-tuple-element.140), channel_id=1, source_target_pairs={{2,0},{0,2},{10,4},{8,6},{6,8},{4,10},{14,12},{12,14},{18,16},{16,... | collective-permute-start | bytes 589832 | tf_op jit(solution)/shard_map/ppermute | solution.py:852
  7.5 4.6 %collective-permute-start.5 = (s32[2]{0:T(128)S(1)}, s32[2]{0:T(128)S(1)}, u32[]{:S(2)}, u32[]{:S(2)}) collective-permute-start(s32[2]{0:T(128)S(1)} %copy-done.54), channel_id=1, source_target_pairs={{0,8},{8,0},{16,24},{24,16},{1,9},{9,1},{17,25},{25,17},{2,10},{10... | collective-permute-start | bytes 32 | tf_op jit(solution)/shard_map/ppermute | solution.py:833
  12.2 6.1 %collective-permute-start.4 = (bf16[192,384]{1,0:T(8,128)(2,1)S(1)}, bf16[192,384]{1,0:T(8,128)(2,1)S(1)}, u32[]{:S(2)}, u32[]{:S(2)}) collective-permute-start(bf16[192,384]{1,0:T(8,128)(2,1)S(1)} %bitcast.46), channel_id=1, source_target_pairs={{0,1},{1,0},{2,3},{3,2},{4,5},{5,4},{6,7},{7,6},{8,9},{9,8},{10,11... | collective-permute-start | bytes 442376 | tf_op jit(solution)/shard_map/ppermute | solution.py:837
  19.0 15.1 %collective-permute-start.9 = (bf16[192,1536]{1,0:T(8,128)(2,1)}, bf16[192,1536]{1,0:T(8,128)(2,1)}, u32[]{:S(2)}, u32[]{:S(2)}) collective-permute-start(bf16[192,1536]{1,0:T(8,128)(2,1)} %bitcast.4.da), channel_id=1, source_target_pairs={{0,16},{8,24},{16,0},{24,8},{1,17},{9,25},{17,1},{25,9},{2,18},{10... | collective-permute-start | bytes 1769480 | tf_op jit(solution)/shard_map/ppermute | solution.py:833
  19.6 12.0 %collective-permute-start.8 = (bf16[192,1152]{1,0:T(8,128)(2,1)S(1)}, bf16[192,1152]{1,0:T(8,128)(2,1)S(1)}, u32[]{:S(2)}, u32[]{:S(2)}) collective-permute-start(bf16[192,1152]{1,0:T(8,128)(2,1)S(1)} %collective-permute-done.2.c), channel_id=1, source_target_pairs={{0,8},{8,0},{16,24},{24,16},{1,9},{9,1},{17,25},{25,17},{2,10},{10... | collective-permute-start | bytes 1327112 | tf_op jit(solution)/shard_map/ppermute | solution.py:833
  19.6 3.6 %collective-permute-start.10 = (bf16[128,768]{1,0:T(8,128)(2,1)S(1)}, bf16[128,768]{1,0:T(8,128)(2,1)S(1)}, u32[]{:S(2)}, u32[]{:S(2)}) collective-permute-start(bf16[128,768]{1,0:T(8,128)(2,1)S(1)} %get-tuple-element.268), channel_id=1, source_target_pairs={{0,0},{2,2},{8,4},{10,6},{4,8},{6,10},{12,12},{14,14},{16,16},{18,... | collective-permute-start | bytes 589832 | tf_op jit(solution)/shard_map/ppermute | solution.py:852
  20.3 5.7 %collective-permute-start.11 = (bf16[128,768]{1,0:T(8,128)(2,1)S(1)}, bf16[128,768]{1,0:T(8,128)(2,1)S(1)}, u32[]{:S(2)}, u32[]{:S(2)}) collective-permute-start(bf16[128,768]{1,0:T(8,128)(2,1)S(1)} %get-tuple-element.267), channel_id=1, source_target_pairs={{2,0},{0,2},{10,4},{8,6},{6,8},{4,10},{14,12},{12,14},{18,16},{16,... | collective-permute-start | bytes 589832 | tf_op jit(solution)/shard_map/ppermute | solution.py:852
  21.5 5.7 %collective-permute-start.6 = (bf16[128,768]{1,0:T(8,128)(2,1)S(1)}, bf16[128,768]{1,0:T(8,128)(2,1)S(1)}, u32[]{:S(2)}, u32[]{:S(2)}) collective-permute-start(bf16[128,768]{1,0:T(8,128)(2,1)S(1)} %collective-permute-done.own0), channel_id=1, source_target_pairs={{0,1},{1,0},{2,3},{3,2},{4,5},{5,4},{6,7},{7,6},{8,9},{9,8},{10,11... | collective-permute-start | bytes 589832 | tf_op jit(solution)/shard_map/ppermute | solution.py:837
  23.2 7.7 %collective-permute-start.7 = (bf16[128,768]{1,0:T(8,128)(2,1)S(1)}, bf16[128,768]{1,0:T(8,128)(2,1)S(1)}, u32[]{:S(2)}, u32[]{:S(2)}) collective-permute-start(bf16[128,768]{1,0:T(8,128)(2,1)S(1)} %collective-permute-done.1.own1), channel_id=1, source_target_pairs={{0,1},{1,0},{2,3},{3,2},{4,5},{5,4},{6,7},{7,6},{8,9},{9,8},{10,11... | collective-permute-start | bytes 589832 | tf_op jit(solution)/shard_map/ppermute | solution.py:837
  40.5 17.5 %copy-start.9 = (bf16[512,768]{1,0:T(8,128)(2,1)}, bf16[512,768]{1,0:T(8,128)(2,1)S(1)}, u32[]{:S(2)}) copy-start(bf16[512,768]{1,0:T(8,128)(2,1)S(1)} %get-tuple-element.160.own_ref) | copy-start | bytes 2359300
  40.5 10.3 %collective-permute-start.12 = (bf16[512,768]{1,0:T(8,128)(2,1)S(1)}, bf16[512,768]{1,0:T(8,128)(2,1)S(1)}, u32[]{:S(2)}, u32[]{:S(2)}) collective-permute-start(bf16[512,768]{1,0:T(8,128)(2,1)S(1)} %get-tuple-element.160.own_ref), channel_id=1, source_target_pairs={{0,8},{8,0},{16,24},{24,16},{1,9},{9,1},{17,25},{25,17},{2,10},{10... | collective-permute-start | bytes 2359304 | tf_op jit(solution)/shard_map/ppermute | solution.py:833
  45.9 12.2 %collective-permute-start.13 = (bf16[128,768]{1,0:T(8,128)(2,1)S(1)}, bf16[128,768]{1,0:T(8,128)(2,1)S(1)}, u32[]{:S(2)}, u32[]{:S(2)}) collective-permute-start(bf16[128,768]{1,0:T(8,128)(2,1)S(1)} %collective-permute-done.10.top0), channel_id=1, source_target_pairs={{0,1},{1,0},{2,3},{3,2},{4,5},{5,4},{6,7},{7,6},{8,9},{9,8},{10,11... | collective-permute-start | bytes 589832 | tf_op jit(solution)/shard_map/ppermute | solution.py:837
  47.6 10.5 %collective-permute-start.14 = (bf16[128,768]{1,0:T(8,128)(2,1)S(1)}, bf16[128,768]{1,0:T(8,128)(2,1)S(1)}, u32[]{:S(2)}, u32[]{:S(2)}) collective-permute-start(bf16[128,768]{1,0:T(8,128)(2,1)S(1)} %collective-permute-done.11.top1), channel_id=1, source_target_pairs={{0,1},{1,0},{2,3},{3,2},{4,5},{5,4},{6,7},{7,6},{8,9},{9,8},{10,11... | collective-permute-start | bytes 589832 | tf_op jit(solution)/shard_map/ppermute | solution.py:837
  49.2 21.1 %collective-permute-start.17 = (bf16[192,2304]{1,0:T(8,128)(2,1)S(1)}, bf16[192,2304]{1,0:T(8,128)(2,1)S(1)}, u32[]{:S(2)}, u32[]{:S(2)}) collective-permute-start(bf16[192,2304]{1,0:T(8,128)(2,1)S(1)} %pad_maximum_fusion.oa.ua), channel_id=1, source_target_pairs={{0,16},{8,24},{16,0},{24,8},{1,17},{9,25},{17,1},{25,9},{2,18},{10... | collective-permute-start | bytes 2654216 | tf_op jit(solution)/shard_map/ppermute | solution.py:833
  50.9 19.6 %copy-start.49 = (bf16[768]{0:T(1024)(128)(2,1)S(1)}, bf16[768]{0:T(1024)(128)(2,1)}, u32[]{:S(2)}) copy-start(bf16[768]{0:T(1024)(128)(2,1)} %param.29) | copy-start | bytes 4612
  50.9 19.6 %copy-start.45 = (bf16[1536]{0:T(1024)(128)(2,1)S(1)}, bf16[1536]{0:T(1024)(128)(2,1)}, u32[]{:S(2)}) copy-start(bf16[1536]{0:T(1024)(128)(2,1)} %param.32) | copy-start | bytes 9220
  50.9 19.6 %copy-start.50 = (bf16[768]{0:T(1024)(128)(2,1)S(1)}, bf16[768]{0:T(1024)(128)(2,1)}, u32[]{:S(2)}) copy-start(bf16[768]{0:T(1024)(128)(2,1)} %param.30) | copy-start | bytes 4612
  50.9 19.6 %copy-start.51 = (bf16[768]{0:T(1024)(128)(2,1)S(1)}, bf16[768]{0:T(1024)(128)(2,1)}, u32[]{:S(2)}) copy-start(bf16[768]{0:T(1024)(128)(2,1)} %param.28) | copy-start | bytes 4612
  58.1 14.8 %copy-start.13 = (bf16[512,384]{1,0:T(8,128)(2,1)}, bf16[512,384]{1,0:T(8,128)(2,1)S(1)}, u32[]{:S(2)}) copy-start(bf16[512,384]{1,0:T(8,128)(2,1)S(1)} %get-tuple-element.167.own_ref.out_ref.refs_4_) | copy-start | bytes 1179652
  58.1 12.2 %collective-permute-start.16 = (bf16[192,2304]{1,0:T(8,128)(2,1)S(1)}, bf16[192,2304]{1,0:T(8,128)(2,1)S(1)}, u32[]{:S(2)}, u32[]{:S(2)}) collective-permute-start(bf16[192,2304]{1,0:T(8,128)(2,1)S(1)} %pad_maximum_fusion.oa.ua), channel_id=1, source_target_pairs={{0,8},{8,0},{16,24},{24,16},{1,9},{9,1},{17,25},{25,17},{2,10},{10... | collective-permute-start | bytes 2654216 | tf_op jit(solution)/shard_map/ppermute | solution.py:833
  58.2 12.1 %collective-permute-start.18 = (bf16[192,1536]{1,0:T(8,128)(2,1)}, bf16[192,1536]{1,0:T(8,128)(2,1)S(1)}, u32[]{:S(2)}, u32[]{:S(2)}) collective-permute-start(bf16[192,1536]{1,0:T(8,128)(2,1)} %bitcast.4.da), channel_id=1, source_target_pairs={{0,8},{8,0},{16,24},{24,16},{1,9},{9,1},{17,25},{25,17},{2,10},{10... | collective-permute-start | bytes 1769480 | tf_op jit(solution)/shard_map/ppermute | solution.py:833
  58.7 11.6 %collective-permute-start.19 = (bf16[192,1536]{1,0:T(8,128)(2,1)}, bf16[192,1536]{1,0:T(8,128)(2,1)S(1)}, u32[]{:S(2)}, u32[]{:S(2)}) collective-permute-start(bf16[192,1536]{1,0:T(8,128)(2,1)} %collective-permute-done.9.dc), channel_id=1, source_target_pairs={{0,8},{8,0},{16,24},{24,16},{1,9},{9,1},{17,25},{25,17},{2,10},{10... | collective-permute-start | bytes 1769480 | tf_op jit(solution)/shard_map/ppermute | solution.py:833
  58.8 11.5 %collective-permute-start.15 = (bf16[512,384]{1,0:T(8,128)(2,1)S(1)}, bf16[512,384]{1,0:T(8,128)(2,1)S(1)}, u32[]{:S(2)}, u32[]{:S(2)}) collective-permute-start(bf16[512,384]{1,0:T(8,128)(2,1)S(1)} %get-tuple-element.167.own_ref.out_ref.refs_4_), channel_id=1, source_target_pairs={{0,1},{1,0},{2,3},{3,2},{4,5},{5,4},{6,7},{7,6},{8,9},{9,8},{10,11... | collective-permute-start | bytes 1179656 | tf_op jit(solution)/shard_map/ppermute | solution.py:837
  70.4 2.5 collective-permute-start.20
  88.8 11.2 %collective-permute-start.21 = (bf16[256,768]{1,0:T(8,128)(2,1)S(1)}, bf16[256,768]{1,0:T(8,128)(2,1)S(1)}, u32[]{:S(2)}, u32[]{:S(2)}) collective-permute-start(bf16[256,768]{1,0:T(8,128)(2,1)S(1)} %get-tuple-element.184), channel_id=1, source_target_pairs={{0,1},{1,0},{2,3},{3,2},{4,5},{5,4},{6,7},{7,6},{8,9},{9,8},{10,11... | collective-permute-start | bytes 1179656 | tf_op jit(solution)/shard_map/ppermute | solution.py:837
  100.1 2.8 %collective-permute-start.22 = (bf16[384,1536]{1,0:T(8,128)(2,1)S(1)}, bf16[384,1536]{1,0:T(8,128)(2,1)S(1)}, u32[]{:S(2)}, u32[]{:S(2)}) collective-permute-start(bf16[384,1536]{1,0:T(8,128)(2,1)S(1)} %get-tuple-element.194), channel_id=1, source_target_pairs={{0,8},{8,0},{16,24},{24,16},{1,9},{9,1},{17,25},{25,17},{2,10},{10... | collective-permute-start | bytes 3538952 | tf_op jit(solution)/shard_map/ppermute | solution.py:833
  102.9 15.9 %collective-permute-start.25 = (bf16[384,1536]{1,0:T(8,128)(2,1)S(1)}, bf16[384,1536]{1,0:T(8,128)(2,1)S(1)}, u32[]{:S(2)}, u32[]{:S(2)}) collective-permute-start(bf16[384,1536]{1,0:T(8,128)(2,1)S(1)} %get-tuple-element.199), channel_id=1, source_target_pairs={{0,8},{8,0},{16,24},{24,16},{1,9},{9,1},{17,25},{25,17},{2,10},{10... | collective-permute-start | bytes 3538952 | tf_op jit(solution)/shard_map/ppermute | solution.py:833
  103.1 15.7 %collective-permute-start.24 = (bf16[192,1536]{1,0:T(8,128)(2,1)S(1)}, bf16[192,1536]{1,0:T(8,128)(2,1)S(1)}, u32[]{:S(2)}, u32[]{:S(2)}) collective-permute-start(bf16[192,1536]{1,0:T(8,128)(2,1)S(1)} %slice_add_fusion.1), channel_id=1, source_target_pairs={{0,16},{8,24},{16,0},{24,8},{1,17},{9,25},{17,1},{25,9},{2,18},{10... | collective-permute-start | bytes 1769480 | tf_op jit(solution)/shard_map/ppermute | solution.py:833
  104.7 11.1 %collective-permute-start.23 = (bf16[256,768]{1,0:T(8,128)(2,1)S(1)}, bf16[256,768]{1,0:T(8,128)(2,1)S(1)}, u32[]{:S(2)}, u32[]{:S(2)}) collective-permute-start(bf16[256,768]{1,0:T(8,128)(2,1)S(1)} %get-tuple-element.196.d_own_ref.refs_2_), channel_id=1, source_target_pairs={{0,1},{1,0},{2,3},{3,2},{4,5},{5,4},{6,7},{7,6},{8,9},{9,8},{10,11... | collective-permute-start | bytes 1179656 | tf_op jit(solution)/shard_map/ppermute | solution.py:837
  118.9 15.3 %collective-permute-start.27 = (bf16[192,1536]{1,0:T(8,128)(2,1)S(1)}, bf16[192,1536]{1,0:T(8,128)(2,1)S(1)}, u32[]{:S(2)}, u32[]{:S(2)}) collective-permute-start(bf16[192,1536]{1,0:T(8,128)(2,1)S(1)} %slice_add_fusion), channel_id=1, source_target_pairs={{0,16},{8,24},{16,0},{24,8},{1,17},{9,25},{17,1},{25,9},{2,18},{10... | collective-permute-start | bytes 1769480 | tf_op jit(solution)/shard_map/ppermute | solution.py:833
  120.6 13.6 %collective-permute-start.26 = (bf16[192,1536]{1,0:T(8,128)(2,1)S(1)}, bf16[192,1536]{1,0:T(8,128)(2,1)S(1)}, u32[]{:S(2)}, u32[]{:S(2)}) collective-permute-start(bf16[192,1536]{1,0:T(8,128)(2,1)S(1)} %add_add_fusion.2), channel_id=1, source_target_pairs={{0,2},{6,4},{1,3},{7,5},{8,10},{14,12},{9,11},{15,13},{16,18},{22,... | collective-permute-start | bytes 1769480 | tf_op jit(solution)/shard_map/ppermute | solution.py:875
  121.9 12.2 %collective-permute-start.28 = (bf16[256,768]{1,0:T(8,128)(2,1)S(1)}, bf16[256,768]{1,0:T(8,128)(2,1)S(1)}, u32[]{:S(2)}, u32[]{:S(2)}) collective-permute-start(bf16[256,768]{1,0:T(8,128)(2,1)S(1)} %copy-done.60), channel_id=1, source_target_pairs={{0,1},{1,0},{2,3},{3,2},{4,5},{5,4},{6,7},{7,6},{8,9},{9,8},{10,11... | collective-permute-start | bytes 1179656 | tf_op jit(solution)/shard_map/ppermute | solution.py:837
  134.2 3.8 %collective-permute-start.29 = (bf16[512,768]{1,0:T(8,128)(2,1)S(1)}, bf16[512,768]{1,0:T(8,128)(2,1)S(1)}, u32[]{:S(2)}, u32[]{:S(2)}) collective-permute-start(bf16[512,768]{1,0:T(8,128)(2,1)S(1)} %get-tuple-element.212), channel_id=1, source_target_pairs={{0,8},{8,0},{16,24},{24,16},{1,9},{9,1},{17,25},{25,17},{2,10},{10... | collective-permute-start | bytes 2359304 | tf_op jit(solution)/shard_map/ppermute | solution.py:833
  134.6 8.9 %collective-permute-start.30 = (bf16[128,768]{1,0:T(8,128)(2,1)S(1)}, bf16[128,768]{1,0:T(8,128)(2,1)S(1)}, u32[]{:S(2)}, u32[]{:S(2)}) collective-permute-start(bf16[128,768]{1,0:T(8,128)(2,1)S(1)} %get-tuple-element.266), channel_id=1, source_target_pairs={{0,0},{2,2},{4,8},{6,10},{8,4},{10,6},{12,12},{14,14},{16,16},{18,... | collective-permute-start | bytes 589832 | tf_op jit(solution)/shard_map/ppermute | solution.py:852
  135.2 8.2 %collective-permute-start.31 = (bf16[128,768]{1,0:T(8,128)(2,1)S(1)}, bf16[128,768]{1,0:T(8,128)(2,1)S(1)}, u32[]{:S(2)}, u32[]{:S(2)}) collective-permute-start(bf16[128,768]{1,0:T(8,128)(2,1)S(1)} %get-tuple-element.265), channel_id=1, source_target_pairs={{0,2},{2,0},{4,10},{6,8},{8,6},{10,4},{12,14},{14,12},{16,18},{18,... | collective-permute-start | bytes 589832 | tf_op jit(solution)/shard_map/ppermute | solution.py:852
  138.0 21.9 %copy-start.32 = (bf16[192,1536]{1,0:T(8,128)(2,1)}, bf16[192,1536]{1,0:T(8,128)(2,1)S(1)}, u32[]{:S(2)}) copy-start(bf16[192,1536]{1,0:T(8,128)(2,1)S(1)} %add_add_fusion.1) | copy-start | bytes 1769476
  139.4 17.6 %copy-start.21 = (bf16[512,768]{1,0:T(8,128)(2,1)S(1)}, bf16[512,768]{1,0:T(8,128)(2,1)}, u32[]{:S(2)}) copy-start(bf16[512,768]{1,0:T(8,128)(2,1)} %copy-done.20) | copy-start | bytes 2359300
  142.7 17.1 %copy-start.5 = (bf16[256,768]{1,0:T(8,128)(2,1)}, bf16[256,768]{1,0:T(8,128)(2,1)S(1)}, u32[]{:S(2)}) copy-start(bf16[256,768]{1,0:T(8,128)(2,1)S(1)} %get-tuple-element.216.own_ref) | copy-start | bytes 1179652
  143.5 22.9 %collective-permute-start.33 = (bf16[192,1536]{1,0:T(8,128)(2,1)S(1)}, bf16[192,1536]{1,0:T(8,128)(2,1)}, u32[]{:S(2)}, u32[]{:S(2)}) collective-permute-start(bf16[192,1536]{1,0:T(8,128)(2,1)S(1)} %add.102), channel_id=1, source_target_pairs={{2,4},{4,2},{3,5},{5,3},{10,12},{12,10},{11,13},{13,11},{18,20},{2... | collective-permute-start | bytes 1769480 | tf_op jit(solution)/shard_map/ppermute | solution.py:879
  144.9 22.5 %collective-permute-start.34 = (bf16[192,1536]{1,0:T(8,128)(2,1)S(1)}, bf16[192,1536]{1,0:T(8,128)(2,1)S(1)}, u32[]{:S(2)}, u32[]{:S(2)}) collective-permute-start(bf16[192,1536]{1,0:T(8,128)(2,1)S(1)} %add_add_fusion.1), channel_id=1, source_target_pairs={{0,2},{6,4},{1,3},{7,5},{8,10},{14,12},{9,11},{15,13},{16,18},{22,... | collective-permute-start | bytes 1769480 | tf_op jit(solution)/shard_map/ppermute | solution.py:875
  155.5 10.1 %collective-permute-start.32 = (bf16[256,768]{1,0:T(8,128)(2,1)S(1)}, bf16[256,768]{1,0:T(8,128)(2,1)S(1)}, u32[]{:S(2)}, u32[]{:S(2)}) collective-permute-start(bf16[256,768]{1,0:T(8,128)(2,1)S(1)} %get-tuple-element.226), channel_id=1, source_target_pairs={{0,1},{1,0},{2,3},{3,2},{4,5},{5,4},{6,7},{7,6},{8,9},{9,8},{10,11... | collective-permute-start | bytes 1179656 | tf_op jit(solution)/shard_map/ppermute | solution.py:837
  168.3 4.8 %collective-permute-start.35 = (bf16[384,1536]{1,0:T(8,128)(2,1)}, bf16[384,1536]{1,0:T(8,128)(2,1)S(1)}, u32[]{:S(2)}, u32[]{:S(2)}) collective-permute-start(bf16[384,1536]{1,0:T(8,128)(2,1)} %get-tuple-element.233), channel_id=1, source_target_pairs={{0,8},{8,0},{16,24},{24,16},{1,9},{9,1},{17,25},{25,17},{2,10},{10... | collective-permute-start | bytes 3538952 | tf_op jit(solution)/shard_map/ppermute | solution.py:833
  168.3 4.8 %collective-permute-start.36 = (f32[5,768]{1,0:T(8,128)}, f32[5,768]{1,0:T(8,128)}, u32[]{:S(2)}, u32[]{:S(2)}) collective-permute-start(f32[5,768]{1,0:T(8,128)} %pad_maximum_fusion.1), channel_id=1, source_target_pairs={{0,1},{1,0},{2,3},{3,2},{4,5},{5,4},{6,7},{7,6},{8,9},{9,8},{10,11... | collective-permute-start | bytes 46088 | tf_op jit(solution)/shard_map/ppermute | solution.py:837
  175.2 1.3 collective-permute-start.37
  177.7 16.6 %collective-permute-start.38 = (bf16[208,1536]{1,0:T(8,128)(2,1)S(1)}, bf16[208,1536]{1,0:T(8,128)(2,1)S(1)}, u32[]{:S(2)}, u32[]{:S(2)}) collective-permute-start(bf16[208,1536]{1,0:T(8,128)(2,1)S(1)} %get-tuple-element.240), channel_id=1, source_target_pairs={{0,16},{8,24},{16,0},{24,8},{1,17},{9,25},{17,1},{25,9},{2,18},{10... | collective-permute-start | bytes 1916936 | tf_op jit(solution)/shard_map/ppermute | solution.py:833
  178.5 10.1 %collective-permute-start.41 = (bf16[128,768]{1,0:T(8,128)(2,1)}, bf16[128,768]{1,0:T(8,128)(2,1)}, u32[]{:S(2)}, u32[]{:S(2)}) collective-permute-start(bf16[128,768]{1,0:T(8,128)(2,1)} %copy-done.36), channel_id=1, source_target_pairs={{0,1},{1,0},{2,3},{3,2},{4,5},{5,4},{6,7},{7,6},{8,9},{9,8},{10,11... | collective-permute-start | bytes 589832 | tf_op jit(solution)/shard_map/ppermute | solution.py:837
  179.0 10.8 %collective-permute-start.42 = (bf16[128,768]{1,0:T(8,128)(2,1)}, bf16[128,768]{1,0:T(8,128)(2,1)}, u32[]{:S(2)}, u32[]{:S(2)}) collective-permute-start(bf16[128,768]{1,0:T(8,128)(2,1)} %copy-done.38), channel_id=1, source_target_pairs={{0,1},{1,0},{2,3},{3,2},{4,5},{5,4},{6,7},{7,6},{8,9},{9,8},{10,11... | collective-permute-start | bytes 589832 | tf_op jit(solution)/shard_map/ppermute | solution.py:837
  180.5 9.3 %collective-permute-start.39 = (bf16[128,768]{1,0:T(8,128)(2,1)}, bf16[128,768]{1,0:T(8,128)(2,1)}, u32[]{:S(2)}, u32[]{:S(2)}) collective-permute-start(bf16[128,768]{1,0:T(8,128)(2,1)} %copy-done.19), channel_id=1, source_target_pairs={{0,0},{2,2},{4,8},{6,10},{8,4},{10,6},{12,12},{14,14},{16,16},{18,... | collective-permute-start | bytes 589832 | tf_op jit(solution)/shard_map/ppermute | solution.py:852
  183.5 7.8 %collective-permute-start.40 = (bf16[128,768]{1,0:T(8,128)(2,1)S(1)}, bf16[128,768]{1,0:T(8,128)(2,1)}, u32[]{:S(2)}, u32[]{:S(2)}) collective-permute-start(bf16[128,768]{1,0:T(8,128)(2,1)S(1)} %get-tuple-element.244), channel_id=1, source_target_pairs={{0,2},{2,0},{4,10},{6,8},{8,6},{10,4},{12,14},{14,12},{16,18},{18,... | collective-permute-start | bytes 589832 | tf_op jit(solution)/shard_map/ppermute | solution.py:852
  194.6 17.2 %collective-permute-start.44 = (bf16[208,1536]{1,0:T(8,128)(2,1)S(1)}, bf16[208,1536]{1,0:T(8,128)(2,1)S(1)}, u32[]{:S(2)}, u32[]{:S(2)}) collective-permute-start(bf16[208,1536]{1,0:T(8,128)(2,1)S(1)} %maximum_select_fusion.2), channel_id=1, source_target_pairs={{0,2},{2,0},{4,6},{6,4},{1,3},{3,1},{5,7},{7,5},{8,10},{10,8},{12,... | collective-permute-start | bytes 1916936 | tf_op jit(solution)/shard_map/ppermute | solution.py:871
  197.2 11.9 %collective-permute-start.43 = (bf16[192,1536]{1,0:T(8,128)(2,1)S(1)}, bf16[192,1536]{1,0:T(8,128)(2,1)S(1)}, u32[]{:S(2)}, u32[]{:S(2)}) collective-permute-start(bf16[192,1536]{1,0:T(8,128)(2,1)S(1)} %add.113), channel_id=1, source_target_pairs={{2,4},{4,2},{3,5},{5,3},{10,12},{12,10},{11,13},{13,11},{18,20},{2... | collective-permute-start | bytes 1769480 | tf_op jit(solution)/shard_map/ppermute | solution.py:879
  197.9 8.1 %collective-permute-start.45 = (bf16[128,768]{1,0:T(8,128)(2,1)}, bf16[128,768]{1,0:T(8,128)(2,1)S(1)}, u32[]{:S(2)}, u32[]{:S(2)}) collective-permute-start(bf16[128,768]{1,0:T(8,128)(2,1)} %collective-permute-done.39), channel_id=1, source_target_pairs={{0,1},{1,0},{2,3},{3,2},{4,5},{5,4},{6,7},{7,6},{8,9},{9,8},{10,11... | collective-permute-start | bytes 589832 | tf_op jit(solution)/shard_map/ppermute | solution.py:837
  198.5 10.5 %collective-permute-start.46 = (bf16[128,768]{1,0:T(8,128)(2,1)}, bf16[128,768]{1,0:T(8,128)(2,1)S(1)}, u32[]{:S(2)}, u32[]{:S(2)}) collective-permute-start(bf16[128,768]{1,0:T(8,128)(2,1)} %collective-permute-done.40), channel_id=1, source_target_pairs={{0,1},{1,0},{2,3},{3,2},{4,5},{5,4},{6,7},{7,6},{8,9},{9,8},{10,11... | collective-permute-start | bytes 589832 | tf_op jit(solution)/shard_map/ppermute | solution.py:837
  211.9 16.7 %collective-permute-start.48 = (bf16[192,1536]{1,0:T(8,128)(2,1)S(1)}, bf16[192,1536]{1,0:T(8,128)(2,1)S(1)}, u32[]{:S(2)}, u32[]{:S(2)}) collective-permute-start(bf16[192,1536]{1,0:T(8,128)(2,1)S(1)} %add.114), channel_id=1, source_target_pairs={{2,0},{4,6},{3,1},{5,7},{10,8},{12,14},{11,9},{13,15},{18,16},{20,... | collective-permute-start | bytes 1769480 | tf_op jit(solution)/shard_map/ppermute | solution.py:883
  213.3 15.3 %collective-permute-start.47 = (bf16[208,1536]{1,0:T(8,128)(2,1)S(1)}, bf16[208,1536]{1,0:T(8,128)(2,1)S(1)}, u32[]{:S(2)}, u32[]{:S(2)}) collective-permute-start(bf16[208,1536]{1,0:T(8,128)(2,1)S(1)} %shard_map.317.left_ref), channel_id=1, source_target_pairs={{2,4},{4,2},{3,5},{5,3},{10,12},{12,10},{11,13},{13,11},{18,20},{2... | collective-permute-start | bytes 1916936 | tf_op jit(solution)/shard_map/ppermute | solution.py:879
  228.8 19.0 %collective-permute-start.49 = (bf16[208,1536]{1,0:T(8,128)(2,1)S(1)}, bf16[208,1536]{1,0:T(8,128)(2,1)S(1)}, u32[]{:S(2)}, u32[]{:S(2)}) collective-permute-start(bf16[208,1536]{1,0:T(8,128)(2,1)S(1)} %shard_map.318), channel_id=1, source_target_pairs={{2,0},{4,6},{3,1},{5,7},{10,8},{12,14},{11,9},{13,15},{18,16},{20,... | collective-permute-start | bytes 1916936 | tf_op jit(solution)/shard_map/ppermute | solution.py:883
  (48 other events, 168.7 us)

commit v3 on v2

--- a/solution.py
+++ b/solution.py
@@ -535,117 +535,141 @@
 CUBE = 0.044715
 
 
+def fetch(parts, columns, out_ref, sems):
+    rows = parts[0].shape[0]
+    mine = lax.axis_index("dp")
+    copies = []
+    for step, part in enumerate(parts):
+        start = pl.multiple_of((mine ^ step) * rows, rows)
+        copy = pltpu.make_async_copy(
+            part.at[:, columns], out_ref.at[pl.ds(start, rows)], sems.at[step]
+        )
+        copy.start()
+        copies.append(copy)
+    return copies
+
+
 def middle_kernel(
     info, rows_ref, own_ref, peer_ref, top0, top1, top2, top3, gain_ref, bias_ref, out_bias_ref,
-    oa, ob, oc, od, ua, ub, uc, ud, da, db, dc, dd, up_bias_ref,
+    up_bias_ref, down_bias_ref, pa, pb, pc, pd, da, db, dc, dd,
     mid_ref, normed_ref, feed_ref, hidden_ref, d_pre_ref, d_own_ref, d_peer_ref,
-    f_own_ref, f_peer_ref, out_ref, g_up_ref, g_down_ref,
-    outs, ups, downs, acc_d, acc_f,
+    part0_ref, part1_ref, out_ref, g_up_ref, g_down_ref,
+    outs, ups, downs, whole_mid, sems,
 ):
-    step = pl.program_id(0)
     rows, width = rows_ref.shape
     half = rows // 2
     local = own_ref.shape[1]
-
-    @pl.when(step == 0)
-    def _():
-        settle((oa, ob, oc, od), outs)
-        out_ref[...] = outs[:, :local]
-        peer = jnp.concatenate([peer_ref[half:, :], peer_ref[:half, :]], axis=0)
-        attention = (
-            dense_nt(own_ref[...], outs[:, :local])
-            + dense_nt(peer, outs[:, local:])
-            + out_bias_ref[...].astype(jnp.float32)
+    hidden_width = up_bias_ref.shape[1]
+    steps = ups.shape[0]
+    tile = hidden_width // steps
+    packs, lasts = (pa, pb, pc, pd), (da, db, dc, dd)
+    waits = [fetch(packs, pl.ds(hidden_width, width), outs, sems.at[0])]
+    for s in range(steps):
+        columns = pl.ds(s * tile, tile)
+        waits.append(fetch(packs, columns, ups.at[s], sems.at[1 + 2 * s]))
+        waits.append(fetch(lasts, columns, downs.at[s], sems.at[2 + 2 * s]))
+
+    real = held(info, 4, rows // 4, width)
+    top = jnp.concatenate([top0[...], top1[...], top2[...], top3[...]], axis=0)
+    feed = jnp.where(real, top.astype(jnp.float32), 0.0)
+    feed_ref[...] = feed.astype(jnp.bfloat16)
+    g_down_ref[...] = jnp.sum(feed, axis=0, keepdims=True)
+    peer = jnp.concatenate([peer_ref[half:, :], peer_ref[:half, :]], axis=0)
+    for copy in waits[0]:
+        copy.wait()
+    out_ref[...] = outs[:, :local]
+    attention = (
+        dense_nt(own_ref[...], outs[:, :local])
+        + dense_nt(peer, outs[:, local:])
+        + out_bias_ref[...].astype(jnp.float32)
+    )
+    mid = rows_ref[...].astype(jnp.float32) + jnp.where(real, attention, 0.0)
+    mid_ref[...] = mid[:half]
+    whole_mid[...] = mid
+    normed, _ = row_stats(mid)
+    normed = normed * gain_ref[...].astype(jnp.float32) + bias_ref[...].astype(jnp.float32)
+    normed_ref[...] = normed.astype(jnp.bfloat16)
+
+    for s in range(steps):
+        columns = slice(s * tile, (s + 1) * tile)
+        for copy in waits[1 + 2 * s] + waits[2 + 2 * s]:
+            copy.wait()
+        pre = dense(normed_ref[...], ups[s]) + up_bias_ref[:, columns].astype(jnp.float32)
+        d_hidden = dense(feed_ref[...], downs[s])
+        square = pre * pre
+        bend = jnp.tanh(pre * (ROOT_TWO_OVER_PI + CUBE * ROOT_TWO_OVER_PI * square))
+        half_up = 0.5 + 0.5 * bend
+        active = pre * half_up
+        slope = half_up + active * (1.0 - bend) * (
+            ROOT_TWO_OVER_PI + 3.0 * CUBE * ROOT_TWO_OVER_PI * square
         )
-        real = held(info, 4, rows // 4, width)
-        mid = rows_ref[...].astype(jnp.float32) + jnp.where(real, attention, 0.0)
-        mid_ref[...] = mid
-        normed, _ = row_stats(mid)
-        normed = normed * gain_ref[...].astype(jnp.float32) + bias_ref[...].astype(jnp.float32)
-        normed_ref[...] = normed.astype(jnp.bfloat16)
-        top = jnp.concatenate([top0[...], top1[...], top2[...], top3[...]], axis=0)
-        feed = jnp.where(real, top.astype(jnp.float32), 0.0)
-        feed_ref[...] = feed.astype(jnp.bfloat16)
-        g_down_ref[...] = jnp.sum(feed, axis=0, keepdims=True)
-        acc_d[...] = jnp.zeros_like(acc_d)
-        acc_f[...] = jnp.zeros_like(acc_f)
-
-    settle((ua, ub, uc, ud), ups)
-    settle((da, db, dc, dd), downs)
-    pre = dense(normed_ref[...], ups[...]) + up_bias_ref[...].astype(jnp.float32)
-    d_hidden = dense(feed_ref[...], downs[...])
-    square = pre * pre
-    bend = jnp.tanh(ROOT_TWO_OVER_PI * pre * (1.0 + CUBE * square))
-    half_up = 0.5 + 0.5 * bend
-    hidden = (pre * half_up).astype(jnp.bfloat16)
-    slope = half_up + (pre * half_up) * (1.0 - bend) * (
-        ROOT_TWO_OVER_PI + 3.0 * CUBE * ROOT_TWO_OVER_PI * square
-    )
-    d_pre = (d_hidden * slope).astype(jnp.bfloat16)
-    hidden_ref[...] = hidden
-    d_pre_ref[...] = d_pre
-    g_up_ref[...] = jnp.sum(d_pre.astype(jnp.float32), axis=0, keepdims=True)
-    acc_d[...] += dense_nt(d_pre, ups[...])
-    acc_f[...] += dense_nt(hidden, downs[...])
-
-    @pl.when(step == pl.num_programs(0) - 1)
-    def _():
-        low = acc_d[...].astype(jnp.bfloat16)
-        d_own_ref[...] = low[:half]
-        d_peer_ref[...] = low[half:]
-        low = acc_f[...].astype(jnp.bfloat16)
-        f_own_ref[...] = low[:half]
-        f_peer_ref[...] = low[half:]
-
-
-def middle_part(info, rows_low, own, peer, top, gain, bias, out_bias, packs, downs, up_bias):
+        hidden_ref[:, columns] = active.astype(jnp.bfloat16)
+        d_pre = (d_hidden * slope).astype(jnp.bfloat16)
+        d_pre_ref[:, columns] = d_pre
+        g_up_ref[:, columns] = jnp.sum(d_pre.astype(jnp.float32), axis=0, keepdims=True)
+
+    def back(left_ref, right_ref):
+        total = 0.0
+        for s in range(steps):
+            total += dense_nt(left_ref[:, s * tile : (s + 1) * tile], right_ref[s])
+        return total
+
+    grad = back(d_pre_ref, ups).astype(jnp.bfloat16)
+    d_own_ref[...] = grad[:half]
+    d_peer_ref[...] = grad[half:]
+    first = lax.axis_index("tensor") == 0
+    share = back(hidden_ref, downs)
+    share += jnp.where(first, down_bias_ref[...].astype(jnp.float32), 0.0)
+    share = jnp.where(real, share, 0.0) + jnp.where(first, whole_mid[...], 0.0)
+    share = share.astype(jnp.bfloat16)
+    for k, part in enumerate((part0_ref, part1_ref)):
+        start = k * (half // 2)
+        part[0] = share[start : start + half // 2]
+        part[1] = share[half + start : half + start + half // 2]
+
+
+def middle_part(
+    info, rows_low, own, peer, top, gain, bias, out_bias, packs, downs, up_bias, down_bias
+):
     rows, width = rows_low.shape
     local = own.shape[1]
-    shard = downs[0].shape[0]
     hidden = up_bias.shape[1]
-    tile = 384
-    fixed = lambda array: pl.BlockSpec(array.shape, lambda i, info: (0,) * len(array.shape))
-    columns = lambda height: pl.BlockSpec((height, tile), lambda i, info: (0, i))
-    outs = pl.BlockSpec((shard, width), lambda i, info: (0, hidden // width))
-    whole = (rows_low, own, peer, *top, gain, bias, out_bias)
+    steps = 2
+    small = (rows_low, own, peer, *top, gain, bias, out_bias, up_bias, down_bias)
+    inside = pl.BlockSpec(memory_space=pltpu.VMEM)
     shapes = (
-        full(rows, width),
+        full(rows // 2, width),
         low(rows, width),
         low(rows, width),
         low(rows, hidden),
         low(rows, hidden),
         low(rows // 2, width),
         low(rows // 2, width),
-        low(rows // 2, width),
-        low(rows // 2, width),
+        low(2, rows // 4, width),
+        low(2, rows // 4, width),
         low(width, local),
         full(1, hidden),
         full(1, width),
     )
-    tiled = (3, 4, 10)
     return pl.pallas_call(
         middle_kernel,
         out_shape=shapes,
-        grid_spec=pltpu.PrefetchScalarGridSpec(
-            num_scalar_prefetch=1,
-            grid=(hidden // tile,),
-            in_specs=[fixed(a) for a in whole] + [outs] * 4 + [columns(shard)] * 8 + [columns(1)],
-            out_specs=tuple(
-                columns(s.shape[0]) if k in tiled else fixed(s) for k, s in enumerate(shapes)
-            ),
-            scratch_shapes=[
-                pltpu.VMEM((width, 2 * local), jnp.bfloat16),
-                pltpu.VMEM((width, tile), jnp.bfloat16),
-                pltpu.VMEM((width, tile), jnp.bfloat16),
-                pltpu.VMEM((rows, width), jnp.float32),
-                pltpu.VMEM((rows, width), jnp.float32),
-            ],
-        ),
-        compiler_params=pltpu.CompilerParams(vmem_limit_bytes=52 << 20),
+        in_specs=[pl.BlockSpec(memory_space=pltpu.SMEM)]
+        + [inside] * len(small)
+        + [pl.BlockSpec(memory_space=pltpu.HBM)] * 8,
+        out_specs=(inside,) * len(shapes),
+        scratch_shapes=[
+            pltpu.VMEM((width, width), jnp.bfloat16),
+            pltpu.VMEM((steps, width, hidden // steps), jnp.bfloat16),
+            pltpu.VMEM((steps, width, hidden // steps), jnp.bfloat16),
+            pltpu.VMEM((rows, width), jnp.float32),
+            pltpu.SemaphoreType.DMA((1 + 2 * steps, 4)),
+        ],
+        compiler_params=pltpu.CompilerParams(vmem_limit_bytes=36 << 20),
         cost_estimate=pl.CostEstimate(
             flops=8 * rows * width * hidden, bytes_accessed=20 << 20, transcendentals=rows * hidden
         ),
-    )(info, *whole, *packs, *packs, *downs, up_bias)
+    )(info, *small, *packs, *downs)
 
 
 def turn_kernel(
@@ -690,7 +714,7 @@
 
 
 def leave_kernel(
-    rows_ref, proj_ref, d_query_ref, d_pair_ref, got_ref,
+    rows_ref, proj_ref, d_query_ref, d_pair_ref, got_ref, sums_two_ref,
     d_proj_ref, own_ref, peer_ref, sums_ref, bias_ref,
 ):
     pair = 2 * HEAD_DIM
@@ -713,19 +737,20 @@
     normed, _ = row_stats(rows_ref[...].astype(jnp.float32))
     sums_ref[0:1, :] = jnp.sum(grad * normed, axis=0, keepdims=True)
     sums_ref[1:2, :] = jnp.sum(grad, axis=0, keepdims=True)
-
-
-def leave(rows_low, proj, d_query, d_pair, got):
+    sums_ref[2:5, :] = sums_two_ref[...]
+
+
+def leave(rows_low, proj, d_query, d_pair, got, sums_two):
     rows, width = rows_low.shape
     columns = proj.shape[1]
     shapes = (
         low(rows, columns),
         low(rows // 2, width),
         low(rows // 2, width),
-        full(2, width),
+        full(5, width),
         full(1, columns),
     )
-    args = (rows_low, proj, d_query, d_pair, got)
+    args = (rows_low, proj, d_query, d_pair, got, sums_two)
     return call_once(leave_kernel, args, shapes, 2 * rows * width * columns)
 
 
@@ -818,14 +843,81 @@
     return call_once(merge_kernel, args, (packet, packet), own.size)
 
 
-def add_kernel(left_ref, right_ref, out_ref, *, rows):
-    out_ref[:rows, :] = left_ref[:rows, :] + right_ref[:rows, :]
-    out_ref[rows:, :] = add_terms(left_ref[rows:, :], right_ref[rows:, :])
-
-
-def add_packets(left, right, rows):
-    kernel = functools.partial(add_kernel, rows=rows)
-    return call_once(kernel, (left, right), (low(*left.shape),), left.size)[0]
+def spread_kernel(left_ref, right_ref, *outs, rows):
+    plane = lax.axis_index("context")
+    terms = add_terms(left_ref[rows:, :], right_ref[rows:, :])
+    piece = rows // 4
+    for step, out in enumerate(outs):
+        start = pl.multiple_of((plane + step) % 4 * piece, piece)
+        out[:piece, :] = left_ref[pl.ds(start, piece), :] + right_ref[pl.ds(start, piece), :]
+        out[piece:, :] = terms
+
+
+def spread(left, right, rows):
+    piece = low(rows // 4 + left.shape[0] - rows, left.shape[1])
+    kernel = functools.partial(spread_kernel, rows=rows)
+    return call_once(kernel, (left, right), (piece,) * 4, left.size)
+
+
+def total_kernel(*refs, piece):
+    parts, (sum_ref, vectors_ref, held_ref) = refs[:4], refs[4:]
+    plane = lax.axis_index("context")
+    f32 = lambda value: value.astype(jnp.float32)
+    total = f32(parts[0][:piece, :]) + f32(parts[1][:piece, :])
+    total += f32(parts[2][:piece, :]) + f32(parts[3][:piece, :])
+    sum_ref[...] = total.astype(jnp.bfloat16)
+    count = vectors_ref.shape[0]
+    for step, part in enumerate(parts):
+        held_ref[(plane + 4 - step) % 4] = f32(part[piece : piece + count, :]) + f32(
+            part[piece + count :, :]
+        )
+    vectors_ref[...] = held_ref[0] + held_ref[1] + held_ref[2] + held_ref[3]
+
+
+def total(parts, piece, count):
+    columns = parts[0].shape[1]
+    shapes = (low(piece, columns), full(count, columns))
+    held_terms = pltpu.VMEM((4, count, columns), jnp.float32)
+    kernel = functools.partial(total_kernel, piece=piece)
+    return call_once(kernel, parts, shapes, 4 * piece * columns, [held_terms])
+
+
+def assemble_kernel(a, b, c, d, query_ref, key_ref, value_ref, out_ref, turned):
+    plane = lax.axis_index("context")
+    piece = a.shape[0]
+    local = query_ref.shape[1]
+    for step, part in enumerate((a, b, c, d)):
+        start = pl.multiple_of((plane + 4 - step) % 4 * piece, piece)
+        here = part[...].astype(jnp.float32)
+        for k, ref in enumerate((query_ref, key_ref, value_ref, turned)):
+            ref[pl.ds(start, piece), :] = here[:, k * local : (k + 1) * local]
+    out_ref[...] = turned[...].T
+
+
+def assemble(parts):
+    piece, columns = parts[0].shape
+    rows, local = 4 * piece, columns // 4
+    shapes = (full(rows, local),) * 3 + (full(local, rows),)
+    turned = pltpu.VMEM((rows, local), jnp.float32)
+    return call_once(assemble_kernel, parts, shapes, 4 * piece * columns, [turned])
+
+
+def vectors_kernel(up_ref, down_ref, proj_ref, mine_ref, theirs_ref, out_ref):
+    width = down_ref.shape[1]
+    sides = mine_ref[...] + theirs_ref[...]
+    out_ref[...] = jnp.zeros_like(out_ref)
+    out_ref[0:1, :] = up_ref[...]
+    for k in range(2):
+        out_ref[1 + k : 2 + k, :width] = sides[2 * k : 2 * k + 1]
+        out_ref[1 + k : 2 + k, width:] = sides[2 * k + 1 : 2 * k + 2]
+    out_ref[3:4, :width] = sides[4:5]
+    out_ref[3:4, width:] = down_ref[...]
+    out_ref[4:5, : proj_ref.shape[1]] = proj_ref[...]
+
+
+def gather_vectors(up, down, proj, mine, theirs):
+    args = (up, down, proj, mine, theirs)
+    return call_once(vectors_kernel, args, (full(8, up.shape[1]),), up.size)[0]
 
 
 def exchange(value, bit):
@@ -863,12 +955,19 @@
     return jnp.where(upper, jnp.stack([peer, own], axis=1), jnp.stack([own, peer], axis=1))
 
 
+def join_shares(mine, theirs, odd, upper):
+    total = lambda a, b: a.astype(jnp.float32) + b[::-1].astype(jnp.float32)
+    values = [total(a, b).astype(jnp.bfloat16) for a, b in zip(mine, theirs)]
+    arranged = jnp.where(odd, jnp.stack(values[::-1]), jnp.stack(values))
+    return jnp.where(upper, arranged[:, ::-1], arranged)
+
+
 def gathered(shard, far_shard):
     return (shard, exchange(shard, 1), far_shard, exchange(far_shard, 1))
 
 
-def edges(value):
-    return lax.ppermute(value, "context", [(0, 1), (1, 0), (2, 3), (3, 2)])
+def turn_planes(value, step):
+    return lax.ppermute(value, "context", [(i, (i + step) % 4) for i in range(4)])
 
 
 def inward(value):
@@ -926,21 +1025,21 @@
     out_own = w_out.T
     out_peer = swap_tensor(out_own)
     lengths_other = exchange(lengths, 1)
-    *rows_parts, proj_far, proj_near, out_peer, lengths_other, w_down, cotangent = together(
-        *rows_parts, proj_far, proj_near, out_peer, lengths_other, w_down, cotangent
+    down_own = w_down.T
+    *rows_parts, proj_far, proj_near, out_peer, lengths_other, down_own, cotangent = together(
+        *rows_parts, proj_far, proj_near, out_peer, lengths_other, down_own, cotangent
     )
 
     rows_parts += [swap_tensor(v) for v in rows_parts]
     proj_last = exchange(proj_far, 1)
-    down_own = w_down.T
     down_far = exchange(down_own, 2)
+    pack_own = jnp.concatenate([w_up, out_own, out_peer], axis=1)
     top_picked = pick_in(cotangent.reshape(by_half), odd, upper)
     top_parts = [route(top_picked[step], step, True) for step in range(2)]
-    *rows_parts, proj_last, down_far, w_up, top_0, top_1 = together(
-        *rows_parts, proj_last, down_far, w_up, *top_parts
-    )
-
-    pack_own = jnp.concatenate([w_up, out_own, out_peer], axis=1)
+    *rows_parts, proj_last, down_far, pack_own, top_0, top_1 = together(
+        *rows_parts, proj_last, down_far, pack_own, *top_parts
+    )
+
     pack_far = exchange(pack_own, 2)
     top_parts = [top_0, top_1, swap_tensor(top_0), swap_tensor(top_1)]
     proj_blocks = (proj_own, proj_near, proj_far, proj_last)
@@ -977,8 +1076,7 @@
         d_pre,
         d_own,
         d_peer,
-        feed_own,
-        feed_peer,
+        *shares,
         out_t,
         grad_up_bias,
         grad_down_bias,
@@ -994,16 +1092,20 @@
         pack_blocks,
         down_blocks,
         row(b_up),
+        row(b_down),
     )
 
     got = swap_tensor(d_peer)
+    share_0 = route(shares[0], 0, False)
     down_own, down_far, down_send = weight_grad((d_feed, hidden))
     up_own, up_far, up_send = weight_grad((normed_two, d_pre))
-    got, down_send, up_send, feed_peer = together(got, down_send, up_send, feed_peer)
+    got, down_send, up_send, share_0, share_1 = together(
+        got, down_send, up_send, share_0, shares[1]
+    )
 
     down_got = exchange(down_send, 1)
     d_middle, d_att, sums_two = turn(info, middle, d_own, got, top_parts[:2], row(ln2_gain))
-    d_att, down_got, up_send = together(d_att, down_got, up_send)
+    d_att, down_got, up_send, share_1 = together(d_att, down_got, up_send, share_1)
 
     shard = down_own.shape[0]
     columns = hidden.shape[1]
@@ -1011,102 +1113,86 @@
     got_1 = exchange(down_far + down_got[shard:], 2)
     down_own = down_own + down_got[:shard]
     up_got = exchange(up_send, 1)
-    d_att_peer, got_1, up_got, feed_peer = together(d_att_peer, got_1, up_got, feed_peer)
+    share_1 = route(share_1, 1, False)
+    d_att_peer, got_1, up_got, share_1 = together(d_att_peer, got_1, up_got, share_1)
 
     sum_1 = down_own + got_1
     got_1 = inward(sum_1)
     got_2 = exchange(up_far + up_got[shard:], 2)
     up_own = up_own + up_got[:shard]
-    feed_got = swap_tensor(feed_peer)
+    share_got = [swap_tensor(v) for v in (share_0, share_1)]
     d_queries, d_pair, d_send = attend_back(
         info, queries, pair_own, pair_other, mixed, d_att, d_att_peer, out_t, logs
     )
-    d_send, got_1, got_2, feed_got = together(d_send, got_1, got_2, feed_got)
-
-    first_row = info[:2, None, None] + lax.broadcasted_iota(jnp.int32, (2, half, 1), 1)
-    feed = feed_own.astype(jnp.float32) + feed_got.astype(jnp.float32) + b_down.astype(jnp.float32)
-    keep = (first_row < length).astype(jnp.float32)
-    output_rows = middle[:block].reshape(2, half, width) + keep * feed.reshape(2, half, width)
-    output_rows = output_rows.astype(jnp.bfloat16)
-    out_near = [route(output_rows[step], step, False) for step in range(2)]
+    d_send, got_1, got_2, *share_got = together(d_send, got_1, got_2, *share_got)
+
+    d_got = exchange(d_send, 1)
     sum_1 = sum_1 + got_1
     sum_2 = up_own + got_2
-    d_proj, one_own, one_peer, sums_one, proj_bias = leave(
-        rows_low, proj, d_queries, d_pair, exchange(d_send, 1)
-    )
-    sides = jnp.concatenate([sums_one, sums_two], axis=0)
-    one_peer, sides, sum_1, sum_2, *out_near = together(one_peer, sides, sum_1, sum_2, *out_near)
-
-    one_got = swap_tensor(one_peer)
     got_1 = across(sum_1)
     got_2 = inward(sum_2)
+    d_proj, one_own, one_peer, sides, proj_bias = leave(
+        rows_low, proj, d_queries, d_pair, d_got, sums_two
+    )
     own, far, send = weight_grad((normed_low, d_proj), (d_att, d_att_peer, mixed))
-    send, one_got, got_1, got_2 = together(send, one_got, got_1, got_2)
-
-    input_rows = finish(rows_low, one_own, one_got, row(ln1_gain), d_middle)
+    one_peer, sides, send, got_1, got_2 = together(one_peer, sides, send, got_1, got_2)
+
     send_got = exchange(send, 1)
     sides_got = swap_tensor(sides)
-    *input_rows, send_got, sides_got = together(*input_rows, send_got, sides_got)
-
-    flat = jnp.concatenate(
-        [proj_bias[0], (sides + sides_got).reshape(-1), grad_up_bias[0], grad_down_bias[0]]
-    )
-    vectors = jnp.pad(flat, (0, 8 * columns - flat.shape[0])).reshape(8, columns)
-    packet, packet_far = merge(own, far, send_got, vectors, exchange(vectors, 1))
+    one_got = swap_tensor(one_peer)
+    sum_1 = sum_1 + got_1
+    sum_2 = sum_2 + got_2
+    got_1 = outward(sum_1)
+    got_2 = across(sum_2)
+    send_got, one_got, got_1, got_2, sides_got = together(
+        send_got, one_got, got_1, got_2, sides_got
+    )
+
+    vectors = gather_vectors(grad_up_bias, grad_down_bias, proj_bias, sides, sides_got)
+    vectors_got = exchange(vectors, 1)
+    input_rows = finish(rows_low, one_own, one_got, row(ln1_gain), d_middle)
+    *input_rows, vectors_got = together(*input_rows, vectors_got)
+
+    packet, packet_far = merge(own, far, send_got, vectors, vectors_got)
     packet_got = exchange(packet_far, 2)
     in_near = [route(input_rows[step], step, False) for step in range(2)]
-    out_far = [swap_tensor(v) for v in out_near]
-    sum_1 = sum_1 + got_1
     sum_2 = sum_2 + got_2
-    packet_got, sum_1, sum_2, *pieces = together(packet_got, sum_1, sum_2, *in_near, *out_far)
-
-    in_near, out_far = pieces[:2], pieces[2:]
-    packet = add_packets(packet, packet_got, shard)
-    padded = jnp.concatenate([sum_1, packet[shard:]], axis=0)
-    got_3 = edges(jnp.where(inner, padded, packet))
-    got_2 = across(sum_2)
+    got_2 = outward(sum_2)
+    grad_down = jnp.where(inner, sum_1, got_1).astype(jnp.float32).T
+    packet_got, got_2, *pieces = together(packet_got, got_2, *in_near, *share_got)
+    in_near, share_got = pieces[:2], pieces[2:]
+
+    quarters = spread(packet, packet_got, shard)
+    arrived = [turn_planes(quarters[step], step) for step in range(1, 4)]
     in_far = [swap_tensor(v) for v in in_near]
-    got_2, got_3, *in_far = together(got_2, got_3, *in_far)
-
-    sum_2 = sum_2 + got_2
-    sum_1 = jnp.where(inner, sum_1, got_3[:shard])
-    packet = add_packets(packet, got_3, shard)
-    packet_got = across(packet)
-    got_2 = outward(sum_2)
+    grad_up = jnp.where(inner, sum_2, got_2).astype(jnp.float32)
+    output = join_shares((share_0, share_1), share_got, odd, upper)
+    pieces = together(quarters[0], *arrived, *in_far)
+
+    in_far = pieces[4:]
+    quarter, vectors = total(pieces[:4], shard // 4, vectors.shape[0])
+    quarters = [quarter] + [turn_planes(quarter, step) for step in range(1, 4)]
     input_grad = join_out(in_near, in_far, odd, upper)
-    grad_down = sum_1.astype(jnp.float32).T
-    packet_got, got_2 = together(packet_got, got_2)
-
-    packet = add_packets(packet, packet_got, shard)
-    packet_got = outward(packet)
-    grad_up = jnp.where(inner, sum_2, got_2).astype(jnp.float32)
-    output = join_out(out_near, out_far, odd, upper)
-    packet = jnp.where(inner, packet, packet_got).astype(jnp.float32)
-
-    count = vectors.shape[0]
-    flat = (packet[shard : shard + count] + packet[shard + count :]).reshape(-1)
-    wide = 3 * local_width
-    ends = [wide + k * width for k in range(6)] + [wide + 5 * width + columns]
-    part = lambda k, size: flat[ends[k] : ends[k] + size]
-    grads = packet[:shard]
+    grad_query, grad_key, grad_value, grad_out = assemble(quarters)
+
     return (
         output.reshape(tokens.shape),
         input_grad.reshape(tokens.shape),
-        part(0, width),
-        part(1, width),
-        grads[:, :local_width],
-        flat[:local_width],
-        grads[:, local_width : 2 * local_width],
-        grads[:, 2 * local_width : wide],
-        flat[2 * local_width : wide],
-        grads[:, wide:].T,
-        part(4, width),
-        part(2, width),
-        part(3, width),
+        vectors[1, :width],
+        vectors[1, width:],
+        grad_query,
+        vectors[4, :local_width],
+        grad_key,
+        grad_value,
+        vectors[4, 2 * local_width : 3 * local_width],
+        grad_out,
+        vectors[3, :width],
+        vectors[2, :width],
+        vectors[2, width:],
         grad_up,
-        part(5, columns),
+        vectors[0],
         grad_down,
-        part(6, width),
+        vectors[3, width:],
     )
 
 

time: 252 us -> 236 us (0.937)
  local copies, waits for them, and re-layouts: 21.2 us -> 10.5 us
  waiting for transfers between devices: 94.8 us -> 102 us
  other arithmetic: 15.9 us -> 9.48 us
  Pallas kernels: 46.4 us -> 42.4 us
    ppermute x2, waiting for transfers between devices: 29.1 us -> 3.41 us  [outward(): return lax.ppermute(value, 'context', [(1, 0), (2, 3)])]
    ppermute x8, waiting for transfers between devices: 3.9 us -> 26 us  [route(): return lax.ppermute(value, ('dp', 'context'), pairs)]
    ppermute x1 -> x6, waiting for transfers between devices: 2.75 us -> 16.6 us  [turn_planes(): lax.ppermute(value, 'context', [(i, (i + step) % 4) for i in range(4)])]
    unnamed x126 -> x73, local copies, waits for them, and re-layouts: 17.6 us -> 8.01 us
    ppermute x15 -> x14, waiting for transfers between devices: 33.6 us -> 24.3 us  [swap_tensor(): return lax.ppermute(value, 'tensor', [(0, 1), (1, 0)])]
    ppermute x1 -> x6, starting transfers between devices: 2.55 us -> 10.1 us  [turn_planes(): lax.ppermute(value, 'context', [(i, (i + step) % 4) for i in range(4)])]
    ppermute x2, waiting for transfers between devices: 1.16 us -> 7.94 us  [inward(): return lax.ppermute(value, 'context', [(0, 1), (3, 2)])]
    pallas_call x1, Pallas kernels: 15 us -> 9.53 us  [middle_part(): pl.pallas_call(middle_kernel, out_shape=shapes, in_specs=[pl.BlockSpec(me...]
  transfers between devices with their start and end apart: 50 -> 53, of which waited for: 23 -> 21; matrix products, arithmetic and copies ran while one was open for 5% -> 4% of each run, Pallas kernels for 12% -> 12%
where the time goes in v3:
time: 236 us; the launch traced here: 235 us
  waiting for transfers between devices  102 us (43%)
  starting transfers between devices  67.8 us (29%)
  Pallas kernels  42.4 us (18%)
  local copies, waits for them, and re-layouts  10.5 us (4%)
  other arithmetic  9.48 us (4%)
  between operations  2.83 us (1%)
    ppermute x8, waiting for transfers between devices, route(): return lax.ppermute(value, ('dp', 'context'), pairs)  26 us
    ppermute x14, waiting for transfers between devices, swap_tensor(): return lax.ppermute(value, 'tensor', [(0, 1), (1, 0)])  24.3 us
    ppermute x19, waiting for transfers between devices, exchange(): return lax.ppermute(value, 'dp', [(i, i ^ bit) for i in range(size)])  24.2 us
    ppermute x19, starting transfers between devices, exchange(): return lax.ppermute(value, 'dp', [(i, i ^ bit) for i in range(size)])  17.9 us
    ppermute x6, waiting for transfers between devices, turn_planes(): lax.ppermute(value, 'context', [(i, (i + step) % 4) for i in range(4)])  16.6 us
    ppermute x14, starting transfers between devices, swap_tensor(): return lax.ppermute(value, 'tensor', [(0, 1), (1, 0)])  15.4 us
    pallas_call x10, Pallas kernels, call_once(): pl.pallas_call(kernel, out_shape=tuple(shapes), grid=(1,), in_specs=[fixe...  11.9 us
    pallas_call x1, Pallas kernels, attend_back(): pl.pallas_call(attend_back_kernel, out_shape=tuple((jax.ShapeDtypeStruct(...  11.1 us
  transfers between devices with their start and end apart: 53, of which 21 were waited for; matrix products, arithmetic and copies ran while one was open for 4% of the time, Pallas kernels for 12%

profile of v3, /device:TPU:0, one launch (start us, length us, event | category | flops | bytes accessed | tf_op | source)
XLA Modules:
  0.0 235.4 jit_solution(6073098470231614103)
XLA Ops:
  0.8 1.4 slice_select_fusion.1
  2.9 2.6 %collective-permute-start.2 = (bf16[192,1152]{1,0:T(8,128)(2,1)S(1)}, bf16[192,1152]{1,0:T(8,128)(2,1)S(1)}, u32[]{:S(2)}, u32[]{:S(2)}) collective-permute-start(bf16[192,1152]{1,0:T(8,128)(2,1)S(1)} %constant_dynamic-update-slice_fusion.a), channel_id=1, source_target_pairs={{0,16},{8,24},{16,0},{24,8},{1,17},{9,25},{17,1},{25,9},{2,18},{10... | collective-permute-start | bytes 1327112 | tf_op jit(solution)/shard_map/ppermute | solution.py:925
  6.1 1.6 collective-permute-start.1
  7.8 3.5 %collective-permute-start.5 = (s32[2]{0:T(128)S(1)}, s32[2]{0:T(128)S(1)}, u32[]{:S(2)}, u32[]{:S(2)}) collective-permute-start(s32[2]{0:T(128)S(1)} %copy-done.34), channel_id=1, source_target_pairs={{0,8},{8,0},{16,24},{24,16},{1,9},{9,1},{17,25},{25,17},{2,10},{10... | collective-permute-start | bytes 32 | tf_op jit(solution)/shard_map/ppermute | solution.py:925
  11.2 0.8 collective-permute-done.5
  12.1 1.5 collective-permute-start.4
  13.7 4.5 %collective-permute-done.4 = bf16[192,384]{1,0:T(8,128)(2,1)S(1)} collective-permute-done((bf16[192,384]{1,0:T(8,128)(2,1)S(1)}, bf16[192,384]{1,0:T(8,128)(2,1)S(1)}, u32[]{:S(2)}, u32[]{:S(2)}) %collective-permute-start.4) | collective-permute-done | bytes 147488 | tf_op jit(solution)/shard_map/ppermute | solution.py:929
  18.1 1.6 collective-permute-start.6
  21.0 1.7 collective-permute-start.11
  22.8 3.3 %collective-permute-done.6.peer0 = bf16[128,768]{1,0:T(8,128)(2,1)S(1)} collective-permute-done((bf16[128,768]{1,0:T(8,128)(2,1)S(1)}, bf16[128,768]{1,0:T(8,128)(2,1)S(1)}, u32[]{:S(2)}, u32[]{:S(2)}) %collective-permute-start.6) | collective-permute-done | bytes 196640 | tf_op jit(solution)/shard_map/ppermute | solution.py:929
  26.8 2.1 collective-permute-done.7.peer1
  28.9 7.4 %collective-permute-done.9.dc = bf16[192,1536]{1,0:T(8,128)(2,1)} collective-permute-done((bf16[192,1536]{1,0:T(8,128)(2,1)S(1)}, bf16[192,1536]{1,0:T(8,128)(2,1)}, u32[]{:S(2)}, u32[]{:S(2)}) %collective-permute-start.9) | collective-permute-done | bytes 589856 | tf_op jit(solution)/shard_map/ppermute | solution.py:925
  36.2 2.1 shard_map.305
  38.3 0.9 copy-done.1
  41.8 1.6 collective-permute-start.13
  44.5 1.0 copy-done.4
  45.5 8.0 %shard_map.306 = (bf16[512,384]{1,0:T(8,128)(2,1)S(1)}, f32[3,2,512]{2,1,0:T(2,128)S(1)}) custom-call(s32[9]{0:T(128)S(1)} %compare_select_fusion.4.info, bf16[512,384]{1,0:T(8,128)(2,1)S(1)} %copy-done.4, bf16[512,768]{1,0:T(8,128)(2,1)S(1)} %get-tuple-element.170.own_ref, bf16[512,768]{1,0:T(8,128)(2,1)} %collective-permute-done.12.other_ref), custom_call_target="tpu_custom_call" | custom-call | flops 3221225472 | bytes 2359296 | tf_op jit(solution)/shard_map/pallas_call | solution.py:331
  54.2 1.5 collective-permute-start.15
  55.7 9.7 %collective-permute-done.17.pc = bf16[192,2304]{1,0:T(8,128)(2,1)S(1)} collective-permute-done((bf16[192,2304]{1,0:T(8,128)(2,1)S(1)}, bf16[192,2304]{1,0:T(8,128)(2,1)S(1)}, u32[]{:S(2)}, u32[]{:S(2)}) %collective-permute-start.17) | collective-permute-done | bytes 884768 | tf_op jit(solution)/shard_map/ppermute | solution.py:925
  65.9 2.3 collective-permute-done.20.pd
  68.2 9.5 %shard_map.307 = (f32[256,768]{1,0:T(8,128)S(1)}, bf16[512,768]{1,0:T(8,128)(2,1)S(1)}, bf16[512,768]{1,0:T(8,128)(2,1)S(1)}, bf16[512,1536]{1,0:T(8,128)(2,1)S(...) custom-call(s32[9]{0:T(128)S(1)} %compare_select_fusion.4.info, ...), custom_call_target="tpu_custom_call" | custom-call | flops 4831838208 | bytes 20971520 | tf_op jit(solution)/shard_map/pallas_call | solution.py:654
  77.7 1.1 copy-done.6
  78.8 0.9 copy-done.8
  80.5 1.5 collective-permute-start.21
  82.1 0.9 collective-permute-start.22
  82.9 1.4 copy-done.7
  84.3 1.6 shard_map.308
  86.0 1.6 shard_map.309
  87.6 4.1 %collective-permute-done.21.got_ref = bf16[256,768]{1,0:T(8,128)(2,1)S(1)} collective-permute-done((bf16[256,768]{1,0:T(8,128)(2,1)S(1)}, bf16[256,768]{1,0:T(8,128)(2,1)S(1)}, u32[]{:S(2)}, u32[]{:S(2)}) %collective-permute-start.21) | collective-permute-done | bytes 393248 | tf_op jit(solution)/shard_map/ppermute | solution.py:929
  91.7 5.2 %collective-permute-start.23 = (bf16[384,1536]{1,0:T(8,128)(2,1)S(1)}, bf16[384,1536]{1,0:T(8,128)(2,1)S(1)}, u32[]{:S(2)}, u32[]{:S(2)}) collective-permute-start(bf16[384,1536]{1,0:T(8,128)(2,1)S(1)} %get-tuple-element.204), channel_id=1, source_target_pairs={{0,8},{8,0},{16,24},{24,16},{1,9},{9,1},{17,25},{25,17},{2,10},{10... | collective-permute-start | bytes 3538952 | tf_op jit(solution)/shard_map/ppermute | solution.py:925
  96.9 1.3 shard_map.310
  98.2 1.2 collective-permute-done.23
  99.8 1.6 collective-permute-start.25
  101.9 1.5 collective-permute-start.30
  103.4 10.0 %collective-permute-done.27 = bf16[2,128,768]{2,1,0:T(8,128)(2,1)S(1)} collective-permute-done((bf16[2,128,768]{2,1,0:T(8,128)(2,1)S(1)}, bf16[2,128,768]{2,1,0:T(8,128)(2,1)S(1)}, u32[]{:S(2)}, u32[]{:S(2)}) %collective-permute-start.27) | collective-permute-done | bytes 393248 | tf_op jit(solution)/shard_map/ppermute | solution.py:944
  113.3 1.9 collective-permute-done.25
  115.8 1.6 collective-permute-start.29
  117.5 1.7 collective-permute-start.28
  119.2 11.1 %shard_map.311 = (bf16[512,384]{1,0:T(8,128)(2,1)S(1)}, bf16[512,768]{1,0:T(8,128)(2,1)S(1)}, bf16[512,768]{1,0:T(8,128)(2,1)S(1)}) custom-call(s32[9]{0:T(128)S(1)} %compare_select_fusion.4.info, bf16[512,384]{1,0:T(8,128)(2,1)S(1)} %copy-done.5, bf16[512,768]{1,0:T(8,128)(2,1)S(1)} %get-tuple-element.170.own_ref, ...), custom_call_target="tpu_custom_call" | custom-call | flops 8053063680 | bytes 4718592 | tf_op jit(solution)/shard_map/pallas_call | solution.py:413
  131.8 7.6 %collective-permute-start.34 = (bf16[192,1536]{1,0:T(8,128)(2,1)S(1)}, bf16[192,1536]{1,0:T(8,128)(2,1)S(1)}, u32[]{:S(2)}, u32[]{:S(2)}) collective-permute-start(bf16[192,1536]{1,0:T(8,128)(2,1)S(1)} %add_add_fusion), channel_id=1, source_target_pairs={{0,2},{6,4},{1,3},{7,5},{8,10},{14,12},{9,11},{15,13},{16,18},{22,... | collective-permute-start | bytes 1769480 | tf_op jit(solution)/shard_map/ppermute | solution.py:974
  139.5 3.3 %shard_map.312 = (bf16[512,1152]{1,0:T(8,128)(2,1)S(1)}, bf16[256,768]{1,0:T(8,128)(2,1)S(1)}, bf16[256,768]{1,0:T(8,128)(2,1)S(1)}, f32[5,768]{1,0:T(8,128)S(1)}, f32[1,1152]{1,0:T(1,128)S(1)}) custom-call(bf16[512,768]{1,0:T(8,128)(2,1)S(1)} %get-tuple-element.168.rows_ref, bf16[768,1152]{1,0:T(8,128)(2,1)} %get-tuple-element.214.proj_ref, ...), custom_call_target="tpu_custom_call" | custom-call | flops 905969664 | bytes 6517248 | tf_op jit(solution)/shard_map/pallas_call | solution.py:452
  142.8 1.8 shard_map.313
  144.7 7.9 %collective-permute-done.34 = bf16[192,1536]{1,0:T(8,128)(2,1)S(1)} collective-permute-done((bf16[192,1536]{1,0:T(8,128)(2,1)S(1)}, bf16[192,1536]{1,0:T(8,128)(2,1)S(1)}, u32[]{:S(2)}, u32[]{:S(2)}) %collective-permute-start.34) | collective-permute-done | bytes 589856 | tf_op jit(solution)/shard_map/ppermute | solution.py:974
  153.0 1.3 collective-permute-start.37
  154.3 0.9 collective-permute-start.38
  155.2 1.6 collective-permute-start.36
  157.3 10.0 %collective-permute-done.39.theirs_ref = f32[5,768]{1,0:T(8,128)S(1)} collective-permute-done((f32[5,768]{1,0:T(8,128)S(1)}, f32[5,768]{1,0:T(8,128)S(1)}, u32[]{:S(2)}, u32[]{:S(2)}) %collective-permute-start.39) | collective-permute-done | bytes 15392 | tf_op jit(solution)/shard_map/ppermute | solution.py:929
  167.3 3.4 %collective-permute-done.37 = bf16[192,1536]{1,0:T(8,128)(2,1)S(1)} collective-permute-done((bf16[192,1536]{1,0:T(8,128)(2,1)S(1)}, bf16[192,1536]{1,0:T(8,128)(2,1)S(1)}, u32[]{:S(2)}, u32[]{:S(2)}) %collective-permute-start.37) | collective-permute-done | bytes 589856 | tf_op jit(solution)/shard_map/ppermute | solution.py:982
  172.8 1.0 add.78
  173.7 1.3 collective-permute-start.42
  175.9 4.5 %collective-permute-start.44 = (bf16[128,768]{1,0:T(8,128)(2,1)S(1)}, bf16[128,768]{1,0:T(8,128)(2,1)S(1)}, u32[]{:S(2)}, u32[]{:S(2)}) collective-permute-start(bf16[128,768]{1,0:T(8,128)(2,1)S(1)} %get-tuple-element.256), channel_id=1, source_target_pairs={{0,2},{2,0},{4,10},{6,8},{8,6},{10,4},{12,14},{14,12},{16,18},{18,... | collective-permute-start | bytes 589832 | tf_op jit(solution)/shard_map/ppermute | solution.py:944
  180.4 2.2 convert_bitcast_fusion
  182.6 16.0 %collective-permute-done.44 = bf16[128,768]{1,0:T(8,128)(2,1)S(1)} collective-permute-done((bf16[128,768]{1,0:T(8,128)(2,1)S(1)}, bf16[128,768]{1,0:T(8,128)(2,1)S(1)}, u32[]{:S(2)}, u32[]{:S(2)}) %collective-permute-start.44) | collective-permute-done | bytes 196640 | tf_op jit(solution)/shard_map/ppermute | solution.py:944
  199.8 3.0 %collective-permute-start.47 = (bf16[64,1536]{1,0:T(8,128)(2,1)S(1)}, bf16[64,1536]{1,0:T(8,128)(2,1)S(1)}, u32[]{:S(2)}, u32[]{:S(2)}) collective-permute-start(bf16[64,1536]{1,0:T(8,128)(2,1)S(1)} %get-tuple-element.266), channel_id=1, source_target_pairs={{0,6},{2,0},{4,2},{6,4},{1,7},{3,1},{5,3},{7,5},{8,14},{10,8},{12,... | collective-permute-start | bytes 589832 | tf_op jit(solution)/shard_map/ppermute | solution.py:970
  202.8 1.5 collective-permute-start.48
  204.8 2.2 select_convert_fusion
  207.2 1.5 collective-permute-done.45.refs_1_
  208.7 5.2 %collective-permute-done.46.refs_2_ = bf16[64,1536]{1,0:T(8,128)(2,1)S(1)} collective-permute-done((bf16[64,1536]{1,0:T(8,128)(2,1)S(1)}, bf16[64,1536]{1,0:T(8,128)(2,1)S(1)}, u32[]{:S(2)}, u32[]{:S(2)}) %collective-permute-start.46) | collective-permute-done | bytes 196640 | tf_op jit(solution)/shard_map/ppermute | solution.py:970
  214.1 5.1 %collective-permute-start.52 = (bf16[48,1536]{1,0:T(8,128)(2,1)S(1)}, bf16[48,1536]{1,0:T(8,128)(2,1)S(1)}, u32[]{:S(2)}, u32[]{:S(2)}) collective-permute-start(bf16[48,1536]{1,0:T(8,128)(2,1)S(1)} %get-tuple-element.276.a), channel_id=1, source_target_pairs={{0,6},{2,0},{4,2},{6,4},{1,7},{3,1},{5,3},{7,5},{8,14},{10,8},{12,... | collective-permute-start | bytes 442376 | tf_op jit(solution)/shard_map/ppermute | solution.py:970
  219.2 1.0 collective-permute-start.51
  220.9 1.4 reverse_select_fusion
  223.6 9.9 %collective-permute-done.51.c = bf16[48,1536]{1,0:T(8,128)(2,1)S(1)} collective-permute-done((bf16[48,1536]{1,0:T(8,128)(2,1)S(1)}, bf16[48,1536]{1,0:T(8,128)(2,1)S(1)}, u32[]{:S(2)}, u32[]{:S(2)}) %collective-permute-start.51) | collective-permute-done | bytes 147488 | tf_op jit(solution)/shard_map/ppermute | solution.py:970
  233.5 1.0 shard_map.319
  234.5 0.9 copy.35
  (167 shorter events, 18.2 us)
Async XLA Ops:
  0.8 19.5 %copy-start.12 = (bf16[2,256,768]{2,1,0:T(8,128)(2,1)S(1)}, bf16[2,256,768]{2,1,0:T(8,128)(2,1)}, u32[]{:S(2)}) copy-start(bf16[2,256,768]{2,1,0:T(8,128)(2,1)} %param.35) | copy-start | bytes 2359300
  2.2 18.1 %copy-start = (bf16[1536,192]{0,1:T(8,128)(2,1)S(1)}, bf16[1536,192]{0,1:T(8,128)(2,1)}, u32[]{:S(2)}) copy-start(bf16[1536,192]{0,1:T(8,128)(2,1)} %param.33) | copy-start | bytes 1769476
  2.3 24.4 %copy-start.13 = (bf16[192,1536]{1,0:T(8,128)(2,1)S(1)}, bf16[192,1536]{1,0:T(8,128)(2,1)}, u32[]{:S(2)}) copy-start(bf16[192,1536]{1,0:T(8,128)(2,1)} %param.31) | copy-start | bytes 1769476
  2.4 15.8 %collective-permute-start.3 = (bf16[192,1152]{1,0:T(8,128)(2,1)S(1)}, bf16[192,1152]{1,0:T(8,128)(2,1)S(1)}, u32[]{:S(2)}, u32[]{:S(2)}) collective-permute-start(bf16[192,1152]{1,0:T(8,128)(2,1)S(1)} %constant_dynamic-update-slice_fusion.a), channel_id=1, source_target_pairs={{0,8},{8,0},{16,24},{24,16},{1,9},{9,1},{17,25},{25,17},{2,10},{10... | collective-permute-start | bytes 1327112 | tf_op jit(solution)/shard_map/ppermute | solution.py:925
  2.9 15.3 %collective-permute-start.2 = (bf16[192,1152]{1,0:T(8,128)(2,1)S(1)}, bf16[192,1152]{1,0:T(8,128)(2,1)S(1)}, u32[]{:S(2)}, u32[]{:S(2)}) collective-permute-start(bf16[192,1152]{1,0:T(8,128)(2,1)S(1)} %constant_dynamic-update-slice_fusion.a), channel_id=1, source_target_pairs={{0,16},{8,24},{16,0},{24,8},{1,17},{9,25},{17,1},{25,9},{2,18},{10... | collective-permute-start | bytes 1327112 | tf_op jit(solution)/shard_map/ppermute | solution.py:925
  5.5 12.7 %collective-permute-start = (bf16[128,768]{1,0:T(8,128)(2,1)S(1)}, bf16[128,768]{1,0:T(8,128)(2,1)S(1)}, u32[]{:S(2)}, u32[]{:S(2)}) collective-permute-start(bf16[128,768]{1,0:T(8,128)(2,1)S(1)} %get-tuple-element.150), channel_id=1, source_target_pairs={{0,0},{2,2},{8,4},{10,6},{4,8},{6,10},{12,12},{14,14},{16,16},{18,... | collective-permute-start | bytes 589832 | tf_op jit(solution)/shard_map/ppermute | solution.py:944
  6.1 12.0 %collective-permute-start.1 = (bf16[128,768]{1,0:T(8,128)(2,1)S(1)}, bf16[128,768]{1,0:T(8,128)(2,1)S(1)}, u32[]{:S(2)}, u32[]{:S(2)}) collective-permute-start(bf16[128,768]{1,0:T(8,128)(2,1)S(1)} %get-tuple-element.151), channel_id=1, source_target_pairs={{2,0},{0,2},{10,4},{8,6},{6,8},{4,10},{14,12},{12,14},{18,16},{16,... | collective-permute-start | bytes 589832 | tf_op jit(solution)/shard_map/ppermute | solution.py:944
  7.8 4.3 %collective-permute-start.5 = (s32[2]{0:T(128)S(1)}, s32[2]{0:T(128)S(1)}, u32[]{:S(2)}, u32[]{:S(2)}) collective-permute-start(s32[2]{0:T(128)S(1)} %copy-done.34), channel_id=1, source_target_pairs={{0,8},{8,0},{16,24},{24,16},{1,9},{9,1},{17,25},{25,17},{2,10},{10... | collective-permute-start | bytes 32 | tf_op jit(solution)/shard_map/ppermute | solution.py:925
  12.1 6.1 %collective-permute-start.4 = (bf16[192,384]{1,0:T(8,128)(2,1)S(1)}, bf16[192,384]{1,0:T(8,128)(2,1)S(1)}, u32[]{:S(2)}, u32[]{:S(2)}) collective-permute-start(bf16[192,384]{1,0:T(8,128)(2,1)S(1)} %bitcast.37), channel_id=1, source_target_pairs={{0,1},{1,0},{2,3},{3,2},{4,5},{5,4},{6,7},{7,6},{8,9},{9,8},{10,11... | collective-permute-start | bytes 442376 | tf_op jit(solution)/shard_map/ppermute | solution.py:929
  18.1 7.9 %collective-permute-start.6 = (bf16[128,768]{1,0:T(8,128)(2,1)S(1)}, bf16[128,768]{1,0:T(8,128)(2,1)S(1)}, u32[]{:S(2)}, u32[]{:S(2)}) collective-permute-start(bf16[128,768]{1,0:T(8,128)(2,1)S(1)} %collective-permute-done.own0), channel_id=1, source_target_pairs={{0,1},{1,0},{2,3},{3,2},{4,5},{5,4},{6,7},{7,6},{8,9},{9,8},{10,11... | collective-permute-start | bytes 589832 | tf_op jit(solution)/shard_map/ppermute | solution.py:929
  19.7 9.1 %collective-permute-start.7 = (bf16[128,768]{1,0:T(8,128)(2,1)S(1)}, bf16[128,768]{1,0:T(8,128)(2,1)S(1)}, u32[]{:S(2)}, u32[]{:S(2)}) collective-permute-start(bf16[128,768]{1,0:T(8,128)(2,1)S(1)} %collective-permute-done.1.own1), channel_id=1, source_target_pairs={{0,1},{1,0},{2,3},{3,2},{4,5},{5,4},{6,7},{7,6},{8,9},{9,8},{10,11... | collective-permute-start | bytes 589832 | tf_op jit(solution)/shard_map/ppermute | solution.py:929
  20.3 8.6 %collective-permute-start.8 = (bf16[192,1152]{1,0:T(8,128)(2,1)S(1)}, bf16[192,1152]{1,0:T(8,128)(2,1)S(1)}, u32[]{:S(2)}, u32[]{:S(2)}) collective-permute-start(bf16[192,1152]{1,0:T(8,128)(2,1)S(1)} %collective-permute-done.2.c), channel_id=1, source_target_pairs={{0,8},{8,0},{16,24},{24,16},{1,9},{9,1},{17,25},{25,17},{2,10},{10... | collective-permute-start | bytes 1327112 | tf_op jit(solution)/shard_map/ppermute | solution.py:925
  20.4 15.8 %collective-permute-start.9 = (bf16[192,1536]{1,0:T(8,128)(2,1)S(1)}, bf16[192,1536]{1,0:T(8,128)(2,1)}, u32[]{:S(2)}, u32[]{:S(2)}) collective-permute-start(bf16[192,1536]{1,0:T(8,128)(2,1)S(1)} %bitcast.26), channel_id=1, source_target_pairs={{0,16},{8,24},{16,0},{24,8},{1,17},{9,25},{17,1},{25,9},{2,18},{10... | collective-permute-start | bytes 1769480 | tf_op jit(solution)/shard_map/ppermute | solution.py:925
  21.0 7.8 %collective-permute-start.11 = (bf16[128,768]{1,0:T(8,128)(2,1)S(1)}, bf16[128,768]{1,0:T(8,128)(2,1)S(1)}, u32[]{:S(2)}, u32[]{:S(2)}) collective-permute-start(bf16[128,768]{1,0:T(8,128)(2,1)S(1)} %get-tuple-element.308), channel_id=1, source_target_pairs={{2,0},{0,2},{10,4},{8,6},{6,8},{4,10},{14,12},{12,14},{18,16},{16,... | collective-permute-start | bytes 589832 | tf_op jit(solution)/shard_map/ppermute | solution.py:944
  26.0 2.8 %collective-permute-start.10 = (bf16[128,768]{1,0:T(8,128)(2,1)S(1)}, bf16[128,768]{1,0:T(8,128)(2,1)S(1)}, u32[]{:S(2)}, u32[]{:S(2)}) collective-permute-start(bf16[128,768]{1,0:T(8,128)(2,1)S(1)} %get-tuple-element.309), channel_id=1, source_target_pairs={{0,0},{2,2},{8,4},{10,6},{4,8},{6,10},{12,12},{14,14},{16,16},{18,... | collective-permute-start | bytes 589832 | tf_op jit(solution)/shard_map/ppermute | solution.py:944
  39.9 4.5 %collective-permute-start.12 = (bf16[512,768]{1,0:T(8,128)(2,1)S(1)}, bf16[512,768]{1,0:T(8,128)(2,1)}, u32[]{:S(2)}, u32[]{:S(2)}) collective-permute-start(bf16[512,768]{1,0:T(8,128)(2,1)S(1)} %get-tuple-element.170.own_ref), channel_id=1, source_target_pairs={{0,8},{8,0},{16,24},{24,16},{1,9},{9,1},{17,25},{25,17},{2,10},{10... | collective-permute-start | bytes 2359304 | tf_op jit(solution)/shard_map/ppermute | solution.py:925
  41.8 11.7 %collective-permute-start.13 = (bf16[128,768]{1,0:T(8,128)(2,1)S(1)}, bf16[128,768]{1,0:T(8,128)(2,1)S(1)}, u32[]{:S(2)}, u32[]{:S(2)}) collective-permute-start(bf16[128,768]{1,0:T(8,128)(2,1)S(1)} %collective-permute-done.10.top0), channel_id=1, source_target_pairs={{0,1},{1,0},{2,3},{3,2},{4,5},{5,4},{6,7},{7,6},{8,9},{9,8},{10,11... | collective-permute-start | bytes 589832 | tf_op jit(solution)/shard_map/ppermute | solution.py:929
  43.4 10.1 %collective-permute-start.14 = (bf16[128,768]{1,0:T(8,128)(2,1)S(1)}, bf16[128,768]{1,0:T(8,128)(2,1)S(1)}, u32[]{:S(2)}, u32[]{:S(2)}) collective-permute-start(bf16[128,768]{1,0:T(8,128)(2,1)S(1)} %collective-permute-done.11.top1), channel_id=1, source_target_pairs={{0,1},{1,0},{2,3},{3,2},{4,5},{5,4},{6,7},{7,6},{8,9},{9,8},{10,11... | collective-permute-start | bytes 589832 | tf_op jit(solution)/shard_map/ppermute | solution.py:929
  43.9 21.5 %collective-permute-start.17 = (bf16[192,2304]{1,0:T(8,128)(2,1)S(1)}, bf16[192,2304]{1,0:T(8,128)(2,1)S(1)}, u32[]{:S(2)}, u32[]{:S(2)}) collective-permute-start(bf16[192,2304]{1,0:T(8,128)(2,1)S(1)} %pad_maximum_fusion.pa), channel_id=1, source_target_pairs={{0,16},{8,24},{16,0},{24,8},{1,17},{9,25},{17,1},{25,9},{2,18},{10... | collective-permute-start | bytes 2654216 | tf_op jit(solution)/shard_map/ppermute | solution.py:925
  45.5 20.3 %copy-start.28 = (bf16[768]{0:T(1024)(128)(2,1)S(1)}, bf16[768]{0:T(1024)(128)(2,1)}, u32[]{:S(2)}) copy-start(bf16[768]{0:T(1024)(128)(2,1)} %param.29) | copy-start | bytes 4612
  45.5 20.3 %copy-start.29 = (bf16[768]{0:T(1024)(128)(2,1)S(1)}, bf16[768]{0:T(1024)(128)(2,1)}, u32[]{:S(2)}) copy-start(bf16[768]{0:T(1024)(128)(2,1)} %param.28) | copy-start | bytes 4612
  45.5 20.3 %copy-start.30 = (bf16[768]{0:T(1024)(128)(2,1)S(1)}, bf16[768]{0:T(1024)(128)(2,1)}, u32[]{:S(2)}) copy-start(bf16[768]{0:T(1024)(128)(2,1)} %param.30) | copy-start | bytes 4612
  45.5 20.4 %copy-start.31 = (bf16[768]{0:T(1024)(128)(2,1)S(1)}, bf16[768]{0:T(1024)(128)(2,1)}, u32[]{:S(2)}) copy-start(bf16[768]{0:T(1024)(128)(2,1)} %param.34) | copy-start | bytes 4612
  45.5 20.4 %copy-start.25 = (bf16[1536]{0:T(1024)(128)(2,1)S(1)}, bf16[1536]{0:T(1024)(128)(2,1)}, u32[]{:S(2)}) copy-start(bf16[1536]{0:T(1024)(128)(2,1)} %param.32) | copy-start | bytes 9220
  53.5 12.1 %collective-permute-start.16 = (bf16[192,2304]{1,0:T(8,128)(2,1)S(1)}, bf16[192,2304]{1,0:T(8,128)(2,1)S(1)}, u32[]{:S(2)}, u32[]{:S(2)}) collective-permute-start(bf16[192,2304]{1,0:T(8,128)(2,1)S(1)} %pad_maximum_fusion.pa), channel_id=1, source_target_pairs={{0,8},{8,0},{16,24},{24,16},{1,9},{9,1},{17,25},{25,17},{2,10},{10... | collective-permute-start | bytes 2654216 | tf_op jit(solution)/shard_map/ppermute | solution.py:925
  53.6 12.0 %collective-permute-start.18 = (bf16[192,1536]{1,0:T(8,128)(2,1)S(1)}, bf16[192,1536]{1,0:T(8,128)(2,1)S(1)}, u32[]{:S(2)}, u32[]{:S(2)}) collective-permute-start(bf16[192,1536]{1,0:T(8,128)(2,1)S(1)} %bitcast.27), channel_id=1, source_target_pairs={{0,8},{8,0},{16,24},{24,16},{1,9},{9,1},{17,25},{25,17},{2,10},{10... | collective-permute-start | bytes 1769480 | tf_op jit(solution)/shard_map/ppermute | solution.py:925
  54.1 11.6 %collective-permute-start.19 = (bf16[192,1536]{1,0:T(8,128)(2,1)}, bf16[192,1536]{1,0:T(8,128)(2,1)S(1)}, u32[]{:S(2)}, u32[]{:S(2)}) collective-permute-start(bf16[192,1536]{1,0:T(8,128)(2,1)} %collective-permute-done.9.dc), channel_id=1, source_target_pairs={{0,8},{8,0},{16,24},{24,16},{1,9},{9,1},{17,25},{25,17},{2,10},{10... | collective-permute-start | bytes 1769480 | tf_op jit(solution)/shard_map/ppermute | solution.py:925
  54.2 11.5 %collective-permute-start.15 = (bf16[512,384]{1,0:T(8,128)(2,1)S(1)}, bf16[512,384]{1,0:T(8,128)(2,1)S(1)}, u32[]{:S(2)}, u32[]{:S(2)}) collective-permute-start(bf16[512,384]{1,0:T(8,128)(2,1)S(1)} %get-tuple-element.176.own_ref.out_ref.refs_4_), channel_id=1, source_target_pairs={{0,1},{1,0},{2,3},{3,2},{4,5},{5,4},{6,7},{7,6},{8,9},{9,8},{10,11... | collective-permute-start | bytes 1179656 | tf_op jit(solution)/shard_map/ppermute | solution.py:929
  65.7 2.5 %collective-permute-start.20 = (bf16[192,2304]{1,0:T(8,128)(2,1)S(1)}, bf16[192,2304]{1,0:T(8,128)(2,1)S(1)}, u32[]{:S(2)}, u32[]{:S(2)}) collective-permute-start(bf16[192,2304]{1,0:T(8,128)(2,1)S(1)} %collective-permute-done.17.pc), channel_id=1, source_target_pairs={{0,8},{8,0},{16,24},{24,16},{1,9},{9,1},{17,25},{25,17},{2,10},{10... | collective-permute-start | bytes 2654216 | tf_op jit(solution)/shard_map/ppermute | solution.py:925
  80.5 11.2 %collective-permute-start.21 = (bf16[256,768]{1,0:T(8,128)(2,1)S(1)}, bf16[256,768]{1,0:T(8,128)(2,1)S(1)}, u32[]{:S(2)}, u32[]{:S(2)}) collective-permute-start(bf16[256,768]{1,0:T(8,128)(2,1)S(1)} %get-tuple-element.193), channel_id=1, source_target_pairs={{0,1},{1,0},{2,3},{3,2},{4,5},{5,4},{6,7},{7,6},{8,9},{9,8},{10,11... | collective-permute-start | bytes 1179656 | tf_op jit(solution)/shard_map/ppermute | solution.py:929
  82.1 9.6 %collective-permute-start.22 = (bf16[2,128,768]{2,1,0:T(8,128)(2,1)S(1)}, bf16[2,128,768]{2,1,0:T(8,128)(2,1)S(1)}, u32[]{:S(2)}, u32[]{:S(2)}) collective-permute-start(bf16[2,128,768]{2,1,0:T(8,128)(2,1)S(1)} %get-tuple-element.200), channel_id=1, source_target_pairs={{0,0},{2,2},{4,8},{6,10},{8,4},{10,6},{12,12},{14,14},{16,16},{18,... | collective-permute-start | bytes 1179656 | tf_op jit(solution)/shard_map/ppermute | solution.py:944
  91.7 7.6 %collective-permute-start.23 = (bf16[384,1536]{1,0:T(8,128)(2,1)S(1)}, bf16[384,1536]{1,0:T(8,128)(2,1)S(1)}, u32[]{:S(2)}, u32[]{:S(2)}) collective-permute-start(bf16[384,1536]{1,0:T(8,128)(2,1)S(1)} %get-tuple-element.204), channel_id=1, source_target_pairs={{0,8},{8,0},{16,24},{24,16},{1,9},{9,1},{17,25},{25,17},{2,10},{10... | collective-permute-start | bytes 3538952 | tf_op jit(solution)/shard_map/ppermute | solution.py:925
  99.4 15.9 %collective-permute-start.26 = (bf16[384,1536]{1,0:T(8,128)(2,1)S(1)}, bf16[384,1536]{1,0:T(8,128)(2,1)S(1)}, u32[]{:S(2)}, u32[]{:S(2)}) collective-permute-start(bf16[384,1536]{1,0:T(8,128)(2,1)S(1)} %get-tuple-element.210), channel_id=1, source_target_pairs={{0,8},{8,0},{16,24},{24,16},{1,9},{9,1},{17,25},{25,17},{2,10},{10... | collective-permute-start | bytes 3538952 | tf_op jit(solution)/shard_map/ppermute | solution.py:925
  99.8 15.4 %collective-permute-start.25 = (bf16[192,1536]{1,0:T(8,128)(2,1)S(1)}, bf16[192,1536]{1,0:T(8,128)(2,1)S(1)}, u32[]{:S(2)}, u32[]{:S(2)}) collective-permute-start(bf16[192,1536]{1,0:T(8,128)(2,1)S(1)} %slice_add_fusion.1), channel_id=1, source_target_pairs={{0,16},{8,24},{16,0},{24,8},{1,17},{9,25},{17,1},{25,9},{2,18},{10... | collective-permute-start | bytes 1769480 | tf_op jit(solution)/shard_map/ppermute | solution.py:925
  101.4 12.0 %collective-permute-start.27 = (bf16[2,128,768]{2,1,0:T(8,128)(2,1)S(1)}, bf16[2,128,768]{2,1,0:T(8,128)(2,1)S(1)}, u32[]{:S(2)}, u32[]{:S(2)}) collective-permute-start(bf16[2,128,768]{2,1,0:T(8,128)(2,1)S(1)} %get-tuple-element.211), channel_id=1, source_target_pairs={{0,2},{2,0},{4,10},{6,8},{8,6},{10,4},{12,14},{14,12},{16,18},{18,... | collective-permute-start | bytes 1179656 | tf_op jit(solution)/shard_map/ppermute | solution.py:944
  101.4 12.0 %collective-permute-start.24 = (bf16[256,768]{1,0:T(8,128)(2,1)S(1)}, bf16[256,768]{1,0:T(8,128)(2,1)S(1)}, u32[]{:S(2)}, u32[]{:S(2)}) collective-permute-start(bf16[256,768]{1,0:T(8,128)(2,1)S(1)} %get-tuple-element.207.d_own_ref.refs_2_), channel_id=1, source_target_pairs={{0,1},{1,0},{2,3},{3,2},{4,5},{5,4},{6,7},{7,6},{8,9},{9,8},{10,11... | collective-permute-start | bytes 1179656 | tf_op jit(solution)/shard_map/ppermute | solution.py:929
  101.9 28.5 %collective-permute-start.30 = (bf16[2,128,768]{2,1,0:T(8,128)(2,1)S(1)}, bf16[2,128,768]{2,1,0:T(8,128)(2,1)S(1)}, u32[]{:S(2)}, u32[]{:S(2)}) collective-permute-start(bf16[2,128,768]{2,1,0:T(8,128)(2,1)S(1)} %collective-permute-done.22), channel_id=1, source_target_pairs={{0,1},{1,0},{2,3},{3,2},{4,5},{5,4},{6,7},{7,6},{8,9},{9,8},{10,11... | collective-permute-start | bytes 1179656 | tf_op jit(solution)/shard_map/ppermute | solution.py:929
  115.2 15.1 %collective-permute-start.31 = (bf16[2,128,768]{2,1,0:T(8,128)(2,1)S(1)}, bf16[2,128,768]{2,1,0:T(8,128)(2,1)S(1)}, u32[]{:S(2)}, u32[]{:S(2)}) collective-permute-start(bf16[2,128,768]{2,1,0:T(8,128)(2,1)S(1)} %collective-permute-done.27), channel_id=1, source_target_pairs={{0,1},{1,0},{2,3},{3,2},{4,5},{5,4},{6,7},{7,6},{8,9},{9,8},{10,11... | collective-permute-start | bytes 1179656 | tf_op jit(solution)/shard_map/ppermute | solution.py:929
  115.8 15.0 %collective-permute-start.29 = (bf16[192,1536]{1,0:T(8,128)(2,1)S(1)}, bf16[192,1536]{1,0:T(8,128)(2,1)S(1)}, u32[]{:S(2)}, u32[]{:S(2)}) collective-permute-start(bf16[192,1536]{1,0:T(8,128)(2,1)S(1)} %slice_add_fusion), channel_id=1, source_target_pairs={{0,16},{8,24},{16,0},{24,8},{1,17},{9,25},{17,1},{25,9},{2,18},{10... | collective-permute-start | bytes 1769480 | tf_op jit(solution)/shard_map/ppermute | solution.py:925
  117.5 13.3 %collective-permute-start.28 = (bf16[192,1536]{1,0:T(8,128)(2,1)S(1)}, bf16[192,1536]{1,0:T(8,128)(2,1)S(1)}, u32[]{:S(2)}, u32[]{:S(2)}) collective-permute-start(bf16[192,1536]{1,0:T(8,128)(2,1)S(1)} %add_add_fusion.1), channel_id=1, source_target_pairs={{0,2},{6,4},{1,3},{7,5},{8,10},{14,12},{9,11},{15,13},{16,18},{22,... | collective-permute-start | bytes 1769480 | tf_op jit(solution)/shard_map/ppermute | solution.py:974
  130.9 13.7 %collective-permute-start.33 = (bf16[192,1536]{1,0:T(8,128)(2,1)S(1)}, bf16[192,1536]{1,0:T(8,128)(2,1)S(1)}, u32[]{:S(2)}, u32[]{:S(2)}) collective-permute-start(bf16[192,1536]{1,0:T(8,128)(2,1)S(1)} %add.73), channel_id=1, source_target_pairs={{2,4},{4,2},{3,5},{5,3},{10,12},{12,10},{11,13},{13,11},{18,20},{2... | collective-permute-start | bytes 1769480 | tf_op jit(solution)/shard_map/ppermute | solution.py:978
  131.6 7.8 %collective-permute-start.32 = (bf16[512,768]{1,0:T(8,128)(2,1)S(1)}, bf16[512,768]{1,0:T(8,128)(2,1)S(1)}, u32[]{:S(2)}, u32[]{:S(2)}) collective-permute-start(bf16[512,768]{1,0:T(8,128)(2,1)S(1)} %get-tuple-element.226), channel_id=1, source_target_pairs={{0,8},{8,0},{16,24},{24,16},{1,9},{9,1},{17,25},{25,17},{2,10},{10... | collective-permute-start | bytes 2359304 | tf_op jit(solution)/shard_map/ppermute | solution.py:925
  131.8 20.8 %collective-permute-start.34 = (bf16[192,1536]{1,0:T(8,128)(2,1)S(1)}, bf16[192,1536]{1,0:T(8,128)(2,1)S(1)}, u32[]{:S(2)}, u32[]{:S(2)}) collective-permute-start(bf16[192,1536]{1,0:T(8,128)(2,1)S(1)} %add_add_fusion), channel_id=1, source_target_pairs={{0,2},{6,4},{1,3},{7,5},{8,10},{14,12},{9,11},{15,13},{16,18},{22,... | collective-permute-start | bytes 1769480 | tf_op jit(solution)/shard_map/ppermute | solution.py:974
  152.6 18.1 %collective-permute-start.35 = (bf16[384,1536]{1,0:T(8,128)(2,1)S(1)}, bf16[384,1536]{1,0:T(8,128)(2,1)S(1)}, u32[]{:S(2)}, u32[]{:S(2)}) collective-permute-start(bf16[384,1536]{1,0:T(8,128)(2,1)S(1)} %get-tuple-element.237), channel_id=1, source_target_pairs={{0,8},{8,0},{16,24},{24,16},{1,9},{9,1},{17,25},{25,17},{2,10},{10... | collective-permute-start | bytes 3538952 | tf_op jit(solution)/shard_map/ppermute | solution.py:925
  153.0 17.8 %collective-permute-start.37 = (bf16[192,1536]{1,0:T(8,128)(2,1)S(1)}, bf16[192,1536]{1,0:T(8,128)(2,1)S(1)}, u32[]{:S(2)}, u32[]{:S(2)}) collective-permute-start(bf16[192,1536]{1,0:T(8,128)(2,1)S(1)} %add.76), channel_id=1, source_target_pairs={{2,0},{4,6},{3,1},{5,7},{10,8},{12,14},{11,9},{13,15},{18,16},{20,... | collective-permute-start | bytes 1769480 | tf_op jit(solution)/shard_map/ppermute | solution.py:982
  154.3 16.5 %collective-permute-start.38 = (bf16[192,1536]{1,0:T(8,128)(2,1)S(1)}, bf16[192,1536]{1,0:T(8,128)(2,1)S(1)}, u32[]{:S(2)}, u32[]{:S(2)}) collective-permute-start(bf16[192,1536]{1,0:T(8,128)(2,1)S(1)} %add.77), channel_id=1, source_target_pairs={{2,4},{4,2},{3,5},{5,3},{10,12},{12,10},{11,13},{13,11},{18,20},{2... | collective-permute-start | bytes 1769480 | tf_op jit(solution)/shard_map/ppermute | solution.py:978
  155.2 12.1 %collective-permute-start.36 = (bf16[256,768]{1,0:T(8,128)(2,1)S(1)}, bf16[256,768]{1,0:T(8,128)(2,1)S(1)}, u32[]{:S(2)}, u32[]{:S(2)}) collective-permute-start(bf16[256,768]{1,0:T(8,128)(2,1)S(1)} %get-tuple-element.238), channel_id=1, source_target_pairs={{0,1},{1,0},{2,3},{3,2},{4,5},{5,4},{6,7},{7,6},{8,9},{9,8},{10,11... | collective-permute-start | bytes 1179656 | tf_op jit(solution)/shard_map/ppermute | solution.py:929
  156.8 10.5 %collective-permute-start.39 = (f32[5,768]{1,0:T(8,128)S(1)}, f32[5,768]{1,0:T(8,128)S(1)}, u32[]{:S(2)}, u32[]{:S(2)}) collective-permute-start(f32[5,768]{1,0:T(8,128)S(1)} %get-tuple-element.241.mine_ref), channel_id=1, source_target_pairs={{0,1},{1,0},{2,3},{3,2},{4,5},{5,4},{6,7},{7,6},{8,9},{9,8},{10,11... | collective-permute-start | bytes 46088 | tf_op jit(solution)/shard_map/ppermute | solution.py:929
  170.8 1.3 collective-permute-start.40
  172.2 26.4 %collective-permute-start.41 = (bf16[208,1536]{1,0:T(8,128)(2,1)S(1)}, bf16[208,1536]{1,0:T(8,128)(2,1)S(1)}, u32[]{:S(2)}, u32[]{:S(2)}) collective-permute-start(bf16[208,1536]{1,0:T(8,128)(2,1)S(1)} %get-tuple-element.253), channel_id=1, source_target_pairs={{0,16},{8,24},{16,0},{24,8},{1,17},{9,25},{17,1},{25,9},{2,18},{10... | collective-permute-start | bytes 1916936 | tf_op jit(solution)/shard_map/ppermute | solution.py:925
  173.7 24.9 %collective-permute-start.42 = (bf16[192,1536]{1,0:T(8,128)(2,1)}, bf16[192,1536]{1,0:T(8,128)(2,1)}, u32[]{:S(2)}, u32[]{:S(2)}) collective-permute-start(bf16[192,1536]{1,0:T(8,128)(2,1)} %add.78), channel_id=1, source_target_pairs={{2,0},{4,6},{3,1},{5,7},{10,8},{12,14},{11,9},{13,15},{18,16},{20,... | collective-permute-start | bytes 1769480 | tf_op jit(solution)/shard_map/ppermute | solution.py:982
  175.0 23.6 %copy-start.16 = (bf16[2,128,768]{2,1,0:T(8,128)(2,1)S(1)}, bf16[2,128,768]{2,1,0:T(8,128)(2,1)}, u32[]{:S(2)}) copy-start(bf16[2,128,768]{2,1,0:T(8,128)(2,1)} %copy-done.15) | copy-start | bytes 1179652
  175.1 23.6 %copy-start.20 = (bf16[2,128,768]{2,1,0:T(8,128)(2,1)S(1)}, bf16[2,128,768]{2,1,0:T(8,128)(2,1)}, u32[]{:S(2)}) copy-start(bf16[2,128,768]{2,1,0:T(8,128)(2,1)} %copy-done.19) | copy-start | bytes 1179652
  175.1 7.5 %collective-permute-start.43 = (bf16[128,768]{1,0:T(8,128)(2,1)S(1)}, bf16[128,768]{1,0:T(8,128)(2,1)S(1)}, u32[]{:S(2)}, u32[]{:S(2)}) collective-permute-start(bf16[128,768]{1,0:T(8,128)(2,1)S(1)} %get-tuple-element.255), channel_id=1, source_target_pairs={{0,0},{2,2},{4,8},{6,10},{8,4},{10,6},{12,12},{14,14},{16,16},{18,... | collective-permute-start | bytes 589832 | tf_op jit(solution)/shard_map/ppermute | solution.py:944
  175.9 22.7 %collective-permute-start.44 = (bf16[128,768]{1,0:T(8,128)(2,1)S(1)}, bf16[128,768]{1,0:T(8,128)(2,1)S(1)}, u32[]{:S(2)}, u32[]{:S(2)}) collective-permute-start(bf16[128,768]{1,0:T(8,128)(2,1)S(1)} %get-tuple-element.256), channel_id=1, source_target_pairs={{0,2},{2,0},{4,10},{6,8},{8,6},{10,4},{12,14},{14,12},{16,18},{18,... | collective-permute-start | bytes 589832 | tf_op jit(solution)/shard_map/ppermute | solution.py:944
  182.6 16.1 %copy-start.18 = (bf16[2,128,768]{2,1,0:T(8,128)(2,1)S(1)}, bf16[2,128,768]{2,1,0:T(8,128)(2,1)}, u32[]{:S(2)}) copy-start(bf16[2,128,768]{2,1,0:T(8,128)(2,1)} %copy-done.17) | copy-start | bytes 1179652
  198.9 9.7 %collective-permute-start.45 = (bf16[64,1536]{1,0:T(8,128)(2,1)S(1)}, bf16[64,1536]{1,0:T(8,128)(2,1)S(1)}, u32[]{:S(2)}, u32[]{:S(2)}) collective-permute-start(bf16[64,1536]{1,0:T(8,128)(2,1)S(1)} %get-tuple-element.264), channel_id=1, source_target_pairs={{0,2},{2,4},{4,6},{6,0},{1,3},{3,5},{5,7},{7,1},{8,10},{10,12},{12... | collective-permute-start | bytes 589832 | tf_op jit(solution)/shard_map/ppermute | solution.py:970
  199.0 14.9 %collective-permute-start.46 = (bf16[64,1536]{1,0:T(8,128)(2,1)S(1)}, bf16[64,1536]{1,0:T(8,128)(2,1)S(1)}, u32[]{:S(2)}, u32[]{:S(2)}) collective-permute-start(bf16[64,1536]{1,0:T(8,128)(2,1)S(1)} %get-tuple-element.265), channel_id=1, source_target_pairs={{0,4},{2,6},{4,0},{6,2},{1,5},{3,7},{5,1},{7,3},{8,12},{10,14},{12... | collective-permute-start | bytes 589832 | tf_op jit(solution)/shard_map/ppermute | solution.py:970
  199.8 14.1 %collective-permute-start.47 = (bf16[64,1536]{1,0:T(8,128)(2,1)S(1)}, bf16[64,1536]{1,0:T(8,128)(2,1)S(1)}, u32[]{:S(2)}, u32[]{:S(2)}) collective-permute-start(bf16[64,1536]{1,0:T(8,128)(2,1)S(1)} %get-tuple-element.266), channel_id=1, source_target_pairs={{0,6},{2,0},{4,2},{6,4},{1,7},{3,1},{5,3},{7,5},{8,14},{10,8},{12,... | collective-permute-start | bytes 589832 | tf_op jit(solution)/shard_map/ppermute | solution.py:970
  202.8 11.1 %collective-permute-start.48 = (bf16[128,768]{1,0:T(8,128)(2,1)S(1)}, bf16[128,768]{1,0:T(8,128)(2,1)S(1)}, u32[]{:S(2)}, u32[]{:S(2)}) collective-permute-start(bf16[128,768]{1,0:T(8,128)(2,1)S(1)} %collective-permute-done.43), channel_id=1, source_target_pairs={{0,1},{1,0},{2,3},{3,2},{4,5},{5,4},{6,7},{7,6},{8,9},{9,8},{10,11... | collective-permute-start | bytes 589832 | tf_op jit(solution)/shard_map/ppermute | solution.py:929
  204.3 9.6 %collective-permute-start.49 = (bf16[128,768]{1,0:T(8,128)(2,1)S(1)}, bf16[128,768]{1,0:T(8,128)(2,1)S(1)}, u32[]{:S(2)}, u32[]{:S(2)}) collective-permute-start(bf16[128,768]{1,0:T(8,128)(2,1)S(1)} %collective-permute-done.44), channel_id=1, source_target_pairs={{0,1},{1,0},{2,3},{3,2},{4,5},{5,4},{6,7},{7,6},{8,9},{9,8},{10,11... | collective-permute-start | bytes 589832 | tf_op jit(solution)/shard_map/ppermute | solution.py:929
  214.1 9.5 %collective-permute-start.52 = (bf16[48,1536]{1,0:T(8,128)(2,1)S(1)}, bf16[48,1536]{1,0:T(8,128)(2,1)S(1)}, u32[]{:S(2)}, u32[]{:S(2)}) collective-permute-start(bf16[48,1536]{1,0:T(8,128)(2,1)S(1)} %get-tuple-element.276.a), channel_id=1, source_target_pairs={{0,6},{2,0},{4,2},{6,4},{1,7},{3,1},{5,3},{7,5},{8,14},{10,8},{12,... | collective-permute-start | bytes 442376 | tf_op jit(solution)/shard_map/ppermute | solution.py:970
  219.2 14.3 %collective-permute-start.51 = (bf16[48,1536]{1,0:T(8,128)(2,1)S(1)}, bf16[48,1536]{1,0:T(8,128)(2,1)S(1)}, u32[]{:S(2)}, u32[]{:S(2)}) collective-permute-start(bf16[48,1536]{1,0:T(8,128)(2,1)S(1)} %get-tuple-element.276.a), channel_id=1, source_target_pairs={{0,4},{2,6},{4,0},{6,2},{1,5},{3,7},{5,1},{7,3},{8,12},{10,14},{12... | collective-permute-start | bytes 442376 | tf_op jit(solution)/shard_map/ppermute | solution.py:970
  220.3 13.2 %collective-permute-start.50 = (bf16[48,1536]{1,0:T(8,128)(2,1)S(1)}, bf16[48,1536]{1,0:T(8,128)(2,1)S(1)}, u32[]{:S(2)}, u32[]{:S(2)}) collective-permute-start(bf16[48,1536]{1,0:T(8,128)(2,1)S(1)} %get-tuple-element.276.a), channel_id=1, source_target_pairs={{0,2},{2,4},{4,6},{6,0},{1,3},{3,5},{5,7},{7,1},{8,10},{10,12},{12... | collective-permute-start | bytes 442376 | tf_op jit(solution)/shard_map/ppermute | solution.py:970
  (24 other events, 98.1 us)

commit v4 on v3

--- a/solution.py
+++ b/solution.py
@@ -347,7 +347,7 @@
                 pl.BlockSpec((1, 2, rows), lambda g, info: (g, 0, 0)),
             ),
         ),
-        compiler_params=pltpu.CompilerParams(vmem_limit_bytes=48 << 20),
+        compiler_params=pltpu.CompilerParams(vmem_limit_bytes=32 << 20),
         cost_estimate=pl.CostEstimate(
             flops=4 * work, bytes_accessed=12 * rows * width, transcendentals=work // (2 * HEAD_DIM)
         ),
@@ -431,7 +431,7 @@
             ],
             out_specs=(narrow, wide, wide),
         ),
-        compiler_params=pltpu.CompilerParams(vmem_limit_bytes=48 << 20),
+        compiler_params=pltpu.CompilerParams(vmem_limit_bytes=32 << 20),
         cost_estimate=pl.CostEstimate(
             flops=10 * work, bytes_accessed=24 * rows * local, transcendentals=work // (2 * HEAD_DIM)
         ),
@@ -456,7 +456,7 @@
         in_specs=[fixed(a) for a in args],
         out_specs=tuple(fixed(s) for s in shapes),
         scratch_shapes=list(scratch),
-        compiler_params=pltpu.CompilerParams(vmem_limit_bytes=48 << 20),
+        compiler_params=pltpu.CompilerParams(vmem_limit_bytes=24 << 20),
         cost_estimate=pl.CostEstimate(flops=flops, bytes_accessed=moved, transcendentals=0),
     )(*args)
 
@@ -554,7 +554,7 @@
     up_bias_ref, down_bias_ref, pa, pb, pc, pd, da, db, dc, dd,
     mid_ref, normed_ref, feed_ref, hidden_ref, d_pre_ref, d_own_ref, d_peer_ref,
     part0_ref, part1_ref, out_ref, g_up_ref, g_down_ref,
-    outs, ups, downs, whole_mid, sems,
+    outs, ups, downs, whole_mid, sent, sems,
 ):
     rows, width = rows_ref.shape
     half = rows // 2
@@ -616,7 +616,9 @@
 
     grad = back(d_pre_ref, ups).astype(jnp.bfloat16)
     d_own_ref[...] = grad[:half]
-    d_peer_ref[...] = grad[half:]
+    sent[...] = grad[half:]
+    leaving = pltpu.make_async_copy(sent, d_peer_ref, sems.at[0, 0])
+    leaving.start()
     first = lax.axis_index("tensor") == 0
     share = back(hidden_ref, downs)
     share += jnp.where(first, down_bias_ref[...].astype(jnp.float32), 0.0)
@@ -626,6 +628,7 @@
         start = k * (half // 2)
         part[0] = share[start : start + half // 2]
         part[1] = share[half + start : half + start + half // 2]
+    leaving.wait()
 
 
 def middle_part(
@@ -637,6 +640,7 @@
     steps = 2
     small = (rows_low, own, peer, *top, gain, bias, out_bias, up_bias, down_bias)
     inside = pl.BlockSpec(memory_space=pltpu.VMEM)
+    outside = pl.BlockSpec(memory_space=pltpu.HBM)
     shapes = (
         full(rows // 2, width),
         low(rows, width),
@@ -657,12 +661,13 @@
         in_specs=[pl.BlockSpec(memory_space=pltpu.SMEM)]
         + [inside] * len(small)
         + [pl.BlockSpec(memory_space=pltpu.HBM)] * 8,
-        out_specs=(inside,) * len(shapes),
+        out_specs=tuple(outside if k == 6 else inside for k in range(len(shapes))),
         scratch_shapes=[
             pltpu.VMEM((width, width), jnp.bfloat16),
             pltpu.VMEM((steps, width, hidden // steps), jnp.bfloat16),
             pltpu.VMEM((steps, width, hidden // steps), jnp.bfloat16),
             pltpu.VMEM((rows, width), jnp.float32),
+            pltpu.VMEM((rows // 2, width), jnp.bfloat16),
             pltpu.SemaphoreType.DMA((1 + 2 * steps, 4)),
         ],
         compiler_params=pltpu.CompilerParams(vmem_limit_bytes=36 << 20),
@@ -706,7 +711,7 @@
             in_specs=[first, fixed(d_own), fixed(got), fixed(top[0]), fixed(top[1]), fixed(gain)],
             out_specs=tuple(fixed(s) for s in shapes),
         ),
-        compiler_params=pltpu.CompilerParams(vmem_limit_bytes=32 << 20),
+        compiler_params=pltpu.CompilerParams(vmem_limit_bytes=24 << 20),
         cost_estimate=pl.CostEstimate(
             flops=40 * half * width, bytes_accessed=4 << 20, transcendentals=half
         ),
@@ -775,7 +780,7 @@
         grid=(1,),
         in_specs=[top_half, fixed(own), fixed(got), fixed(gain), fixed(d_mid)],
         out_specs=(fixed(piece), fixed(piece)),
-        compiler_params=pltpu.CompilerParams(vmem_limit_bytes=32 << 20),
+        compiler_params=pltpu.CompilerParams(vmem_limit_bytes=24 << 20),
         cost_estimate=pl.CostEstimate(
             flops=20 * half * width, bytes_accessed=4 << 20, transcendentals=half
         ),
@@ -920,6 +925,53 @@
     return call_once(vectors_kernel, args, (full(8, up.shape[1]),), up.size)[0]
 
 
+def part_of(ref, index, count):
+    start = index * count
+    return ref[pl.ds(start if isinstance(start, int) else pl.multiple_of(start, count), count), :]
+
+
+def cut_kernel(*refs, bits):
+    plane = lax.axis_index("context")
+    outs = refs[2 * len(bits) :]
+    for k, bit in enumerate(bits):
+        left, right = refs[2 * k], refs[2 * k + 1]
+        index = plane % 2 if bit == 1 else plane // 2
+        count = left.shape[0] // 2
+        for out, half in ((outs[2 * k], index), (outs[2 * k + 1], 1 - index)):
+            out[...] = part_of(left, half, count) + part_of(right, half, count)
+
+
+def cut_sums(*pairs):
+    args = [array for left, right, _ in pairs for array in (left, right)]
+    shapes = [low(left.shape[0] // 2, left.shape[1]) for left, _, _ in pairs for _ in range(2)]
+    kernel = functools.partial(cut_kernel, bits=tuple(bit for _, _, bit in pairs))
+    return call_once(kernel, args, shapes, sum(a.size for a in args))
+
+
+def glue_kernel(mine_ref, theirs_ref, left_ref, right_ref, glued_ref, sum_ref):
+    second = lax.axis_index("context") // 2
+    count = mine_ref.shape[0]
+    for ref, index in ((mine_ref, second), (theirs_ref, 1 - second)):
+        glued_ref[pl.ds(pl.multiple_of(index * count, count), count), :] = ref[...]
+    sum_ref[...] = left_ref[...] + right_ref[...]
+
+
+def glue_and_add(mine, theirs, left, right):
+    shapes = (low(2 * mine.shape[0], mine.shape[1]), low(*left.shape))
+    return call_once(glue_kernel, (mine, theirs, left, right), shapes, left.size)
+
+
+def add_cut_kernel(a_ref, b_ref, left_ref, right_ref, sum_ref, keep_ref, send_ref):
+    sum_ref[...] = a_ref[...] + b_ref[...]
+    cut_kernel(left_ref, right_ref, keep_ref, send_ref, bits=(2,))
+
+
+def add_and_cut(a, b, left, right):
+    part = low(left.shape[0] // 2, left.shape[1])
+    shapes = (low(*a.shape), part, part)
+    return call_once(add_cut_kernel, (a, b, left, right), shapes, 2 * a.size)
+
+
 def exchange(value, bit):
     size = lax.axis_size("dp")
     return lax.ppermute(value, "dp", [(i, i ^ bit) for i in range(size)])
@@ -970,16 +1022,14 @@
     return lax.ppermute(value, "context", [(i, (i + step) % 4) for i in range(4)])
 
 
-def inward(value):
-    return lax.ppermute(value, "context", [(0, 1), (3, 2)])
-
-
-def across(value):
-    return lax.ppermute(value, "context", [(1, 2), (2, 1)])
-
-
-def outward(value):
-    return lax.ppermute(value, "context", [(1, 0), (2, 3)])
+def swap_planes(value, bit):
+    return lax.ppermute(value, "context", [(i, i ^ bit) for i in range(4)])
+
+
+def stack_rows(mine, theirs, second):
+    return jnp.where(
+        second, jnp.concatenate([theirs, mine], axis=0), jnp.concatenate([mine, theirs], axis=0)
+    )
 
 
 def per_device_planes(
@@ -1011,7 +1061,7 @@
     side = lax.axis_index("tensor")
     odd = plane % 2 == 1
     upper = side == 1
-    inner = (plane == 1) | (plane == 2)
+    upper_half = plane >= 2
     row = lambda vector: vector.reshape(1, -1)
 
     by_half = (2, 2, half, width)
@@ -1051,7 +1101,6 @@
     piece = jnp.where(quarter < 2, side, 1 - side)
     starts = (2 * core + (quarter % 2 ^ plane % 2)) * block + piece * half
     info = jnp.where(index < 8, starts, length)
-
     rows_low, normed_low, queries, pair_own, proj = enter(
         rows_parts, row(ln1_gain), row(ln1_bias), row(b_query), row(b_value), proj_blocks
     )
@@ -1096,16 +1145,13 @@
     )
 
     got = swap_tensor(d_peer)
-    share_0 = route(shares[0], 0, False)
     down_own, down_far, down_send = weight_grad((d_feed, hidden))
     up_own, up_far, up_send = weight_grad((normed_two, d_pre))
-    got, down_send, up_send, share_0, share_1 = together(
-        got, down_send, up_send, share_0, shares[1]
-    )
+    got, down_send, up_send, *shares = together(got, down_send, up_send, *shares)
 
     down_got = exchange(down_send, 1)
     d_middle, d_att, sums_two = turn(info, middle, d_own, got, top_parts[:2], row(ln2_gain))
-    d_att, down_got, up_send, share_1 = together(d_att, down_got, up_send, share_1)
+    d_att, down_got, up_send, *shares = together(d_att, down_got, up_send, *shares)
 
     shard = down_own.shape[0]
     columns = hidden.shape[1]
@@ -1113,37 +1159,41 @@
     got_1 = exchange(down_far + down_got[shard:], 2)
     down_own = down_own + down_got[:shard]
     up_got = exchange(up_send, 1)
+    share_0 = route(shares[0], 0, False)
+    up_own, up_far = up_own + up_got[:shard], up_far + up_got[shard:]
+    d_att_peer, got_1, up_own, up_far, share_0, share_1 = together(
+        d_att_peer, got_1, up_own, up_far, share_0, shares[1]
+    )
+
+    half_1, sent = cut_sums((down_own, got_1, 1))
+    got_1 = swap_planes(sent, 1)
+    got_2 = exchange(up_far, 2)
     share_1 = route(share_1, 1, False)
-    d_att_peer, got_1, up_got, share_1 = together(d_att_peer, got_1, up_got, share_1)
-
-    sum_1 = down_own + got_1
-    got_1 = inward(sum_1)
-    got_2 = exchange(up_far + up_got[shard:], 2)
-    up_own = up_own + up_got[:shard]
-    share_got = [swap_tensor(v) for v in (share_0, share_1)]
     d_queries, d_pair, d_send = attend_back(
         info, queries, pair_own, pair_other, mixed, d_att, d_att_peer, out_t, logs
     )
-    d_send, got_1, got_2, *share_got = together(d_send, got_1, got_2, *share_got)
+    d_send, got_1, got_2, share_0, share_1 = together(d_send, got_1, got_2, share_0, share_1)
+
 
     d_got = exchange(d_send, 1)
-    sum_1 = sum_1 + got_1
-    sum_2 = up_own + got_2
-    got_1 = across(sum_1)
-    got_2 = inward(sum_2)
+    quarter_1, sent_1, half_2, sent_2 = cut_sums((half_1, got_1, 2), (up_own, got_2, 1))
+    got_1 = swap_planes(sent_1, 2)
+    got_2 = swap_planes(sent_2, 1)
     d_proj, one_own, one_peer, sides, proj_bias = leave(
         rows_low, proj, d_queries, d_pair, d_got, sums_two
     )
     own, far, send = weight_grad((normed_low, d_proj), (d_att, d_att_peer, mixed))
-    one_peer, sides, send, got_1, got_2 = together(one_peer, sides, send, got_1, got_2)
-
-    send_got = exchange(send, 1)
+    share_got = [swap_tensor(share_0)]
+    one_peer, sides, send, got_1, got_2, *share_got = together(
+        one_peer, sides, send, got_1, got_2, *share_got
+    )
+
+    quarter_1, quarter_2, sent = add_and_cut(quarter_1, got_1, half_2, got_2)
+    got_1 = swap_planes(quarter_1, 2)
+    got_2 = swap_planes(sent, 2)
     sides_got = swap_tensor(sides)
     one_got = swap_tensor(one_peer)
-    sum_1 = sum_1 + got_1
-    sum_2 = sum_2 + got_2
-    got_1 = outward(sum_1)
-    got_2 = across(sum_2)
+    send_got = exchange(send, 1)
     send_got, one_got, got_1, got_2, sides_got = together(
         send_got, one_got, got_1, got_2, sides_got
     )
@@ -1151,30 +1201,33 @@
     vectors = gather_vectors(grad_up_bias, grad_down_bias, proj_bias, sides, sides_got)
     vectors_got = exchange(vectors, 1)
     input_rows = finish(rows_low, one_own, one_got, row(ln1_gain), d_middle)
-    *input_rows, vectors_got = together(*input_rows, vectors_got)
+    *input_rows, vectors_got, share_1 = together(*input_rows, vectors_got, share_1)
 
     packet, packet_far = merge(own, far, send_got, vectors, vectors_got)
     packet_got = exchange(packet_far, 2)
+    share_got.append(swap_tensor(share_1))
     in_near = [route(input_rows[step], step, False) for step in range(2)]
-    sum_2 = sum_2 + got_2
-    got_2 = outward(sum_2)
-    grad_down = jnp.where(inner, sum_1, got_1).astype(jnp.float32).T
-    packet_got, got_2, *pieces = together(packet_got, got_2, *in_near, *share_got)
+    half_1, quarter_2 = glue_and_add(quarter_1, got_1, quarter_2, got_2)
+    got_1 = swap_planes(half_1, 1)
+    got_2 = swap_planes(quarter_2, 2)
+    packet_got, got_1, got_2, *pieces = together(packet_got, got_1, got_2, *in_near, *share_got)
     in_near, share_got = pieces[:2], pieces[2:]
 
     quarters = spread(packet, packet_got, shard)
     arrived = [turn_planes(quarters[step], step) for step in range(1, 4)]
     in_far = [swap_tensor(v) for v in in_near]
-    grad_up = jnp.where(inner, sum_2, got_2).astype(jnp.float32)
+    half_2 = stack_rows(quarter_2, got_2, upper_half)
+    got_2 = swap_planes(half_2, 1)
+    grad_down = stack_rows(half_1, got_1, odd).astype(jnp.float32).T
     output = join_shares((share_0, share_1), share_got, odd, upper)
-    pieces = together(quarters[0], *arrived, *in_far)
+    *pieces, got_2 = together(quarters[0], *arrived, *in_far, got_2)
 
     in_far = pieces[4:]
     quarter, vectors = total(pieces[:4], shard // 4, vectors.shape[0])
     quarters = [quarter] + [turn_planes(quarter, step) for step in range(1, 4)]
     input_grad = join_out(in_near, in_far, odd, upper)
+    grad_up = stack_rows(half_2, got_2, odd).astype(jnp.float32)
     grad_query, grad_key, grad_value, grad_out = assemble(quarters)
-
     return (
         output.reshape(tokens.shape),
         input_grad.reshape(tokens.shape),

time: 236 us -> 222 us (0.941)
  starting transfers between devices: 67.8 us -> 55.3 us
  local copies, waits for them, and re-layouts: 10.5 us -> 7.54 us
    ppermute x8, waiting for transfers between devices: 26 us -> 11.6 us  [route(): return lax.ppermute(value, ('dp', 'context'), pairs)]
    ppermute x6 -> x8, starting transfers between devices: 13.5 us -> 7.5 us  [swap_planes(): return lax.ppermute(value, 'context', [(i, i ^ bit) for i in range(4)])]
    ppermute x6 -> x8, waiting for transfers between devices: 11.4 us -> 17.3 us  [swap_planes(): return lax.ppermute(value, 'context', [(i, i ^ bit) for i in range(4)])]
    ppermute x14, waiting for transfers between devices: 24.3 us -> 30.2 us  [swap_tensor(): return lax.ppermute(value, 'tensor', [(0, 1), (1, 0)])]
    ppermute x6, starting transfers between devices: 10.1 us -> 6.35 us  [turn_planes(): lax.ppermute(value, 'context', [(i, (i + step) % 4) for i in range(4)])]
    ppermute x19, waiting for transfers between devices: 24.2 us -> 27.3 us  [exchange(): return lax.ppermute(value, 'dp', [(i, i ^ bit) for i in range(size)])]
    unnamed x73 -> x65, local copies, waits for them, and re-layouts: 8.01 us -> 5.02 us
    ppermute x8, starting transfers between devices: 10.9 us -> 7.94 us  [route(): return lax.ppermute(value, ('dp', 'context'), pairs)]
  transfers between devices with their start and end apart: 53 -> 55, of which waited for: 21 -> 26; matrix products, arithmetic and copies ran while one was open for 4% -> 4% of each run, Pallas kernels for 12% -> 13%
where the time goes in v4:
time: 222 us
  waiting for transfers between devices  104 us (47%)
  starting transfers between devices  55.3 us (25%)
  Pallas kernels  42.8 us (19%)
  other arithmetic  9.32 us (4%)
  local copies, waits for them, and re-layouts  7.54 us (3%)
  between operations  2.72 us (1%)
    ppermute x14, waiting for transfers between devices, swap_tensor(): return lax.ppermute(value, 'tensor', [(0, 1), (1, 0)])  30.2 us
    ppermute x19, waiting for transfers between devices, exchange(): return lax.ppermute(value, 'dp', [(i, i ^ bit) for i in range(size)])  27.3 us
    ppermute x6, waiting for transfers between devices, turn_planes(): lax.ppermute(value, 'context', [(i, (i + step) % 4) for i in range(4)])  18 us
    ppermute x8, waiting for transfers between devices, swap_planes(): return lax.ppermute(value, 'context', [(i, i ^ bit) for i in range(4)])  17.3 us
    ppermute x19, starting transfers between devices, exchange(): return lax.ppermute(value, 'dp', [(i, i ^ bit) for i in range(size)])  17 us
    ppermute x14, starting transfers between devices, swap_tensor(): return lax.ppermute(value, 'tensor', [(0, 1), (1, 0)])  16.5 us
    ppermute x8, waiting for transfers between devices, route(): return lax.ppermute(value, ('dp', 'context'), pairs)  11.6 us
    pallas_call x1, Pallas kernels, attend_back(): pl.pallas_call(attend_back_kernel, out_shape=tuple((jax.ShapeDtypeStruct(...  11.2 us
  transfers between devices with their start and end apart: 55, of which 26 were waited for; matrix products, arithmetic and copies ran while one was open for 4% of the time, Pallas kernels for 13%

profile of v4, /device:TPU:0, one launch (start us, length us, event | category | flops | bytes accessed | tf_op | source)
XLA Modules:
  0.0 222.0 jit_solution(12121085577971274053)
XLA Ops:
  0.8 1.4 slice_select_fusion.1
  2.9 2.6 %collective-permute-start.2 = (bf16[192,1152]{1,0:T(8,128)(2,1)S(1)}, bf16[192,1152]{1,0:T(8,128)(2,1)S(1)}, u32[]{:S(2)}, u32[]{:S(2)}) collective-permute-start(bf16[192,1152]{1,0:T(8,128)(2,1)S(1)} %constant_dynamic-update-slice_fusion.a), channel_id=1, source_target_pairs={{0,16},{8,24},{16,0},{24,8},{1,17},{9,25},{17,1},{25,9},{2,18},{10... | collective-permute-start | bytes 1327112 | tf_op jit(solution)/shard_map/ppermute | solution.py:977
  6.1 1.6 collective-permute-start.1
  7.8 3.5 %collective-permute-start.5 = (s32[2]{0:T(128)S(1)}, s32[2]{0:T(128)S(1)}, u32[]{:S(2)}, u32[]{:S(2)}) collective-permute-start(s32[2]{0:T(128)S(1)} %copy-done.30), channel_id=1, source_target_pairs={{0,8},{8,0},{16,24},{24,16},{1,9},{9,1},{17,25},{25,17},{2,10},{10... | collective-permute-start | bytes 32 | tf_op jit(solution)/shard_map/ppermute | solution.py:977
  12.1 1.5 collective-permute-start.4
  13.7 4.5 %collective-permute-done.4 = bf16[192,384]{1,0:T(8,128)(2,1)S(1)} collective-permute-done((bf16[192,384]{1,0:T(8,128)(2,1)S(1)}, bf16[192,384]{1,0:T(8,128)(2,1)S(1)}, u32[]{:S(2)}, u32[]{:S(2)}) %collective-permute-start.4) | collective-permute-done | bytes 147488 | tf_op jit(solution)/shard_map/ppermute | solution.py:981
  18.1 1.6 collective-permute-start.6
  21.0 1.7 collective-permute-start.11
  22.8 3.3 %collective-permute-done.6.peer0 = bf16[128,768]{1,0:T(8,128)(2,1)S(1)} collective-permute-done((bf16[128,768]{1,0:T(8,128)(2,1)S(1)}, bf16[128,768]{1,0:T(8,128)(2,1)S(1)}, u32[]{:S(2)}, u32[]{:S(2)}) %collective-permute-start.6) | collective-permute-done | bytes 196640 | tf_op jit(solution)/shard_map/ppermute | solution.py:981
  26.8 2.1 collective-permute-done.7.peer1
  29.6 6.6 %collective-permute-done.9.dc = bf16[192,1536]{1,0:T(8,128)(2,1)} collective-permute-done((bf16[192,1536]{1,0:T(8,128)(2,1)S(1)}, bf16[192,1536]{1,0:T(8,128)(2,1)}, u32[]{:S(2)}, u32[]{:S(2)}) %collective-permute-start.9) | collective-permute-done | bytes 589856 | tf_op jit(solution)/shard_map/ppermute | solution.py:977
  36.2 2.5 %shard_map.305 = (bf16[512,768]{1,0:T(8,128)(2,1)S(1)}, bf16[512,768]{1,0:T(8,128)(2,1)S(1)}, bf16[512,384]{1,0:T(8,128)(2,1)S(1)}, bf16[512,768]{1,0:T(8,128)(2,1)}, bf16[768,1152]{1,0:T(8,128)(2,1)S(1)}) custom-call(bf16[128,768]{1,0:T(8,128)(2,1)S(1)} %collective-permute-done.own0, bf16[128,768]{1,0:T(8,128)(2,1)S(1)} %collective-permute-done.1.own1, ...), custom_call_target="tpu_custom_call" | custom-call | flops 905969664 | bytes 7082496 | tf_op jit(solution)/shard_map/pallas_call | solution.py:452
  42.5 1.6 collective-permute-start.13
  45.5 1.0 copy-done.9
  46.5 8.1 %shard_map.306 = (bf16[512,384]{1,0:T(8,128)(2,1)S(1)}, f32[3,2,512]{2,1,0:T(2,128)S(1)}) custom-call(s32[9]{0:T(128)S(1)} %compare_select_fusion.4.info, bf16[512,384]{1,0:T(8,128)(2,1)S(1)} %copy-done.9, bf16[512,768]{1,0:T(8,128)(2,1)} %get-tuple-element.189.own_ref, bf16[512,768]{1,0:T(8,128)(2,1)} %collective-permute-done.12.other_ref), custom_call_target="tpu_custom_call" | custom-call | flops 3221225472 | bytes 2359296 | tf_op jit(solution)/shard_map/pallas_call | solution.py:331
  55.3 1.5 collective-permute-start.15
  56.8 9.1 %collective-permute-done.17.pc = bf16[192,2304]{1,0:T(8,128)(2,1)S(1)} collective-permute-done((bf16[192,2304]{1,0:T(8,128)(2,1)S(1)}, bf16[192,2304]{1,0:T(8,128)(2,1)S(1)}, u32[]{:S(2)}, u32[]{:S(2)}) %collective-permute-start.17) | collective-permute-done | bytes 884768 | tf_op jit(solution)/shard_map/ppermute | solution.py:977
  67.0 2.3 %collective-permute-done.20.pd = bf16[192,2304]{1,0:T(8,128)(2,1)S(1)} collective-permute-done((bf16[192,2304]{1,0:T(8,128)(2,1)S(1)}, bf16[192,2304]{1,0:T(8,128)(2,1)S(1)}, u32[]{:S(2)}, u32[]{:S(2)}) %collective-permute-start.20) | collective-permute-done | bytes 884768 | tf_op jit(solution)/shard_map/ppermute | solution.py:977
  69.3 10.8 %shard_map.307 = (f32[256,768]{1,0:T(8,128)S(1)}, bf16[512,768]{1,0:T(8,128)(2,1)S(1)}, bf16[512,768]{1,0:T(8,128)(2,1)S(1)}, bf16[512,1536]{1,0:T(8,128)(2,1)S(...) custom-call(s32[9]{0:T(128)S(1)} %compare_select_fusion.4.info, ...), custom_call_target="tpu_custom_call" | custom-call | flops 4831838208 | bytes 20971520 | tf_op jit(solution)/shard_map/pallas_call | solution.py:658
  80.0 1.6 collective-permute-start.21
  81.6 1.6 shard_map.308
  83.2 1.6 shard_map.309
  84.8 6.4 %collective-permute-done.21.got_ref = bf16[256,768]{1,0:T(8,128)(2,1)S(1)} collective-permute-done((bf16[256,768]{1,0:T(8,128)(2,1)S(1)}, bf16[256,768]{1,0:T(8,128)(2,1)S(1)}, u32[]{:S(2)}, u32[]{:S(2)}) %collective-permute-start.21) | collective-permute-done | bytes 393248 | tf_op jit(solution)/shard_map/ppermute | solution.py:981
  91.3 1.3 shard_map.310
  92.6 1.5 collective-permute-done.22
  94.4 1.2 collective-permute-start.24
  96.3 1.6 collective-permute-start.23
  98.0 6.1 %collective-permute-done.23.d_peer_ref.refs_3_ = bf16[256,768]{1,0:T(8,128)(2,1)S(1)} collective-permute-done((bf16[256,768]{1,0:T(8,128)(2,1)S(1)}, bf16[256,768]{1,0:T(8,128)(2,1)S(1)}, u32[]{:S(2)}, u32[]{:S(2)}) %collective-permute-start.23) | collective-permute-done | bytes 393248 | tf_op jit(solution)/shard_map/ppermute | solution.py:981
  104.1 5.9 %collective-permute-done.24.refs_1_ = bf16[192,1536]{1,0:T(8,128)(2,1)S(1)} collective-permute-done((bf16[192,1536]{1,0:T(8,128)(2,1)S(1)}, bf16[192,1536]{1,0:T(8,128)(2,1)S(1)}, u32[]{:S(2)}, u32[]{:S(2)}) %collective-permute-start.24) | collective-permute-done | bytes 589856 | tf_op jit(solution)/shard_map/ppermute | solution.py:977
  111.0 1.2 collective-permute-start.29
  112.2 1.1 collective-permute-start.28
  113.3 11.2 %shard_map.311 = (bf16[512,384]{1,0:T(8,128)(2,1)S(1)}, bf16[512,768]{1,0:T(8,128)(2,1)S(1)}, bf16[512,768]{1,0:T(8,128)(2,1)S(1)}) custom-call(s32[9]{0:T(128)S(1)} %compare_select_fusion.4.info, bf16[512,384]{1,0:T(8,128)(2,1)S(1)} %copy-done.10, bf16[512,768]{1,0:T(8,128)(2,1)} %get-tuple-element.189.own_ref, ...), custom_call_target="tpu_custom_call" | custom-call | flops 8053063680 | bytes 4718592 | tf_op jit(solution)/shard_map/pallas_call | solution.py:413
  124.5 1.3 collective-permute-done.29
  126.2 3.9 %collective-permute-start.30 = (bf16[512,768]{1,0:T(8,128)(2,1)S(1)}, bf16[512,768]{1,0:T(8,128)(2,1)S(1)}, u32[]{:S(2)}, u32[]{:S(2)}) collective-permute-start(bf16[512,768]{1,0:T(8,128)(2,1)S(1)} %get-tuple-element.247), channel_id=1, source_target_pairs={{0,8},{8,0},{16,24},{24,16},{1,9},{9,1},{17,25},{25,17},{2,10},{10... | collective-permute-start | bytes 2359304 | tf_op jit(solution)/shard_map/ppermute | solution.py:977
  130.0 1.5 collective-permute-start.33
  132.6 1.8 shard_map.313
  134.3 1.8 shard_map.314
  136.2 5.2 %collective-permute-done.31.b_ref = bf16[48,1536]{1,0:T(8,128)(2,1)S(1)} collective-permute-done((bf16[48,1536]{1,0:T(8,128)(2,1)S(1)}, bf16[48,1536]{1,0:T(8,128)(2,1)S(1)}, u32[]{:S(2)}, u32[]{:S(2)}) %collective-permute-start.31) | collective-permute-done | bytes 147488 | tf_op jit(solution)/shard_map/ppermute | solution.py:1026
  141.3 2.2 collective-permute-done.32.right_ref
  144.2 1.3 collective-permute-start.37
  145.5 1.7 collective-permute-start.36
  147.1 1.5 collective-permute-start.38
  148.7 6.9 %collective-permute-done.38.theirs_ref = f32[5,768]{1,0:T(8,128)S(1)} collective-permute-done((f32[5,768]{1,0:T(8,128)S(1)}, f32[5,768]{1,0:T(8,128)S(1)}, u32[]{:S(2)}, u32[]{:S(2)}) %collective-permute-start.38) | collective-permute-done | bytes 15392 | tf_op jit(solution)/shard_map/ppermute | solution.py:981
  155.6 1.9 collective-permute-done.37.right_ref
  157.5 3.0 %collective-permute-done.36.theirs_ref = bf16[48,1536]{1,0:T(8,128)(2,1)S(1)} collective-permute-done((bf16[48,1536]{1,0:T(8,128)(2,1)S(1)}, bf16[48,1536]{1,0:T(8,128)(2,1)S(1)}, u32[]{:S(2)}, u32[]{:S(2)}) %collective-permute-start.36) | collective-permute-done | bytes 147488 | tf_op jit(solution)/shard_map/ppermute | solution.py:1026
  162.0 1.6 collective-permute-start.40
  163.5 1.5 collective-permute-start.45
  166.0 1.3 collective-permute-start.43
  167.4 5.0 %collective-permute-done.42 = bf16[48,1536]{1,0:T(8,128)(2,1)S(1)} collective-permute-done((bf16[48,1536]{1,0:T(8,128)(2,1)S(1)}, bf16[48,1536]{1,0:T(8,128)(2,1)S(1)}, u32[]{:S(2)}, u32[]{:S(2)}) %collective-permute-start.42) | collective-permute-done | bytes 147488 | tf_op jit(solution)/shard_map/ppermute | solution.py:1026
  173.0 10.3 %collective-permute-done.44 = bf16[128,768]{1,0:T(8,128)(2,1)} collective-permute-done((bf16[128,768]{1,0:T(8,128)(2,1)S(1)}, bf16[128,768]{1,0:T(8,128)(2,1)}, u32[]{:S(2)}, u32[]{:S(2)}) %collective-permute-start.44) | collective-permute-done | bytes 196640 | tf_op jit(solution)/shard_map/ppermute | solution.py:996
  183.4 1.1 fusion.1
  184.6 2.6 %collective-permute-start.47 = (bf16[64,1536]{1,0:T(8,128)(2,1)S(1)}, bf16[64,1536]{1,0:T(8,128)(2,1)S(1)}, u32[]{:S(2)}, u32[]{:S(2)}) collective-permute-start(bf16[64,1536]{1,0:T(8,128)(2,1)S(1)} %get-tuple-element.300), channel_id=1, source_target_pairs={{0,4},{2,6},{4,0},{6,2},{1,5},{3,7},{5,1},{7,3},{8,12},{10,14},{12... | collective-permute-start | bytes 589832 | tf_op jit(solution)/shard_map/ppermute | solution.py:1022
  187.3 1.8 collective-permute-start.51
  189.1 2.2 convert_bitcast_fusion
  192.1 2.2 collective-permute-done.46.refs_1_
  194.8 1.3 maximum_select_fusion.5
  196.2 4.4 %collective-permute-done.47.refs_2_ = bf16[64,1536]{1,0:T(8,128)(2,1)S(1)} collective-permute-done((bf16[64,1536]{1,0:T(8,128)(2,1)S(1)}, bf16[64,1536]{1,0:T(8,128)(2,1)S(1)}, u32[]{:S(2)}, u32[]{:S(2)}) %collective-permute-start.47) | collective-permute-done | bytes 196640 | tf_op jit(solution)/shard_map/ppermute | solution.py:1022
  200.6 5.3 %collective-permute-done.48.refs_3_ = bf16[64,1536]{1,0:T(8,128)(2,1)S(1)} collective-permute-done((bf16[64,1536]{1,0:T(8,128)(2,1)S(1)}, bf16[64,1536]{1,0:T(8,128)(2,1)S(1)}, u32[]{:S(2)}, u32[]{:S(2)}) %collective-permute-start.48) | collective-permute-done | bytes 196640 | tf_op jit(solution)/shard_map/ppermute | solution.py:1022
  206.1 1.1 collective-permute-start.54
  207.6 1.9 collective-permute-start.52
  210.2 1.1 fusion
  211.4 1.4 reverse_select_fusion
  214.1 6.1 %collective-permute-done.53.c = bf16[48,1536]{1,0:T(8,128)(2,1)S(1)} collective-permute-done((bf16[48,1536]{1,0:T(8,128)(2,1)S(1)}, bf16[48,1536]{1,0:T(8,128)(2,1)S(1)}, u32[]{:S(2)}, u32[]{:S(2)}) %collective-permute-start.53) | collective-permute-done | bytes 147488 | tf_op jit(solution)/shard_map/ppermute | solution.py:1022
  220.2 1.0 shard_map.323
  (162 shorter events, 22.3 us)
Async XLA Ops:
  0.8 19.5 %copy-start.11 = (bf16[2,256,768]{2,1,0:T(8,128)(2,1)S(1)}, bf16[2,256,768]{2,1,0:T(8,128)(2,1)}, u32[]{:S(2)}) copy-start(bf16[2,256,768]{2,1,0:T(8,128)(2,1)} %param.35) | copy-start | bytes 2359300
  2.3 24.4 %copy-start.12 = (bf16[192,1536]{1,0:T(8,128)(2,1)S(1)}, bf16[192,1536]{1,0:T(8,128)(2,1)}, u32[]{:S(2)}) copy-start(bf16[192,1536]{1,0:T(8,128)(2,1)} %param.31) | copy-start | bytes 1769476
  2.4 15.8 %collective-permute-start.3 = (bf16[192,1152]{1,0:T(8,128)(2,1)S(1)}, bf16[192,1152]{1,0:T(8,128)(2,1)S(1)}, u32[]{:S(2)}, u32[]{:S(2)}) collective-permute-start(bf16[192,1152]{1,0:T(8,128)(2,1)S(1)} %constant_dynamic-update-slice_fusion.a), channel_id=1, source_target_pairs={{0,8},{8,0},{16,24},{24,16},{1,9},{9,1},{17,25},{25,17},{2,10},{10... | collective-permute-start | bytes 1327112 | tf_op jit(solution)/shard_map/ppermute | solution.py:977
  2.9 15.3 %collective-permute-start.2 = (bf16[192,1152]{1,0:T(8,128)(2,1)S(1)}, bf16[192,1152]{1,0:T(8,128)(2,1)S(1)}, u32[]{:S(2)}, u32[]{:S(2)}) collective-permute-start(bf16[192,1152]{1,0:T(8,128)(2,1)S(1)} %constant_dynamic-update-slice_fusion.a), channel_id=1, source_target_pairs={{0,16},{8,24},{16,0},{24,8},{1,17},{9,25},{17,1},{25,9},{2,18},{10... | collective-permute-start | bytes 1327112 | tf_op jit(solution)/shard_map/ppermute | solution.py:977
  5.5 12.7 %collective-permute-start = (bf16[128,768]{1,0:T(8,128)(2,1)S(1)}, bf16[128,768]{1,0:T(8,128)(2,1)S(1)}, u32[]{:S(2)}, u32[]{:S(2)}) collective-permute-start(bf16[128,768]{1,0:T(8,128)(2,1)S(1)} %get-tuple-element.168), channel_id=1, source_target_pairs={{0,0},{2,2},{8,4},{10,6},{4,8},{6,10},{12,12},{14,14},{16,16},{18,... | collective-permute-start | bytes 589832 | tf_op jit(solution)/shard_map/ppermute | solution.py:996
  6.1 12.0 %collective-permute-start.1 = (bf16[128,768]{1,0:T(8,128)(2,1)S(1)}, bf16[128,768]{1,0:T(8,128)(2,1)S(1)}, u32[]{:S(2)}, u32[]{:S(2)}) collective-permute-start(bf16[128,768]{1,0:T(8,128)(2,1)S(1)} %get-tuple-element.169), channel_id=1, source_target_pairs={{2,0},{0,2},{10,4},{8,6},{6,8},{4,10},{14,12},{12,14},{18,16},{16,... | collective-permute-start | bytes 589832 | tf_op jit(solution)/shard_map/ppermute | solution.py:996
  7.8 4.3 %collective-permute-start.5 = (s32[2]{0:T(128)S(1)}, s32[2]{0:T(128)S(1)}, u32[]{:S(2)}, u32[]{:S(2)}) collective-permute-start(s32[2]{0:T(128)S(1)} %copy-done.30), channel_id=1, source_target_pairs={{0,8},{8,0},{16,24},{24,16},{1,9},{9,1},{17,25},{25,17},{2,10},{10... | collective-permute-start | bytes 32 | tf_op jit(solution)/shard_map/ppermute | solution.py:977
  12.1 6.1 %collective-permute-start.4 = (bf16[192,384]{1,0:T(8,128)(2,1)S(1)}, bf16[192,384]{1,0:T(8,128)(2,1)S(1)}, u32[]{:S(2)}, u32[]{:S(2)}) collective-permute-start(bf16[192,384]{1,0:T(8,128)(2,1)S(1)} %bitcast.35), channel_id=1, source_target_pairs={{0,1},{1,0},{2,3},{3,2},{4,5},{5,4},{6,7},{7,6},{8,9},{9,8},{10,11... | collective-permute-start | bytes 442376 | tf_op jit(solution)/shard_map/ppermute | solution.py:981
  18.1 7.9 %collective-permute-start.6 = (bf16[128,768]{1,0:T(8,128)(2,1)S(1)}, bf16[128,768]{1,0:T(8,128)(2,1)S(1)}, u32[]{:S(2)}, u32[]{:S(2)}) collective-permute-start(bf16[128,768]{1,0:T(8,128)(2,1)S(1)} %collective-permute-done.own0), channel_id=1, source_target_pairs={{0,1},{1,0},{2,3},{3,2},{4,5},{5,4},{6,7},{7,6},{8,9},{9,8},{10,11... | collective-permute-start | bytes 589832 | tf_op jit(solution)/shard_map/ppermute | solution.py:981
  19.7 9.1 %collective-permute-start.7 = (bf16[128,768]{1,0:T(8,128)(2,1)S(1)}, bf16[128,768]{1,0:T(8,128)(2,1)S(1)}, u32[]{:S(2)}, u32[]{:S(2)}) collective-permute-start(bf16[128,768]{1,0:T(8,128)(2,1)S(1)} %collective-permute-done.1.own1), channel_id=1, source_target_pairs={{0,1},{1,0},{2,3},{3,2},{4,5},{5,4},{6,7},{7,6},{8,9},{9,8},{10,11... | collective-permute-start | bytes 589832 | tf_op jit(solution)/shard_map/ppermute | solution.py:981
  20.3 8.6 %collective-permute-start.8 = (bf16[192,1152]{1,0:T(8,128)(2,1)S(1)}, bf16[192,1152]{1,0:T(8,128)(2,1)S(1)}, u32[]{:S(2)}, u32[]{:S(2)}) collective-permute-start(bf16[192,1152]{1,0:T(8,128)(2,1)S(1)} %collective-permute-done.2.c), channel_id=1, source_target_pairs={{0,8},{8,0},{16,24},{24,16},{1,9},{9,1},{17,25},{25,17},{2,10},{10... | collective-permute-start | bytes 1327112 | tf_op jit(solution)/shard_map/ppermute | solution.py:977
  20.4 15.8 %collective-permute-start.9 = (bf16[192,1536]{1,0:T(8,128)(2,1)S(1)}, bf16[192,1536]{1,0:T(8,128)(2,1)}, u32[]{:S(2)}, u32[]{:S(2)}) collective-permute-start(bf16[192,1536]{1,0:T(8,128)(2,1)S(1)} %bitcast.26), channel_id=1, source_target_pairs={{0,16},{8,24},{16,0},{24,8},{1,17},{9,25},{17,1},{25,9},{2,18},{10... | collective-permute-start | bytes 1769480 | tf_op jit(solution)/shard_map/ppermute | solution.py:977
  21.0 7.8 %collective-permute-start.11 = (bf16[128,768]{1,0:T(8,128)(2,1)S(1)}, bf16[128,768]{1,0:T(8,128)(2,1)S(1)}, u32[]{:S(2)}, u32[]{:S(2)}) collective-permute-start(bf16[128,768]{1,0:T(8,128)(2,1)S(1)} %get-tuple-element.348), channel_id=1, source_target_pairs={{2,0},{0,2},{10,4},{8,6},{6,8},{4,10},{14,12},{12,14},{18,16},{16,... | collective-permute-start | bytes 589832 | tf_op jit(solution)/shard_map/ppermute | solution.py:996
  26.0 2.8 %collective-permute-start.10 = (bf16[128,768]{1,0:T(8,128)(2,1)S(1)}, bf16[128,768]{1,0:T(8,128)(2,1)S(1)}, u32[]{:S(2)}, u32[]{:S(2)}) collective-permute-start(bf16[128,768]{1,0:T(8,128)(2,1)S(1)} %get-tuple-element.349), channel_id=1, source_target_pairs={{0,0},{2,2},{8,4},{10,6},{4,8},{6,10},{12,12},{14,14},{16,16},{18,... | collective-permute-start | bytes 589832 | tf_op jit(solution)/shard_map/ppermute | solution.py:996
  40.4 5.1 %collective-permute-start.12 = (bf16[512,768]{1,0:T(8,128)(2,1)}, bf16[512,768]{1,0:T(8,128)(2,1)}, u32[]{:S(2)}, u32[]{:S(2)}) collective-permute-start(bf16[512,768]{1,0:T(8,128)(2,1)} %get-tuple-element.189.own_ref), channel_id=1, source_target_pairs={{0,8},{8,0},{16,24},{24,16},{1,9},{9,1},{17,25},{25,17},{2,10},{10... | collective-permute-start | bytes 2359304 | tf_op jit(solution)/shard_map/ppermute | solution.py:977
  42.5 12.1 %collective-permute-start.13 = (bf16[128,768]{1,0:T(8,128)(2,1)}, bf16[128,768]{1,0:T(8,128)(2,1)S(1)}, u32[]{:S(2)}, u32[]{:S(2)}) collective-permute-start(bf16[128,768]{1,0:T(8,128)(2,1)} %copy-done.2), channel_id=1, source_target_pairs={{0,1},{1,0},{2,3},{3,2},{4,5},{5,4},{6,7},{7,6},{8,9},{9,8},{10,11... | collective-permute-start | bytes 589832 | tf_op jit(solution)/shard_map/ppermute | solution.py:981
  44.0 10.6 %collective-permute-start.14 = (bf16[128,768]{1,0:T(8,128)(2,1)}, bf16[128,768]{1,0:T(8,128)(2,1)S(1)}, u32[]{:S(2)}, u32[]{:S(2)}) collective-permute-start(bf16[128,768]{1,0:T(8,128)(2,1)} %copy-done), channel_id=1, source_target_pairs={{0,1},{1,0},{2,3},{3,2},{4,5},{5,4},{6,7},{7,6},{8,9},{9,8},{10,11... | collective-permute-start | bytes 589832 | tf_op jit(solution)/shard_map/ppermute | solution.py:981
  44.6 21.3 %collective-permute-start.17 = (bf16[192,2304]{1,0:T(8,128)(2,1)S(1)}, bf16[192,2304]{1,0:T(8,128)(2,1)S(1)}, u32[]{:S(2)}, u32[]{:S(2)}) collective-permute-start(bf16[192,2304]{1,0:T(8,128)(2,1)S(1)} %pad_maximum_fusion.pa), channel_id=1, source_target_pairs={{0,16},{8,24},{16,0},{24,8},{1,17},{9,25},{17,1},{25,9},{2,18},{10... | collective-permute-start | bytes 2654216 | tf_op jit(solution)/shard_map/ppermute | solution.py:977
  46.5 20.4 %copy-start.24 = (bf16[768]{0:T(1024)(128)(2,1)S(1)}, bf16[768]{0:T(1024)(128)(2,1)}, u32[]{:S(2)}) copy-start(bf16[768]{0:T(1024)(128)(2,1)} %param.29) | copy-start | bytes 4612
  46.5 20.4 %copy-start.25 = (bf16[768]{0:T(1024)(128)(2,1)S(1)}, bf16[768]{0:T(1024)(128)(2,1)}, u32[]{:S(2)}) copy-start(bf16[768]{0:T(1024)(128)(2,1)} %param.28) | copy-start | bytes 4612
  46.5 20.4 %copy-start.26 = (bf16[768]{0:T(1024)(128)(2,1)S(1)}, bf16[768]{0:T(1024)(128)(2,1)}, u32[]{:S(2)}) copy-start(bf16[768]{0:T(1024)(128)(2,1)} %param.30) | copy-start | bytes 4612
  46.5 20.5 %copy-start.27 = (bf16[768]{0:T(1024)(128)(2,1)S(1)}, bf16[768]{0:T(1024)(128)(2,1)}, u32[]{:S(2)}) copy-start(bf16[768]{0:T(1024)(128)(2,1)} %param.34) | copy-start | bytes 4612
  46.5 20.5 %copy-start.21 = (bf16[1536]{0:T(1024)(128)(2,1)S(1)}, bf16[1536]{0:T(1024)(128)(2,1)}, u32[]{:S(2)}) copy-start(bf16[1536]{0:T(1024)(128)(2,1)} %param.32) | copy-start | bytes 9220
  46.5 22.8 %copy-start.1 = (bf16[128,768]{1,0:T(8,128)(2,1)S(1)}, bf16[128,768]{1,0:T(8,128)(2,1)}, u32[]{:S(2)}) copy-start(bf16[128,768]{1,0:T(8,128)(2,1)} %copy-done) | copy-start | bytes 589828
  46.5 22.8 %copy-start.3 = (bf16[128,768]{1,0:T(8,128)(2,1)S(1)}, bf16[128,768]{1,0:T(8,128)(2,1)}, u32[]{:S(2)}) copy-start(bf16[128,768]{1,0:T(8,128)(2,1)} %copy-done.2) | copy-start | bytes 589828
  54.6 12.1 %collective-permute-start.16 = (bf16[192,2304]{1,0:T(8,128)(2,1)S(1)}, bf16[192,2304]{1,0:T(8,128)(2,1)S(1)}, u32[]{:S(2)}, u32[]{:S(2)}) collective-permute-start(bf16[192,2304]{1,0:T(8,128)(2,1)S(1)} %pad_maximum_fusion.pa), channel_id=1, source_target_pairs={{0,8},{8,0},{16,24},{24,16},{1,9},{9,1},{17,25},{25,17},{2,10},{10... | collective-permute-start | bytes 2654216 | tf_op jit(solution)/shard_map/ppermute | solution.py:977
  54.7 12.0 %collective-permute-start.18 = (bf16[192,1536]{1,0:T(8,128)(2,1)S(1)}, bf16[192,1536]{1,0:T(8,128)(2,1)S(1)}, u32[]{:S(2)}, u32[]{:S(2)}) collective-permute-start(bf16[192,1536]{1,0:T(8,128)(2,1)S(1)} %bitcast.27), channel_id=1, source_target_pairs={{0,8},{8,0},{16,24},{24,16},{1,9},{9,1},{17,25},{25,17},{2,10},{10... | collective-permute-start | bytes 1769480 | tf_op jit(solution)/shard_map/ppermute | solution.py:977
  55.2 11.6 %collective-permute-start.19 = (bf16[192,1536]{1,0:T(8,128)(2,1)}, bf16[192,1536]{1,0:T(8,128)(2,1)S(1)}, u32[]{:S(2)}, u32[]{:S(2)}) collective-permute-start(bf16[192,1536]{1,0:T(8,128)(2,1)} %collective-permute-done.9.dc), channel_id=1, source_target_pairs={{0,8},{8,0},{16,24},{24,16},{1,9},{9,1},{17,25},{25,17},{2,10},{10... | collective-permute-start | bytes 1769480 | tf_op jit(solution)/shard_map/ppermute | solution.py:977
  55.3 11.5 %collective-permute-start.15 = (bf16[512,384]{1,0:T(8,128)(2,1)S(1)}, bf16[512,384]{1,0:T(8,128)(2,1)S(1)}, u32[]{:S(2)}, u32[]{:S(2)}) collective-permute-start(bf16[512,384]{1,0:T(8,128)(2,1)S(1)} %get-tuple-element.195.own_ref.out_ref.refs_4_), channel_id=1, source_target_pairs={{0,1},{1,0},{2,3},{3,2},{4,5},{5,4},{6,7},{7,6},{8,9},{9,8},{10,11... | collective-permute-start | bytes 1179656 | tf_op jit(solution)/shard_map/ppermute | solution.py:981
  66.8 2.5 %collective-permute-start.20 = (bf16[192,2304]{1,0:T(8,128)(2,1)S(1)}, bf16[192,2304]{1,0:T(8,128)(2,1)S(1)}, u32[]{:S(2)}, u32[]{:S(2)}) collective-permute-start(bf16[192,2304]{1,0:T(8,128)(2,1)S(1)} %collective-permute-done.17.pc), channel_id=1, source_target_pairs={{0,8},{8,0},{16,24},{24,16},{1,9},{9,1},{17,25},{25,17},{2,10},{10... | collective-permute-start | bytes 2654216 | tf_op jit(solution)/shard_map/ppermute | solution.py:977
  80.0 11.2 %collective-permute-start.21 = (bf16[256,768]{1,0:T(8,128)(2,1)S(1)}, bf16[256,768]{1,0:T(8,128)(2,1)S(1)}, u32[]{:S(2)}, u32[]{:S(2)}) collective-permute-start(bf16[256,768]{1,0:T(8,128)(2,1)S(1)} %get-tuple-element.212), channel_id=1, source_target_pairs={{0,1},{1,0},{2,3},{3,2},{4,5},{5,4},{6,7},{7,6},{8,9},{9,8},{10,11... | collective-permute-start | bytes 1179656 | tf_op jit(solution)/shard_map/ppermute | solution.py:981
  91.3 2.8 %collective-permute-start.22 = (bf16[384,1536]{1,0:T(8,128)(2,1)S(1)}, bf16[384,1536]{1,0:T(8,128)(2,1)S(1)}, u32[]{:S(2)}, u32[]{:S(2)}) collective-permute-start(bf16[384,1536]{1,0:T(8,128)(2,1)S(1)} %get-tuple-element.223), channel_id=1, source_target_pairs={{0,8},{8,0},{16,24},{24,16},{1,9},{9,1},{17,25},{25,17},{2,10},{10... | collective-permute-start | bytes 3538952 | tf_op jit(solution)/shard_map/ppermute | solution.py:977
  94.1 3.7 %collective-permute-start.25 = (bf16[384,1536]{1,0:T(8,128)(2,1)S(1)}, bf16[384,1536]{1,0:T(8,128)(2,1)S(1)}, u32[]{:S(2)}, u32[]{:S(2)}) collective-permute-start(bf16[384,1536]{1,0:T(8,128)(2,1)S(1)} %get-tuple-element.231), channel_id=1, source_target_pairs={{0,8},{8,0},{16,24},{24,16},{1,9},{9,1},{17,25},{25,17},{2,10},{10... | collective-permute-start | bytes 3538952 | tf_op jit(solution)/shard_map/ppermute | solution.py:977
  94.4 15.7 %collective-permute-start.24 = (bf16[192,1536]{1,0:T(8,128)(2,1)S(1)}, bf16[192,1536]{1,0:T(8,128)(2,1)S(1)}, u32[]{:S(2)}, u32[]{:S(2)}) collective-permute-start(bf16[192,1536]{1,0:T(8,128)(2,1)S(1)} %get-tuple-element.345), channel_id=1, source_target_pairs={{0,16},{8,24},{16,0},{24,8},{1,17},{9,25},{17,1},{25,9},{2,18},{10... | collective-permute-start | bytes 1769480 | tf_op jit(solution)/shard_map/ppermute | solution.py:977
  95.6 2.4 %collective-permute-start.26 = (bf16[2,128,768]{2,1,0:T(8,128)(2,1)S(1)}, bf16[2,128,768]{2,1,0:T(8,128)(2,1)S(1)}, u32[]{:S(2)}, u32[]{:S(2)}) collective-permute-start(bf16[2,128,768]{2,1,0:T(8,128)(2,1)S(1)} %get-tuple-element.233), channel_id=1, source_target_pairs={{0,0},{2,2},{4,8},{6,10},{8,4},{10,6},{12,12},{14,14},{16,16},{18,... | collective-permute-start | bytes 1179656 | tf_op jit(solution)/shard_map/ppermute | solution.py:996
  96.3 7.8 %collective-permute-start.23 = (bf16[256,768]{1,0:T(8,128)(2,1)S(1)}, bf16[256,768]{1,0:T(8,128)(2,1)S(1)}, u32[]{:S(2)}, u32[]{:S(2)}) collective-permute-start(bf16[256,768]{1,0:T(8,128)(2,1)S(1)} %get-tuple-element.227.d_own_ref.refs_2_), channel_id=1, source_target_pairs={{0,1},{1,0},{2,3},{3,2},{4,5},{5,4},{6,7},{7,6},{8,9},{9,8},{10,11... | collective-permute-start | bytes 1179656 | tf_op jit(solution)/shard_map/ppermute | solution.py:981
  110.1 14.4 %collective-permute-start.27 = (bf16[96,1536]{1,0:T(8,128)(2,1)S(1)}, bf16[96,1536]{1,0:T(8,128)(2,1)S(1)}, u32[]{:S(2)}, u32[]{:S(2)}) collective-permute-start(bf16[96,1536]{1,0:T(8,128)(2,1)S(1)} %get-tuple-element.243), channel_id=1, source_target_pairs={{0,2},{2,0},{4,6},{6,4},{1,3},{3,1},{5,7},{7,5},{8,10},{10,8},{12,... | collective-permute-start | bytes 884744 | tf_op jit(solution)/shard_map/ppermute | solution.py:1026
  111.0 14.9 %collective-permute-start.29 = (bf16[2,128,768]{2,1,0:T(8,128)(2,1)S(1)}, bf16[2,128,768]{2,1,0:T(8,128)(2,1)}, u32[]{:S(2)}, u32[]{:S(2)}) collective-permute-start(bf16[2,128,768]{2,1,0:T(8,128)(2,1)S(1)} %get-tuple-element.246), channel_id=1, source_target_pairs={{0,2},{2,0},{4,10},{6,8},{8,6},{10,4},{12,14},{14,12},{16,18},{18,... | collective-permute-start | bytes 1179656 | tf_op jit(solution)/shard_map/ppermute | solution.py:996
  112.2 14.0 %collective-permute-start.28 = (bf16[192,1536]{1,0:T(8,128)(2,1)S(1)}, bf16[192,1536]{1,0:T(8,128)(2,1)S(1)}, u32[]{:S(2)}, u32[]{:S(2)}) collective-permute-start(bf16[192,1536]{1,0:T(8,128)(2,1)S(1)} %get-tuple-element.244), channel_id=1, source_target_pairs={{0,16},{8,24},{16,0},{24,8},{1,17},{9,25},{17,1},{25,9},{2,18},{10... | collective-permute-start | bytes 1769480 | tf_op jit(solution)/shard_map/ppermute | solution.py:977
  126.2 6.4 %collective-permute-start.30 = (bf16[512,768]{1,0:T(8,128)(2,1)S(1)}, bf16[512,768]{1,0:T(8,128)(2,1)S(1)}, u32[]{:S(2)}, u32[]{:S(2)}) collective-permute-start(bf16[512,768]{1,0:T(8,128)(2,1)S(1)} %get-tuple-element.247), channel_id=1, source_target_pairs={{0,8},{8,0},{16,24},{24,16},{1,9},{9,1},{17,25},{25,17},{2,10},{10... | collective-permute-start | bytes 2359304 | tf_op jit(solution)/shard_map/ppermute | solution.py:977
  130.0 13.5 %collective-permute-start.33 = (bf16[2,128,768]{2,1,0:T(8,128)(2,1)S(1)}, bf16[2,128,768]{2,1,0:T(8,128)(2,1)S(1)}, u32[]{:S(2)}, u32[]{:S(2)}) collective-permute-start(bf16[2,128,768]{2,1,0:T(8,128)(2,1)S(1)} %collective-permute-done.26), channel_id=1, source_target_pairs={{0,1},{1,0},{2,3},{3,2},{4,5},{5,4},{6,7},{7,6},{8,9},{9,8},{10,11... | collective-permute-start | bytes 1179656 | tf_op jit(solution)/shard_map/ppermute | solution.py:981
  131.6 11.9 %collective-permute-start.32 = (bf16[96,1536]{1,0:T(8,128)(2,1)S(1)}, bf16[96,1536]{1,0:T(8,128)(2,1)S(1)}, u32[]{:S(2)}, u32[]{:S(2)}) collective-permute-start(bf16[96,1536]{1,0:T(8,128)(2,1)S(1)} %get-tuple-element.260), channel_id=1, source_target_pairs={{0,2},{2,0},{4,6},{6,4},{1,3},{3,1},{5,7},{7,5},{8,10},{10,8},{12,... | collective-permute-start | bytes 884744 | tf_op jit(solution)/shard_map/ppermute | solution.py:1026
  131.7 9.6 %collective-permute-start.31 = (bf16[48,1536]{1,0:T(8,128)(2,1)S(1)}, bf16[48,1536]{1,0:T(8,128)(2,1)S(1)}, u32[]{:S(2)}, u32[]{:S(2)}) collective-permute-start(bf16[48,1536]{1,0:T(8,128)(2,1)S(1)} %get-tuple-element.259), channel_id=1, source_target_pairs={{0,4},{2,6},{4,0},{6,2},{1,5},{3,7},{5,1},{7,3},{8,12},{10,14},{12... | collective-permute-start | bytes 442376 | tf_op jit(solution)/shard_map/ppermute | solution.py:1026
  143.5 17.0 %collective-permute-start.34 = (bf16[384,1536]{1,0:T(8,128)(2,1)S(1)}, bf16[384,1536]{1,0:T(8,128)(2,1)S(1)}, u32[]{:S(2)}, u32[]{:S(2)}) collective-permute-start(bf16[384,1536]{1,0:T(8,128)(2,1)S(1)} %get-tuple-element.262), channel_id=1, source_target_pairs={{0,8},{8,0},{16,24},{24,16},{1,9},{9,1},{17,25},{25,17},{2,10},{10... | collective-permute-start | bytes 3538952 | tf_op jit(solution)/shard_map/ppermute | solution.py:977
  143.5 17.0 %collective-permute-start.35 = (bf16[256,768]{1,0:T(8,128)(2,1)S(1)}, bf16[256,768]{1,0:T(8,128)(2,1)S(1)}, u32[]{:S(2)}, u32[]{:S(2)}) collective-permute-start(bf16[256,768]{1,0:T(8,128)(2,1)S(1)} %get-tuple-element.263), channel_id=1, source_target_pairs={{0,1},{1,0},{2,3},{3,2},{4,5},{5,4},{6,7},{7,6},{8,9},{9,8},{10,11... | collective-permute-start | bytes 1179656 | tf_op jit(solution)/shard_map/ppermute | solution.py:981
  144.2 13.3 %collective-permute-start.37 = (bf16[48,1536]{1,0:T(8,128)(2,1)S(1)}, bf16[48,1536]{1,0:T(8,128)(2,1)S(1)}, u32[]{:S(2)}, u32[]{:S(2)}) collective-permute-start(bf16[48,1536]{1,0:T(8,128)(2,1)S(1)} %get-tuple-element.269), channel_id=1, source_target_pairs={{0,4},{2,6},{4,0},{6,2},{1,5},{3,7},{5,1},{7,3},{8,12},{10,14},{12... | collective-permute-start | bytes 442376 | tf_op jit(solution)/shard_map/ppermute | solution.py:1026
  145.5 15.0 %collective-permute-start.36 = (bf16[48,1536]{1,0:T(8,128)(2,1)S(1)}, bf16[48,1536]{1,0:T(8,128)(2,1)S(1)}, u32[]{:S(2)}, u32[]{:S(2)}) collective-permute-start(bf16[48,1536]{1,0:T(8,128)(2,1)S(1)} %get-tuple-element.268.mine_ref), channel_id=1, source_target_pairs={{0,4},{2,6},{4,0},{6,2},{1,5},{3,7},{5,1},{7,3},{8,12},{10,14},{12... | collective-permute-start | bytes 442376 | tf_op jit(solution)/shard_map/ppermute | solution.py:1026
  147.1 8.4 %collective-permute-start.38 = (f32[5,768]{1,0:T(8,128)S(1)}, f32[5,768]{1,0:T(8,128)S(1)}, u32[]{:S(2)}, u32[]{:S(2)}) collective-permute-start(f32[5,768]{1,0:T(8,128)S(1)} %get-tuple-element.270.mine_ref), channel_id=1, source_target_pairs={{0,1},{1,0},{2,3},{3,2},{4,5},{5,4},{6,7},{7,6},{8,9},{9,8},{10,11... | collective-permute-start | bytes 46088 | tf_op jit(solution)/shard_map/ppermute | solution.py:981
  160.5 1.3 collective-permute-start.39
  162.0 21.4 %collective-permute-start.40 = (bf16[208,1536]{1,0:T(8,128)(2,1)S(1)}, bf16[208,1536]{1,0:T(8,128)(2,1)S(1)}, u32[]{:S(2)}, u32[]{:S(2)}) collective-permute-start(bf16[208,1536]{1,0:T(8,128)(2,1)S(1)} %get-tuple-element.285), channel_id=1, source_target_pairs={{0,16},{8,24},{16,0},{24,8},{1,17},{9,25},{17,1},{25,9},{2,18},{10... | collective-permute-start | bytes 1916936 | tf_op jit(solution)/shard_map/ppermute | solution.py:977
  163.5 19.8 %collective-permute-start.45 = (bf16[2,128,768]{2,1,0:T(8,128)(2,1)}, bf16[2,128,768]{2,1,0:T(8,128)(2,1)S(1)}, u32[]{:S(2)}, u32[]{:S(2)}) collective-permute-start(bf16[2,128,768]{2,1,0:T(8,128)(2,1)} %collective-permute-done.29), channel_id=1, source_target_pairs={{0,1},{1,0},{2,3},{3,2},{4,5},{5,4},{6,7},{7,6},{8,9},{9,8},{10,11... | collective-permute-start | bytes 1179656 | tf_op jit(solution)/shard_map/ppermute | solution.py:981
  165.1 7.2 %collective-permute-start.42 = (bf16[48,1536]{1,0:T(8,128)(2,1)S(1)}, bf16[48,1536]{1,0:T(8,128)(2,1)S(1)}, u32[]{:S(2)}, u32[]{:S(2)}) collective-permute-start(bf16[48,1536]{1,0:T(8,128)(2,1)S(1)} %get-tuple-element.290), channel_id=1, source_target_pairs={{0,4},{2,6},{4,0},{6,2},{1,5},{3,7},{5,1},{7,3},{8,12},{10,14},{12... | collective-permute-start | bytes 442376 | tf_op jit(solution)/shard_map/ppermute | solution.py:1026
  165.2 18.2 %collective-permute-start.41 = (bf16[96,1536]{1,0:T(8,128)(2,1)S(1)}, bf16[96,1536]{1,0:T(8,128)(2,1)}, u32[]{:S(2)}, u32[]{:S(2)}) collective-permute-start(bf16[96,1536]{1,0:T(8,128)(2,1)S(1)} %get-tuple-element.289), channel_id=1, source_target_pairs={{0,2},{2,0},{4,6},{6,4},{1,3},{3,1},{5,7},{7,5},{8,10},{10,8},{12,... | collective-permute-start | bytes 884744 | tf_op jit(solution)/shard_map/ppermute | solution.py:1026
  166.0 7.0 %collective-permute-start.43 = (bf16[128,768]{1,0:T(8,128)(2,1)S(1)}, bf16[128,768]{1,0:T(8,128)(2,1)}, u32[]{:S(2)}, u32[]{:S(2)}) collective-permute-start(bf16[128,768]{1,0:T(8,128)(2,1)S(1)} %get-tuple-element.291), channel_id=1, source_target_pairs={{0,0},{2,2},{4,8},{6,10},{8,4},{10,6},{12,12},{14,14},{16,16},{18,... | collective-permute-start | bytes 589832 | tf_op jit(solution)/shard_map/ppermute | solution.py:996
  173.0 10.3 %collective-permute-start.44 = (bf16[128,768]{1,0:T(8,128)(2,1)S(1)}, bf16[128,768]{1,0:T(8,128)(2,1)}, u32[]{:S(2)}, u32[]{:S(2)}) collective-permute-start(bf16[128,768]{1,0:T(8,128)(2,1)S(1)} %get-tuple-element.292), channel_id=1, source_target_pairs={{0,2},{2,0},{4,10},{6,8},{8,6},{10,4},{12,14},{14,12},{16,18},{18,... | collective-permute-start | bytes 589832 | tf_op jit(solution)/shard_map/ppermute | solution.py:996
  184.5 9.7 %collective-permute-start.46 = (bf16[64,1536]{1,0:T(8,128)(2,1)S(1)}, bf16[64,1536]{1,0:T(8,128)(2,1)S(1)}, u32[]{:S(2)}, u32[]{:S(2)}) collective-permute-start(bf16[64,1536]{1,0:T(8,128)(2,1)S(1)} %get-tuple-element.299), channel_id=1, source_target_pairs={{0,2},{2,4},{4,6},{6,0},{1,3},{3,5},{5,7},{7,1},{8,10},{10,12},{12... | collective-permute-start | bytes 589832 | tf_op jit(solution)/shard_map/ppermute | solution.py:1022
  184.6 16.0 %collective-permute-start.47 = (bf16[64,1536]{1,0:T(8,128)(2,1)S(1)}, bf16[64,1536]{1,0:T(8,128)(2,1)S(1)}, u32[]{:S(2)}, u32[]{:S(2)}) collective-permute-start(bf16[64,1536]{1,0:T(8,128)(2,1)S(1)} %get-tuple-element.300), channel_id=1, source_target_pairs={{0,4},{2,6},{4,0},{6,2},{1,5},{3,7},{5,1},{7,3},{8,12},{10,14},{12... | collective-permute-start | bytes 589832 | tf_op jit(solution)/shard_map/ppermute | solution.py:1022
  187.3 18.6 %collective-permute-start.51 = (bf16[96,1536]{1,0:T(8,128)(2,1)S(1)}, bf16[96,1536]{1,0:T(8,128)(2,1)S(1)}, u32[]{:S(2)}, u32[]{:S(2)}) collective-permute-start(bf16[96,1536]{1,0:T(8,128)(2,1)S(1)} %maximum_select_fusion.6), channel_id=1, source_target_pairs={{0,2},{2,0},{4,6},{6,4},{1,3},{3,1},{5,7},{7,5},{8,10},{10,8},{12,... | collective-permute-start | bytes 884744 | tf_op jit(solution)/shard_map/ppermute | solution.py:1026
  191.4 14.5 %collective-permute-start.48 = (bf16[64,1536]{1,0:T(8,128)(2,1)S(1)}, bf16[64,1536]{1,0:T(8,128)(2,1)S(1)}, u32[]{:S(2)}, u32[]{:S(2)}) collective-permute-start(bf16[64,1536]{1,0:T(8,128)(2,1)S(1)} %get-tuple-element.301), channel_id=1, source_target_pairs={{0,6},{2,0},{4,2},{6,4},{1,7},{3,1},{5,3},{7,5},{8,14},{10,8},{12,... | collective-permute-start | bytes 589832 | tf_op jit(solution)/shard_map/ppermute | solution.py:1022
  191.6 14.3 %collective-permute-start.49 = (bf16[128,768]{1,0:T(8,128)(2,1)}, bf16[128,768]{1,0:T(8,128)(2,1)S(1)}, u32[]{:S(2)}, u32[]{:S(2)}) collective-permute-start(bf16[128,768]{1,0:T(8,128)(2,1)} %collective-permute-done.43), channel_id=1, source_target_pairs={{0,1},{1,0},{2,3},{3,2},{4,5},{5,4},{6,7},{7,6},{8,9},{9,8},{10,11... | collective-permute-start | bytes 589832 | tf_op jit(solution)/shard_map/ppermute | solution.py:981
  194.3 11.6 %collective-permute-start.50 = (bf16[128,768]{1,0:T(8,128)(2,1)}, bf16[128,768]{1,0:T(8,128)(2,1)S(1)}, u32[]{:S(2)}, u32[]{:S(2)}) collective-permute-start(bf16[128,768]{1,0:T(8,128)(2,1)} %collective-permute-done.44), channel_id=1, source_target_pairs={{0,1},{1,0},{2,3},{3,2},{4,5},{5,4},{6,7},{7,6},{8,9},{9,8},{10,11... | collective-permute-start | bytes 589832 | tf_op jit(solution)/shard_map/ppermute | solution.py:981
  206.1 8.0 %collective-permute-start.54 = (bf16[48,1536]{1,0:T(8,128)(2,1)S(1)}, bf16[48,1536]{1,0:T(8,128)(2,1)S(1)}, u32[]{:S(2)}, u32[]{:S(2)}) collective-permute-start(bf16[48,1536]{1,0:T(8,128)(2,1)S(1)} %get-tuple-element.312.a), channel_id=1, source_target_pairs={{0,6},{2,0},{4,2},{6,4},{1,7},{3,1},{5,3},{7,5},{8,14},{10,8},{12,... | collective-permute-start | bytes 442376 | tf_op jit(solution)/shard_map/ppermute | solution.py:1022
  207.2 13.0 %collective-permute-start.53 = (bf16[48,1536]{1,0:T(8,128)(2,1)S(1)}, bf16[48,1536]{1,0:T(8,128)(2,1)S(1)}, u32[]{:S(2)}, u32[]{:S(2)}) collective-permute-start(bf16[48,1536]{1,0:T(8,128)(2,1)S(1)} %get-tuple-element.312.a), channel_id=1, source_target_pairs={{0,4},{2,6},{4,0},{6,2},{1,5},{3,7},{5,1},{7,3},{8,12},{10,14},{12... | collective-permute-start | bytes 442376 | tf_op jit(solution)/shard_map/ppermute | solution.py:1022
  207.6 12.5 %collective-permute-start.52 = (bf16[48,1536]{1,0:T(8,128)(2,1)S(1)}, bf16[48,1536]{1,0:T(8,128)(2,1)S(1)}, u32[]{:S(2)}, u32[]{:S(2)}) collective-permute-start(bf16[48,1536]{1,0:T(8,128)(2,1)S(1)} %get-tuple-element.312.a), channel_id=1, source_target_pairs={{0,2},{2,4},{4,6},{6,0},{1,3},{3,5},{5,7},{7,1},{8,10},{10,12},{12... | collective-permute-start | bytes 442376 | tf_op jit(solution)/shard_map/ppermute | solution.py:1022
  (22 other events, 161.6 us)

commit v5 on v4

--- a/solution.py
+++ b/solution.py
@@ -1183,10 +1183,7 @@
         rows_low, proj, d_queries, d_pair, d_got, sums_two
     )
     own, far, send = weight_grad((normed_low, d_proj), (d_att, d_att_peer, mixed))
-    share_got = [swap_tensor(share_0)]
-    one_peer, sides, send, got_1, got_2, *share_got = together(
-        one_peer, sides, send, got_1, got_2, *share_got
-    )
+    one_peer, sides, send, got_1, got_2 = together(one_peer, sides, send, got_1, got_2)
 
     quarter_1, quarter_2, sent = add_and_cut(quarter_1, got_1, half_2, got_2)
     got_1 = swap_planes(quarter_1, 2)
@@ -1201,32 +1198,41 @@
     vectors = gather_vectors(grad_up_bias, grad_down_bias, proj_bias, sides, sides_got)
     vectors_got = exchange(vectors, 1)
     input_rows = finish(rows_low, one_own, one_got, row(ln1_gain), d_middle)
-    *input_rows, vectors_got, share_1 = together(*input_rows, vectors_got, share_1)
+    *input_rows, vectors_got, share_0, share_1 = together(
+        *input_rows, vectors_got, share_0, share_1
+    )
 
     packet, packet_far = merge(own, far, send_got, vectors, vectors_got)
     packet_got = exchange(packet_far, 2)
-    share_got.append(swap_tensor(share_1))
+    share_got = [swap_tensor(share_0)]
     in_near = [route(input_rows[step], step, False) for step in range(2)]
     half_1, quarter_2 = glue_and_add(quarter_1, got_1, quarter_2, got_2)
     got_1 = swap_planes(half_1, 1)
     got_2 = swap_planes(quarter_2, 2)
-    packet_got, got_1, got_2, *pieces = together(packet_got, got_1, got_2, *in_near, *share_got)
+    packet_got, got_1, got_2, share_1, *pieces = together(
+        packet_got, got_1, got_2, share_1, *in_near, *share_got
+    )
     in_near, share_got = pieces[:2], pieces[2:]
 
     quarters = spread(packet, packet_got, shard)
     arrived = [turn_planes(quarters[step], step) for step in range(1, 4)]
     in_far = [swap_tensor(v) for v in in_near]
+    share_got.append(swap_tensor(share_1))
     half_2 = stack_rows(quarter_2, got_2, upper_half)
     got_2 = swap_planes(half_2, 1)
+    arrived[0], half_1, got_1 = together(arrived[0], half_1, got_1)
     grad_down = stack_rows(half_1, got_1, odd).astype(jnp.float32).T
-    output = join_shares((share_0, share_1), share_got, odd, upper)
-    *pieces, got_2 = together(quarters[0], *arrived, *in_far, got_2)
-
-    in_far = pieces[4:]
+    *pieces, got_2 = together(quarters[0], *arrived, *in_far, *share_got, got_2)
+
+    in_far, share_got = pieces[4:6], pieces[6:]
     quarter, vectors = total(pieces[:4], shard // 4, vectors.shape[0])
     quarters = [quarter] + [turn_planes(quarter, step) for step in range(1, 4)]
     input_grad = join_out(in_near, in_far, odd, upper)
+    output = join_shares((share_0, share_1), share_got, odd, upper)
     grad_up = stack_rows(half_2, got_2, odd).astype(jnp.float32)
+    *quarters, input_grad, output, grad_up, grad_down = together(
+        *quarters, input_grad, output, grad_up, grad_down
+    )
     grad_query, grad_key, grad_value, grad_out = assemble(quarters)
     return (
         output.reshape(tokens.shape),

time: 222 us -> 220 us (level)
    ppermute x6, waiting for transfers between devices: 18 us -> 14.4 us  [turn_planes(): lax.ppermute(value, 'context', [(i, (i + step) % 4) for i in range(4)])]
  transfers between devices with their start and end apart: 55 -> 55, of which waited for: 26 -> 28; matrix products, arithmetic and copies ran while one was open for 4% -> 4% of each run, Pallas kernels for 13% -> 13%
where the time goes in v5:
time: 220 us; the launch traced here: 219 us
  waiting for transfers between devices  102 us (46%)
  starting transfers between devices  56.3 us (26%)
  Pallas kernels  43.1 us (20%)
  other arithmetic  7.83 us (4%)
  local copies, waits for them, and re-layouts  7.54 us (3%)
  between operations  2.69 us (1%)
    ppermute x14, waiting for transfers between devices, swap_tensor(): return lax.ppermute(value, 'tensor', [(0, 1), (1, 0)])  31.2 us
    ppermute x19, waiting for transfers between devices, exchange(): return lax.ppermute(value, 'dp', [(i, i ^ bit) for i in range(size)])  26.9 us
    ppermute x8, waiting for transfers between devices, swap_planes(): return lax.ppermute(value, 'context', [(i, i ^ bit) for i in range(4)])  17.6 us
    ppermute x14, starting transfers between devices, swap_tensor(): return lax.ppermute(value, 'tensor', [(0, 1), (1, 0)])  17.4 us
    ppermute x19, starting transfers between devices, exchange(): return lax.ppermute(value, 'dp', [(i, i ^ bit) for i in range(size)])  16.9 us
    ppermute x6, waiting for transfers between devices, turn_planes(): lax.ppermute(value, 'context', [(i, (i + step) % 4) for i in range(4)])  14.4 us
    ppermute x8, waiting for transfers between devices, route(): return lax.ppermute(value, ('dp', 'context'), pairs)  11.7 us
    pallas_call x1, Pallas kernels, attend_back(): pl.pallas_call(attend_back_kernel, out_shape=tuple((jax.ShapeDtypeStruct(...  11.2 us
  transfers between devices with their start and end apart: 55, of which 28 were waited for; matrix products, arithmetic and copies ran while one was open for 4% of the time, Pallas kernels for 13%

profile of v5, /device:TPU:0, one launch (start us, length us, event | category | flops | bytes accessed | tf_op | source)
XLA Modules:
  0.0 219.3 jit_solution(3709755958013371686)
XLA Ops:
  0.8 1.4 slice_select_fusion.1
  2.9 2.6 %collective-permute-start.2 = (bf16[192,1152]{1,0:T(8,128)(2,1)S(1)}, bf16[192,1152]{1,0:T(8,128)(2,1)S(1)}, u32[]{:S(2)}, u32[]{:S(2)}) collective-permute-start(bf16[192,1152]{1,0:T(8,128)(2,1)S(1)} %constant_dynamic-update-slice_fusion.a), channel_id=1, source_target_pairs={{0,16},{8,24},{16,0},{24,8},{1,17},{9,25},{17,1},{25,9},{2,18},{10... | collective-permute-start | bytes 1327112 | tf_op jit(solution)/shard_map/ppermute | solution.py:977
  6.1 1.6 collective-permute-start.1
  7.8 3.5 %collective-permute-start.5 = (s32[2]{0:T(128)S(1)}, s32[2]{0:T(128)S(1)}, u32[]{:S(2)}, u32[]{:S(2)}) collective-permute-start(s32[2]{0:T(128)S(1)} %copy-done.30), channel_id=1, source_target_pairs={{0,8},{8,0},{16,24},{24,16},{1,9},{9,1},{17,25},{25,17},{2,10},{10... | collective-permute-start | bytes 32 | tf_op jit(solution)/shard_map/ppermute | solution.py:977
  12.1 1.5 collective-permute-start.4
  13.7 4.5 %collective-permute-done.4 = bf16[192,384]{1,0:T(8,128)(2,1)S(1)} collective-permute-done((bf16[192,384]{1,0:T(8,128)(2,1)S(1)}, bf16[192,384]{1,0:T(8,128)(2,1)S(1)}, u32[]{:S(2)}, u32[]{:S(2)}) %collective-permute-start.4) | collective-permute-done | bytes 147488 | tf_op jit(solution)/shard_map/ppermute | solution.py:981
  18.1 1.6 collective-permute-start.6
  21.0 1.7 collective-permute-start.11
  22.8 3.3 %collective-permute-done.6.peer0 = bf16[128,768]{1,0:T(8,128)(2,1)S(1)} collective-permute-done((bf16[128,768]{1,0:T(8,128)(2,1)S(1)}, bf16[128,768]{1,0:T(8,128)(2,1)S(1)}, u32[]{:S(2)}, u32[]{:S(2)}) %collective-permute-start.6) | collective-permute-done | bytes 196640 | tf_op jit(solution)/shard_map/ppermute | solution.py:981
  26.8 2.1 collective-permute-done.7.peer1
  29.6 6.6 %collective-permute-done.9.dc = bf16[192,1536]{1,0:T(8,128)(2,1)} collective-permute-done((bf16[192,1536]{1,0:T(8,128)(2,1)S(1)}, bf16[192,1536]{1,0:T(8,128)(2,1)}, u32[]{:S(2)}, u32[]{:S(2)}) %collective-permute-start.9) | collective-permute-done | bytes 589856 | tf_op jit(solution)/shard_map/ppermute | solution.py:977
  36.2 2.6 %shard_map.305 = (bf16[512,768]{1,0:T(8,128)(2,1)S(1)}, bf16[512,768]{1,0:T(8,128)(2,1)S(1)}, bf16[512,384]{1,0:T(8,128)(2,1)S(1)}, bf16[512,768]{1,0:T(8,128)(2,1)}, bf16[768,1152]{1,0:T(8,128)(2,1)S(1)}) custom-call(bf16[128,768]{1,0:T(8,128)(2,1)S(1)} %collective-permute-done.own0, bf16[128,768]{1,0:T(8,128)(2,1)S(1)} %collective-permute-done.1.own1, ...), custom_call_target="tpu_custom_call" | custom-call | flops 905969664 | bytes 7082496 | tf_op jit(solution)/shard_map/pallas_call | solution.py:452
  42.5 1.6 collective-permute-start.13
  45.5 1.0 copy-done.9
  46.5 8.1 %shard_map.306 = (bf16[512,384]{1,0:T(8,128)(2,1)S(1)}, f32[3,2,512]{2,1,0:T(2,128)S(1)}) custom-call(s32[9]{0:T(128)S(1)} %compare_select_fusion.4.info, bf16[512,384]{1,0:T(8,128)(2,1)S(1)} %copy-done.9, bf16[512,768]{1,0:T(8,128)(2,1)} %get-tuple-element.203.own_ref, bf16[512,768]{1,0:T(8,128)(2,1)} %collective-permute-done.12.other_ref), custom_call_target="tpu_custom_call" | custom-call | flops 3221225472 | bytes 2359296 | tf_op jit(solution)/shard_map/pallas_call | solution.py:331
  55.3 1.5 collective-permute-start.15
  56.9 9.1 %collective-permute-done.17.pc = bf16[192,2304]{1,0:T(8,128)(2,1)S(1)} collective-permute-done((bf16[192,2304]{1,0:T(8,128)(2,1)S(1)}, bf16[192,2304]{1,0:T(8,128)(2,1)S(1)}, u32[]{:S(2)}, u32[]{:S(2)}) %collective-permute-start.17) | collective-permute-done | bytes 884768 | tf_op jit(solution)/shard_map/ppermute | solution.py:977
  67.0 2.3 %collective-permute-done.20.pd = bf16[192,2304]{1,0:T(8,128)(2,1)S(1)} collective-permute-done((bf16[192,2304]{1,0:T(8,128)(2,1)S(1)}, bf16[192,2304]{1,0:T(8,128)(2,1)S(1)}, u32[]{:S(2)}, u32[]{:S(2)}) %collective-permute-start.20) | collective-permute-done | bytes 884768 | tf_op jit(solution)/shard_map/ppermute | solution.py:977
  69.3 10.9 %shard_map.307 = (f32[256,768]{1,0:T(8,128)S(1)}, bf16[512,768]{1,0:T(8,128)(2,1)S(1)}, bf16[512,768]{1,0:T(8,128)(2,1)S(1)}, bf16[512,1536]{1,0:T(8,128)(2,1)S(...) custom-call(s32[9]{0:T(128)S(1)} %compare_select_fusion.4.info, ...), custom_call_target="tpu_custom_call" | custom-call | flops 4831838208 | bytes 20971520 | tf_op jit(solution)/shard_map/pallas_call | solution.py:658
  80.2 1.6 collective-permute-start.21
  81.8 1.6 shard_map.308
  83.4 1.6 shard_map.309
  85.0 6.4 %collective-permute-done.21.got_ref = bf16[256,768]{1,0:T(8,128)(2,1)S(1)} collective-permute-done((bf16[256,768]{1,0:T(8,128)(2,1)S(1)}, bf16[256,768]{1,0:T(8,128)(2,1)S(1)}, u32[]{:S(2)}, u32[]{:S(2)}) %collective-permute-start.21) | collective-permute-done | bytes 393248 | tf_op jit(solution)/shard_map/ppermute | solution.py:981
  91.4 1.3 shard_map.310
  92.7 1.5 collective-permute-done.22
  94.5 1.2 collective-permute-start.24
  95.7 1.4 collective-permute-start.26
  97.1 1.5 collective-permute-start.23
  98.8 6.6 %collective-permute-done.23.d_peer_ref.refs_3_ = bf16[256,768]{1,0:T(8,128)(2,1)S(1)} collective-permute-done((bf16[256,768]{1,0:T(8,128)(2,1)S(1)}, bf16[256,768]{1,0:T(8,128)(2,1)S(1)}, u32[]{:S(2)}, u32[]{:S(2)}) %collective-permute-start.23) | collective-permute-done | bytes 393248 | tf_op jit(solution)/shard_map/ppermute | solution.py:981
  105.4 4.8 %collective-permute-done.24.refs_1_ = bf16[192,1536]{1,0:T(8,128)(2,1)S(1)} collective-permute-done((bf16[192,1536]{1,0:T(8,128)(2,1)S(1)}, bf16[192,1536]{1,0:T(8,128)(2,1)S(1)}, u32[]{:S(2)}, u32[]{:S(2)}) %collective-permute-start.24) | collective-permute-done | bytes 589856 | tf_op jit(solution)/shard_map/ppermute | solution.py:977
  111.1 1.2 collective-permute-start.29
  112.3 1.1 collective-permute-start.28
  113.5 11.2 %shard_map.311 = (bf16[512,384]{1,0:T(8,128)(2,1)S(1)}, bf16[512,768]{1,0:T(8,128)(2,1)S(1)}, bf16[512,768]{1,0:T(8,128)(2,1)S(1)}) custom-call(s32[9]{0:T(128)S(1)} %compare_select_fusion.4.info, bf16[512,384]{1,0:T(8,128)(2,1)S(1)} %copy-done.10, bf16[512,768]{1,0:T(8,128)(2,1)} %get-tuple-element.203.own_ref, ...), custom_call_target="tpu_custom_call" | custom-call | flops 8053063680 | bytes 4718592 | tf_op jit(solution)/shard_map/pallas_call | solution.py:413
  124.7 1.4 collective-permute-done.29
  126.3 3.8 %collective-permute-start.30 = (bf16[512,768]{1,0:T(8,128)(2,1)S(1)}, bf16[512,768]{1,0:T(8,128)(2,1)S(1)}, u32[]{:S(2)}, u32[]{:S(2)}) collective-permute-start(bf16[512,768]{1,0:T(8,128)(2,1)S(1)} %get-tuple-element.261), channel_id=1, source_target_pairs={{0,8},{8,0},{16,24},{24,16},{1,9},{9,1},{17,25},{25,17},{2,10},{10... | collective-permute-start | bytes 2359304 | tf_op jit(solution)/shard_map/ppermute | solution.py:977
  132.0 1.8 shard_map.313
  133.8 1.8 shard_map.314
  135.6 4.5 %collective-permute-done.31.b_ref = bf16[48,1536]{1,0:T(8,128)(2,1)S(1)} collective-permute-done((bf16[48,1536]{1,0:T(8,128)(2,1)S(1)}, bf16[48,1536]{1,0:T(8,128)(2,1)S(1)}, u32[]{:S(2)}, u32[]{:S(2)}) %collective-permute-start.31) | collective-permute-done | bytes 147488 | tf_op jit(solution)/shard_map/ppermute | solution.py:1026
  140.1 2.2 %collective-permute-done.32.right_ref = bf16[96,1536]{1,0:T(8,128)(2,1)S(1)} collective-permute-done((bf16[96,1536]{1,0:T(8,128)(2,1)S(1)}, bf16[96,1536]{1,0:T(8,128)(2,1)S(1)}, u32[]{:S(2)}, u32[]{:S(2)}) %collective-permute-start.32) | collective-permute-done | bytes 294944 | tf_op jit(solution)/shard_map/ppermute | solution.py:1026
  142.3 1.5 collective-permute-start.34
  143.9 1.3 collective-permute-start.36
  145.2 1.7 collective-permute-start.35
  147.4 7.0 %collective-permute-done.37.theirs_ref = f32[5,768]{1,0:T(8,128)S(1)} collective-permute-done((f32[5,768]{1,0:T(8,128)S(1)}, f32[5,768]{1,0:T(8,128)S(1)}, u32[]{:S(2)}, u32[]{:S(2)}) %collective-permute-start.37) | collective-permute-done | bytes 15392 | tf_op jit(solution)/shard_map/ppermute | solution.py:981
  154.4 2.9 %collective-permute-done.36.right_ref = bf16[48,1536]{1,0:T(8,128)(2,1)S(1)} collective-permute-done((bf16[48,1536]{1,0:T(8,128)(2,1)S(1)}, bf16[48,1536]{1,0:T(8,128)(2,1)S(1)}, u32[]{:S(2)}, u32[]{:S(2)}) %collective-permute-start.36) | collective-permute-done | bytes 147488 | tf_op jit(solution)/shard_map/ppermute | solution.py:1026
  157.3 3.0 %collective-permute-done.35.theirs_ref = bf16[48,1536]{1,0:T(8,128)(2,1)S(1)} collective-permute-done((bf16[48,1536]{1,0:T(8,128)(2,1)S(1)}, bf16[48,1536]{1,0:T(8,128)(2,1)S(1)}, u32[]{:S(2)}, u32[]{:S(2)}) %collective-permute-start.35) | collective-permute-done | bytes 147488 | tf_op jit(solution)/shard_map/ppermute | solution.py:1026
  161.8 1.5 collective-permute-start.39
  165.0 1.3 collective-permute-start.42
  166.3 5.0 %collective-permute-done.41 = bf16[48,1536]{1,0:T(8,128)(2,1)S(1)} collective-permute-done((bf16[48,1536]{1,0:T(8,128)(2,1)S(1)}, bf16[48,1536]{1,0:T(8,128)(2,1)S(1)}, u32[]{:S(2)}, u32[]{:S(2)}) %collective-permute-start.41) | collective-permute-done | bytes 147488 | tf_op jit(solution)/shard_map/ppermute | solution.py:1026
  172.0 10.2 %collective-permute-done.43 = bf16[128,768]{1,0:T(8,128)(2,1)} collective-permute-done((bf16[128,768]{1,0:T(8,128)(2,1)S(1)}, bf16[128,768]{1,0:T(8,128)(2,1)}, u32[]{:S(2)}, u32[]{:S(2)}) %collective-permute-start.43) | collective-permute-done | bytes 196640 | tf_op jit(solution)/shard_map/ppermute | solution.py:996
  182.4 2.7 %collective-permute-start.46 = (bf16[64,1536]{1,0:T(8,128)(2,1)S(1)}, bf16[64,1536]{1,0:T(8,128)(2,1)S(1)}, u32[]{:S(2)}, u32[]{:S(2)}) collective-permute-start(bf16[64,1536]{1,0:T(8,128)(2,1)S(1)} %get-tuple-element.313), channel_id=1, source_target_pairs={{0,4},{2,6},{4,0},{6,2},{1,5},{3,7},{5,1},{7,3},{8,12},{10,14},{12... | collective-permute-start | bytes 589832 | tf_op jit(solution)/shard_map/ppermute | solution.py:1022
  185.0 1.5 collective-permute-start.50
  186.6 1.8 collective-permute-start.51
  188.5 3.5 %collective-permute-done.45.refs_1_ = bf16[64,1536]{1,0:T(8,128)(2,1)S(1)} collective-permute-done((bf16[64,1536]{1,0:T(8,128)(2,1)S(1)}, bf16[64,1536]{1,0:T(8,128)(2,1)S(1)}, u32[]{:S(2)}, u32[]{:S(2)}) %collective-permute-start.45) | collective-permute-done | bytes 196640 | tf_op jit(solution)/shard_map/ppermute | solution.py:1022
  192.0 1.5 collective-permute-start.48
  193.5 4.8 %collective-permute-done.46.refs_2_ = bf16[64,1536]{1,0:T(8,128)(2,1)S(1)} collective-permute-done((bf16[64,1536]{1,0:T(8,128)(2,1)S(1)}, bf16[64,1536]{1,0:T(8,128)(2,1)S(1)}, u32[]{:S(2)}, u32[]{:S(2)}) %collective-permute-start.46) | collective-permute-done | bytes 196640 | tf_op jit(solution)/shard_map/ppermute | solution.py:1022
  198.3 1.5 collective-permute-start.49
  199.9 1.3 maximum_select_fusion.5
  201.1 2.5 %collective-permute-done.47.refs_3_ = bf16[64,1536]{1,0:T(8,128)(2,1)S(1)} collective-permute-done((bf16[64,1536]{1,0:T(8,128)(2,1)S(1)}, bf16[64,1536]{1,0:T(8,128)(2,1)S(1)}, u32[]{:S(2)}, u32[]{:S(2)}) %collective-permute-start.47) | collective-permute-done | bytes 196640 | tf_op jit(solution)/shard_map/ppermute | solution.py:1022
  206.1 1.3 collective-permute-start.52
  207.3 1.2 fusion.2
  209.5 1.4 reverse_select_fusion
  210.9 1.7 convert_bitcast_fusion
  213.9 3.5 %collective-permute-done.53.c = bf16[48,1536]{1,0:T(8,128)(2,1)S(1)} collective-permute-done((bf16[48,1536]{1,0:T(8,128)(2,1)S(1)}, bf16[48,1536]{1,0:T(8,128)(2,1)S(1)}, u32[]{:S(2)}, u32[]{:S(2)}) %collective-permute-start.53) | collective-permute-done | bytes 147488 | tf_op jit(solution)/shard_map/ppermute | solution.py:1022
  217.4 1.0 shard_map.323
  (161 shorter events, 23.8 us)
Async XLA Ops:
  0.8 19.5 %copy-start.11 = (bf16[2,256,768]{2,1,0:T(8,128)(2,1)S(1)}, bf16[2,256,768]{2,1,0:T(8,128)(2,1)}, u32[]{:S(2)}) copy-start(bf16[2,256,768]{2,1,0:T(8,128)(2,1)} %param.35) | copy-start | bytes 2359300
  2.3 24.4 %copy-start.12 = (bf16[192,1536]{1,0:T(8,128)(2,1)S(1)}, bf16[192,1536]{1,0:T(8,128)(2,1)}, u32[]{:S(2)}) copy-start(bf16[192,1536]{1,0:T(8,128)(2,1)} %param.31) | copy-start | bytes 1769476
  2.4 15.8 %collective-permute-start.3 = (bf16[192,1152]{1,0:T(8,128)(2,1)S(1)}, bf16[192,1152]{1,0:T(8,128)(2,1)S(1)}, u32[]{:S(2)}, u32[]{:S(2)}) collective-permute-start(bf16[192,1152]{1,0:T(8,128)(2,1)S(1)} %constant_dynamic-update-slice_fusion.a), channel_id=1, source_target_pairs={{0,8},{8,0},{16,24},{24,16},{1,9},{9,1},{17,25},{25,17},{2,10},{10... | collective-permute-start | bytes 1327112 | tf_op jit(solution)/shard_map/ppermute | solution.py:977
  2.9 15.3 %collective-permute-start.2 = (bf16[192,1152]{1,0:T(8,128)(2,1)S(1)}, bf16[192,1152]{1,0:T(8,128)(2,1)S(1)}, u32[]{:S(2)}, u32[]{:S(2)}) collective-permute-start(bf16[192,1152]{1,0:T(8,128)(2,1)S(1)} %constant_dynamic-update-slice_fusion.a), channel_id=1, source_target_pairs={{0,16},{8,24},{16,0},{24,8},{1,17},{9,25},{17,1},{25,9},{2,18},{10... | collective-permute-start | bytes 1327112 | tf_op jit(solution)/shard_map/ppermute | solution.py:977
  5.5 12.7 %collective-permute-start = (bf16[128,768]{1,0:T(8,128)(2,1)S(1)}, bf16[128,768]{1,0:T(8,128)(2,1)S(1)}, u32[]{:S(2)}, u32[]{:S(2)}) collective-permute-start(bf16[128,768]{1,0:T(8,128)(2,1)S(1)} %get-tuple-element.181), channel_id=1, source_target_pairs={{0,0},{2,2},{8,4},{10,6},{4,8},{6,10},{12,12},{14,14},{16,16},{18,... | collective-permute-start | bytes 589832 | tf_op jit(solution)/shard_map/ppermute | solution.py:996
  6.1 12.0 %collective-permute-start.1 = (bf16[128,768]{1,0:T(8,128)(2,1)S(1)}, bf16[128,768]{1,0:T(8,128)(2,1)S(1)}, u32[]{:S(2)}, u32[]{:S(2)}) collective-permute-start(bf16[128,768]{1,0:T(8,128)(2,1)S(1)} %get-tuple-element.182), channel_id=1, source_target_pairs={{2,0},{0,2},{10,4},{8,6},{6,8},{4,10},{14,12},{12,14},{18,16},{16,... | collective-permute-start | bytes 589832 | tf_op jit(solution)/shard_map/ppermute | solution.py:996
  7.8 4.3 %collective-permute-start.5 = (s32[2]{0:T(128)S(1)}, s32[2]{0:T(128)S(1)}, u32[]{:S(2)}, u32[]{:S(2)}) collective-permute-start(s32[2]{0:T(128)S(1)} %copy-done.30), channel_id=1, source_target_pairs={{0,8},{8,0},{16,24},{24,16},{1,9},{9,1},{17,25},{25,17},{2,10},{10... | collective-permute-start | bytes 32 | tf_op jit(solution)/shard_map/ppermute | solution.py:977
  12.1 6.1 %collective-permute-start.4 = (bf16[192,384]{1,0:T(8,128)(2,1)S(1)}, bf16[192,384]{1,0:T(8,128)(2,1)S(1)}, u32[]{:S(2)}, u32[]{:S(2)}) collective-permute-start(bf16[192,384]{1,0:T(8,128)(2,1)S(1)} %bitcast.35), channel_id=1, source_target_pairs={{0,1},{1,0},{2,3},{3,2},{4,5},{5,4},{6,7},{7,6},{8,9},{9,8},{10,11... | collective-permute-start | bytes 442376 | tf_op jit(solution)/shard_map/ppermute | solution.py:981
  18.1 7.9 %collective-permute-start.6 = (bf16[128,768]{1,0:T(8,128)(2,1)S(1)}, bf16[128,768]{1,0:T(8,128)(2,1)S(1)}, u32[]{:S(2)}, u32[]{:S(2)}) collective-permute-start(bf16[128,768]{1,0:T(8,128)(2,1)S(1)} %collective-permute-done.own0), channel_id=1, source_target_pairs={{0,1},{1,0},{2,3},{3,2},{4,5},{5,4},{6,7},{7,6},{8,9},{9,8},{10,11... | collective-permute-start | bytes 589832 | tf_op jit(solution)/shard_map/ppermute | solution.py:981
  19.7 9.1 %collective-permute-start.7 = (bf16[128,768]{1,0:T(8,128)(2,1)S(1)}, bf16[128,768]{1,0:T(8,128)(2,1)S(1)}, u32[]{:S(2)}, u32[]{:S(2)}) collective-permute-start(bf16[128,768]{1,0:T(8,128)(2,1)S(1)} %collective-permute-done.1.own1), channel_id=1, source_target_pairs={{0,1},{1,0},{2,3},{3,2},{4,5},{5,4},{6,7},{7,6},{8,9},{9,8},{10,11... | collective-permute-start | bytes 589832 | tf_op jit(solution)/shard_map/ppermute | solution.py:981
  20.3 8.6 %collective-permute-start.8 = (bf16[192,1152]{1,0:T(8,128)(2,1)S(1)}, bf16[192,1152]{1,0:T(8,128)(2,1)S(1)}, u32[]{:S(2)}, u32[]{:S(2)}) collective-permute-start(bf16[192,1152]{1,0:T(8,128)(2,1)S(1)} %collective-permute-done.2.c), channel_id=1, source_target_pairs={{0,8},{8,0},{16,24},{24,16},{1,9},{9,1},{17,25},{25,17},{2,10},{10... | collective-permute-start | bytes 1327112 | tf_op jit(solution)/shard_map/ppermute | solution.py:977
  20.4 15.8 %collective-permute-start.9 = (bf16[192,1536]{1,0:T(8,128)(2,1)S(1)}, bf16[192,1536]{1,0:T(8,128)(2,1)}, u32[]{:S(2)}, u32[]{:S(2)}) collective-permute-start(bf16[192,1536]{1,0:T(8,128)(2,1)S(1)} %bitcast.26), channel_id=1, source_target_pairs={{0,16},{8,24},{16,0},{24,8},{1,17},{9,25},{17,1},{25,9},{2,18},{10... | collective-permute-start | bytes 1769480 | tf_op jit(solution)/shard_map/ppermute | solution.py:977
  21.0 7.8 %collective-permute-start.11 = (bf16[128,768]{1,0:T(8,128)(2,1)S(1)}, bf16[128,768]{1,0:T(8,128)(2,1)S(1)}, u32[]{:S(2)}, u32[]{:S(2)}) collective-permute-start(bf16[128,768]{1,0:T(8,128)(2,1)S(1)} %get-tuple-element.374), channel_id=1, source_target_pairs={{2,0},{0,2},{10,4},{8,6},{6,8},{4,10},{14,12},{12,14},{18,16},{16,... | collective-permute-start | bytes 589832 | tf_op jit(solution)/shard_map/ppermute | solution.py:996
  26.0 2.8 %collective-permute-start.10 = (bf16[128,768]{1,0:T(8,128)(2,1)S(1)}, bf16[128,768]{1,0:T(8,128)(2,1)S(1)}, u32[]{:S(2)}, u32[]{:S(2)}) collective-permute-start(bf16[128,768]{1,0:T(8,128)(2,1)S(1)} %get-tuple-element.375), channel_id=1, source_target_pairs={{0,0},{2,2},{8,4},{10,6},{4,8},{6,10},{12,12},{14,14},{16,16},{18,... | collective-permute-start | bytes 589832 | tf_op jit(solution)/shard_map/ppermute | solution.py:996
  40.4 5.1 %collective-permute-start.12 = (bf16[512,768]{1,0:T(8,128)(2,1)}, bf16[512,768]{1,0:T(8,128)(2,1)}, u32[]{:S(2)}, u32[]{:S(2)}) collective-permute-start(bf16[512,768]{1,0:T(8,128)(2,1)} %get-tuple-element.203.own_ref), channel_id=1, source_target_pairs={{0,8},{8,0},{16,24},{24,16},{1,9},{9,1},{17,25},{25,17},{2,10},{10... | collective-permute-start | bytes 2359304 | tf_op jit(solution)/shard_map/ppermute | solution.py:977
  42.5 12.2 %collective-permute-start.13 = (bf16[128,768]{1,0:T(8,128)(2,1)}, bf16[128,768]{1,0:T(8,128)(2,1)S(1)}, u32[]{:S(2)}, u32[]{:S(2)}) collective-permute-start(bf16[128,768]{1,0:T(8,128)(2,1)} %copy-done.2), channel_id=1, source_target_pairs={{0,1},{1,0},{2,3},{3,2},{4,5},{5,4},{6,7},{7,6},{8,9},{9,8},{10,11... | collective-permute-start | bytes 589832 | tf_op jit(solution)/shard_map/ppermute | solution.py:981
  44.1 10.6 %collective-permute-start.14 = (bf16[128,768]{1,0:T(8,128)(2,1)}, bf16[128,768]{1,0:T(8,128)(2,1)S(1)}, u32[]{:S(2)}, u32[]{:S(2)}) collective-permute-start(bf16[128,768]{1,0:T(8,128)(2,1)} %copy-done), channel_id=1, source_target_pairs={{0,1},{1,0},{2,3},{3,2},{4,5},{5,4},{6,7},{7,6},{8,9},{9,8},{10,11... | collective-permute-start | bytes 589832 | tf_op jit(solution)/shard_map/ppermute | solution.py:981
  44.6 21.3 %collective-permute-start.17 = (bf16[192,2304]{1,0:T(8,128)(2,1)S(1)}, bf16[192,2304]{1,0:T(8,128)(2,1)S(1)}, u32[]{:S(2)}, u32[]{:S(2)}) collective-permute-start(bf16[192,2304]{1,0:T(8,128)(2,1)S(1)} %pad_maximum_fusion.pa), channel_id=1, source_target_pairs={{0,16},{8,24},{16,0},{24,8},{1,17},{9,25},{17,1},{25,9},{2,18},{10... | collective-permute-start | bytes 2654216 | tf_op jit(solution)/shard_map/ppermute | solution.py:977
  46.5 20.4 %copy-start.24 = (bf16[768]{0:T(1024)(128)(2,1)S(1)}, bf16[768]{0:T(1024)(128)(2,1)}, u32[]{:S(2)}) copy-start(bf16[768]{0:T(1024)(128)(2,1)} %param.29) | copy-start | bytes 4612
  46.5 20.4 %copy-start.25 = (bf16[768]{0:T(1024)(128)(2,1)S(1)}, bf16[768]{0:T(1024)(128)(2,1)}, u32[]{:S(2)}) copy-start(bf16[768]{0:T(1024)(128)(2,1)} %param.28) | copy-start | bytes 4612
  46.5 20.4 %copy-start.26 = (bf16[768]{0:T(1024)(128)(2,1)S(1)}, bf16[768]{0:T(1024)(128)(2,1)}, u32[]{:S(2)}) copy-start(bf16[768]{0:T(1024)(128)(2,1)} %param.30) | copy-start | bytes 4612
  46.5 20.5 %copy-start.27 = (bf16[768]{0:T(1024)(128)(2,1)S(1)}, bf16[768]{0:T(1024)(128)(2,1)}, u32[]{:S(2)}) copy-start(bf16[768]{0:T(1024)(128)(2,1)} %param.34) | copy-start | bytes 4612
  46.5 20.5 %copy-start.21 = (bf16[1536]{0:T(1024)(128)(2,1)S(1)}, bf16[1536]{0:T(1024)(128)(2,1)}, u32[]{:S(2)}) copy-start(bf16[1536]{0:T(1024)(128)(2,1)} %param.32) | copy-start | bytes 9220
  46.5 22.8 %copy-start.1 = (bf16[128,768]{1,0:T(8,128)(2,1)S(1)}, bf16[128,768]{1,0:T(8,128)(2,1)}, u32[]{:S(2)}) copy-start(bf16[128,768]{1,0:T(8,128)(2,1)} %copy-done) | copy-start | bytes 589828
  46.5 22.8 %copy-start.3 = (bf16[128,768]{1,0:T(8,128)(2,1)S(1)}, bf16[128,768]{1,0:T(8,128)(2,1)}, u32[]{:S(2)}) copy-start(bf16[128,768]{1,0:T(8,128)(2,1)} %copy-done.2) | copy-start | bytes 589828
  54.7 12.1 %collective-permute-start.16 = (bf16[192,2304]{1,0:T(8,128)(2,1)S(1)}, bf16[192,2304]{1,0:T(8,128)(2,1)S(1)}, u32[]{:S(2)}, u32[]{:S(2)}) collective-permute-start(bf16[192,2304]{1,0:T(8,128)(2,1)S(1)} %pad_maximum_fusion.pa), channel_id=1, source_target_pairs={{0,8},{8,0},{16,24},{24,16},{1,9},{9,1},{17,25},{25,17},{2,10},{10... | collective-permute-start | bytes 2654216 | tf_op jit(solution)/shard_map/ppermute | solution.py:977
  54.8 12.0 %collective-permute-start.18 = (bf16[192,1536]{1,0:T(8,128)(2,1)S(1)}, bf16[192,1536]{1,0:T(8,128)(2,1)S(1)}, u32[]{:S(2)}, u32[]{:S(2)}) collective-permute-start(bf16[192,1536]{1,0:T(8,128)(2,1)S(1)} %bitcast.27), channel_id=1, source_target_pairs={{0,8},{8,0},{16,24},{24,16},{1,9},{9,1},{17,25},{25,17},{2,10},{10... | collective-permute-start | bytes 1769480 | tf_op jit(solution)/shard_map/ppermute | solution.py:977
  55.2 11.6 %collective-permute-start.19 = (bf16[192,1536]{1,0:T(8,128)(2,1)}, bf16[192,1536]{1,0:T(8,128)(2,1)S(1)}, u32[]{:S(2)}, u32[]{:S(2)}) collective-permute-start(bf16[192,1536]{1,0:T(8,128)(2,1)} %collective-permute-done.9.dc), channel_id=1, source_target_pairs={{0,8},{8,0},{16,24},{24,16},{1,9},{9,1},{17,25},{25,17},{2,10},{10... | collective-permute-start | bytes 1769480 | tf_op jit(solution)/shard_map/ppermute | solution.py:977
  55.3 11.5 %collective-permute-start.15 = (bf16[512,384]{1,0:T(8,128)(2,1)S(1)}, bf16[512,384]{1,0:T(8,128)(2,1)S(1)}, u32[]{:S(2)}, u32[]{:S(2)}) collective-permute-start(bf16[512,384]{1,0:T(8,128)(2,1)S(1)} %get-tuple-element.209.own_ref.out_ref.refs_4_), channel_id=1, source_target_pairs={{0,1},{1,0},{2,3},{3,2},{4,5},{5,4},{6,7},{7,6},{8,9},{9,8},{10,11... | collective-permute-start | bytes 1179656 | tf_op jit(solution)/shard_map/ppermute | solution.py:981
  66.8 2.5 %collective-permute-start.20 = (bf16[192,2304]{1,0:T(8,128)(2,1)S(1)}, bf16[192,2304]{1,0:T(8,128)(2,1)S(1)}, u32[]{:S(2)}, u32[]{:S(2)}) collective-permute-start(bf16[192,2304]{1,0:T(8,128)(2,1)S(1)} %collective-permute-done.17.pc), channel_id=1, source_target_pairs={{0,8},{8,0},{16,24},{24,16},{1,9},{9,1},{17,25},{25,17},{2,10},{10... | collective-permute-start | bytes 2654216 | tf_op jit(solution)/shard_map/ppermute | solution.py:977
  80.2 11.2 %collective-permute-start.21 = (bf16[256,768]{1,0:T(8,128)(2,1)S(1)}, bf16[256,768]{1,0:T(8,128)(2,1)S(1)}, u32[]{:S(2)}, u32[]{:S(2)}) collective-permute-start(bf16[256,768]{1,0:T(8,128)(2,1)S(1)} %get-tuple-element.226), channel_id=1, source_target_pairs={{0,1},{1,0},{2,3},{3,2},{4,5},{5,4},{6,7},{7,6},{8,9},{9,8},{10,11... | collective-permute-start | bytes 1179656 | tf_op jit(solution)/shard_map/ppermute | solution.py:981
  91.4 2.8 %collective-permute-start.22 = (bf16[384,1536]{1,0:T(8,128)(2,1)S(1)}, bf16[384,1536]{1,0:T(8,128)(2,1)S(1)}, u32[]{:S(2)}, u32[]{:S(2)}) collective-permute-start(bf16[384,1536]{1,0:T(8,128)(2,1)S(1)} %get-tuple-element.237), channel_id=1, source_target_pairs={{0,8},{8,0},{16,24},{24,16},{1,9},{9,1},{17,25},{25,17},{2,10},{10... | collective-permute-start | bytes 3538952 | tf_op jit(solution)/shard_map/ppermute | solution.py:977
  94.2 4.4 %collective-permute-start.25 = (bf16[384,1536]{1,0:T(8,128)(2,1)S(1)}, bf16[384,1536]{1,0:T(8,128)(2,1)S(1)}, u32[]{:S(2)}, u32[]{:S(2)}) collective-permute-start(bf16[384,1536]{1,0:T(8,128)(2,1)S(1)} %get-tuple-element.245), channel_id=1, source_target_pairs={{0,8},{8,0},{16,24},{24,16},{1,9},{9,1},{17,25},{25,17},{2,10},{10... | collective-permute-start | bytes 3538952 | tf_op jit(solution)/shard_map/ppermute | solution.py:977
  94.5 15.7 %collective-permute-start.24 = (bf16[192,1536]{1,0:T(8,128)(2,1)S(1)}, bf16[192,1536]{1,0:T(8,128)(2,1)S(1)}, u32[]{:S(2)}, u32[]{:S(2)}) collective-permute-start(bf16[192,1536]{1,0:T(8,128)(2,1)S(1)} %get-tuple-element.371), channel_id=1, source_target_pairs={{0,16},{8,24},{16,0},{24,8},{1,17},{9,25},{17,1},{25,9},{2,18},{10... | collective-permute-start | bytes 1769480 | tf_op jit(solution)/shard_map/ppermute | solution.py:977
  95.7 3.1 %collective-permute-start.26 = (bf16[2,128,768]{2,1,0:T(8,128)(2,1)S(1)}, bf16[2,128,768]{2,1,0:T(8,128)(2,1)}, u32[]{:S(2)}, u32[]{:S(2)}) collective-permute-start(bf16[2,128,768]{2,1,0:T(8,128)(2,1)S(1)} %get-tuple-element.247), channel_id=1, source_target_pairs={{0,0},{2,2},{4,8},{6,10},{8,4},{10,6},{12,12},{14,14},{16,16},{18,... | collective-permute-start | bytes 1179656 | tf_op jit(solution)/shard_map/ppermute | solution.py:996
  97.1 8.2 %collective-permute-start.23 = (bf16[256,768]{1,0:T(8,128)(2,1)S(1)}, bf16[256,768]{1,0:T(8,128)(2,1)S(1)}, u32[]{:S(2)}, u32[]{:S(2)}) collective-permute-start(bf16[256,768]{1,0:T(8,128)(2,1)S(1)} %get-tuple-element.241.d_own_ref.refs_2_), channel_id=1, source_target_pairs={{0,1},{1,0},{2,3},{3,2},{4,5},{5,4},{6,7},{7,6},{8,9},{9,8},{10,11... | collective-permute-start | bytes 1179656 | tf_op jit(solution)/shard_map/ppermute | solution.py:981
  110.3 14.4 %collective-permute-start.27 = (bf16[96,1536]{1,0:T(8,128)(2,1)S(1)}, bf16[96,1536]{1,0:T(8,128)(2,1)S(1)}, u32[]{:S(2)}, u32[]{:S(2)}) collective-permute-start(bf16[96,1536]{1,0:T(8,128)(2,1)S(1)} %get-tuple-element.257), channel_id=1, source_target_pairs={{0,2},{2,0},{4,6},{6,4},{1,3},{3,1},{5,7},{7,5},{8,10},{10,8},{12,... | collective-permute-start | bytes 884744 | tf_op jit(solution)/shard_map/ppermute | solution.py:1026
  111.1 15.0 %collective-permute-start.29 = (bf16[2,128,768]{2,1,0:T(8,128)(2,1)S(1)}, bf16[2,128,768]{2,1,0:T(8,128)(2,1)S(1)}, u32[]{:S(2)}, u32[]{:S(2)}) collective-permute-start(bf16[2,128,768]{2,1,0:T(8,128)(2,1)S(1)} %get-tuple-element.260), channel_id=1, source_target_pairs={{0,2},{2,0},{4,10},{6,8},{8,6},{10,4},{12,14},{14,12},{16,18},{18,... | collective-permute-start | bytes 1179656 | tf_op jit(solution)/shard_map/ppermute | solution.py:996
  112.3 14.0 %collective-permute-start.28 = (bf16[192,1536]{1,0:T(8,128)(2,1)S(1)}, bf16[192,1536]{1,0:T(8,128)(2,1)S(1)}, u32[]{:S(2)}, u32[]{:S(2)}) collective-permute-start(bf16[192,1536]{1,0:T(8,128)(2,1)S(1)} %get-tuple-element.258), channel_id=1, source_target_pairs={{0,16},{8,24},{16,0},{24,8},{1,17},{9,25},{17,1},{25,9},{2,18},{10... | collective-permute-start | bytes 1769480 | tf_op jit(solution)/shard_map/ppermute | solution.py:977
  126.3 5.7 %collective-permute-start.30 = (bf16[512,768]{1,0:T(8,128)(2,1)S(1)}, bf16[512,768]{1,0:T(8,128)(2,1)S(1)}, u32[]{:S(2)}, u32[]{:S(2)}) collective-permute-start(bf16[512,768]{1,0:T(8,128)(2,1)S(1)} %get-tuple-element.261), channel_id=1, source_target_pairs={{0,8},{8,0},{16,24},{24,16},{1,9},{9,1},{17,25},{25,17},{2,10},{10... | collective-permute-start | bytes 2359304 | tf_op jit(solution)/shard_map/ppermute | solution.py:977
  130.2 12.1 %collective-permute-start.32 = (bf16[96,1536]{1,0:T(8,128)(2,1)S(1)}, bf16[96,1536]{1,0:T(8,128)(2,1)S(1)}, u32[]{:S(2)}, u32[]{:S(2)}) collective-permute-start(bf16[96,1536]{1,0:T(8,128)(2,1)S(1)} %get-tuple-element.274), channel_id=1, source_target_pairs={{0,2},{2,0},{4,6},{6,4},{1,3},{3,1},{5,7},{7,5},{8,10},{10,8},{12,... | collective-permute-start | bytes 884744 | tf_op jit(solution)/shard_map/ppermute | solution.py:1026
  130.3 9.9 %collective-permute-start.31 = (bf16[48,1536]{1,0:T(8,128)(2,1)S(1)}, bf16[48,1536]{1,0:T(8,128)(2,1)S(1)}, u32[]{:S(2)}, u32[]{:S(2)}) collective-permute-start(bf16[48,1536]{1,0:T(8,128)(2,1)S(1)} %get-tuple-element.273), channel_id=1, source_target_pairs={{0,4},{2,6},{4,0},{6,2},{1,5},{3,7},{5,1},{7,3},{8,12},{10,14},{12... | collective-permute-start | bytes 442376 | tf_op jit(solution)/shard_map/ppermute | solution.py:1026
  142.3 18.0 %collective-permute-start.33 = (bf16[384,1536]{1,0:T(8,128)(2,1)S(1)}, bf16[384,1536]{1,0:T(8,128)(2,1)S(1)}, u32[]{:S(2)}, u32[]{:S(2)}) collective-permute-start(bf16[384,1536]{1,0:T(8,128)(2,1)S(1)} %get-tuple-element.275), channel_id=1, source_target_pairs={{0,8},{8,0},{16,24},{24,16},{1,9},{9,1},{17,25},{25,17},{2,10},{10... | collective-permute-start | bytes 3538952 | tf_op jit(solution)/shard_map/ppermute | solution.py:977
  142.3 18.0 %collective-permute-start.34 = (bf16[256,768]{1,0:T(8,128)(2,1)S(1)}, bf16[256,768]{1,0:T(8,128)(2,1)S(1)}, u32[]{:S(2)}, u32[]{:S(2)}) collective-permute-start(bf16[256,768]{1,0:T(8,128)(2,1)S(1)} %get-tuple-element.276), channel_id=1, source_target_pairs={{0,1},{1,0},{2,3},{3,2},{4,5},{5,4},{6,7},{7,6},{8,9},{9,8},{10,11... | collective-permute-start | bytes 1179656 | tf_op jit(solution)/shard_map/ppermute | solution.py:981
  143.9 13.4 %collective-permute-start.36 = (bf16[48,1536]{1,0:T(8,128)(2,1)S(1)}, bf16[48,1536]{1,0:T(8,128)(2,1)S(1)}, u32[]{:S(2)}, u32[]{:S(2)}) collective-permute-start(bf16[48,1536]{1,0:T(8,128)(2,1)S(1)} %get-tuple-element.282), channel_id=1, source_target_pairs={{0,4},{2,6},{4,0},{6,2},{1,5},{3,7},{5,1},{7,3},{8,12},{10,14},{12... | collective-permute-start | bytes 442376 | tf_op jit(solution)/shard_map/ppermute | solution.py:1026
  145.2 15.2 %collective-permute-start.35 = (bf16[48,1536]{1,0:T(8,128)(2,1)S(1)}, bf16[48,1536]{1,0:T(8,128)(2,1)S(1)}, u32[]{:S(2)}, u32[]{:S(2)}) collective-permute-start(bf16[48,1536]{1,0:T(8,128)(2,1)S(1)} %get-tuple-element.281.mine_ref), channel_id=1, source_target_pairs={{0,4},{2,6},{4,0},{6,2},{1,5},{3,7},{5,1},{7,3},{8,12},{10,14},{12... | collective-permute-start | bytes 442376 | tf_op jit(solution)/shard_map/ppermute | solution.py:1026
  146.9 7.5 %collective-permute-start.37 = (f32[5,768]{1,0:T(8,128)S(1)}, f32[5,768]{1,0:T(8,128)S(1)}, u32[]{:S(2)}, u32[]{:S(2)}) collective-permute-start(f32[5,768]{1,0:T(8,128)S(1)} %get-tuple-element.283.mine_ref), channel_id=1, source_target_pairs={{0,1},{1,0},{2,3},{3,2},{4,5},{5,4},{6,7},{7,6},{8,9},{9,8},{10,11... | collective-permute-start | bytes 46088 | tf_op jit(solution)/shard_map/ppermute | solution.py:981
  160.4 1.3 collective-permute-start.38
  161.8 20.4 %collective-permute-start.39 = (bf16[208,1536]{1,0:T(8,128)(2,1)S(1)}, bf16[208,1536]{1,0:T(8,128)(2,1)S(1)}, u32[]{:S(2)}, u32[]{:S(2)}) collective-permute-start(bf16[208,1536]{1,0:T(8,128)(2,1)S(1)} %get-tuple-element.298), channel_id=1, source_target_pairs={{0,16},{8,24},{16,0},{24,8},{1,17},{9,25},{17,1},{25,9},{2,18},{10... | collective-permute-start | bytes 1916936 | tf_op jit(solution)/shard_map/ppermute | solution.py:977
  163.4 18.8 %collective-permute-start.44 = (bf16[2,128,768]{2,1,0:T(8,128)(2,1)}, bf16[2,128,768]{2,1,0:T(8,128)(2,1)}, u32[]{:S(2)}, u32[]{:S(2)}) collective-permute-start(bf16[2,128,768]{2,1,0:T(8,128)(2,1)} %collective-permute-done.26), channel_id=1, source_target_pairs={{0,1},{1,0},{2,3},{3,2},{4,5},{5,4},{6,7},{7,6},{8,9},{9,8},{10,11... | collective-permute-start | bytes 1179656 | tf_op jit(solution)/shard_map/ppermute | solution.py:981
  163.9 7.3 %collective-permute-start.41 = (bf16[48,1536]{1,0:T(8,128)(2,1)S(1)}, bf16[48,1536]{1,0:T(8,128)(2,1)S(1)}, u32[]{:S(2)}, u32[]{:S(2)}) collective-permute-start(bf16[48,1536]{1,0:T(8,128)(2,1)S(1)} %get-tuple-element.303), channel_id=1, source_target_pairs={{0,4},{2,6},{4,0},{6,2},{1,5},{3,7},{5,1},{7,3},{8,12},{10,14},{12... | collective-permute-start | bytes 442376 | tf_op jit(solution)/shard_map/ppermute | solution.py:1026
  164.0 18.2 %collective-permute-start.40 = (bf16[96,1536]{1,0:T(8,128)(2,1)S(1)}, bf16[96,1536]{1,0:T(8,128)(2,1)S(1)}, u32[]{:S(2)}, u32[]{:S(2)}) collective-permute-start(bf16[96,1536]{1,0:T(8,128)(2,1)S(1)} %get-tuple-element.331), channel_id=1, source_target_pairs={{0,2},{2,0},{4,6},{6,4},{1,3},{3,1},{5,7},{7,5},{8,10},{10,8},{12,... | collective-permute-start | bytes 884744 | tf_op jit(solution)/shard_map/ppermute | solution.py:1026
  165.0 7.0 %collective-permute-start.42 = (bf16[128,768]{1,0:T(8,128)(2,1)S(1)}, bf16[128,768]{1,0:T(8,128)(2,1)}, u32[]{:S(2)}, u32[]{:S(2)}) collective-permute-start(bf16[128,768]{1,0:T(8,128)(2,1)S(1)} %get-tuple-element.305), channel_id=1, source_target_pairs={{0,0},{2,2},{4,8},{6,10},{8,4},{10,6},{12,12},{14,14},{16,16},{18,... | collective-permute-start | bytes 589832 | tf_op jit(solution)/shard_map/ppermute | solution.py:996
  171.9 10.2 %collective-permute-start.43 = (bf16[128,768]{1,0:T(8,128)(2,1)S(1)}, bf16[128,768]{1,0:T(8,128)(2,1)}, u32[]{:S(2)}, u32[]{:S(2)}) collective-permute-start(bf16[128,768]{1,0:T(8,128)(2,1)S(1)} %get-tuple-element.306), channel_id=1, source_target_pairs={{0,2},{2,0},{4,10},{6,8},{8,6},{10,4},{12,14},{14,12},{16,18},{18,... | collective-permute-start | bytes 589832 | tf_op jit(solution)/shard_map/ppermute | solution.py:996
  182.3 9.7 %collective-permute-start.45 = (bf16[64,1536]{1,0:T(8,128)(2,1)S(1)}, bf16[64,1536]{1,0:T(8,128)(2,1)S(1)}, u32[]{:S(2)}, u32[]{:S(2)}) collective-permute-start(bf16[64,1536]{1,0:T(8,128)(2,1)S(1)} %get-tuple-element.310), channel_id=1, source_target_pairs={{0,2},{2,4},{4,6},{6,0},{1,3},{3,5},{5,7},{7,1},{8,10},{10,12},{12... | collective-permute-start | bytes 589832 | tf_op jit(solution)/shard_map/ppermute | solution.py:1022
  182.4 16.0 %collective-permute-start.46 = (bf16[64,1536]{1,0:T(8,128)(2,1)S(1)}, bf16[64,1536]{1,0:T(8,128)(2,1)S(1)}, u32[]{:S(2)}, u32[]{:S(2)}) collective-permute-start(bf16[64,1536]{1,0:T(8,128)(2,1)S(1)} %get-tuple-element.313), channel_id=1, source_target_pairs={{0,4},{2,6},{4,0},{6,2},{1,5},{3,7},{5,1},{7,3},{8,12},{10,14},{12... | collective-permute-start | bytes 589832 | tf_op jit(solution)/shard_map/ppermute | solution.py:1022
  185.0 19.2 %collective-permute-start.50 = (bf16[2,128,768]{2,1,0:T(8,128)(2,1)S(1)}, bf16[2,128,768]{2,1,0:T(8,128)(2,1)S(1)}, u32[]{:S(2)}, u32[]{:S(2)}) collective-permute-start(bf16[2,128,768]{2,1,0:T(8,128)(2,1)S(1)} %collective-permute-done.29), channel_id=1, source_target_pairs={{0,1},{1,0},{2,3},{3,2},{4,5},{5,4},{6,7},{7,6},{8,9},{9,8},{10,11... | collective-permute-start | bytes 1179656 | tf_op jit(solution)/shard_map/ppermute | solution.py:981
  186.6 17.6 %collective-permute-start.51 = (bf16[96,1536]{1,0:T(8,128)(2,1)S(1)}, bf16[96,1536]{1,0:T(8,128)(2,1)S(1)}, u32[]{:S(2)}, u32[]{:S(2)}) collective-permute-start(bf16[96,1536]{1,0:T(8,128)(2,1)S(1)} %maximum_select_fusion.6), channel_id=1, source_target_pairs={{0,2},{2,0},{4,6},{6,4},{1,3},{3,1},{5,7},{7,5},{8,10},{10,8},{12,... | collective-permute-start | bytes 884744 | tf_op jit(solution)/shard_map/ppermute | solution.py:1026
  188.4 15.3 %collective-permute-start.47 = (bf16[64,1536]{1,0:T(8,128)(2,1)S(1)}, bf16[64,1536]{1,0:T(8,128)(2,1)S(1)}, u32[]{:S(2)}, u32[]{:S(2)}) collective-permute-start(bf16[64,1536]{1,0:T(8,128)(2,1)S(1)} %get-tuple-element.314), channel_id=1, source_target_pairs={{0,6},{2,0},{4,2},{6,4},{1,7},{3,1},{5,3},{7,5},{8,14},{10,8},{12,... | collective-permute-start | bytes 589832 | tf_op jit(solution)/shard_map/ppermute | solution.py:1022
  192.0 11.6 %collective-permute-start.48 = (bf16[128,768]{1,0:T(8,128)(2,1)}, bf16[128,768]{1,0:T(8,128)(2,1)S(1)}, u32[]{:S(2)}, u32[]{:S(2)}) collective-permute-start(bf16[128,768]{1,0:T(8,128)(2,1)} %collective-permute-done.42), channel_id=1, source_target_pairs={{0,1},{1,0},{2,3},{3,2},{4,5},{5,4},{6,7},{7,6},{8,9},{9,8},{10,11... | collective-permute-start | bytes 589832 | tf_op jit(solution)/shard_map/ppermute | solution.py:981
  198.3 5.9 %collective-permute-start.49 = (bf16[128,768]{1,0:T(8,128)(2,1)}, bf16[128,768]{1,0:T(8,128)(2,1)S(1)}, u32[]{:S(2)}, u32[]{:S(2)}) collective-permute-start(bf16[128,768]{1,0:T(8,128)(2,1)} %collective-permute-done.43), channel_id=1, source_target_pairs={{0,1},{1,0},{2,3},{3,2},{4,5},{5,4},{6,7},{7,6},{8,9},{9,8},{10,11... | collective-permute-start | bytes 589832 | tf_op jit(solution)/shard_map/ppermute | solution.py:981
  204.3 9.5 %collective-permute-start.54 = (bf16[48,1536]{1,0:T(8,128)(2,1)S(1)}, bf16[48,1536]{1,0:T(8,128)(2,1)S(1)}, u32[]{:S(2)}, u32[]{:S(2)}) collective-permute-start(bf16[48,1536]{1,0:T(8,128)(2,1)S(1)} %get-tuple-element.335.a), channel_id=1, source_target_pairs={{0,6},{2,0},{4,2},{6,4},{1,7},{3,1},{5,3},{7,5},{8,14},{10,8},{12,... | collective-permute-start | bytes 442376 | tf_op jit(solution)/shard_map/ppermute | solution.py:1022
  205.1 12.3 %collective-permute-start.53 = (bf16[48,1536]{1,0:T(8,128)(2,1)S(1)}, bf16[48,1536]{1,0:T(8,128)(2,1)S(1)}, u32[]{:S(2)}, u32[]{:S(2)}) collective-permute-start(bf16[48,1536]{1,0:T(8,128)(2,1)S(1)} %get-tuple-element.335.a), channel_id=1, source_target_pairs={{0,4},{2,6},{4,0},{6,2},{1,5},{3,7},{5,1},{7,3},{8,12},{10,14},{12... | collective-permute-start | bytes 442376 | tf_op jit(solution)/shard_map/ppermute | solution.py:1022
  206.1 11.3 %collective-permute-start.52 = (bf16[48,1536]{1,0:T(8,128)(2,1)S(1)}, bf16[48,1536]{1,0:T(8,128)(2,1)S(1)}, u32[]{:S(2)}, u32[]{:S(2)}) collective-permute-start(bf16[48,1536]{1,0:T(8,128)(2,1)S(1)} %get-tuple-element.335.a), channel_id=1, source_target_pairs={{0,2},{2,4},{4,6},{6,0},{1,3},{3,5},{5,7},{7,1},{8,10},{10,12},{12... | collective-permute-start | bytes 442376 | tf_op jit(solution)/shard_map/ppermute | solution.py:1022
  (22 other events, 141.2 us)

commit v6 on v5

--- a/solution.py
+++ b/solution.py
@@ -1081,18 +1081,7 @@
     )
 
     rows_parts += [swap_tensor(v) for v in rows_parts]
-    proj_last = exchange(proj_far, 1)
-    down_far = exchange(down_own, 2)
-    pack_own = jnp.concatenate([w_up, out_own, out_peer], axis=1)
-    top_picked = pick_in(cotangent.reshape(by_half), odd, upper)
-    top_parts = [route(top_picked[step], step, True) for step in range(2)]
-    *rows_parts, proj_last, down_far, pack_own, top_0, top_1 = together(
-        *rows_parts, proj_last, down_far, pack_own, *top_parts
-    )
-
-    pack_far = exchange(pack_own, 2)
-    top_parts = [top_0, top_1, swap_tensor(top_0), swap_tensor(top_1)]
-    proj_blocks = (proj_own, proj_near, proj_far, proj_last)
+    rows_parts[2], lengths, lengths_other = together(rows_parts[2], lengths, lengths_other)
     lengths_near = jnp.where(plane // 2 == near, lengths, lengths_other)
     length = jnp.where(odd, lengths_near[1], lengths_near[0])
     index = jnp.arange(9, dtype=jnp.int32)
@@ -1101,6 +1090,18 @@
     piece = jnp.where(quarter < 2, side, 1 - side)
     starts = (2 * core + (quarter % 2 ^ plane % 2)) * block + piece * half
     info = jnp.where(index < 8, starts, length)
+    proj_last = exchange(proj_far, 1)
+    down_far = exchange(down_own, 2)
+    pack_own = jnp.concatenate([w_up, out_own, out_peer], axis=1)
+    top_picked = pick_in(cotangent.reshape(by_half), odd, upper)
+    top_parts = [route(top_picked[step], step, True) for step in range(2)]
+    *rows_parts, proj_last, down_far, pack_own, info, top_0, top_1 = together(
+        *rows_parts, proj_last, down_far, pack_own, info, *top_parts
+    )
+
+    pack_far = exchange(pack_own, 2)
+    top_parts = [top_0, top_1, swap_tensor(top_0), swap_tensor(top_1)]
+    proj_blocks = (proj_own, proj_near, proj_far, proj_last)
     rows_low, normed_low, queries, pair_own, proj = enter(
         rows_parts, row(ln1_gain), row(ln1_bias), row(b_query), row(b_value), proj_blocks
     )

time: 220 us -> 218 us (level)
  other arithmetic: 7.83 us -> 10.8 us
    ppermute x8, starting transfers between devices: 7.55 us -> 10.7 us  [swap_planes(): return lax.ppermute(value, 'context', [(i, i ^ bit) for i in range(4)])]
    unnamed x65 -> x51, local copies, waits for them, and re-layouts: 5.02 us -> 3.78 us
  transfers between devices with their start and end apart: 55 -> 55, of which waited for: 28 -> 27; matrix products, arithmetic and copies ran while one was open for 4% -> 5% of each run, Pallas kernels for 13% -> 12%
where the time goes in v6:
time: 218 us
  waiting for transfers between devices  101 us (46%)
  starting transfers between devices  56 us (26%)
  Pallas kernels  41.6 us (19%)
  other arithmetic  10.8 us (5%)
  local copies, waits for them, and re-layouts  6.3 us (3%)
  between operations  2.61 us (1%)
    ppermute x14, waiting for transfers between devices, swap_tensor(): return lax.ppermute(value, 'tensor', [(0, 1), (1, 0)])  30 us
    ppermute x19, waiting for transfers between devices, exchange(): return lax.ppermute(value, 'dp', [(i, i ^ bit) for i in range(size)])  26.4 us
    ppermute x14, starting transfers between devices, swap_tensor(): return lax.ppermute(value, 'tensor', [(0, 1), (1, 0)])  17.5 us
    ppermute x8, waiting for transfers between devices, swap_planes(): return lax.ppermute(value, 'context', [(i, i ^ bit) for i in range(4)])  17.1 us
    ppermute x19, starting transfers between devices, exchange(): return lax.ppermute(value, 'dp', [(i, i ^ bit) for i in range(size)])  15.3 us
    ppermute x6, waiting for transfers between devices, turn_planes(): lax.ppermute(value, 'context', [(i, (i + step) % 4) for i in range(4)])  15.1 us
    ppermute x8, waiting for transfers between devices, route(): return lax.ppermute(value, ('dp', 'context'), pairs)  12.1 us
    pallas_call x14, Pallas kernels, call_once(): pl.pallas_call(kernel, out_shape=tuple(shapes), grid=(1,), in_specs=[fixe...  11.5 us
  transfers between devices with their start and end apart: 55, of which 27 were waited for; matrix products, arithmetic and copies ran while one was open for 5% of the time, Pallas kernels for 12%

profile of v6, /device:TPU:0, one launch (start us, length us, event | category | flops | bytes accessed | tf_op | source)
XLA Modules:
  0.0 218.0 jit_solution(5267448540309660138)
XLA Ops:
  0.8 1.4 slice_select_fusion.1
  2.9 2.6 %collective-permute-start.2 = (bf16[192,1152]{1,0:T(8,128)(2,1)S(1)}, bf16[192,1152]{1,0:T(8,128)(2,1)}, u32[]{:S(2)}, u32[]{:S(2)}) collective-permute-start(bf16[192,1152]{1,0:T(8,128)(2,1)S(1)} %constant_dynamic-update-slice_fusion.a), channel_id=1, source_target_pairs={{0,16},{8,24},{16,0},{24,8},{1,17},{9,25},{17,1},{25,9},{2,18},{10... | collective-permute-start | bytes 1327112 | tf_op jit(solution)/shard_map/ppermute | solution.py:977
  6.1 1.6 collective-permute-start.1
  7.8 3.5 %collective-permute-start.5 = (s32[2]{0:T(128)S(1)}, s32[2]{0:T(128)S(1)}, u32[]{:S(2)}, u32[]{:S(2)}) collective-permute-start(s32[2]{0:T(128)S(1)} %copy-done.20), channel_id=1, source_target_pairs={{0,8},{8,0},{16,24},{24,16},{1,9},{9,1},{17,25},{25,17},{2,10},{10... | collective-permute-start | bytes 32 | tf_op jit(solution)/shard_map/ppermute | solution.py:977
  12.6 1.5 collective-permute-start.4
  14.2 4.5 %collective-permute-done.4 = bf16[192,384]{1,0:T(8,128)(2,1)S(1)} collective-permute-done((bf16[192,384]{1,0:T(8,128)(2,1)S(1)}, bf16[192,384]{1,0:T(8,128)(2,1)S(1)}, u32[]{:S(2)}, u32[]{:S(2)}) %collective-permute-start.4) | collective-permute-done | bytes 147488 | tf_op jit(solution)/shard_map/ppermute | solution.py:981
  18.7 1.6 collective-permute-start.6
  22.1 1.6 collective-permute-start.10
  24.3 1.3 pad_maximum_fusion.pa
  25.5 1.0 collective-permute-done.6.peer0
  27.2 2.4 %collective-permute-start.8 = (bf16[192,1152]{1,0:T(8,128)(2,1)}, bf16[192,1152]{1,0:T(8,128)(2,1)}, u32[]{:S(2)}, u32[]{:S(2)}) collective-permute-start(bf16[192,1152]{1,0:T(8,128)(2,1)} %collective-permute-done.2.c), channel_id=1, source_target_pairs={{0,8},{8,0},{16,24},{24,16},{1,9},{9,1},{17,25},{25,17},{2,10},{10... | collective-permute-start | bytes 1327112 | tf_op jit(solution)/shard_map/ppermute | solution.py:977
  31.6 5.5 %collective-permute-done.9.dc = bf16[192,1536]{1,0:T(8,128)(2,1)S(1)} collective-permute-done((bf16[192,1536]{1,0:T(8,128)(2,1)S(1)}, bf16[192,1536]{1,0:T(8,128)(2,1)S(1)}, u32[]{:S(2)}, u32[]{:S(2)}) %collective-permute-start.9) | collective-permute-done | bytes 589856 | tf_op jit(solution)/shard_map/ppermute | solution.py:977
  37.1 0.9 copy-done.2
  38.1 3.0 %shard_map.305 = (bf16[512,768]{1,0:T(8,128)(2,1)S(1)}, bf16[512,768]{1,0:T(8,128)(2,1)S(1)}, bf16[512,384]{1,0:T(8,128)(2,1)S(1)}, bf16[512,768]{1,0:T(8,128)(2,1)S(1)}, bf16[768,1152]{1,0:T(8,128)(2,1)S(1)}) custom-call(bf16[128,768]{1,0:T(8,128)(2,1)S(1)} %collective-permute-done.own0, bf16[128,768]{1,0:T(8,128)(2,1)} %collective-permute-done.1.own1, ...), custom_call_target="tpu_custom_call" | custom-call | flops 905969664 | bytes 7082496 | tf_op jit(solution)/shard_map/pallas_call | solution.py:452
  41.1 2.7 %collective-permute-start.12 = (bf16[512,768]{1,0:T(8,128)(2,1)S(1)}, bf16[512,768]{1,0:T(8,128)(2,1)S(1)}, u32[]{:S(2)}, u32[]{:S(2)}) collective-permute-start(bf16[512,768]{1,0:T(8,128)(2,1)S(1)} %get-tuple-element.211.own_ref), channel_id=1, source_target_pairs={{0,8},{8,0},{16,24},{24,16},{1,9},{9,1},{17,25},{25,17},{2,10},{10... | collective-permute-start | bytes 2359304 | tf_op jit(solution)/shard_map/ppermute | solution.py:977
  43.8 1.5 collective-permute-start.13
  46.4 7.0 %shard_map.306 = (bf16[512,384]{1,0:T(8,128)(2,1)S(1)}, f32[3,2,512]{2,1,0:T(2,128)S(1)}) custom-call(s32[9]{0:T(128)S(1)} %compare_select_fusion.4.info, bf16[512,384]{1,0:T(8,128)(2,1)S(1)} %get-tuple-element.210.query_ref, bf16[512,768]{1,0:T(8,128)(2,1)S(1)} %get-tuple-element.211.own_ref, bf16[512,768]{1,0:T(8,128)(2,1)S(1)} %collective-permute-done.12.other_ref), custom_call_target="tpu_custom_call" | custom-call | flops 3221225472 | bytes 2359296 | tf_op jit(solution)/shard_map/pallas_call | solution.py:331
  53.4 1.5 collective-permute-done.14.top3
  55.4 1.5 collective-permute-start.15
  56.9 10.0 %collective-permute-done.17.pc = bf16[192,2304]{1,0:T(8,128)(2,1)S(1)} collective-permute-done((bf16[192,2304]{1,0:T(8,128)(2,1)S(1)}, bf16[192,2304]{1,0:T(8,128)(2,1)S(1)}, u32[]{:S(2)}, u32[]{:S(2)}) %collective-permute-start.17) | collective-permute-done | bytes 884768 | tf_op jit(solution)/shard_map/ppermute | solution.py:977
  67.1 2.3 %collective-permute-done.20.pd = bf16[192,2304]{1,0:T(8,128)(2,1)S(1)} collective-permute-done((bf16[192,2304]{1,0:T(8,128)(2,1)S(1)}, bf16[192,2304]{1,0:T(8,128)(2,1)S(1)}, u32[]{:S(2)}, u32[]{:S(2)}) %collective-permute-start.20) | collective-permute-done | bytes 884768 | tf_op jit(solution)/shard_map/ppermute | solution.py:977
  69.4 10.9 %shard_map.307 = (f32[256,768]{1,0:T(8,128)S(1)}, bf16[512,768]{1,0:T(8,128)(2,1)S(1)}, bf16[512,768]{1,0:T(8,128)(2,1)S(1)}, bf16[512,1536]{1,0:T(8,128)(2,1)S(...) custom-call(s32[9]{0:T(128)S(1)} %compare_select_fusion.4.info, ...), custom_call_target="tpu_custom_call" | custom-call | flops 4831838208 | bytes 20971520 | tf_op jit(solution)/shard_map/pallas_call | solution.py:658
  80.3 1.6 collective-permute-start.21
  81.9 1.6 shard_map.308
  83.5 1.6 shard_map.309
  85.1 6.5 %collective-permute-done.21.got_ref = bf16[256,768]{1,0:T(8,128)(2,1)S(1)} collective-permute-done((bf16[256,768]{1,0:T(8,128)(2,1)S(1)}, bf16[256,768]{1,0:T(8,128)(2,1)S(1)}, u32[]{:S(2)}, u32[]{:S(2)}) %collective-permute-start.21) | collective-permute-done | bytes 393248 | tf_op jit(solution)/shard_map/ppermute | solution.py:981
  91.5 1.3 shard_map.310
  92.8 1.5 collective-permute-done.22
  95.9 1.6 collective-permute-start.23
  97.7 9.0 %collective-permute-done.23.d_peer_ref.refs_3_ = bf16[256,768]{1,0:T(8,128)(2,1)S(1)} collective-permute-done((bf16[256,768]{1,0:T(8,128)(2,1)S(1)}, bf16[256,768]{1,0:T(8,128)(2,1)S(1)}, u32[]{:S(2)}, u32[]{:S(2)}) %collective-permute-start.23) | collective-permute-done | bytes 393248 | tf_op jit(solution)/shard_map/ppermute | solution.py:981
  106.7 3.6 %collective-permute-done.24.refs_1_ = bf16[192,1536]{1,0:T(8,128)(2,1)S(1)} collective-permute-done((bf16[192,1536]{1,0:T(8,128)(2,1)S(1)}, bf16[192,1536]{1,0:T(8,128)(2,1)S(1)}, u32[]{:S(2)}, u32[]{:S(2)}) %collective-permute-start.24) | collective-permute-done | bytes 589856 | tf_op jit(solution)/shard_map/ppermute | solution.py:977
  110.4 1.5 collective-permute-start.27
  113.0 10.4 %shard_map.311 = (bf16[512,384]{1,0:T(8,128)(2,1)S(1)}, bf16[512,768]{1,0:T(8,128)(2,1)S(1)}, bf16[512,768]{1,0:T(8,128)(2,1)S(1)}) custom-call(s32[9]{0:T(128)S(1)} %compare_select_fusion.4.info, bf16[512,384]{1,0:T(8,128)(2,1)S(1)} %get-tuple-element.210.query_ref, bf16[512,768]{1,0:T(8,128)(2,1)S(1)} %get-tuple-element.211.own_ref, ...), custom_call_target="tpu_custom_call" | custom-call | flops 8053063680 | bytes 4718592 | tf_op jit(solution)/shard_map/pallas_call | solution.py:413
  123.4 2.9 %collective-permute-done.29 = bf16[2,128,768]{2,1,0:T(8,128)(2,1)S(1)} collective-permute-done((bf16[2,128,768]{2,1,0:T(8,128)(2,1)S(1)}, bf16[2,128,768]{2,1,0:T(8,128)(2,1)S(1)}, u32[]{:S(2)}, u32[]{:S(2)}) %collective-permute-start.29) | collective-permute-done | bytes 393248 | tf_op jit(solution)/shard_map/ppermute | solution.py:996
  126.3 1.6 collective-permute-done.28.refs_3_
  130.3 1.8 shard_map.313
  132.1 1.9 shard_map.314
  134.0 5.1 %collective-permute-done.31.b_ref = bf16[48,1536]{1,0:T(8,128)(2,1)S(1)} collective-permute-done((bf16[48,1536]{1,0:T(8,128)(2,1)S(1)}, bf16[48,1536]{1,0:T(8,128)(2,1)S(1)}, u32[]{:S(2)}, u32[]{:S(2)}) %collective-permute-start.31) | collective-permute-done | bytes 147488 | tf_op jit(solution)/shard_map/ppermute | solution.py:1026
  139.1 1.6 collective-permute-done.32.right_ref
  140.7 1.5 collective-permute-start.34
  142.3 1.8 collective-permute-start.36
  144.1 1.2 collective-permute-start.35
  145.8 7.0 %collective-permute-done.37.theirs_ref = f32[5,768]{1,0:T(8,128)S(1)} collective-permute-done((f32[5,768]{1,0:T(8,128)S(1)}, f32[5,768]{1,0:T(8,128)S(1)}, u32[]{:S(2)}, u32[]{:S(2)}) %collective-permute-start.37) | collective-permute-done | bytes 15392 | tf_op jit(solution)/shard_map/ppermute | solution.py:981
  152.8 2.3 %collective-permute-done.36.right_ref = bf16[48,1536]{1,0:T(8,128)(2,1)S(1)} collective-permute-done((bf16[48,1536]{1,0:T(8,128)(2,1)S(1)}, bf16[48,1536]{1,0:T(8,128)(2,1)S(1)}, u32[]{:S(2)}, u32[]{:S(2)}) %collective-permute-start.36) | collective-permute-done | bytes 147488 | tf_op jit(solution)/shard_map/ppermute | solution.py:1026
  155.1 3.1 %collective-permute-done.35.theirs_ref = bf16[48,1536]{1,0:T(8,128)(2,1)S(1)} collective-permute-done((bf16[48,1536]{1,0:T(8,128)(2,1)S(1)}, bf16[48,1536]{1,0:T(8,128)(2,1)S(1)}, u32[]{:S(2)}, u32[]{:S(2)}) %collective-permute-start.35) | collective-permute-done | bytes 147488 | tf_op jit(solution)/shard_map/ppermute | solution.py:1026
  160.9 2.3 %collective-permute-start.40 = (bf16[96,1536]{1,0:T(8,128)(2,1)S(1)}, bf16[96,1536]{1,0:T(8,128)(2,1)}, u32[]{:S(2)}, u32[]{:S(2)}) collective-permute-start(bf16[96,1536]{1,0:T(8,128)(2,1)S(1)} %get-tuple-element.339), channel_id=1, source_target_pairs={{0,2},{2,0},{4,6},{6,4},{1,3},{3,1},{5,7},{7,5},{8,10},{10,8},{12,... | collective-permute-start | bytes 884744 | tf_op jit(solution)/shard_map/ppermute | solution.py:1026
  163.1 1.3 collective-permute-start.42
  164.5 5.0 %collective-permute-done.41 = bf16[48,1536]{1,0:T(8,128)(2,1)S(1)} collective-permute-done((bf16[48,1536]{1,0:T(8,128)(2,1)S(1)}, bf16[48,1536]{1,0:T(8,128)(2,1)S(1)}, u32[]{:S(2)}, u32[]{:S(2)}) %collective-permute-start.41) | collective-permute-done | bytes 147488 | tf_op jit(solution)/shard_map/ppermute | solution.py:1026
  170.1 9.1 %collective-permute-done.43 = bf16[128,768]{1,0:T(8,128)(2,1)} collective-permute-done((bf16[128,768]{1,0:T(8,128)(2,1)S(1)}, bf16[128,768]{1,0:T(8,128)(2,1)}, u32[]{:S(2)}, u32[]{:S(2)}) %collective-permute-start.43) | collective-permute-done | bytes 196640 | tf_op jit(solution)/shard_map/ppermute | solution.py:996
  179.4 2.5 %collective-permute-start.46 = (bf16[64,1536]{1,0:T(8,128)(2,1)S(1)}, bf16[64,1536]{1,0:T(8,128)(2,1)S(1)}, u32[]{:S(2)}, u32[]{:S(2)}) collective-permute-start(bf16[64,1536]{1,0:T(8,128)(2,1)S(1)} %get-tuple-element.321), channel_id=1, source_target_pairs={{0,4},{2,6},{4,0},{6,2},{1,5},{3,7},{5,1},{7,3},{8,12},{10,14},{12... | collective-permute-start | bytes 589832 | tf_op jit(solution)/shard_map/ppermute | solution.py:1022
  181.9 1.5 collective-permute-start.50
  183.4 2.0 collective-permute-start.51
  185.5 3.6 %collective-permute-done.45.refs_1_ = bf16[64,1536]{1,0:T(8,128)(2,1)S(1)} collective-permute-done((bf16[64,1536]{1,0:T(8,128)(2,1)S(1)}, bf16[64,1536]{1,0:T(8,128)(2,1)S(1)}, u32[]{:S(2)}, u32[]{:S(2)}) %collective-permute-start.45) | collective-permute-done | bytes 196640 | tf_op jit(solution)/shard_map/ppermute | solution.py:1022
  189.1 1.6 collective-permute-start.48
  190.6 5.6 %collective-permute-done.46.refs_2_ = bf16[64,1536]{1,0:T(8,128)(2,1)S(1)} collective-permute-done((bf16[64,1536]{1,0:T(8,128)(2,1)S(1)}, bf16[64,1536]{1,0:T(8,128)(2,1)S(1)}, u32[]{:S(2)}, u32[]{:S(2)}) %collective-permute-start.46) | collective-permute-done | bytes 196640 | tf_op jit(solution)/shard_map/ppermute | solution.py:1022
  196.2 1.6 collective-permute-start.49
  197.8 1.3 maximum_select_fusion.5
  199.0 2.5 %collective-permute-done.47.refs_3_ = bf16[64,1536]{1,0:T(8,128)(2,1)S(1)} collective-permute-done((bf16[64,1536]{1,0:T(8,128)(2,1)S(1)}, bf16[64,1536]{1,0:T(8,128)(2,1)S(1)}, u32[]{:S(2)}, u32[]{:S(2)}) %collective-permute-start.47) | collective-permute-done | bytes 196640 | tf_op jit(solution)/shard_map/ppermute | solution.py:1022
  203.9 1.3 collective-permute-start.52
  205.2 1.1 fusion.2
  207.2 1.4 reverse_select_fusion
  208.6 2.8 %convert_bitcast_fusion = (f32[1536,192]{0,1:T(8,128)}, f32[192,1536]{1,0:T(8,128)}) fusion(bf16[96,1536]{1,0:T(8,128)(2,1)S(1)} %get-tuple-element.339, bf16[96,1536]{1,0:T(8,128)(2,1)} %collective-permute-done.40, pred[]{:T(512)S(6)} %eq.16, bf16[96,1536]{1,0:T(8,128)(2,1)S(1)} %collective-permute-done.51, bf16[96,1536]{1,0:T(8,128)(2,1)S(1)} %maximum_select_fusion.6), kind=kLoop, calls=%fused_computation.1 | loop fusion | flops 5898240 | bytes 3538945 | tf_op jit(solution)/shard_map/transpose | solution.py:1225
  212.7 3.5 %collective-permute-done.53.c = bf16[48,1536]{1,0:T(8,128)(2,1)S(1)} collective-permute-done((bf16[48,1536]{1,0:T(8,128)(2,1)S(1)}, bf16[48,1536]{1,0:T(8,128)(2,1)S(1)}, u32[]{:S(2)}, u32[]{:S(2)}) %collective-permute-start.53) | collective-permute-done | bytes 147488 | tf_op jit(solution)/shard_map/ppermute | solution.py:1022
  216.2 1.0 shard_map.323
  (147 shorter events, 22.9 us)
Async XLA Ops:
  0.8 13.4 %copy-start.12 = (bf16[768]{0:T(1024)(128)(2,1)S(1)}, bf16[768]{0:T(1024)(128)(2,1)}, u32[]{:S(2)}) copy-start(bf16[768]{0:T(1024)(128)(2,1)} %param.20) | copy-start | bytes 4612
  0.8 13.4 %copy-start.13 = (bf16[768]{0:T(1024)(128)(2,1)S(1)}, bf16[768]{0:T(1024)(128)(2,1)}, u32[]{:S(2)}) copy-start(bf16[768]{0:T(1024)(128)(2,1)} %param.21) | copy-start | bytes 4612
  0.8 20.0 %copy-start.3 = (bf16[2,256,768]{2,1,0:T(8,128)(2,1)S(1)}, bf16[2,256,768]{2,1,0:T(8,128)(2,1)}, u32[]{:S(2)}) copy-start(bf16[2,256,768]{2,1,0:T(8,128)(2,1)} %param.35) | copy-start | bytes 2359300
  2.3 21.4 %copy-start = (bf16[1536,192]{0,1:T(8,128)(2,1)S(1)}, bf16[1536,192]{0,1:T(8,128)(2,1)}, u32[]{:S(2)}) copy-start(bf16[1536,192]{0,1:T(8,128)(2,1)} %param.33) | copy-start | bytes 1769476
  2.4 16.3 %collective-permute-start.3 = (bf16[192,1152]{1,0:T(8,128)(2,1)S(1)}, bf16[192,1152]{1,0:T(8,128)(2,1)S(1)}, u32[]{:S(2)}, u32[]{:S(2)}) collective-permute-start(bf16[192,1152]{1,0:T(8,128)(2,1)S(1)} %constant_dynamic-update-slice_fusion.a), channel_id=1, source_target_pairs={{0,8},{8,0},{16,24},{24,16},{1,9},{9,1},{17,25},{25,17},{2,10},{10... | collective-permute-start | bytes 1327112 | tf_op jit(solution)/shard_map/ppermute | solution.py:977
  2.9 15.8 %collective-permute-start.2 = (bf16[192,1152]{1,0:T(8,128)(2,1)S(1)}, bf16[192,1152]{1,0:T(8,128)(2,1)}, u32[]{:S(2)}, u32[]{:S(2)}) collective-permute-start(bf16[192,1152]{1,0:T(8,128)(2,1)S(1)} %constant_dynamic-update-slice_fusion.a), channel_id=1, source_target_pairs={{0,16},{8,24},{16,0},{24,8},{1,17},{9,25},{17,1},{25,9},{2,18},{10... | collective-permute-start | bytes 1327112 | tf_op jit(solution)/shard_map/ppermute | solution.py:977
  5.4 13.2 %collective-permute-start = (bf16[128,768]{1,0:T(8,128)(2,1)S(1)}, bf16[128,768]{1,0:T(8,128)(2,1)S(1)}, u32[]{:S(2)}, u32[]{:S(2)}) collective-permute-start(bf16[128,768]{1,0:T(8,128)(2,1)S(1)} %get-tuple-element.185), channel_id=1, source_target_pairs={{0,0},{2,2},{8,4},{10,6},{4,8},{6,10},{12,12},{14,14},{16,16},{18,... | collective-permute-start | bytes 589832 | tf_op jit(solution)/shard_map/ppermute | solution.py:996
  6.1 12.5 %collective-permute-start.1 = (bf16[128,768]{1,0:T(8,128)(2,1)S(1)}, bf16[128,768]{1,0:T(8,128)(2,1)}, u32[]{:S(2)}, u32[]{:S(2)}) collective-permute-start(bf16[128,768]{1,0:T(8,128)(2,1)S(1)} %get-tuple-element.186), channel_id=1, source_target_pairs={{2,0},{0,2},{10,4},{8,6},{6,8},{4,10},{14,12},{12,14},{18,16},{16,... | collective-permute-start | bytes 589832 | tf_op jit(solution)/shard_map/ppermute | solution.py:996
  7.8 4.3 %collective-permute-start.5 = (s32[2]{0:T(128)S(1)}, s32[2]{0:T(128)S(1)}, u32[]{:S(2)}, u32[]{:S(2)}) collective-permute-start(s32[2]{0:T(128)S(1)} %copy-done.20), channel_id=1, source_target_pairs={{0,8},{8,0},{16,24},{24,16},{1,9},{9,1},{17,25},{25,17},{2,10},{10... | collective-permute-start | bytes 32 | tf_op jit(solution)/shard_map/ppermute | solution.py:977
  12.6 6.1 %collective-permute-start.4 = (bf16[192,384]{1,0:T(8,128)(2,1)S(1)}, bf16[192,384]{1,0:T(8,128)(2,1)S(1)}, u32[]{:S(2)}, u32[]{:S(2)}) collective-permute-start(bf16[192,384]{1,0:T(8,128)(2,1)S(1)} %bitcast.36), channel_id=1, source_target_pairs={{0,1},{1,0},{2,3},{3,2},{4,5},{5,4},{6,7},{7,6},{8,9},{9,8},{10,11... | collective-permute-start | bytes 442376 | tf_op jit(solution)/shard_map/ppermute | solution.py:981
  18.7 7.9 %collective-permute-start.6 = (bf16[128,768]{1,0:T(8,128)(2,1)S(1)}, bf16[128,768]{1,0:T(8,128)(2,1)S(1)}, u32[]{:S(2)}, u32[]{:S(2)}) collective-permute-start(bf16[128,768]{1,0:T(8,128)(2,1)S(1)} %collective-permute-done.own0), channel_id=1, source_target_pairs={{0,1},{1,0},{2,3},{3,2},{4,5},{5,4},{6,7},{7,6},{8,9},{9,8},{10,11... | collective-permute-start | bytes 589832 | tf_op jit(solution)/shard_map/ppermute | solution.py:981
  20.2 11.3 %collective-permute-start.7 = (bf16[128,768]{1,0:T(8,128)(2,1)}, bf16[128,768]{1,0:T(8,128)(2,1)}, u32[]{:S(2)}, u32[]{:S(2)}) collective-permute-start(bf16[128,768]{1,0:T(8,128)(2,1)} %collective-permute-done.1.own1), channel_id=1, source_target_pairs={{0,1},{1,0},{2,3},{3,2},{4,5},{5,4},{6,7},{7,6},{8,9},{9,8},{10,11... | collective-permute-start | bytes 589832 | tf_op jit(solution)/shard_map/ppermute | solution.py:981
  21.6 10.0 %collective-permute-start.11 = (bf16[128,768]{1,0:T(8,128)(2,1)}, bf16[128,768]{1,0:T(8,128)(2,1)S(1)}, u32[]{:S(2)}, u32[]{:S(2)}) collective-permute-start(bf16[128,768]{1,0:T(8,128)(2,1)} %get-tuple-element.382), channel_id=1, source_target_pairs={{2,0},{0,2},{10,4},{8,6},{6,8},{4,10},{14,12},{12,14},{18,16},{16,... | collective-permute-start | bytes 589832 | tf_op jit(solution)/shard_map/ppermute | solution.py:996
  22.1 9.4 %collective-permute-start.10 = (bf16[128,768]{1,0:T(8,128)(2,1)}, bf16[128,768]{1,0:T(8,128)(2,1)S(1)}, u32[]{:S(2)}, u32[]{:S(2)}) collective-permute-start(bf16[128,768]{1,0:T(8,128)(2,1)} %get-tuple-element.383), channel_id=1, source_target_pairs={{0,0},{2,2},{8,4},{10,6},{4,8},{6,10},{12,12},{14,14},{16,16},{18,... | collective-permute-start | bytes 589832 | tf_op jit(solution)/shard_map/ppermute | solution.py:996
  23.7 13.4 %collective-permute-start.9 = (bf16[192,1536]{1,0:T(8,128)(2,1)S(1)}, bf16[192,1536]{1,0:T(8,128)(2,1)S(1)}, u32[]{:S(2)}, u32[]{:S(2)}) collective-permute-start(bf16[192,1536]{1,0:T(8,128)(2,1)S(1)} %bitcast.26), channel_id=1, source_target_pairs={{0,16},{8,24},{16,0},{24,8},{1,17},{9,25},{17,1},{25,9},{2,18},{10... | collective-permute-start | bytes 1769480 | tf_op jit(solution)/shard_map/ppermute | solution.py:977
  27.2 4.4 %collective-permute-start.8 = (bf16[192,1152]{1,0:T(8,128)(2,1)}, bf16[192,1152]{1,0:T(8,128)(2,1)}, u32[]{:S(2)}, u32[]{:S(2)}) collective-permute-start(bf16[192,1152]{1,0:T(8,128)(2,1)} %collective-permute-done.2.c), channel_id=1, source_target_pairs={{0,8},{8,0},{16,24},{24,16},{1,9},{9,1},{17,25},{25,17},{2,10},{10... | collective-permute-start | bytes 1327112 | tf_op jit(solution)/shard_map/ppermute | solution.py:977
  41.1 5.2 %collective-permute-start.12 = (bf16[512,768]{1,0:T(8,128)(2,1)S(1)}, bf16[512,768]{1,0:T(8,128)(2,1)S(1)}, u32[]{:S(2)}, u32[]{:S(2)}) collective-permute-start(bf16[512,768]{1,0:T(8,128)(2,1)S(1)} %get-tuple-element.211.own_ref), channel_id=1, source_target_pairs={{0,8},{8,0},{16,24},{24,16},{1,9},{9,1},{17,25},{25,17},{2,10},{10... | collective-permute-start | bytes 2359304 | tf_op jit(solution)/shard_map/ppermute | solution.py:977
  43.8 9.6 %collective-permute-start.13 = (bf16[128,768]{1,0:T(8,128)(2,1)S(1)}, bf16[128,768]{1,0:T(8,128)(2,1)S(1)}, u32[]{:S(2)}, u32[]{:S(2)}) collective-permute-start(bf16[128,768]{1,0:T(8,128)(2,1)S(1)} %collective-permute-done.10.top0), channel_id=1, source_target_pairs={{0,1},{1,0},{2,3},{3,2},{4,5},{5,4},{6,7},{7,6},{8,9},{9,8},{10,11... | collective-permute-start | bytes 589832 | tf_op jit(solution)/shard_map/ppermute | solution.py:981
  45.3 9.6 %collective-permute-start.14 = (bf16[128,768]{1,0:T(8,128)(2,1)S(1)}, bf16[128,768]{1,0:T(8,128)(2,1)S(1)}, u32[]{:S(2)}, u32[]{:S(2)}) collective-permute-start(bf16[128,768]{1,0:T(8,128)(2,1)S(1)} %collective-permute-done.11.top1), channel_id=1, source_target_pairs={{0,1},{1,0},{2,3},{3,2},{4,5},{5,4},{6,7},{7,6},{8,9},{9,8},{10,11... | collective-permute-start | bytes 589832 | tf_op jit(solution)/shard_map/ppermute | solution.py:981
  45.8 21.1 %collective-permute-start.17 = (bf16[192,2304]{1,0:T(8,128)(2,1)S(1)}, bf16[192,2304]{1,0:T(8,128)(2,1)S(1)}, u32[]{:S(2)}, u32[]{:S(2)}) collective-permute-start(bf16[192,2304]{1,0:T(8,128)(2,1)S(1)} %pad_maximum_fusion.pa), channel_id=1, source_target_pairs={{0,16},{8,24},{16,0},{24,8},{1,17},{9,25},{17,1},{25,9},{2,18},{10... | collective-permute-start | bytes 2654216 | tf_op jit(solution)/shard_map/ppermute | solution.py:977
  46.3 20.7 %copy-start.14 = (bf16[768]{0:T(1024)(128)(2,1)S(1)}, bf16[768]{0:T(1024)(128)(2,1)}, u32[]{:S(2)}) copy-start(bf16[768]{0:T(1024)(128)(2,1)} %param.29) | copy-start | bytes 4612
  46.3 20.7 %copy-start.15 = (bf16[768]{0:T(1024)(128)(2,1)S(1)}, bf16[768]{0:T(1024)(128)(2,1)}, u32[]{:S(2)}) copy-start(bf16[768]{0:T(1024)(128)(2,1)} %param.28) | copy-start | bytes 4612
  46.3 20.7 %copy-start.16 = (bf16[768]{0:T(1024)(128)(2,1)S(1)}, bf16[768]{0:T(1024)(128)(2,1)}, u32[]{:S(2)}) copy-start(bf16[768]{0:T(1024)(128)(2,1)} %param.30) | copy-start | bytes 4612
  46.4 20.7 %copy-start.17 = (bf16[768]{0:T(1024)(128)(2,1)S(1)}, bf16[768]{0:T(1024)(128)(2,1)}, u32[]{:S(2)}) copy-start(bf16[768]{0:T(1024)(128)(2,1)} %param.34) | copy-start | bytes 4612
  46.4 20.7 %copy-start.11 = (bf16[1536]{0:T(1024)(128)(2,1)S(1)}, bf16[1536]{0:T(1024)(128)(2,1)}, u32[]{:S(2)}) copy-start(bf16[1536]{0:T(1024)(128)(2,1)} %param.32) | copy-start | bytes 9220
  54.9 12.1 %collective-permute-start.16 = (bf16[192,2304]{1,0:T(8,128)(2,1)S(1)}, bf16[192,2304]{1,0:T(8,128)(2,1)S(1)}, u32[]{:S(2)}, u32[]{:S(2)}) collective-permute-start(bf16[192,2304]{1,0:T(8,128)(2,1)S(1)} %pad_maximum_fusion.pa), channel_id=1, source_target_pairs={{0,8},{8,0},{16,24},{24,16},{1,9},{9,1},{17,25},{25,17},{2,10},{10... | collective-permute-start | bytes 2654216 | tf_op jit(solution)/shard_map/ppermute | solution.py:977
  54.9 12.0 %collective-permute-start.18 = (bf16[192,1536]{1,0:T(8,128)(2,1)S(1)}, bf16[192,1536]{1,0:T(8,128)(2,1)S(1)}, u32[]{:S(2)}, u32[]{:S(2)}) collective-permute-start(bf16[192,1536]{1,0:T(8,128)(2,1)S(1)} %bitcast.27), channel_id=1, source_target_pairs={{0,8},{8,0},{16,24},{24,16},{1,9},{9,1},{17,25},{25,17},{2,10},{10... | collective-permute-start | bytes 1769480 | tf_op jit(solution)/shard_map/ppermute | solution.py:977
  55.4 11.5 %collective-permute-start.19 = (bf16[192,1536]{1,0:T(8,128)(2,1)S(1)}, bf16[192,1536]{1,0:T(8,128)(2,1)S(1)}, u32[]{:S(2)}, u32[]{:S(2)}) collective-permute-start(bf16[192,1536]{1,0:T(8,128)(2,1)S(1)} %collective-permute-done.9.dc), channel_id=1, source_target_pairs={{0,8},{8,0},{16,24},{24,16},{1,9},{9,1},{17,25},{25,17},{2,10},{10... | collective-permute-start | bytes 1769480 | tf_op jit(solution)/shard_map/ppermute | solution.py:977
  55.4 11.5 %collective-permute-start.15 = (bf16[512,384]{1,0:T(8,128)(2,1)S(1)}, bf16[512,384]{1,0:T(8,128)(2,1)S(1)}, u32[]{:S(2)}, u32[]{:S(2)}) collective-permute-start(bf16[512,384]{1,0:T(8,128)(2,1)S(1)} %get-tuple-element.217.own_ref.out_ref.refs_4_), channel_id=1, source_target_pairs={{0,1},{1,0},{2,3},{3,2},{4,5},{5,4},{6,7},{7,6},{8,9},{9,8},{10,11... | collective-permute-start | bytes 1179656 | tf_op jit(solution)/shard_map/ppermute | solution.py:981
  66.9 2.5 %collective-permute-start.20 = (bf16[192,2304]{1,0:T(8,128)(2,1)S(1)}, bf16[192,2304]{1,0:T(8,128)(2,1)S(1)}, u32[]{:S(2)}, u32[]{:S(2)}) collective-permute-start(bf16[192,2304]{1,0:T(8,128)(2,1)S(1)} %collective-permute-done.17.pc), channel_id=1, source_target_pairs={{0,8},{8,0},{16,24},{24,16},{1,9},{9,1},{17,25},{25,17},{2,10},{10... | collective-permute-start | bytes 2654216 | tf_op jit(solution)/shard_map/ppermute | solution.py:977
  80.3 11.2 %collective-permute-start.21 = (bf16[256,768]{1,0:T(8,128)(2,1)S(1)}, bf16[256,768]{1,0:T(8,128)(2,1)S(1)}, u32[]{:S(2)}, u32[]{:S(2)}) collective-permute-start(bf16[256,768]{1,0:T(8,128)(2,1)S(1)} %get-tuple-element.234), channel_id=1, source_target_pairs={{0,1},{1,0},{2,3},{3,2},{4,5},{5,4},{6,7},{7,6},{8,9},{9,8},{10,11... | collective-permute-start | bytes 1179656 | tf_op jit(solution)/shard_map/ppermute | solution.py:981
  91.5 2.8 %collective-permute-start.22 = (bf16[384,1536]{1,0:T(8,128)(2,1)S(1)}, bf16[384,1536]{1,0:T(8,128)(2,1)S(1)}, u32[]{:S(2)}, u32[]{:S(2)}) collective-permute-start(bf16[384,1536]{1,0:T(8,128)(2,1)S(1)} %get-tuple-element.245), channel_id=1, source_target_pairs={{0,8},{8,0},{16,24},{24,16},{1,9},{9,1},{17,25},{25,17},{2,10},{10... | collective-permute-start | bytes 3538952 | tf_op jit(solution)/shard_map/ppermute | solution.py:977
  94.4 3.1 %collective-permute-start.25 = (bf16[384,1536]{1,0:T(8,128)(2,1)S(1)}, bf16[384,1536]{1,0:T(8,128)(2,1)S(1)}, u32[]{:S(2)}, u32[]{:S(2)}) collective-permute-start(bf16[384,1536]{1,0:T(8,128)(2,1)S(1)} %get-tuple-element.253), channel_id=1, source_target_pairs={{0,8},{8,0},{16,24},{24,16},{1,9},{9,1},{17,25},{25,17},{2,10},{10... | collective-permute-start | bytes 3538952 | tf_op jit(solution)/shard_map/ppermute | solution.py:977
  94.6 15.7 %collective-permute-start.24 = (bf16[192,1536]{1,0:T(8,128)(2,1)S(1)}, bf16[192,1536]{1,0:T(8,128)(2,1)S(1)}, u32[]{:S(2)}, u32[]{:S(2)}) collective-permute-start(bf16[192,1536]{1,0:T(8,128)(2,1)S(1)} %get-tuple-element.379), channel_id=1, source_target_pairs={{0,16},{8,24},{16,0},{24,8},{1,17},{9,25},{17,1},{25,9},{2,18},{10... | collective-permute-start | bytes 1769480 | tf_op jit(solution)/shard_map/ppermute | solution.py:977
  95.3 2.5 %collective-permute-start.26 = (bf16[2,128,768]{2,1,0:T(8,128)(2,1)S(1)}, bf16[2,128,768]{2,1,0:T(8,128)(2,1)S(1)}, u32[]{:S(2)}, u32[]{:S(2)}) collective-permute-start(bf16[2,128,768]{2,1,0:T(8,128)(2,1)S(1)} %get-tuple-element.255), channel_id=1, source_target_pairs={{0,0},{2,2},{4,8},{6,10},{8,4},{10,6},{12,12},{14,14},{16,16},{18,... | collective-permute-start | bytes 1179656 | tf_op jit(solution)/shard_map/ppermute | solution.py:996
  95.9 10.8 %collective-permute-start.23 = (bf16[256,768]{1,0:T(8,128)(2,1)S(1)}, bf16[256,768]{1,0:T(8,128)(2,1)S(1)}, u32[]{:S(2)}, u32[]{:S(2)}) collective-permute-start(bf16[256,768]{1,0:T(8,128)(2,1)S(1)} %get-tuple-element.249.d_own_ref.refs_2_), channel_id=1, source_target_pairs={{0,1},{1,0},{2,3},{3,2},{4,5},{5,4},{6,7},{7,6},{8,9},{9,8},{10,11... | collective-permute-start | bytes 1179656 | tf_op jit(solution)/shard_map/ppermute | solution.py:981
  110.4 13.0 %collective-permute-start.27 = (bf16[96,1536]{1,0:T(8,128)(2,1)S(1)}, bf16[96,1536]{1,0:T(8,128)(2,1)S(1)}, u32[]{:S(2)}, u32[]{:S(2)}) collective-permute-start(bf16[96,1536]{1,0:T(8,128)(2,1)S(1)} %get-tuple-element.265), channel_id=1, source_target_pairs={{0,2},{2,0},{4,6},{6,4},{1,3},{3,1},{5,7},{7,5},{8,10},{10,8},{12,... | collective-permute-start | bytes 884744 | tf_op jit(solution)/shard_map/ppermute | solution.py:1026
  111.9 14.4 %collective-permute-start.29 = (bf16[2,128,768]{2,1,0:T(8,128)(2,1)S(1)}, bf16[2,128,768]{2,1,0:T(8,128)(2,1)S(1)}, u32[]{:S(2)}, u32[]{:S(2)}) collective-permute-start(bf16[2,128,768]{2,1,0:T(8,128)(2,1)S(1)} %get-tuple-element.268), channel_id=1, source_target_pairs={{0,2},{2,0},{4,10},{6,8},{8,6},{10,4},{12,14},{14,12},{16,18},{18,... | collective-permute-start | bytes 1179656 | tf_op jit(solution)/shard_map/ppermute | solution.py:996
  112.5 15.5 %collective-permute-start.28 = (bf16[192,1536]{1,0:T(8,128)(2,1)S(1)}, bf16[192,1536]{1,0:T(8,128)(2,1)S(1)}, u32[]{:S(2)}, u32[]{:S(2)}) collective-permute-start(bf16[192,1536]{1,0:T(8,128)(2,1)S(1)} %get-tuple-element.266), channel_id=1, source_target_pairs={{0,16},{8,24},{16,0},{24,8},{1,17},{9,25},{17,1},{25,9},{2,18},{10... | collective-permute-start | bytes 1769480 | tf_op jit(solution)/shard_map/ppermute | solution.py:977
  128.0 2.3 %collective-permute-start.30 = (bf16[512,768]{1,0:T(8,128)(2,1)S(1)}, bf16[512,768]{1,0:T(8,128)(2,1)S(1)}, u32[]{:S(2)}, u32[]{:S(2)}) collective-permute-start(bf16[512,768]{1,0:T(8,128)(2,1)S(1)} %get-tuple-element.269), channel_id=1, source_target_pairs={{0,8},{8,0},{16,24},{24,16},{1,9},{9,1},{17,25},{25,17},{2,10},{10... | collective-permute-start | bytes 2359304 | tf_op jit(solution)/shard_map/ppermute | solution.py:977
  128.1 12.6 %collective-permute-start.32 = (bf16[96,1536]{1,0:T(8,128)(2,1)S(1)}, bf16[96,1536]{1,0:T(8,128)(2,1)S(1)}, u32[]{:S(2)}, u32[]{:S(2)}) collective-permute-start(bf16[96,1536]{1,0:T(8,128)(2,1)S(1)} %get-tuple-element.282), channel_id=1, source_target_pairs={{0,2},{2,0},{4,6},{6,4},{1,3},{3,1},{5,7},{7,5},{8,10},{10,8},{12,... | collective-permute-start | bytes 884744 | tf_op jit(solution)/shard_map/ppermute | solution.py:1026
  129.0 10.1 %collective-permute-start.31 = (bf16[48,1536]{1,0:T(8,128)(2,1)S(1)}, bf16[48,1536]{1,0:T(8,128)(2,1)S(1)}, u32[]{:S(2)}, u32[]{:S(2)}) collective-permute-start(bf16[48,1536]{1,0:T(8,128)(2,1)S(1)} %get-tuple-element.281), channel_id=1, source_target_pairs={{0,4},{2,6},{4,0},{6,2},{1,5},{3,7},{5,1},{7,3},{8,12},{10,14},{12... | collective-permute-start | bytes 442376 | tf_op jit(solution)/shard_map/ppermute | solution.py:1026
  140.7 17.4 %collective-permute-start.33 = (bf16[384,1536]{1,0:T(8,128)(2,1)S(1)}, bf16[384,1536]{1,0:T(8,128)(2,1)S(1)}, u32[]{:S(2)}, u32[]{:S(2)}) collective-permute-start(bf16[384,1536]{1,0:T(8,128)(2,1)S(1)} %get-tuple-element.283), channel_id=1, source_target_pairs={{0,8},{8,0},{16,24},{24,16},{1,9},{9,1},{17,25},{25,17},{2,10},{10... | collective-permute-start | bytes 3538952 | tf_op jit(solution)/shard_map/ppermute | solution.py:977
  140.7 17.4 %collective-permute-start.34 = (bf16[256,768]{1,0:T(8,128)(2,1)S(1)}, bf16[256,768]{1,0:T(8,128)(2,1)S(1)}, u32[]{:S(2)}, u32[]{:S(2)}) collective-permute-start(bf16[256,768]{1,0:T(8,128)(2,1)S(1)} %get-tuple-element.284), channel_id=1, source_target_pairs={{0,1},{1,0},{2,3},{3,2},{4,5},{5,4},{6,7},{7,6},{8,9},{9,8},{10,11... | collective-permute-start | bytes 1179656 | tf_op jit(solution)/shard_map/ppermute | solution.py:981
  142.3 12.8 %collective-permute-start.36 = (bf16[48,1536]{1,0:T(8,128)(2,1)S(1)}, bf16[48,1536]{1,0:T(8,128)(2,1)S(1)}, u32[]{:S(2)}, u32[]{:S(2)}) collective-permute-start(bf16[48,1536]{1,0:T(8,128)(2,1)S(1)} %get-tuple-element.290), channel_id=1, source_target_pairs={{0,4},{2,6},{4,0},{6,2},{1,5},{3,7},{5,1},{7,3},{8,12},{10,14},{12... | collective-permute-start | bytes 442376 | tf_op jit(solution)/shard_map/ppermute | solution.py:1026
  144.1 14.0 %collective-permute-start.35 = (bf16[48,1536]{1,0:T(8,128)(2,1)S(1)}, bf16[48,1536]{1,0:T(8,128)(2,1)S(1)}, u32[]{:S(2)}, u32[]{:S(2)}) collective-permute-start(bf16[48,1536]{1,0:T(8,128)(2,1)S(1)} %get-tuple-element.289.mine_ref), channel_id=1, source_target_pairs={{0,4},{2,6},{4,0},{6,2},{1,5},{3,7},{5,1},{7,3},{8,12},{10,14},{12... | collective-permute-start | bytes 442376 | tf_op jit(solution)/shard_map/ppermute | solution.py:1026
  145.3 7.5 %collective-permute-start.37 = (f32[5,768]{1,0:T(8,128)S(1)}, f32[5,768]{1,0:T(8,128)S(1)}, u32[]{:S(2)}, u32[]{:S(2)}) collective-permute-start(f32[5,768]{1,0:T(8,128)S(1)} %get-tuple-element.291.mine_ref), channel_id=1, source_target_pairs={{0,1},{1,0},{2,3},{3,2},{4,5},{5,4},{6,7},{7,6},{8,9},{9,8},{10,11... | collective-permute-start | bytes 46088 | tf_op jit(solution)/shard_map/ppermute | solution.py:981
  158.2 1.3 collective-permute-start.38
  159.6 19.6 %collective-permute-start.39 = (bf16[208,1536]{1,0:T(8,128)(2,1)S(1)}, bf16[208,1536]{1,0:T(8,128)(2,1)S(1)}, u32[]{:S(2)}, u32[]{:S(2)}) collective-permute-start(bf16[208,1536]{1,0:T(8,128)(2,1)S(1)} %get-tuple-element.306), channel_id=1, source_target_pairs={{0,16},{8,24},{16,0},{24,8},{1,17},{9,25},{17,1},{25,9},{2,18},{10... | collective-permute-start | bytes 1916936 | tf_op jit(solution)/shard_map/ppermute | solution.py:977
  160.2 19.0 %collective-permute-start.44 = (bf16[2,128,768]{2,1,0:T(8,128)(2,1)S(1)}, bf16[2,128,768]{2,1,0:T(8,128)(2,1)}, u32[]{:S(2)}, u32[]{:S(2)}) collective-permute-start(bf16[2,128,768]{2,1,0:T(8,128)(2,1)S(1)} %collective-permute-done.26), channel_id=1, source_target_pairs={{0,1},{1,0},{2,3},{3,2},{4,5},{5,4},{6,7},{7,6},{8,9},{9,8},{10,11... | collective-permute-start | bytes 1179656 | tf_op jit(solution)/shard_map/ppermute | solution.py:981
  160.8 8.7 %collective-permute-start.41 = (bf16[48,1536]{1,0:T(8,128)(2,1)S(1)}, bf16[48,1536]{1,0:T(8,128)(2,1)S(1)}, u32[]{:S(2)}, u32[]{:S(2)}) collective-permute-start(bf16[48,1536]{1,0:T(8,128)(2,1)S(1)} %get-tuple-element.311), channel_id=1, source_target_pairs={{0,4},{2,6},{4,0},{6,2},{1,5},{3,7},{5,1},{7,3},{8,12},{10,14},{12... | collective-permute-start | bytes 442376 | tf_op jit(solution)/shard_map/ppermute | solution.py:1026
  160.9 18.4 %collective-permute-start.40 = (bf16[96,1536]{1,0:T(8,128)(2,1)S(1)}, bf16[96,1536]{1,0:T(8,128)(2,1)}, u32[]{:S(2)}, u32[]{:S(2)}) collective-permute-start(bf16[96,1536]{1,0:T(8,128)(2,1)S(1)} %get-tuple-element.339), channel_id=1, source_target_pairs={{0,2},{2,0},{4,6},{6,4},{1,3},{3,1},{5,7},{7,5},{8,10},{10,8},{12,... | collective-permute-start | bytes 884744 | tf_op jit(solution)/shard_map/ppermute | solution.py:1026
  163.1 7.0 %collective-permute-start.42 = (bf16[128,768]{1,0:T(8,128)(2,1)S(1)}, bf16[128,768]{1,0:T(8,128)(2,1)}, u32[]{:S(2)}, u32[]{:S(2)}) collective-permute-start(bf16[128,768]{1,0:T(8,128)(2,1)S(1)} %get-tuple-element.313), channel_id=1, source_target_pairs={{0,0},{2,2},{4,8},{6,10},{8,4},{10,6},{12,12},{14,14},{16,16},{18,... | collective-permute-start | bytes 589832 | tf_op jit(solution)/shard_map/ppermute | solution.py:996
  170.1 9.1 %collective-permute-start.43 = (bf16[128,768]{1,0:T(8,128)(2,1)S(1)}, bf16[128,768]{1,0:T(8,128)(2,1)}, u32[]{:S(2)}, u32[]{:S(2)}) collective-permute-start(bf16[128,768]{1,0:T(8,128)(2,1)S(1)} %get-tuple-element.314), channel_id=1, source_target_pairs={{0,2},{2,0},{4,10},{6,8},{8,6},{10,4},{12,14},{14,12},{16,18},{18,... | collective-permute-start | bytes 589832 | tf_op jit(solution)/shard_map/ppermute | solution.py:996
  179.3 9.7 %collective-permute-start.45 = (bf16[64,1536]{1,0:T(8,128)(2,1)S(1)}, bf16[64,1536]{1,0:T(8,128)(2,1)S(1)}, u32[]{:S(2)}, u32[]{:S(2)}) collective-permute-start(bf16[64,1536]{1,0:T(8,128)(2,1)S(1)} %get-tuple-element.318), channel_id=1, source_target_pairs={{0,2},{2,4},{4,6},{6,0},{1,3},{3,5},{5,7},{7,1},{8,10},{10,12},{12... | collective-permute-start | bytes 589832 | tf_op jit(solution)/shard_map/ppermute | solution.py:1022
  179.4 16.8 %collective-permute-start.46 = (bf16[64,1536]{1,0:T(8,128)(2,1)S(1)}, bf16[64,1536]{1,0:T(8,128)(2,1)S(1)}, u32[]{:S(2)}, u32[]{:S(2)}) collective-permute-start(bf16[64,1536]{1,0:T(8,128)(2,1)S(1)} %get-tuple-element.321), channel_id=1, source_target_pairs={{0,4},{2,6},{4,0},{6,2},{1,5},{3,7},{5,1},{7,3},{8,12},{10,14},{12... | collective-permute-start | bytes 589832 | tf_op jit(solution)/shard_map/ppermute | solution.py:1022
  181.9 20.2 %collective-permute-start.50 = (bf16[2,128,768]{2,1,0:T(8,128)(2,1)S(1)}, bf16[2,128,768]{2,1,0:T(8,128)(2,1)S(1)}, u32[]{:S(2)}, u32[]{:S(2)}) collective-permute-start(bf16[2,128,768]{2,1,0:T(8,128)(2,1)S(1)} %collective-permute-done.29), channel_id=1, source_target_pairs={{0,1},{1,0},{2,3},{3,2},{4,5},{5,4},{6,7},{7,6},{8,9},{9,8},{10,11... | collective-permute-start | bytes 1179656 | tf_op jit(solution)/shard_map/ppermute | solution.py:981
  183.4 18.6 %collective-permute-start.51 = (bf16[96,1536]{1,0:T(8,128)(2,1)S(1)}, bf16[96,1536]{1,0:T(8,128)(2,1)S(1)}, u32[]{:S(2)}, u32[]{:S(2)}) collective-permute-start(bf16[96,1536]{1,0:T(8,128)(2,1)S(1)} %maximum_select_fusion.6), channel_id=1, source_target_pairs={{0,2},{2,0},{4,6},{6,4},{1,3},{3,1},{5,7},{7,5},{8,10},{10,8},{12,... | collective-permute-start | bytes 884744 | tf_op jit(solution)/shard_map/ppermute | solution.py:1026
  185.4 16.1 %collective-permute-start.47 = (bf16[64,1536]{1,0:T(8,128)(2,1)S(1)}, bf16[64,1536]{1,0:T(8,128)(2,1)S(1)}, u32[]{:S(2)}, u32[]{:S(2)}) collective-permute-start(bf16[64,1536]{1,0:T(8,128)(2,1)S(1)} %get-tuple-element.322), channel_id=1, source_target_pairs={{0,6},{2,0},{4,2},{6,4},{1,7},{3,1},{5,3},{7,5},{8,14},{10,8},{12,... | collective-permute-start | bytes 589832 | tf_op jit(solution)/shard_map/ppermute | solution.py:1022
  189.1 12.5 %collective-permute-start.48 = (bf16[128,768]{1,0:T(8,128)(2,1)}, bf16[128,768]{1,0:T(8,128)(2,1)S(1)}, u32[]{:S(2)}, u32[]{:S(2)}) collective-permute-start(bf16[128,768]{1,0:T(8,128)(2,1)} %collective-permute-done.42), channel_id=1, source_target_pairs={{0,1},{1,0},{2,3},{3,2},{4,5},{5,4},{6,7},{7,6},{8,9},{9,8},{10,11... | collective-permute-start | bytes 589832 | tf_op jit(solution)/shard_map/ppermute | solution.py:981
  196.2 5.9 %collective-permute-start.49 = (bf16[128,768]{1,0:T(8,128)(2,1)}, bf16[128,768]{1,0:T(8,128)(2,1)S(1)}, u32[]{:S(2)}, u32[]{:S(2)}) collective-permute-start(bf16[128,768]{1,0:T(8,128)(2,1)} %collective-permute-done.43), channel_id=1, source_target_pairs={{0,1},{1,0},{2,3},{3,2},{4,5},{5,4},{6,7},{7,6},{8,9},{9,8},{10,11... | collective-permute-start | bytes 589832 | tf_op jit(solution)/shard_map/ppermute | solution.py:981
  202.2 10.5 %collective-permute-start.54 = (bf16[48,1536]{1,0:T(8,128)(2,1)S(1)}, bf16[48,1536]{1,0:T(8,128)(2,1)S(1)}, u32[]{:S(2)}, u32[]{:S(2)}) collective-permute-start(bf16[48,1536]{1,0:T(8,128)(2,1)S(1)} %get-tuple-element.343.a), channel_id=1, source_target_pairs={{0,6},{2,0},{4,2},{6,4},{1,7},{3,1},{5,3},{7,5},{8,14},{10,8},{12,... | collective-permute-start | bytes 442376 | tf_op jit(solution)/shard_map/ppermute | solution.py:1022
  203.1 13.1 %collective-permute-start.53 = (bf16[48,1536]{1,0:T(8,128)(2,1)S(1)}, bf16[48,1536]{1,0:T(8,128)(2,1)S(1)}, u32[]{:S(2)}, u32[]{:S(2)}) collective-permute-start(bf16[48,1536]{1,0:T(8,128)(2,1)S(1)} %get-tuple-element.343.a), channel_id=1, source_target_pairs={{0,4},{2,6},{4,0},{6,2},{1,5},{3,7},{5,1},{7,3},{8,12},{10,14},{12... | collective-permute-start | bytes 442376 | tf_op jit(solution)/shard_map/ppermute | solution.py:1022
  203.9 12.2 %collective-permute-start.52 = (bf16[48,1536]{1,0:T(8,128)(2,1)S(1)}, bf16[48,1536]{1,0:T(8,128)(2,1)S(1)}, u32[]{:S(2)}, u32[]{:S(2)}) collective-permute-start(bf16[48,1536]{1,0:T(8,128)(2,1)S(1)} %get-tuple-element.343.a), channel_id=1, source_target_pairs={{0,2},{2,4},{4,6},{6,0},{1,3},{3,5},{5,7},{7,1},{8,10},{10,12},{12... | collective-permute-start | bytes 442376 | tf_op jit(solution)/shard_map/ppermute | solution.py:1022
  (15 other events, 89.2 us)
